TPU v7x, 256 devices: a whole 4x4x8 slice. The times are simulated.
256 devices in a mesh: px: 32 (over y, x, z_hi), py: 8 (over z_lo, core).
Axes of the slice: x: 4, y: 4, z: 8 (z_hi: 2, z_lo: 4; z = z_hi * 4 + z_lo), core: 2. Of those that a mesh axis runs over, the one named last changes fastest.
Arguments:
- levels: int32 [512, 8192], P('px', 'py'), may hold values from 0 to 15
- conv_table: bfloat16 [64, 144], replicated, may hold values from -2 to 2
- conv_bias: float32 [64], replicated, may hold values from -3 to 3
- mix_weight: bfloat16 [64, 64], replicated, may hold values from -0.75 to 0.75
- mix_bias: float32 [64], replicated, may hold values from -3 to 3
- decoder: bfloat16 [5, 40, 64], replicated, may hold values from -0.15625 to 0.15625
- green_rows: float32 [8, 2, 64, 512], P(None, None, None, 'px'), may hold values from -0.25 to 0.25
- green_cols: float32 [8, 2, 64, 8192], P(None, None, None, 'py'), may hold values from -0.0625 to 0.0625
- focal_order: int32 [64], replicated, may hold values from 0 to 63, each once
Outputs:
- focal: float32 [8, 64, 512], P('py', 'px')
Inputs may be any that keep to these rules, and one draw needn't show every extreme that they name: `focal_order`: each of the 64 focal rows appears exactly once.
All inputs are finite; a program needn't handle non-finite values.
Results may differ from a plain program's by a relative error of at most 0.0045.
Values sent between devices are 32-bit elements; how exact they have to be, the bound alone decides.
No kernel may reach another device: no remote copies, remote signals or barrier semaphores. Data moves between devices by JAX's collectives and lax.ppermute only.
A program may use at most 128 MiB of HBM per device.

v0:
```python
import jax
import jax.numpy as jnp
from jax import lax
from jax.experimental import pallas as pl
from jax.experimental.pallas import tpu as pltpu
from jax.sharding import PartitionSpec as P

HIGH = lax.Precision.HIGHEST
F32 = jnp.float32
BF16 = jnp.bfloat16
NT = (((1,), (1,)), ((), ()))
TN = (((0,), (0,)), ((), ()))

ROWS = 16
COLS = 1024
HID = 64
LEVELS = 16
CH = 8
KS = 5
Z = 8
U = 64
V = 64
HALO = 4
ROWS_EXT = ROWS + HALO
SLOT = 64
BLOCK = 4
REL_ORDER = (0, 2, 4, 6, 1, 3, 5, 7)

GELU_A = 0.7978845608028654
GELU_B = GELU_A * 0.044715


def iota(shape, dim):
    return lax.broadcasted_iota(jnp.int32, shape, dim)


def twice_gelu(x):
    return x + x * jnp.tanh(x * (GELU_A + GELU_B * (x * x)))


def split3(x):
    a = lax.reduce_precision(x, 8, 7)
    b = lax.reduce_precision(x - a, 8, 7)
    return a.astype(BF16), b.astype(BF16), (x - a - b).astype(BF16)


def pack_kernel(idx_ref, lev_ref, rows_ref, cols_ref, to_x_ref, to_y_ref, to_d_ref):
    lev = lev_ref[...].astype(F32)
    to_x_ref[:, :COLS] = lev[8:, :]
    pick = (iota((8, ROWS), 1) == iota((8, ROWS), 0) + (ROWS - 8)).astype(F32)
    rows = rows_ref[...].reshape(2 * U, ROWS)
    to_x_ref[:, COLS:] = lax.dot_general(
        pick, rows, NT, precision=HIGH, preferred_element_type=F32
    )
    to_d_ref[...] = lev[8:, COLS - 128 :]
    to_y_ref[:ROWS, :] = lev[:, COLS - 128 :]
    pick = (iota((8, 128), 1) == iota((8, 128), 0) + (128 - HALO)).astype(F32)
    cols = cols_ref[...].reshape(Z * 2 * V, 128)
    edge = lax.dot_general(pick, cols, NT, precision=HIGH, preferred_element_type=F32)
    for z in range(Z):
        to_y_ref[ROWS + HALO * z : ROWS + HALO * (z + 1), :] = edge[
            :HALO, 128 * z : 128 * (z + 1)
        ]


def pack(idx, levels, green_rows, green_cols):
    return pl.pallas_call(
        pack_kernel,
        grid_spec=pltpu.PrefetchScalarGridSpec(
            num_scalar_prefetch=1,
            grid=(1,),
            in_specs=[
                pl.BlockSpec((ROWS, COLS), lambda i, s: (0, 0)),
                pl.BlockSpec((1, 2, U, ROWS), lambda i, s: (s[1], 0, 0, 0)),
                pl.BlockSpec((Z, 2, V, 128), lambda i, s: (0, 0, 0, COLS // 128 - 1)),
            ],
            out_specs=[
                pl.BlockSpec((8, COLS + 128), lambda i, s: (0, 0)),
                pl.BlockSpec((ROWS + Z * HALO, 128), lambda i, s: (0, 0)),
                pl.BlockSpec((8, 128), lambda i, s: (0, 0)),
            ],
        ),
        out_shape=[
            jax.ShapeDtypeStruct((8, COLS + 128), F32),
            jax.ShapeDtypeStruct((ROWS + Z * HALO, 128), F32),
            jax.ShapeDtypeStruct((8, 128), F32),
        ],
        name="pack",
    )(idx, levels, green_rows, green_cols)


def split_kernel(idx_ref, cols_ref, hi_ref, lo_ref):
    x = cols_ref[...].reshape(2 * V, COLS)
    hi = x.astype(BF16)
    hi_ref[0] = hi
    lo_ref[0] = (x - hi.astype(F32)).astype(BF16)


def split_cols(idx, green_cols):
    def plane(g, s):
        rel = jnp.where(g < 4, 2 * g, 2 * g - 7)
        return (s[1] ^ rel, 0, 0, 0)

    return pl.pallas_call(
        split_kernel,
        grid_spec=pltpu.PrefetchScalarGridSpec(
            num_scalar_prefetch=1,
            grid=(Z,),
            in_specs=[pl.BlockSpec((1, 2, V, COLS), plane)],
            out_specs=[pl.BlockSpec((1, 2 * V, COLS), lambda g, s: (g, 0, 0))] * 2,
        ),
        out_shape=[jax.ShapeDtypeStruct((Z, 2 * V, COLS), BF16)] * 2,
        name="split_cols",
    )(idx, green_cols)


def field_kernel(
    idx_ref, lev_ref, from_x_ref, from_y_ref, from_d_ref, conv_ref, mix_ref, dec_ref,
    hi_ref, lo_ref, keep_ref, send_ref,
    ext_ref, hot_ref, hid_ref, feat_ref, nf_ref, edge_ref,
):
    first_y = idx_ref[1] == 0
    main = jnp.concatenate([from_x_ref[:, :COLS], lev_ref[...].astype(F32)], axis=0)
    left = jnp.concatenate([from_d_ref[...], from_y_ref[:ROWS, :]], axis=0)
    ext = jnp.concatenate([left, main], axis=1)
    lane = iota((24, COLS), 1)
    for b in range(3):
        window = pltpu.roll(ext, 3 - b, 1)[:, 128:]
        if b != 1:
            cut = first_y & (lane == (2 if b == 0 else 1))
            window = jnp.where(cut, -1.0, window)
        ext_ref[b] = window
    level_ids = iota((LEVELS, COLS), 0).astype(F32)
    ones = jnp.ones((LEVELS, COLS), BF16)

    def make_hot(q, _):
        for b in range(3):
            row = jnp.broadcast_to(ext_ref[b, pl.ds(q + 5, 1), :], (LEVELS, COLS))
            hot_ref[pl.ds(q * SLOT + b * LEVELS, LEVELS), :] = jnp.where(
                row == level_ids, 1.0, 0.0
            ).astype(BF16)
        hot_ref[pl.ds(q * SLOT + 3 * LEVELS, LEVELS), :] = ones
        return 0

    lax.fori_loop(0, ROWS + 2, make_hot, 0)
    hid_ref[2 * HID :, :] = ones
    feat_ref[: BLOCK * HID, :] = jnp.zeros((BLOCK * HID, COLS), BF16)
    feat_ref[(BLOCK + ROWS) * HID :, :] = jnp.zeros((BLOCK * HID, COLS), BF16)

    def features(i, _):
        pre = jnp.dot(
            conv_ref[jnp.minimum(i, 2)],
            hot_ref[pl.ds(i * 2 * SLOT, 4 * SLOT), :],
            preferred_element_type=F32,
        )
        hid_ref[: 2 * HID, :] = twice_gelu(pre).astype(BF16)
        mixed = jnp.dot(mix_ref[...], hid_ref[...], preferred_element_type=F32)
        feat_ref[pl.ds((BLOCK + 2 * i) * HID, 2 * HID), :] = twice_gelu(mixed).astype(BF16)
        return 0

    lax.fori_loop(0, ROWS // 2, features, 0)

    lane = iota((1, COLS), 1)
    near = iota((1, 128), 1)
    keep_main, keep_edge = [], []
    for s in range(KS):
        k = KS - 1 - s
        ok = lane < COLS - k
        ok = ok & ((lane + k >= 2) | jnp.logical_not(first_y))
        keep_main.append(ok.astype(F32))
        ok = (near >= s) & (near < HALO)
        ok = ok & ((near - s < 2) | jnp.logical_not(first_y))
        keep_edge.append(ok.astype(F32))
    half = BLOCK * CH // 2

    def near_field(i, _):
        taps = jnp.dot(
            dec_ref[jnp.minimum(i, 2)],
            feat_ref[pl.ds(i * BLOCK * HID, 2 * BLOCK * HID), :],
            preferred_element_type=F32,
        )
        acc = jnp.zeros((2 * half, COLS), F32)
        edge = jnp.zeros((2 * half, 128), F32)
        for s in range(KS):
            part = taps[2 * half * s : 2 * half * (s + 1), :]
            k = KS - 1 - s
            moved = part if k == 0 else pltpu.roll(part, COLS - k, 1)
            acc = acc + moved * keep_main[s]
            part = part[:, :128]
            moved = part if s == 0 else pltpu.roll(part, s, 1)
            edge = edge + moved * keep_edge[s]
        hi = acc.astype(BF16)
        lo = (acc - hi.astype(F32)).astype(BF16)
        for k in range(2):
            at = k * ROWS_EXT * 4 + i * half
            nf_ref[pl.ds(at, half), :] = hi[k * half : (k + 1) * half]
            nf_ref[pl.ds(at + ROWS_EXT * CH, half), :] = lo[k * half : (k + 1) * half]
            edge_ref[pl.ds(at, half), :] = edge[k * half : (k + 1) * half]
        return 0

    lax.fori_loop(0, ROWS_EXT // BLOCK, near_field, 0)

    n = ROWS_EXT * CH
    m = n // 2
    lane = iota((1, 128), 1)
    sign = jnp.where(lane < V, -1.0, 1.0)

    for g in range(Z):
        hi = hi_ref[g]
        out = lax.dot_general(nf_ref[...], hi, NT, preferred_element_type=F32)
        out = out[:n] + out[n:]
        out = out + lax.dot_general(nf_ref[:n, :], lo_ref[g], NT, preferred_element_type=F32)
        rel = REL_ORDER[g]
        z = idx_ref[1] ^ rel
        green = from_y_ref[pl.ds(ROWS + HALO * z, HALO), :]
        green = jnp.concatenate([green, jnp.zeros((4, 128), F32)], axis=0)
        out = out + jnp.dot(
            edge_ref[:, :8], green, precision=HIGH, preferred_element_type=F32
        )
        total = out[:m] + sign * pltpu.roll(out[m:], V, 1)
        if g < 4:
            keep_ref[g] = total
        else:
            send_ref[g - 4] = total


def field(idx, levels, from_x, from_y, from_d, conv_w, mix_w, dec_w, hi, lo):
    m = ROWS_EXT * CH // 2
    return pl.pallas_call(
        field_kernel,
        in_specs=[pl.BlockSpec(memory_space=pltpu.SMEM)]
        + [pl.BlockSpec(memory_space=pltpu.VMEM)] * 9,
        out_specs=[pl.BlockSpec(memory_space=pltpu.VMEM)] * 2,
        out_shape=[jax.ShapeDtypeStruct((4, m, 128), F32)] * 2,
        scratch_shapes=[
            pltpu.VMEM((3, 24, COLS), F32),
            pltpu.VMEM(((ROWS + 2) * SLOT, COLS), BF16),
            pltpu.VMEM((2 * HID + LEVELS, COLS), BF16),
            pltpu.VMEM(((ROWS + 2 * BLOCK) * HID, COLS), BF16),
            pltpu.VMEM((2 * ROWS_EXT * CH, COLS), BF16),
            pltpu.VMEM((ROWS_EXT * CH, 128), F32),
        ],
        compiler_params=pltpu.CompilerParams(vmem_limit_bytes=40 << 20),
        name="field",
    )(idx, levels, from_x, from_y, from_d, conv_w, mix_w, dec_w, hi, lo)


def rows_kernel(idx_ref, order_ref, rows_ref, from_x_ref, out_ref):
    n = ROWS_EXT * 4
    own = rows_ref[...].reshape(2 * U, ROWS)
    spread = (iota((ROWS, n), 1) // 4 == iota((ROWS, n), 0) + HALO).astype(F32)
    wide = jnp.dot(own, spread, precision=HIGH, preferred_element_type=F32)
    spread = (iota((8, n), 1) // 4 == iota((8, n), 0) - (8 - HALO)).astype(F32)
    wide = wide + lax.dot_general(
        from_x_ref[:, COLS:], spread, TN, precision=HIGH, preferred_element_type=F32
    )
    pick = (order_ref[...] == iota((U, U * 4), 0)).astype(F32)
    mask = (iota((U * 4, n), 0) % 4 == iota((U * 4, n), 1) % 4).astype(F32)
    for j in range(2):
        out_ref[j] = mask * lax.dot_general(
            pick, wide[j * U : (j + 1) * U], TN, precision=HIGH, preferred_element_type=F32
        )


def row_factors(idx, order, green_rows, from_x):
    n = ROWS_EXT * 4
    return pl.pallas_call(
        rows_kernel,
        grid_spec=pltpu.PrefetchScalarGridSpec(
            num_scalar_prefetch=1,
            grid=(1,),
            in_specs=[
                pl.BlockSpec((1, U * 4), lambda i, s: (0, 0)),
                pl.BlockSpec((1, 2, U, ROWS), lambda i, s: (s[1], 0, 0, 0)),
                pl.BlockSpec((8, COLS + 128), lambda i, s: (0, 0)),
            ],
            out_specs=pl.BlockSpec((2, U * 4, n), lambda i, s: (0, 0, 0)),
        ),
        out_shape=jax.ShapeDtypeStruct((2, U * 4, n), F32),
        name="row_factors",
    )(idx, order, green_rows, from_x)


def focal_kernel(rows_ref, a_ref, b_ref, c_ref, d_ref, out_ref):
    t = (a_ref[...] + b_ref[...]) + (c_ref[...] + d_ref[...])
    re = jnp.dot(rows_ref[0], t, precision=HIGH, preferred_element_type=F32)
    im = jnp.dot(rows_ref[1], t, precision=HIGH, preferred_element_type=F32)
    sign = jnp.where(iota((1, 128), 1) < V, -1.0, 1.0)
    out_ref[...] = (re + sign * pltpu.roll(im, V, 1)).reshape(out_ref.shape)


def focal_share(rows, a, b, c, d):
    return pl.pallas_call(
        focal_kernel,
        in_specs=[pl.BlockSpec(memory_space=pltpu.VMEM)] * 5,
        out_specs=pl.BlockSpec(memory_space=pltpu.VMEM),
        out_shape=jax.ShapeDtypeStruct((U // 2, 8, 128), F32),
        name="focal_share",
    )(rows, a, b, c, d)


def total_kernel(x_ref, out_ref):
    s = jnp.sum(x_ref[...], axis=0)
    for u in range(2):
        for k in range(2):
            for p in range(4):
                at = (k * 4 + p) * V
                out_ref[0, u : u + 1, at : at + V] = s[u * 4 + p : u * 4 + p + 1, k * V : (k + 1) * V]


def total(parts):
    return pl.pallas_call(
        total_kernel,
        in_specs=[pl.BlockSpec(memory_space=pltpu.VMEM)],
        out_specs=pl.BlockSpec(memory_space=pltpu.VMEM),
        out_shape=jax.ShapeDtypeStruct((1, 2, 8 * V), F32),
        name="total",
    )(parts)


def conv_weights(conv_table, conv_bias, first_x):
    table = conv_table.reshape(HID, 3, 3 * LEVELS)
    bias = jnp.stack(split3(conv_bias), axis=1)
    bias = jnp.pad(bias, ((0, 0), (0, LEVELS - 3)))[:, None, :]
    bias = jnp.pad(bias, ((0, 0), (1, 1), (0, 0)))
    slots = jnp.concatenate([table, bias], axis=2).reshape(HID, 3 * SLOT)
    both = jnp.concatenate(
        [jnp.pad(slots, ((0, 0), (0, SLOT))), jnp.pad(slots, ((0, 0), (SLOT, 0)))], axis=0
    )
    col = jnp.arange(4 * SLOT)
    hot = col % SLOT < 3 * LEVELS
    last = first_x & hot & (col // SLOT == 3)
    head = first_x & hot & (col // SLOT == 0)
    zero = jnp.zeros((), BF16)
    return jnp.stack([jnp.where(last, zero, both), jnp.where(head, zero, both), both])


def mix_weights(mix_weight, mix_bias):
    w = mix_weight * jnp.asarray(0.5, BF16)
    bias = jnp.stack(split3(mix_bias), axis=1)
    top = jnp.concatenate([w, jnp.zeros_like(w)], axis=1)
    low = jnp.concatenate([jnp.zeros_like(w), w], axis=1)
    tail = jnp.pad(bias, ((0, 0), (0, LEVELS - 3)))
    return jnp.concatenate(
        [jnp.concatenate([top, low], axis=0), jnp.concatenate([tail, tail], axis=0)], axis=1
    )


def decoder_weights(decoder, first_x):
    d = decoder * jnp.asarray(0.5, BF16)
    d = d[::-1].reshape(KS, KS, 2, 4, HID).transpose(1, 2, 3, 0, 4)
    rows = [
        jnp.pad(d, ((0, 0), (0, 0), (0, 0), (r, BLOCK - 1 - r), (0, 0))) for r in range(BLOCK)
    ]
    w = jnp.stack(rows, axis=2).reshape(KS * CH * BLOCK, 2 * BLOCK * HID)
    at = jnp.arange(2 * BLOCK * HID) // HID
    zero = jnp.zeros((), BF16)
    return jnp.stack(
        [jnp.where(first_x & (at >= 6), zero, w), jnp.where(first_x & (at < 2), zero, w), w]
    )


def on_device(
    levels, conv_table, conv_bias, mix_weight, mix_bias, decoder, green_rows, green_cols, focal_order
):
    count_px = lax.axis_size("px")
    count_py = lax.axis_size("py")
    ix = lax.axis_index("px")
    iy = lax.axis_index("py")
    idx = jnp.stack([ix, iy]).astype(jnp.int32)
    to_x, to_y, to_d = pack(idx, levels, green_rows, green_cols)
    next_x = [(i, (i + 1) % count_px) for i in range(count_px)]
    next_y = [(i, (i + 1) % count_py) for i in range(count_py)]
    next_d = [
        (i * count_py + j, ((i + 1) % count_px) * count_py + (j + 1) % count_py)
        for i in range(count_px)
        for j in range(count_py)
    ]
    from_x = lax.ppermute(to_x, "px", next_x)
    from_d = lax.ppermute(to_d, ("px", "py"), next_d)
    from_y = lax.ppermute(to_y, "py", next_y)
    hi, lo = split_cols(idx, green_cols)
    first_x = ix == 0
    conv_w = conv_weights(conv_table, conv_bias, first_x)
    mix_w = mix_weights(mix_weight, mix_bias)
    dec_w = decoder_weights(decoder, first_x)
    order = jnp.broadcast_to(focal_order[:, None], (U, 4)).reshape(1, U * 4)
    keep, send = field(idx, levels, from_x, from_y, from_d, conv_w, mix_w, dec_w, hi, lo)
    rows = row_factors(idx, order, green_rows, from_x)

    def swap(x, mask):
        return lax.ppermute(x, "py", [(i, i ^ mask) for i in range(count_py)])

    part = keep + swap(send, 1)
    b, c, d = (swap(part[i], 2 * i) for i in (1, 2, 3))
    share = focal_share(rows, part[0], b, c, d)
    return total(lax.all_to_all(share, "px", 0, 0))


def solution(mesh):
    return jax.shard_map(
        on_device,
        mesh=mesh,
        in_specs=(
            P("px", "py"),
            P(),
            P(),
            P(),
            P(),
            P(),
            P(None, None, None, "px"),
            P(None, None, None, "py"),
            P(),
        ),
        out_specs=P("py", "px", None),
        check_vma=False,
    )
```

profile of v0, /device:TPU:2, one launch (start us, length us, event | category | flops | bytes accessed | tf_op | source)
XLA Modules:
  0.0 75.5 jit_solution(6169341326640294054)
XLA Ops:
  0.0 1.9 %copy.33.rows_ref = f32[8,2,64,16]{3,2,1,0:T(8,128)} copy(f32[8,2,64,16]{2,3,1,0:T(8,128)} %param.15) | data formatting | bytes 131072 | tf_op args[6]
  1.9 0.6 pad_add_fusion.idx_ref
  2.5 0.0 copy-start.5
  2.5 3.2 %pack.1 = (f32[8,1152]{1,0:T(8,128)}, f32[48,128]{1,0:T(8,128)}, f32[8,128]{1,0:T(8,128)}) custom-call(s32[2]{0:T(128)} %pad_add_fusion.idx_ref, s32[16,1024]{1,0:T(8,128)} %lev_ref.3, f32[8,2,64,16]{3,2,1,0:T(8,128)} %copy.33.rows_ref, f32[8,2,64,1024]{3,2,1,0:T(8,128)} %cols_ref.3), custom_call_target="tpu_custom_call" | custom-call | tf_op jit(solution)/shard_map/pack/pallas_call | solution.py:67
  5.7 6.6 %collective-permute-start.2 = (f32[8,128]{1,0:T(8,128)}, f32[8,128]{1,0:T(8,128)S(1)}, u32[]{:S(2)}, u32[]{:S(2)}) collective-permute-start(f32[8,128]{1,0:T(8,128)} %get-tuple-element.14), channel_id=1, source_target_pairs={{0,9},{1,10},{2,11},{3,12},{4,13},{5,14},{6,15},{7,8},{8,17},{9,18... | collective-permute-start | bytes 12296 | tf_op jit(solution)/shard_map/ppermute | solution.py:380
  12.3 0.2 collective-permute-start.1
  12.6 0.6 collective-permute-start
  13.1 0.0 copy-done.12
  13.2 0.0 copy-done.13
  13.2 0.1 pad_maximum_fusion.4
  13.3 0.0 copy-done.10
  13.3 0.1 copy.37
  13.4 0.0 copy-done.9
  13.4 0.1 copy.34
  13.6 0.1 copy.35
  13.7 0.0 copy-done.5
  13.7 0.1 pad_bitcast_fusion.5
  13.8 0.1 pad_bitcast_fusion.3
  13.9 0.1 pad_maximum_fusion.1
  14.0 0.2 reshape.178
  14.3 0.1 pad_maximum_fusion.dec_ref
  14.4 0.1 fusion.8.mix_ref
  14.5 7.5 %split_cols.1 = (bf16[8,128,1024]{2,1,0:T(8,128)(2,1)}, bf16[8,128,1024]{2,1,0:T(8,128)(2,1)}) custom-call(s32[2]{0:T(128)} %pad_add_fusion.idx_ref, f32[8,2,64,1024]{3,2,1,0:T(8,128)} %cols_ref.3), custom_call_target="tpu_custom_call" | custom-call | tf_op jit(solution)/shard_map/split_cols/pallas_call | solution.py:104
  22.0 0.0 collective-permute-done.2.from_d_ref
  22.0 0.0 collective-permute-done.1.from_y_ref
  22.0 0.6 collective-permute-done.from_x_ref
  22.6 0.0 copy-done.2
  22.7 1.6 %copy-done = bf16[8,128,1024]{2,1,0:T(8,128)(2,1)S(1)} copy-done((bf16[8,128,1024]{2,1,0:T(8,128)(2,1)S(1)}, bf16[8,128,1024]{2,1,0:T(8,128)(2,1)}, u32[]{:S(2)}) %copy-start) | copy-done | bytes 2097176
  24.3 1.6 %copy-done.1 = bf16[8,128,1024]{2,1,0:T(8,128)(2,1)S(1)} copy-done((bf16[8,128,1024]{2,1,0:T(8,128)(2,1)S(1)}, bf16[8,128,1024]{2,1,0:T(8,128)(2,1)}, u32[]{:S(2)}) %copy-start.1) | copy-done | bytes 2097176
  25.8 10.7 %field.1 = (f32[4,80,128]{2,1,0:T(8,128)S(1)}, f32[4,80,128]{2,1,0:T(8,128)S(1)}) custom-call(s32[2]{0:T(128)S(1)} %copy-done.4, s32[16,1024]{1,0:T(8,128)S(1)} %copy-done.2, f32[8,1152]{1,0:T(8,128)S(1)} %collective-permute-done.from_x_ref, f32[48,128]{1,0:T(8,128)S(1)} %collective-permute-done.1.from_y_ref, ...), custom_call_target="tpu_custom_call" | custom-call | tf_op jit(solution)/shard_map/field/pallas_call | solution.py:229
  36.6 0.2 collective-permute-start.3
  36.8 1.3 %collective-permute-done.3 = f32[4,80,128]{2,1,0:T(8,128)S(1)} collective-permute-done((f32[4,80,128]{2,1,0:T(8,128)S(1)}, f32[4,80,128]{2,1,0:T(8,128)S(1)}, u32[]{:S(2)}, u32[]{:S(2)}) %collective-permute-start.3) | collective-permute-done | bytes 163872 | tf_op jit(solution)/shard_map/ppermute | solution.py:392
  38.1 0.6 slice_bitcast_fusion
  38.7 2.9 %collective-permute-start.6 = (f32[80,128]{1,0:T(8,128)S(1)}, f32[80,128]{1,0:T(8,128)S(1)}, u32[]{:S(2)}, u32[]{:S(2)}) collective-permute-start(f32[80,128]{1,0:T(8,128)S(1)} %get-tuple-element.19), channel_id=1, source_target_pairs={{0,6},{1,7},{2,4},{3,5},{4,2},{5,3},{6,0},{7,1},{8,14},{9,15},{10,... | collective-permute-start | bytes 122888 | tf_op jit(solution)/shard_map/ppermute | solution.py:392
  41.6 0.2 collective-permute-start.5
  41.8 1.4 %collective-permute-start.4 = (f32[80,128]{1,0:T(8,128)S(1)}, f32[80,128]{1,0:T(8,128)S(1)}, u32[]{:S(2)}, u32[]{:S(2)}) collective-permute-start(f32[80,128]{1,0:T(8,128)S(1)} %get-tuple-element.21), channel_id=1, source_target_pairs={{0,2},{1,3},{2,0},{3,1},{4,6},{5,7},{6,4},{7,5},{8,10},{9,11},{10,... | collective-permute-start | bytes 122888 | tf_op jit(solution)/shard_map/ppermute | solution.py:392
  43.1 0.1 broadcast_in_dim.33
  43.2 0.7 reshape.174.order_ref
  43.9 3.0 %row_factors.1.rows_ref = f32[2,256,80]{2,1,0:T(8,128)} custom-call(s32[2]{0:T(128)} %pad_add_fusion.idx_ref, s32[1,256]{1,0:T(1,128)} %reshape.174.order_ref, f32[8,2,64,16]{3,2,1,0:T(8,128)} %copy.33.rows_ref, f32[8,1152]{1,0:T(8,128)} %copy-done.3), custom_call_target="tpu_custom_call" | custom-call | tf_op jit(solution)/shard_map/row_factors/pallas_call | solution.py:267
  46.9 0.0 collective-permute-done.6.d_ref
  46.9 0.0 collective-permute-done.5.c_ref
  46.9 0.0 collective-permute-done.4.b_ref
  47.0 0.6 copy-done.6
  47.6 0.0 copy-done.7
  47.6 0.0 copy-done.8
  47.6 2.1 %focal_share.1 = f32[32,8,128]{2,1,0:T(8,128)} custom-call(f32[2,256,80]{2,1,0:T(8,128)} %row_factors.1.rows_ref, f32[80,128]{1,0:T(8,128)} %get-tuple-element.22.a_ref, f32[80,128]{1,0:T(8,128)} %copy-done.8, f32[80,128]{1,0:T(8,128)} %copy-done.7, f32[80,128]{1,0:T(8,128)} %copy-done.6), custom_call_target="tpu_custom_call" | custom-call | tf_op jit(solution)/shard_map/focal_share/pallas_call | solution.py:293
  49.7 24.2 %all_to_all.5.x_ref = f32[32,8,128]{2,1,0:T(8,128)} all-to-all(f32[32,8,128]{2,1,0:T(8,128)} %focal_share.1), channel_id=1, replica_groups=mesh['px'=32,'py'=8] {'px'}, dimensions={0} | all-to-all | bytes 262144 | tf_op jit(solution)/shard_map/all_to_all | solution.py:397
  73.9 1.6 %total.1 = f32[1,2,512]{2,1,0:T(2,128)} custom-call(f32[32,8,128]{2,1,0:T(8,128)} %all_to_all.5.x_ref), custom_call_target="tpu_custom_call" | custom-call | tf_op jit(solution)/shard_map/total/pallas_call | solution.py:312
  (31 shorter events, 0.2 us)
Async XLA Ops:
  2.5 10.6 %copy-start.12 = (f32[64]{0:T(128)S(1)}, f32[64]{0:T(128)}, u32[]{:S(2)}) copy-start(f32[64]{0:T(128)} %param.11) | copy-start | bytes 772
  2.5 10.6 %copy-start.13 = (f32[64]{0:T(128)S(1)}, f32[64]{0:T(128)}, u32[]{:S(2)}) copy-start(f32[64]{0:T(128)} %param.13) | copy-start | bytes 772
  2.5 10.8 %copy-start.10 = (bf16[64,64]{1,0:T(8,128)(2,1)S(1)}, bf16[64,64]{1,0:T(8,128)(2,1)}, u32[]{:S(2)}) copy-start(bf16[64,64]{1,0:T(8,128)(2,1)} %param.12) | copy-start | bytes 24580
  2.5 10.9 %copy-start.9 = (bf16[64,144]{1,0:T(8,128)(2,1)S(1)}, bf16[64,144]{1,0:T(8,128)(2,1)}, u32[]{:S(2)}) copy-start(bf16[64,144]{1,0:T(8,128)(2,1)} %param.10) | copy-start | bytes 55300
  2.5 11.1 %copy-start.5 = (bf16[5,40,64]{2,1,0:T(8,128)(2,1)S(1)}, bf16[5,40,64]{2,1,0:T(8,128)(2,1)}, u32[]{:S(2)}) copy-start(bf16[5,40,64]{2,1,0:T(8,128)(2,1)} %param.14) | copy-start | bytes 76804
  5.7 16.3 %collective-permute-start.2 = (f32[8,128]{1,0:T(8,128)}, f32[8,128]{1,0:T(8,128)S(1)}, u32[]{:S(2)}, u32[]{:S(2)}) collective-permute-start(f32[8,128]{1,0:T(8,128)} %get-tuple-element.14), channel_id=1, source_target_pairs={{0,9},{1,10},{2,11},{3,12},{4,13},{5,14},{6,15},{7,8},{8,17},{9,18... | collective-permute-start | bytes 12296 | tf_op jit(solution)/shard_map/ppermute | solution.py:380
  12.3 9.7 %collective-permute-start.1 = (f32[48,128]{1,0:T(8,128)}, f32[48,128]{1,0:T(8,128)S(1)}, u32[]{:S(2)}, u32[]{:S(2)}) collective-permute-start(f32[48,128]{1,0:T(8,128)} %get-tuple-element.13), channel_id=1, source_target_pairs={{0,1},{1,2},{2,3},{3,4},{4,5},{5,6},{6,7},{7,0},{8,9},{9,10},{10,1... | collective-permute-start | bytes 73736 | tf_op jit(solution)/shard_map/ppermute | solution.py:381
  12.6 10.1 %collective-permute-start = (f32[8,1152]{1,0:T(8,128)}, f32[8,1152]{1,0:T(8,128)S(1)}, u32[]{:S(2)}, u32[]{:S(2)}) collective-permute-start(f32[8,1152]{1,0:T(8,128)} %get-tuple-element.12), channel_id=1, source_target_pairs={{0,8},{8,16},{16,24},{24,32},{32,40},{40,48},{48,56},{56,64},{64,7... | collective-permute-start | bytes 110600 | tf_op jit(solution)/shard_map/ppermute | solution.py:379
  14.5 8.1 %copy-start.2 = (s32[16,1024]{1,0:T(8,128)S(1)}, s32[16,1024]{1,0:T(8,128)}, u32[]{:S(2)}) copy-start(s32[16,1024]{1,0:T(8,128)} %lev_ref.3) | copy-start | bytes 196612
  14.5 8.1 %copy-start.4 = (s32[2]{0:T(128)S(1)}, s32[2]{0:T(128)}, u32[]{:S(2)}) copy-start(s32[2]{0:T(128)} %pad_add_fusion.idx_ref) | copy-start | bytes 28
  22.6 14.0 %copy-start.3 = (f32[8,1152]{1,0:T(8,128)}, f32[8,1152]{1,0:T(8,128)S(1)}, u32[]{:S(2)}) copy-start(f32[8,1152]{1,0:T(8,128)S(1)} %collective-permute-done.from_x_ref) | copy-start | bytes 110596
  22.6 1.6 %copy-start = (bf16[8,128,1024]{2,1,0:T(8,128)(2,1)S(1)}, bf16[8,128,1024]{2,1,0:T(8,128)(2,1)}, u32[]{:S(2)}) copy-start(bf16[8,128,1024]{2,1,0:T(8,128)(2,1)} %get-tuple-element.15.hi_ref) | copy-start | bytes 6291460
  24.3 1.6 %copy-start.1 = (bf16[8,128,1024]{2,1,0:T(8,128)(2,1)S(1)}, bf16[8,128,1024]{2,1,0:T(8,128)(2,1)}, u32[]{:S(2)}) copy-start(bf16[8,128,1024]{2,1,0:T(8,128)(2,1)} %get-tuple-element.16.lo_ref) | copy-start | bytes 6291460
  25.8 17.3 %copy-start.11 = (s32[64]{0:T(128)S(1)}, s32[64]{0:T(128)}, u32[]{:S(2)}) copy-start(s32[64]{0:T(128)} %param.17) | copy-start | bytes 772
  36.6 1.5 %collective-permute-start.3 = (f32[4,80,128]{2,1,0:T(8,128)S(1)}, f32[4,80,128]{2,1,0:T(8,128)S(1)}, u32[]{:S(2)}, u32[]{:S(2)}) collective-permute-start(f32[4,80,128]{2,1,0:T(8,128)S(1)} %get-tuple-element.18), channel_id=1, source_target_pairs={{0,1},{1,0},{2,3},{3,2},{4,5},{5,4},{6,7},{7,6},{8,9},{9,8},{10,11... | collective-permute-start | bytes 491528 | tf_op jit(solution)/shard_map/ppermute | solution.py:392
  38.7 8.2 %collective-permute-start.6 = (f32[80,128]{1,0:T(8,128)S(1)}, f32[80,128]{1,0:T(8,128)S(1)}, u32[]{:S(2)}, u32[]{:S(2)}) collective-permute-start(f32[80,128]{1,0:T(8,128)S(1)} %get-tuple-element.19), channel_id=1, source_target_pairs={{0,6},{1,7},{2,4},{3,5},{4,2},{5,3},{6,0},{7,1},{8,14},{9,15},{10,... | collective-permute-start | bytes 122888 | tf_op jit(solution)/shard_map/ppermute | solution.py:392
  41.6 5.3 %collective-permute-start.5 = (f32[80,128]{1,0:T(8,128)S(1)}, f32[80,128]{1,0:T(8,128)S(1)}, u32[]{:S(2)}, u32[]{:S(2)}) collective-permute-start(f32[80,128]{1,0:T(8,128)S(1)} %get-tuple-element.20), channel_id=1, source_target_pairs={{0,4},{1,5},{2,6},{3,7},{4,0},{5,1},{6,2},{7,3},{8,12},{9,13},{10,... | collective-permute-start | bytes 122888 | tf_op jit(solution)/shard_map/ppermute | solution.py:392
  41.8 5.2 %collective-permute-start.4 = (f32[80,128]{1,0:T(8,128)S(1)}, f32[80,128]{1,0:T(8,128)S(1)}, u32[]{:S(2)}, u32[]{:S(2)}) collective-permute-start(f32[80,128]{1,0:T(8,128)S(1)} %get-tuple-element.21), channel_id=1, source_target_pairs={{0,2},{1,3},{2,0},{3,1},{4,6},{5,7},{6,4},{7,5},{8,10},{9,11},{10,... | collective-permute-start | bytes 122888 | tf_op jit(solution)/shard_map/ppermute | solution.py:392
  46.9 0.6 copy-start.6
  46.9 0.6 copy-start.7
  47.0 0.6 copy-start.8
where the time goes:
time: 76.1 us; the launch traced here: 75.5 us
  Pallas kernels  28.1 us (37%)
  blocking collectives  24.2 us (32%)
  starting transfers between devices  12 us (16%)
  local copies, waits for them, and re-layouts  7.89 us (10%)
  waiting for transfers between devices  1.94 us (3%)
  other arithmetic  1.09 us (1%)
    all_to_all x1, blocking collectives, on_device(): return total(lax.all_to_all(share, 'px', 0, 0))  24.2 us
    pallas_call x1, Pallas kernels, field(): pl.pallas_call(field_kernel, in_specs=[pl.BlockSpec(memory_space=pltpu.SM...  10.7 us
    pallas_call x1, Pallas kernels, split_cols(): pl.pallas_call(split_kernel, grid_spec=pltpu.PrefetchScalarGridSpec(num_s...  7.48 us
    ppermute x1, starting transfers between devices, on_device(): from_d = lax.ppermute(to_d, ('px', 'py'), next_d)  6.63 us
    unnamed x30, local copies, waits for them, and re-layouts  5.88 us
    ppermute x4, starting transfers between devices, swap(): return lax.ppermute(x, 'py', [(i, i ^ mask) for i in range(count_py)])  4.59 us
    pallas_call x1, Pallas kernels, pack(): pl.pallas_call(pack_kernel, grid_spec=pltpu.PrefetchScalarGridSpec(num_sc...  3.15 us
    pallas_call x1, Pallas kernels, row_factors(): pl.pallas_call(rows_kernel, grid_spec=pltpu.PrefetchScalarGridSpec(num_sc...  3.05 us
  transfers between devices with their start and end apart: 7, of which 2 were waited for; matrix products, arithmetic and copies ran while one was open for 3% of the time, Pallas kernels for 14%

commit v1 on v0

v1 whole, which is shorter than its diff:
```python
import jax
import jax.numpy as jnp
from jax import lax
from jax.experimental import pallas as pl
from jax.experimental.pallas import tpu as pltpu
from jax.sharding import PartitionSpec as P

HIGH = lax.Precision.HIGHEST
F32 = jnp.float32
BF16 = jnp.bfloat16
NT = (((1,), (1,)), ((), ()))
TN = (((0,), (0,)), ((), ()))

ROWS = 16
COLS = 1024
HID = 64
LEVELS = 16
CH = 8
KS = 5
Z = 8
U = 64
V = 64
HALO = 4
ROWS_EXT = ROWS + HALO
SLOT = 64
BLOCK = 4
REL_ORDER = (0, 2, 4, 6, 1, 3, 5, 7)
PART = ROWS_EXT * CH // 2
VMEM = pl.BlockSpec(memory_space=pltpu.VMEM)
HBM = pl.BlockSpec(memory_space=pltpu.HBM)


def params(mib):
    return pltpu.CompilerParams(vmem_limit_bytes=mib << 20)

GELU_A = 0.7978845608028654
GELU_B = GELU_A * 0.044715


def iota(shape, dim):
    return lax.broadcasted_iota(jnp.int32, shape, dim)


def twice_gelu(x):
    return x + x * jnp.tanh(x * (GELU_A + GELU_B * (x * x)))


def split3(x):
    a = lax.reduce_precision(x, 8, 7)
    b = lax.reduce_precision(x - a, 8, 7)
    return a.astype(BF16), b.astype(BF16), (x - a - b).astype(BF16)


def pack_kernel(lev_hbm, rows_hbm, cols_hbm, to_x_ref, to_y_ref, to_d_ref, lev_ref, tile_ref, rows_ref, cols_ref, sems):
    z = lax.axis_index("py")
    last = pl.ds(COLS - 128, 128)
    copies = [
        pltpu.make_async_copy(cols_hbm.at[:, :, :, last], cols_ref, sems.at[0]),
        pltpu.make_async_copy(lev_hbm.at[pl.ds(8, 8), :], lev_ref, sems.at[1]),
        pltpu.make_async_copy(lev_hbm.at[:, last], tile_ref, sems.at[2]),
        pltpu.make_async_copy(rows_hbm.at[z], rows_ref, sems.at[3]),
    ]
    for copy in copies:
        copy.start()
    for copy in copies[1:]:
        copy.wait()
    to_x_ref[:, :COLS] = lev_ref[...].astype(F32)
    to_x_ref[:, COLS:] = jnp.concatenate([rows_ref[0, 8:, :], rows_ref[1, 8:, :]], axis=1)
    tile = tile_ref[...].astype(F32)
    to_d_ref[...] = tile[8:, :]
    to_y_ref[:ROWS, :] = tile
    copies[0].wait()
    for i in range(Z):
        edge = cols_ref[i].reshape(2 * V, 128).T
        to_y_ref[ROWS + HALO * i : ROWS + HALO * (i + 1), :] = edge[128 - HALO :, :]


def pack(levels, rows_t, green_cols):
    return pl.pallas_call(
        pack_kernel,
        in_specs=[HBM] * 3,
        out_specs=[VMEM] * 3,
        out_shape=[
            jax.ShapeDtypeStruct((8, COLS + 128), F32),
            jax.ShapeDtypeStruct((ROWS + Z * HALO, 128), F32),
            jax.ShapeDtypeStruct((8, 128), F32),
        ],
        scratch_shapes=[
            pltpu.VMEM((8, COLS), jnp.int32),
            pltpu.VMEM((ROWS, 128), jnp.int32),
            pltpu.VMEM((2, ROWS, U), F32),
            pltpu.VMEM((Z, 2, V, 128), F32),
            pltpu.SemaphoreType.DMA((4,)),
        ],
        compiler_params=params(4),
        name="pack",
    )(*(pltpu.with_memory_space_constraint(x, pltpu.HBM) for x in (levels, rows_t, green_cols)))


def one_hot(row, level_ids):
    row = jnp.broadcast_to(row, level_ids.shape)
    return jnp.where(row == level_ids, 1.0, 0.0).astype(BF16)


def inner_kernel(lev_ref, conv_ref, mix_ref, cols_hbm, feat_ref, hi_ref, lo_ref, ext_ref, hot_ref, hid_ref, cols_ref, sems):
    z = lax.axis_index("py")
    copies = [
        pltpu.make_async_copy(cols_hbm.at[z ^ REL_ORDER[g]], cols_ref.at[g], sems.at[g])
        for g in range(Z)
    ]
    for copy in copies:
        copy.start()
    wide = COLS - 128
    lev = lev_ref[...].astype(F32)
    for b in range(3):
        ext_ref[b] = pltpu.roll(lev, 3 - b, 1)[:, 128:]
    level_ids = iota((LEVELS, wide), 0).astype(F32)
    ones = jnp.ones((LEVELS, wide), BF16)

    def make_hot(q, _):
        for b in range(3):
            hot_ref[pl.ds(q * SLOT + b * LEVELS, LEVELS), :] = one_hot(
                ext_ref[b, pl.ds(q + 1, 1), :], level_ids
            )
        hot_ref[pl.ds(q * SLOT + 3 * LEVELS, LEVELS), :] = ones
        return 0

    lax.fori_loop(0, ROWS - 2, make_hot, 0)
    hid_ref[2 * HID :, :] = ones
    feat_ref[: BLOCK * HID, :] = jnp.zeros((BLOCK * HID, COLS), BF16)
    feat_ref[(BLOCK + ROWS) * HID :, :] = jnp.zeros((BLOCK * HID, COLS), BF16)

    def features(i, _):
        pre = jnp.dot(
            conv_ref[2], hot_ref[pl.ds(i * 2 * SLOT, 4 * SLOT), :], preferred_element_type=F32
        )
        hid_ref[: 2 * HID, :] = twice_gelu(pre).astype(BF16)
        mixed = jnp.dot(mix_ref[...], hid_ref[...], preferred_element_type=F32)
        feat_ref[pl.ds((2 * BLOCK + 2 * i) * HID, 2 * HID), 128:] = twice_gelu(mixed).astype(BF16)
        return 0

    lax.fori_loop(0, ROWS // 2 - 2, features, 0)
    for copy in copies:
        copy.wait()

    def split(g, _):
        x = cols_ref[g].reshape(2 * V, COLS)
        hi = x.astype(BF16)
        hi_ref[g] = hi
        lo_ref[g] = (x - hi.astype(F32)).astype(BF16)
        return 0

    lax.fori_loop(0, Z, split, 0)


def inner(levels, conv_w, mix_w, green_cols):
    wide = COLS - 128
    return pl.pallas_call(
        inner_kernel,
        in_specs=[VMEM] * 3 + [HBM],
        out_specs=[VMEM] * 3,
        out_shape=[
            jax.ShapeDtypeStruct(((ROWS + 2 * BLOCK) * HID, COLS), BF16),
            jax.ShapeDtypeStruct((Z, 2 * V, COLS), BF16),
            jax.ShapeDtypeStruct((Z, 2 * V, COLS), BF16),
        ],
        scratch_shapes=[
            pltpu.VMEM((3, ROWS, wide), F32),
            pltpu.VMEM(((ROWS - 2) * SLOT, wide), BF16),
            pltpu.VMEM((2 * HID + LEVELS, wide), BF16),
            pltpu.VMEM((Z, 2, V, COLS), F32),
            pltpu.SemaphoreType.DMA((Z,)),
        ],
        compiler_params=params(24),
        name="inner",
    )(levels, conv_w, mix_w, pltpu.with_memory_space_constraint(green_cols, pltpu.HBM))


def split2(x):
    hi = x.astype(BF16)
    return hi, (x - hi.astype(F32)).astype(BF16)


def make_row_factors(from_x_ref, rows_ref, order_ref, out_ref):
    green = jnp.concatenate([rows_ref[0], rows_ref[1]], axis=1)
    green = jnp.concatenate([from_x_ref[:, COLS:], green], axis=0)
    n = ROWS + 8
    pick = (order_ref[...] == iota((U, U * 4), 0)).astype(BF16)
    spread = (iota((PART, n), 0) // 4 == iota((PART, n), 1) - (8 - HALO)).astype(BF16)
    mask = iota((PART, U * 4), 0) % 4 == iota((PART, U * 4), 1) % 4
    for i, part in enumerate(split2(green)):
        for j in range(2):
            ordered = jnp.dot(part[:, j * U : (j + 1) * U], pick, preferred_element_type=F32)
            wide = jnp.dot(spread, ordered.astype(BF16), preferred_element_type=F32)
            wide = jnp.where(mask, wide, 0.0)
            out_ref[i, j * U * 4 : (j + 1) * U * 4, :] = wide.T.astype(BF16)


def field_kernel(
    lev_ref, from_x_ref, from_y_ref, from_d_ref, conv_ref, mix_ref, dec_ref, rows_hbm, order_ref,
    hi_ref, lo_ref, _, keep_ref, send_ref, factor_ref, feat_ref,
    ext_ref, hot_ref, hid_ref, nf_ref, edge_ref, rows_ref, sem,
):
    iy = lax.axis_index("py")
    copy = pltpu.make_async_copy(rows_hbm.at[iy], rows_ref, sem)
    copy.start()
    first_y = iy == 0
    main = jnp.concatenate([from_x_ref[:, :COLS], lev_ref[...].astype(F32)], axis=0)
    left = jnp.concatenate([from_d_ref[...], from_y_ref[:ROWS, :]], axis=0)
    ext = jnp.concatenate([left, main], axis=1)
    lane = iota((24, COLS), 1)
    for b in range(3):
        window = pltpu.roll(ext, 3 - b, 1)[:, 128:]
        if b != 1:
            cut = first_y & (lane == (2 if b == 0 else 1))
            window = jnp.where(cut, -1.0, window)
        ext_ref[b] = window
    level_ids = iota((LEVELS, COLS), 0).astype(F32)
    ones = jnp.ones((LEVELS, COLS), BF16)
    for o in range(4):
        for b in range(3):
            at = pl.ds(o * SLOT + b * LEVELS, LEVELS)
            for w in range(2):
                q = 2 * w + o
                hot_ref[w, at, :] = one_hot(ext_ref[b, q + 5 : q + 6, :], level_ids)
            for t in range(6):
                q = 2 * t + 4 + o
                hot_ref[2, at, t * 128 : (t + 1) * 128] = one_hot(
                    ext_ref[b, q + 5 : q + 6, :128], level_ids[:, :128]
                )
            hot_ref[2, at, 768:] = jnp.zeros((LEVELS, COLS - 768), BF16)
        for w in range(3):
            hot_ref[w, pl.ds(o * SLOT + 3 * LEVELS, LEVELS), :] = ones
    hid_ref[2 * HID :, :] = ones

    def features(w):
        pre = jnp.dot(conv_ref[w], hot_ref[w], preferred_element_type=F32)
        hid_ref[: 2 * HID, :] = twice_gelu(pre).astype(BF16)
        mixed = jnp.dot(mix_ref[...], hid_ref[...], preferred_element_type=F32)
        return twice_gelu(mixed).astype(BF16)

    def whole_rows(w, _):
        feat_ref[pl.ds((BLOCK + 2 * w) * HID, 2 * HID), :] = features(w)
        return 0

    lax.fori_loop(0, 2, whole_rows, 0)
    tiles = features(2)
    for t in range(6):
        at = (2 * BLOCK + 2 * t) * HID
        feat_ref[at : at + 2 * HID, :128] = tiles[:, t * 128 : (t + 1) * 128]

    lane = iota((1, COLS), 1)
    near = iota((1, 128), 1)
    keep_main, keep_edge = [], []
    for s in range(KS):
        k = KS - 1 - s
        ok = lane < COLS - k
        ok = ok & ((lane + k >= 2) | jnp.logical_not(first_y))
        keep_main.append(ok.astype(F32))
        ok = (near >= s) & (near < HALO)
        ok = ok & ((near - s < 2) | jnp.logical_not(first_y))
        keep_edge.append(ok.astype(F32))
    half = BLOCK * CH // 2

    def near_field(i, _):
        taps = jnp.dot(
            dec_ref[jnp.minimum(i, 2)],
            feat_ref[pl.ds(i * BLOCK * HID, 2 * BLOCK * HID), :],
            preferred_element_type=F32,
        )
        acc = jnp.zeros((2 * half, COLS), F32)
        edge = jnp.zeros((2 * half, 128), F32)
        for s in range(KS):
            part = taps[2 * half * s : 2 * half * (s + 1), :]
            k = KS - 1 - s
            moved = part if k == 0 else pltpu.roll(part, COLS - k, 1)
            acc = acc + moved * keep_main[s]
            part = part[:, :128]
            moved = part if s == 0 else pltpu.roll(part, s, 1)
            edge = edge + moved * keep_edge[s]
        hi, lo = split2(acc)
        for k in range(2):
            at = k * PART + i * half
            nf_ref[pl.ds(at, half), :] = hi[k * half : (k + 1) * half]
            nf_ref[pl.ds(at + 2 * PART, half), :] = lo[k * half : (k + 1) * half]
            edge_ref[pl.ds(at, half), :] = edge[k * half : (k + 1) * half]
        return 0

    lax.fori_loop(0, ROWS_EXT // BLOCK, near_field, 0)

    n = 2 * PART
    sign = jnp.where(iota((1, 128), 1) < V, -1.0, 1.0)
    for g in range(Z):
        out = lax.dot_general(nf_ref[...], hi_ref[g], NT, preferred_element_type=F32)
        out = out[:n] + out[n:]
        out = out + lax.dot_general(nf_ref[:n, :], lo_ref[g], NT, preferred_element_type=F32)
        green = from_y_ref[pl.ds(ROWS + HALO * (iy ^ REL_ORDER[g]), HALO), :]
        green = jnp.concatenate([green, jnp.zeros((4, 128), F32)], axis=0)
        out = out + jnp.dot(
            edge_ref[:, :8], green, precision=HIGH, preferred_element_type=F32
        )
        total = out[:PART] + sign * pltpu.roll(out[PART:], V, 1)
        if g < 4:
            keep_ref[g] = total
        else:
            send_ref[g - 4] = total
    copy.wait()
    make_row_factors(from_x_ref, rows_ref, order_ref, factor_ref)


def field(levels, from_x, from_y, from_d, conv_w, mix_w, dec_w, rows, order, hi, lo, feat):
    return pl.pallas_call(
        field_kernel,
        in_specs=[VMEM] * 7 + [HBM] + [VMEM] * 4,
        out_specs=[VMEM] * 4,
        out_shape=[
            jax.ShapeDtypeStruct((4, PART, 128), F32),
            jax.ShapeDtypeStruct((4, PART, 128), F32),
            jax.ShapeDtypeStruct((2, 2 * U * 4, PART), BF16),
            jax.ShapeDtypeStruct(feat.shape, BF16),
        ],
        input_output_aliases={11: 3},
        scratch_shapes=[
            pltpu.VMEM((3, 24, COLS), F32),
            pltpu.VMEM((3, 4 * SLOT, COLS), BF16),
            pltpu.VMEM((2 * HID + LEVELS, COLS), BF16),
            pltpu.VMEM((4 * PART, COLS), BF16),
            pltpu.VMEM((2 * PART, 128), F32),
            pltpu.VMEM((2, ROWS, U), F32),
            pltpu.SemaphoreType.DMA,
        ],
        compiler_params=params(24),
        name="field",
    )(
        levels, from_x, from_y, from_d, conv_w, mix_w, dec_w,
        pltpu.with_memory_space_constraint(rows, pltpu.HBM), order, hi, lo, feat,
    )


def focal_kernel(factor_ref, keep_ref, got_ref, b_ref, c_ref, d_ref, out_ref):
    t = ((keep_ref[0] + got_ref[0]) + b_ref[...]) + (c_ref[...] + d_ref[...])
    hi, lo = split2(t)
    out = jnp.dot(factor_ref[0], hi, preferred_element_type=F32)
    out = out + jnp.dot(factor_ref[1], hi, preferred_element_type=F32)
    out = out + jnp.dot(factor_ref[0], lo, preferred_element_type=F32)
    n = U * 4
    sign = jnp.where(iota((1, 128), 1) < V, -1.0, 1.0)
    out_ref[...] = (out[:n] + sign * pltpu.roll(out[n:], V, 1)).reshape(out_ref.shape)


def focal_share(factors, keep, got, b, c, d):
    return pl.pallas_call(
        focal_kernel,
        in_specs=[VMEM] * 6,
        out_specs=VMEM,
        out_shape=jax.ShapeDtypeStruct((U // 2, 8, 128), F32),
        compiler_params=params(4),
        name="focal_share",
    )(factors, keep, got, b, c, d)


def total_kernel(x_ref, out_ref):
    s = jnp.sum(x_ref[...], axis=0)
    for u in range(2):
        for k in range(2):
            for p in range(4):
                at = (k * 4 + p) * V
                row = u * 4 + p
                out_ref[0, u : u + 1, at : at + V] = s[row : row + 1, k * V : (k + 1) * V]


def total(parts):
    return pl.pallas_call(
        total_kernel,
        in_specs=[VMEM],
        out_specs=VMEM,
        out_shape=jax.ShapeDtypeStruct((1, 2, 8 * V), F32),
        compiler_params=params(4),
        name="total",
    )(parts)


def conv_weights(conv_table, conv_bias, first_x):
    table = conv_table.reshape(HID, 3, 3 * LEVELS)
    bias = jnp.stack(split3(conv_bias), axis=1)
    bias = jnp.pad(bias, ((0, 0), (0, LEVELS - 3)))[:, None, :]
    bias = jnp.pad(bias, ((0, 0), (1, 1), (0, 0)))
    slots = jnp.concatenate([table, bias], axis=2).reshape(HID, 3 * SLOT)
    both = jnp.concatenate(
        [jnp.pad(slots, ((0, 0), (0, SLOT))), jnp.pad(slots, ((0, 0), (SLOT, 0)))], axis=0
    )
    col = jnp.arange(4 * SLOT)
    hot = col % SLOT < 3 * LEVELS
    last = first_x & hot & (col // SLOT == 3)
    head = first_x & hot & (col // SLOT == 0)
    zero = jnp.zeros((), BF16)
    return jnp.stack([jnp.where(last, zero, both), jnp.where(head, zero, both), both])


def mix_weights(mix_weight, mix_bias):
    w = mix_weight * jnp.asarray(0.5, BF16)
    bias = jnp.stack(split3(mix_bias), axis=1)
    top = jnp.concatenate([w, jnp.zeros_like(w)], axis=1)
    low = jnp.concatenate([jnp.zeros_like(w), w], axis=1)
    tail = jnp.pad(bias, ((0, 0), (0, LEVELS - 3)))
    return jnp.concatenate(
        [jnp.concatenate([top, low], axis=0), jnp.concatenate([tail, tail], axis=0)], axis=1
    )


def decoder_weights(decoder, first_x):
    d = decoder * jnp.asarray(0.5, BF16)
    d = d[::-1].reshape(KS, KS, 2, 4, HID).transpose(1, 2, 3, 0, 4)
    rows = [
        jnp.pad(d, ((0, 0), (0, 0), (0, 0), (r, BLOCK - 1 - r), (0, 0))) for r in range(BLOCK)
    ]
    w = jnp.stack(rows, axis=2).reshape(KS * CH * BLOCK, 2 * BLOCK * HID)
    at = jnp.arange(2 * BLOCK * HID) // HID
    zero = jnp.zeros((), BF16)
    return jnp.stack(
        [jnp.where(first_x & (at >= 6), zero, w), jnp.where(first_x & (at < 2), zero, w), w]
    )


def on_device(
    levels, conv_table, conv_bias, mix_weight, mix_bias, decoder, green_rows, green_cols, focal_order
):
    count_px = lax.axis_size("px")
    count_py = lax.axis_size("py")
    rows_t = jnp.swapaxes(green_rows, 2, 3)
    to_x, to_y, to_d = pack(levels, rows_t, green_cols)
    next_x = [(i, (i + 1) % count_px) for i in range(count_px)]
    next_y = [(i, (i + 1) % count_py) for i in range(count_py)]
    next_d = [
        (i * count_py + j, ((i + 1) % count_px) * count_py + (j + 1) % count_py)
        for i in range(count_px)
        for j in range(count_py)
    ]
    from_x = lax.ppermute(to_x, "px", next_x)
    from_d = lax.ppermute(to_d, ("px", "py"), next_d)
    from_y = lax.ppermute(to_y, "py", next_y)
    first_x = lax.axis_index("px") == 0
    conv_w = conv_weights(conv_table, conv_bias, first_x)
    mix_w = mix_weights(mix_weight, mix_bias)
    dec_w = decoder_weights(decoder, first_x)
    order = jnp.broadcast_to(focal_order[:, None], (U, 4)).reshape(1, U * 4)
    feat, hi, lo = inner(levels, conv_w, mix_w, green_cols)
    keep, send, factors, _ = field(
        levels, from_x, from_y, from_d, conv_w, mix_w, dec_w, rows_t, order, hi, lo, feat
    )

    def swap(x, mask):
        return lax.ppermute(x, "py", [(i, i ^ mask) for i in range(count_py)])

    got = swap(send, 1)
    b, c, d = (swap(keep[i] + got[i], 2 * i) for i in (1, 2, 3))
    share = focal_share(factors, keep, got, b, c, d)
    return total(lax.all_to_all(share, "px", 0, 0))


def solution(mesh):
    return jax.shard_map(
        on_device,
        mesh=mesh,
        in_specs=(
            P("px", "py"),
            P(),
            P(),
            P(),
            P(),
            P(),
            P(None, None, None, "px"),
            P(None, None, None, "py"),
            P(),
        ),
        out_specs=P("py", "px", None),
        check_vma=False,
    )
```

time: 76.1 us -> 58.3 us (0.77)
  Pallas kernels: 28.1 us -> 14.6 us
  local copies, waits for them, and re-layouts: 7.89 us -> 0.96 us
  waiting for transfers between devices: 1.94 us -> 7.18 us
  blocking collectives: 24.2 us -> 22.1 us
    pallas_call x6 -> x5, Pallas kernels: 28.1 us -> 14.6 us  [the longest x1 7.66 us: field(): pl.pallas_call(field_kernel, in_specs=[VMEM] * 7 + [HBM] + [VMEM] * 4, ou...]
    unnamed x30 -> x15, local copies, waits for them, and re-layouts: 5.88 us -> 0.14 us
    ppermute x4, waiting for transfers between devices: 1.29 us -> 4.06 us  [swap(): return lax.ppermute(x, 'py', [(i, i ^ mask) for i in range(count_py)])]
    ppermute x1, waiting for transfers between devices: 0.64 us -> 3.12 us  [on_device(): from_x = lax.ppermute(to_x, 'px', next_x)]
    all_to_all x1, blocking collectives: 24.2 us -> 22.1 us  [on_device(): return total(lax.all_to_all(share, 'px', 0, 0))]
  transfers between devices with their start and end apart: 7 -> 7, of which waited for: 2 -> 4; matrix products, arithmetic and copies ran while one was open for 3% -> 2% of each run, Pallas kernels for 14% -> 8%
where the time goes in v1:
time: 58.3 us; the launch traced here: 57.7 us
  blocking collectives  22.1 us (38%)
  Pallas kernels  14.6 us (25%)
  starting transfers between devices  12.2 us (21%)
  waiting for transfers between devices  7.18 us (12%)
  local copies, waits for them, and re-layouts  0.96 us (2%)
    all_to_all x1, blocking collectives, on_device(): return total(lax.all_to_all(share, 'px', 0, 0))  22.1 us
    pallas_call x1, Pallas kernels, field(): pl.pallas_call(field_kernel, in_specs=[VMEM] * 7 + [HBM] + [VMEM] * 4, ou...  7.66 us
    ppermute x1, starting transfers between devices, on_device(): from_d = lax.ppermute(to_d, ('px', 'py'), next_d)  6.71 us
    ppermute x4, starting transfers between devices, swap(): return lax.ppermute(x, 'py', [(i, i ^ mask) for i in range(count_py)])  4.68 us
    pallas_call x1, Pallas kernels, inner(): pl.pallas_call(inner_kernel, in_specs=[VMEM] * 3 + [HBM], out_specs=[VMEM...  4.58 us
    ppermute x4, waiting for transfers between devices, swap(): return lax.ppermute(x, 'py', [(i, i ^ mask) for i in range(count_py)])  4.06 us
    ppermute x1, waiting for transfers between devices, on_device(): from_x = lax.ppermute(to_x, 'px', next_x)  3.12 us
    pallas_call x1, Pallas kernels, pack(): pl.pallas_call(pack_kernel, in_specs=[HBM] * 3, out_specs=[VMEM] * 3, out...  1.34 us
  transfers between devices with their start and end apart: 7, of which 4 were waited for; matrix products, arithmetic and copies ran while one was open for 2% of the time, Pallas kernels for 8%

profile of v1, /device:TPU:2, one launch (start us, length us, event | category | flops | bytes accessed | tf_op | source)
XLA Modules:
  0.0 57.7 jit_solution(12696292859564044748)
XLA Ops:
  0.0 0.0 copy-start.5
  0.0 0.0 copy-start.6
  0.0 0.0 copy-start.3
  0.0 0.0 copy-start.2
  0.0 0.0 copy-start.1
  0.0 1.3 %pack.1 = (f32[8,1152]{1,0:T(8,128)S(1)}, f32[48,128]{1,0:T(8,128)S(1)}, f32[8,128]{1,0:T(8,128)S(1)}) custom-call(s32[16,1024]{1,0:T(8,128)} %lev_ref.3, f32[8,2,16,64]{3,2,1,0:T(8,128)} %bitcast.49, f32[8,2,64,1024]{3,2,1,0:T(8,128)} %cols_hbm.3), custom_call_target="tpu_custom_call" | custom-call | tf_op jit(solution)/shard_map/pack/pallas_call | solution.py:79
  1.4 0.0 copy-start.4
  1.4 0.0 copy-start
  1.4 6.7 %collective-permute-start.2 = (f32[8,128]{1,0:T(8,128)S(1)}, f32[8,128]{1,0:T(8,128)S(1)}, u32[]{:S(2)}, u32[]{:S(2)}) collective-permute-start(f32[8,128]{1,0:T(8,128)S(1)} %get-tuple-element.16), channel_id=1, source_target_pairs={{0,9},{1,10},{2,11},{3,12},{4,13},{5,14},{6,15},{7,8},{8,17},{9,18... | collective-permute-start | bytes 12296 | tf_op jit(solution)/shard_map/ppermute | solution.py:440
  8.1 0.2 collective-permute-start.1
  8.3 0.6 collective-permute-start
  8.9 0.0 copy-done.5
  8.9 0.0 copy-done.6
  9.0 0.1 pad_maximum_fusion.4
  9.1 0.0 copy-done.3
  9.1 0.1 copy.32
  9.2 0.0 copy-done.2
  9.2 0.1 copy.29
  9.4 0.1 copy.30
  9.5 0.0 copy-done.1
  9.5 0.1 pad_bitcast_fusion.5
  9.6 0.1 pad_bitcast_fusion.3
  9.7 0.1 pad_maximum_fusion.1
  9.8 0.2 reshape.180
  10.1 0.1 pad_maximum_fusion.dec_ref
  10.2 0.1 fusion.8.mix_ref
  10.3 0.0 copy-done.4
  10.3 0.1 broadcast_in_dim.40
  10.4 0.1 reshape.181.order_ref
  10.5 0.0 copy-done
  10.5 4.6 %inner.1 = (bf16[1536,1024]{1,0:T(8,128)(2,1)S(1)}, bf16[8,128,1024]{2,1,0:T(8,128)(2,1)S(1)}, bf16[8,128,1024]{2,1,0:T(8,128)(2,1)S(1)}) custom-call(s32[16,1024]{1,0:T(8,128)S(1)} %copy-done, bf16[3,128,256]{2,1,0:T(8,128)(2,1)S(1)} %pad_maximum_fusion.2.conv_ref, bf16[128,144]{1,0:T(8,128)(2,1)S(1)} %fusion.8.mix_ref, f32[8,2,64,1024]{3,2,1,0:T(8,128)} %cols_hbm.3), custom_call_target="tpu_custom_call" | custom-call | tf_op jit(solution)/shard_map/inner/pallas_call | solution.py:158
  15.1 0.0 collective-permute-done.2.from_d_ref
  15.1 0.0 collective-permute-done.1.from_y_ref
  15.1 3.1 %collective-permute-done.from_x_ref = f32[8,1152]{1,0:T(8,128)S(1)} collective-permute-done((f32[8,1152]{1,0:T(8,128)S(1)}, f32[8,1152]{1,0:T(8,128)S(1)}, u32[]{:S(2)}, u32[]{:S(2)}) %collective-permute-start) | collective-permute-done | bytes 36896 | tf_op jit(solution)/shard_map/ppermute | solution.py:439
  18.2 7.7 %field.1 = (f32[4,80,128]{2,1,0:T(8,128)S(1)}, f32[4,80,128]{2,1,0:T(8,128)S(1)}, bf16[2,512,80]{2,1,0:T(8,128)(2,1)S(1)}, bf16[1536,1024]{1,0:T(8,128)(2,1)S(1)}) custom-call(s32[16,1024]{1,0:T(8,128)S(1)} %copy-done, f32[8,1152]{1,0:T(8,128)S(1)} %collective-permute-done.from_x_ref, ...), custom_call_target="tpu_custom_call", output_to_operand_aliasing={{3}: (11, {})} | custom-call | tf_op jit(solution)/shard_map/field/pallas_call | solution.py:312
  25.9 0.2 collective-permute-start.3
  26.1 1.3 %collective-permute-done.3.got_ref = f32[4,80,128]{2,1,0:T(8,128)S(1)} collective-permute-done((f32[4,80,128]{2,1,0:T(8,128)S(1)}, f32[4,80,128]{2,1,0:T(8,128)S(1)}, u32[]{:S(2)}, u32[]{:S(2)}) %collective-permute-start.3) | collective-permute-done | bytes 163872 | tf_op jit(solution)/shard_map/ppermute | solution.py:453
  27.4 1.2 %collective-permute-start.6 = (f32[80,128]{1,0:T(8,128)S(1)}, f32[80,128]{1,0:T(8,128)S(1)}, u32[]{:S(2)}, u32[]{:S(2)}) collective-permute-start(f32[80,128]{1,0:T(8,128)S(1)} %get-tuple-element.23), channel_id=1, source_target_pairs={{0,6},{1,7},{2,4},{3,5},{4,2},{5,3},{6,0},{7,1},{8,14},{9,15},{10,... | collective-permute-start | bytes 122888 | tf_op jit(solution)/shard_map/ppermute | solution.py:453
  28.6 0.6 %collective-permute-start.5 = (f32[80,128]{1,0:T(8,128)S(1)}, f32[80,128]{1,0:T(8,128)S(1)}, u32[]{:S(2)}, u32[]{:S(2)}) collective-permute-start(f32[80,128]{1,0:T(8,128)S(1)} %get-tuple-element.24), channel_id=1, source_target_pairs={{0,4},{1,5},{2,6},{3,7},{4,0},{5,1},{6,2},{7,3},{8,12},{9,13},{10,... | collective-permute-start | bytes 122888 | tf_op jit(solution)/shard_map/ppermute | solution.py:453
  29.2 2.7 %collective-permute-start.4 = (f32[80,128]{1,0:T(8,128)S(1)}, f32[80,128]{1,0:T(8,128)S(1)}, u32[]{:S(2)}, u32[]{:S(2)}) collective-permute-start(f32[80,128]{1,0:T(8,128)S(1)} %get-tuple-element.25), channel_id=1, source_target_pairs={{0,2},{1,3},{2,0},{3,1},{4,6},{5,7},{6,4},{7,5},{8,10},{9,11},{10,... | collective-permute-start | bytes 122888 | tf_op jit(solution)/shard_map/ppermute | solution.py:453
  31.9 1.6 %collective-permute-done.6.d_ref = f32[80,128]{1,0:T(8,128)S(1)} collective-permute-done((f32[80,128]{1,0:T(8,128)S(1)}, f32[80,128]{1,0:T(8,128)S(1)}, u32[]{:S(2)}, u32[]{:S(2)}) %collective-permute-start.6) | collective-permute-done | bytes 40992 | tf_op jit(solution)/shard_map/ppermute | solution.py:453
  33.4 1.2 %collective-permute-done.5.c_ref = f32[80,128]{1,0:T(8,128)S(1)} collective-permute-done((f32[80,128]{1,0:T(8,128)S(1)}, f32[80,128]{1,0:T(8,128)S(1)}, u32[]{:S(2)}, u32[]{:S(2)}) %collective-permute-start.5) | collective-permute-done | bytes 40992 | tf_op jit(solution)/shard_map/ppermute | solution.py:453
  34.6 0.0 collective-permute-done.4.b_ref
  34.6 0.3 focal_share.1
  35.0 22.1 %all_to_all.5.x_ref = f32[32,8,128]{2,1,0:T(8,128)S(1)} all-to-all(f32[32,8,128]{2,1,0:T(8,128)S(1)} %focal_share.1), channel_id=1, replica_groups=mesh['px'=32,'py'=8] {'px'}, dimensions={0} | all-to-all | bytes 262144 | tf_op jit(solution)/shard_map/all_to_all | solution.py:458
  57.0 0.7 %total.1 = f32[1,2,512]{2,1,0:T(2,128)} custom-call(f32[32,8,128]{2,1,0:T(8,128)S(1)} %all_to_all.5.x_ref), custom_call_target="tpu_custom_call" | custom-call | tf_op jit(solution)/shard_map/total/pallas_call | solution.py:373
  (15 shorter events, 0.2 us)
Async XLA Ops:
  0.0 8.9 %copy-start.5 = (f32[64]{0:T(128)S(1)}, f32[64]{0:T(128)}, u32[]{:S(2)}) copy-start(f32[64]{0:T(128)} %param.11) | copy-start | bytes 772
  0.0 8.9 %copy-start.6 = (f32[64]{0:T(128)S(1)}, f32[64]{0:T(128)}, u32[]{:S(2)}) copy-start(f32[64]{0:T(128)} %param.13) | copy-start | bytes 772
  0.0 9.1 %copy-start.3 = (bf16[64,64]{1,0:T(8,128)(2,1)S(1)}, bf16[64,64]{1,0:T(8,128)(2,1)}, u32[]{:S(2)}) copy-start(bf16[64,64]{1,0:T(8,128)(2,1)} %param.12) | copy-start | bytes 24580
  0.0 9.2 %copy-start.2 = (bf16[64,144]{1,0:T(8,128)(2,1)S(1)}, bf16[64,144]{1,0:T(8,128)(2,1)}, u32[]{:S(2)}) copy-start(bf16[64,144]{1,0:T(8,128)(2,1)} %param.10) | copy-start | bytes 55300
  0.0 9.4 %copy-start.1 = (bf16[5,40,64]{2,1,0:T(8,128)(2,1)S(1)}, bf16[5,40,64]{2,1,0:T(8,128)(2,1)}, u32[]{:S(2)}) copy-start(bf16[5,40,64]{2,1,0:T(8,128)(2,1)} %param.14) | copy-start | bytes 76804
  1.4 8.9 %copy-start.4 = (s32[64]{0:T(128)S(1)}, s32[64]{0:T(128)}, u32[]{:S(2)}) copy-start(s32[64]{0:T(128)} %param.17) | copy-start | bytes 772
  1.4 9.1 %copy-start = (s32[16,1024]{1,0:T(8,128)S(1)}, s32[16,1024]{1,0:T(8,128)}, u32[]{:S(2)}) copy-start(s32[16,1024]{1,0:T(8,128)} %lev_ref.3) | copy-start | bytes 196612
  1.4 13.7 %collective-permute-start.2 = (f32[8,128]{1,0:T(8,128)S(1)}, f32[8,128]{1,0:T(8,128)S(1)}, u32[]{:S(2)}, u32[]{:S(2)}) collective-permute-start(f32[8,128]{1,0:T(8,128)S(1)} %get-tuple-element.16), channel_id=1, source_target_pairs={{0,9},{1,10},{2,11},{3,12},{4,13},{5,14},{6,15},{7,8},{8,17},{9,18... | collective-permute-start | bytes 12296 | tf_op jit(solution)/shard_map/ppermute | solution.py:440
  8.1 7.0 %collective-permute-start.1 = (f32[48,128]{1,0:T(8,128)S(1)}, f32[48,128]{1,0:T(8,128)S(1)}, u32[]{:S(2)}, u32[]{:S(2)}) collective-permute-start(f32[48,128]{1,0:T(8,128)S(1)} %get-tuple-element.15), channel_id=1, source_target_pairs={{0,1},{1,2},{2,3},{3,4},{4,5},{5,6},{6,7},{7,0},{8,9},{9,10},{10,1... | collective-permute-start | bytes 73736 | tf_op jit(solution)/shard_map/ppermute | solution.py:441
  8.3 9.9 %collective-permute-start = (f32[8,1152]{1,0:T(8,128)S(1)}, f32[8,1152]{1,0:T(8,128)S(1)}, u32[]{:S(2)}, u32[]{:S(2)}) collective-permute-start(f32[8,1152]{1,0:T(8,128)S(1)} %get-tuple-element.14), channel_id=1, source_target_pairs={{0,8},{8,16},{16,24},{24,32},{32,40},{40,48},{48,56},{56,64},{64,7... | collective-permute-start | bytes 110600 | tf_op jit(solution)/shard_map/ppermute | solution.py:439
  25.9 1.5 %collective-permute-start.3 = (f32[4,80,128]{2,1,0:T(8,128)S(1)}, f32[4,80,128]{2,1,0:T(8,128)S(1)}, u32[]{:S(2)}, u32[]{:S(2)}) collective-permute-start(f32[4,80,128]{2,1,0:T(8,128)S(1)} %get-tuple-element.22), channel_id=1, source_target_pairs={{0,1},{1,0},{2,3},{3,2},{4,5},{5,4},{6,7},{7,6},{8,9},{9,8},{10,11... | collective-permute-start | bytes 491528 | tf_op jit(solution)/shard_map/ppermute | solution.py:453
  27.4 6.0 %collective-permute-start.6 = (f32[80,128]{1,0:T(8,128)S(1)}, f32[80,128]{1,0:T(8,128)S(1)}, u32[]{:S(2)}, u32[]{:S(2)}) collective-permute-start(f32[80,128]{1,0:T(8,128)S(1)} %get-tuple-element.23), channel_id=1, source_target_pairs={{0,6},{1,7},{2,4},{3,5},{4,2},{5,3},{6,0},{7,1},{8,14},{9,15},{10,... | collective-permute-start | bytes 122888 | tf_op jit(solution)/shard_map/ppermute | solution.py:453
  28.6 6.1 %collective-permute-start.5 = (f32[80,128]{1,0:T(8,128)S(1)}, f32[80,128]{1,0:T(8,128)S(1)}, u32[]{:S(2)}, u32[]{:S(2)}) collective-permute-start(f32[80,128]{1,0:T(8,128)S(1)} %get-tuple-element.24), channel_id=1, source_target_pairs={{0,4},{1,5},{2,6},{3,7},{4,0},{5,1},{6,2},{7,3},{8,12},{9,13},{10,... | collective-permute-start | bytes 122888 | tf_op jit(solution)/shard_map/ppermute | solution.py:453
  29.2 5.5 %collective-permute-start.4 = (f32[80,128]{1,0:T(8,128)S(1)}, f32[80,128]{1,0:T(8,128)S(1)}, u32[]{:S(2)}, u32[]{:S(2)}) collective-permute-start(f32[80,128]{1,0:T(8,128)S(1)} %get-tuple-element.25), channel_id=1, source_target_pairs={{0,2},{1,3},{2,0},{3,1},{4,6},{5,7},{6,4},{7,5},{8,10},{9,11},{10,... | collective-permute-start | bytes 122888 | tf_op jit(solution)/shard_map/ppermute | solution.py:453

commit v2 on v1

v2 whole, which is shorter than its diff:
```python
import jax
import jax.numpy as jnp
from jax import lax
from jax.experimental import pallas as pl
from jax.experimental.pallas import tpu as pltpu
from jax.sharding import PartitionSpec as P

HIGH = lax.Precision.HIGHEST
F32 = jnp.float32
BF16 = jnp.bfloat16
NT = (((1,), (1,)), ((), ()))
TN = (((0,), (0,)), ((), ()))

ROWS = 16
COLS = 1024
HID = 64
LEVELS = 16
CH = 8
KS = 5
Z = 8
U = 64
V = 64
HALO = 4
ROWS_EXT = ROWS + HALO
SLOT = 3 * LEVELS
WINDOW = 4 * SLOT
BLOCK = 4
REL_ORDER = (0, 2, 4, 6, 1, 3, 5, 7)
PART = ROWS_EXT * CH // 2
HALF = BLOCK * CH // 2
VMEM = pl.BlockSpec(memory_space=pltpu.VMEM)
HBM = pl.BlockSpec(memory_space=pltpu.HBM)


def params(mib):
    return pltpu.CompilerParams(vmem_limit_bytes=mib << 20)

GELU_A = 0.7978845608028654
GELU_B = GELU_A * 0.044715


def iota(shape, dim):
    return lax.broadcasted_iota(jnp.int32, shape, dim)


def twice_gelu(x):
    return x + x * jnp.tanh(x * (GELU_A + GELU_B * (x * x)))


def split2(x):
    hi = x.astype(BF16)
    return hi, (x - hi.astype(F32)).astype(BF16)


def hbm(x):
    return pltpu.with_memory_space_constraint(x, pltpu.HBM)


def pack_y_kernel(lev_hbm, cols_hbm, out_ref, tile_ref, cols_ref, sems):
    last = pl.ds(COLS - 128, 128)
    copies = [
        pltpu.make_async_copy(cols_hbm.at[:, :, :, last], cols_ref, sems.at[0]),
        pltpu.make_async_copy(lev_hbm.at[:, last], tile_ref, sems.at[1]),
    ]
    for copy in copies:
        copy.start()
    copies[1].wait()
    out_ref[:ROWS, :] = tile_ref[...].astype(F32)
    copies[0].wait()
    for i in range(Z):
        edge = cols_ref[i].reshape(2 * V, 128).T
        out_ref[ROWS + HALO * i : ROWS + HALO * (i + 1), :] = edge[128 - HALO :, :]


def pack_y(levels, green_cols):
    return pl.pallas_call(
        pack_y_kernel,
        in_specs=[HBM] * 2,
        out_specs=VMEM,
        out_shape=jax.ShapeDtypeStruct((ROWS + Z * HALO, 128), F32),
        scratch_shapes=[
            pltpu.VMEM((ROWS, 128), jnp.int32),
            pltpu.VMEM((Z, 2, V, 128), F32),
            pltpu.SemaphoreType.DMA((2,)),
        ],
        compiler_params=params(4),
        name="pack_y",
    )(hbm(levels), hbm(green_cols))


def pack_x_kernel(lev_ref, rows_ref, from_y_ref, out_ref):
    z = lax.axis_index("py")
    out_ref[:, :128] = from_y_ref[8:ROWS, :]
    out_ref[:, 128 : 128 + COLS] = lev_ref[8:, :].astype(F32)
    out_ref[:, 128 + COLS :] = jnp.concatenate(
        [rows_ref[z, 0, 8:, :], rows_ref[z, 1, 8:, :]], axis=1
    )


def pack_x(levels, rows_t, from_y):
    return pl.pallas_call(
        pack_x_kernel,
        in_specs=[VMEM] * 3,
        out_specs=VMEM,
        out_shape=jax.ShapeDtypeStruct((8, COLS + 256), F32),
        compiler_params=params(4),
        name="pack_x",
    )(levels, rows_t, from_y)


def one_hot(row, level_ids):
    row = jnp.broadcast_to(row, level_ids.shape)
    return jnp.where(row == level_ids, 1.0, 0.0).astype(BF16)


def features(window, conv, conv_bias, mix, mix_bias):
    pre = jnp.dot(conv, window, preferred_element_type=F32) + conv_bias
    hidden = twice_gelu(pre).astype(BF16)
    mixed = jnp.dot(mix, hidden, preferred_element_type=F32) + mix_bias
    return twice_gelu(mixed).astype(BF16)


def inner_kernel(
    lev_ref, conv_ref, cb_ref, mix_ref, mb_ref, cols_hbm, feat_ref, cols_ref, ext_ref, hot_ref, sems
):
    z = lax.axis_index("py")
    copies = [
        pltpu.make_async_copy(cols_hbm.at[z ^ REL_ORDER[g]], cols_ref.at[g], sems.at[g])
        for g in range(Z)
    ]
    for copy in copies:
        copy.start()
    wide = COLS - 128
    lev = lev_ref[...].astype(F32)
    for b in range(3):
        ext_ref[b] = pltpu.roll(lev, 3 - b, 1)[:, 128:]
    level_ids = iota((LEVELS, wide), 0).astype(F32)

    def make_hot(q, _):
        for b in range(3):
            hot_ref[pl.ds(q * SLOT + b * LEVELS, LEVELS), :] = one_hot(
                ext_ref[b, pl.ds(q + 1, 1), :], level_ids
            )
        return 0

    lax.fori_loop(0, ROWS - 2, make_hot, 0, unroll=2)
    feat_ref[: BLOCK * HID, :] = jnp.zeros((BLOCK * HID, COLS), BF16)
    feat_ref[(BLOCK + ROWS) * HID :, :] = jnp.zeros((BLOCK * HID, COLS), BF16)
    conv_bias = jnp.broadcast_to(cb_ref[...], (2 * HID, wide))
    mix_bias = jnp.broadcast_to(mb_ref[...], (2 * HID, wide))
    for i in range(ROWS // 2 - 2):
        at = (2 * BLOCK + 2 * i) * HID
        feat_ref[at : at + 2 * HID, 128:] = features(
            hot_ref[i * 2 * SLOT : i * 2 * SLOT + WINDOW, :],
            conv_ref[...], conv_bias, mix_ref[...], mix_bias,
        )
    for copy in copies:
        copy.wait()


def inner(levels, conv_w, conv_b, mix_w, mix_b, green_cols):
    wide = COLS - 128
    return pl.pallas_call(
        inner_kernel,
        in_specs=[VMEM] * 5 + [HBM],
        out_specs=[VMEM] * 2,
        out_shape=[
            jax.ShapeDtypeStruct(((ROWS + 2 * BLOCK) * HID, COLS), BF16),
            jax.ShapeDtypeStruct((Z, 2, V, COLS), F32),
        ],
        scratch_shapes=[
            pltpu.VMEM((3, ROWS, wide), F32),
            pltpu.VMEM(((ROWS - 2) * SLOT, wide), BF16),
            pltpu.SemaphoreType.DMA((Z,)),
        ],
        compiler_params=params(16),
        name="inner",
    )(levels, conv_w, conv_b, mix_w, mix_b, hbm(green_cols))


def split_kernel(cols_ref, hi_ref, lo_ref):
    def split(g, _):
        hi_ref[g], lo_ref[g] = split2(cols_ref[g].reshape(2 * V, COLS))
        return 0

    lax.fori_loop(0, Z, split, 0)


def split_cols(cols):
    return pl.pallas_call(
        split_kernel,
        in_specs=[VMEM],
        out_specs=[VMEM] * 2,
        out_shape=[jax.ShapeDtypeStruct((Z, 2 * V, COLS), BF16)] * 2,
        compiler_params=params(4),
        name="split_cols",
    )(cols)


def column_sum(hi_ref, lo_ref, nf_ref, edge_ref, from_y_ref, out_ref, first):
    iy = lax.axis_index("py")
    n = 2 * PART
    sign = jnp.where(iota((1, 128), 1) < V, -1.0, 1.0)
    hi = hi_ref[first : first + 4].reshape(8 * V, COLS)
    lo = lo_ref[first : first + 4].reshape(8 * V, COLS)
    both = lax.dot_general(hi, nf_ref[:n, :], NT, preferred_element_type=F32)
    both = both + lax.dot_general(lo, nf_ref[:n, :], NT, preferred_element_type=F32)
    both = both + lax.dot_general(hi, nf_ref[n:, :], NT, preferred_element_type=F32)
    for g in range(4):
        out = both[2 * V * g : 2 * V * (g + 1)].T
        z = iy ^ REL_ORDER[first + g]
        green = from_y_ref[pl.ds(ROWS + HALO * z, HALO), :]
        green = jnp.concatenate([green, jnp.zeros((4, 128), F32)], axis=0)
        out = out + jnp.dot(edge_ref[:, :8], green, precision=HIGH, preferred_element_type=F32)
        out_ref[g] = out[:PART] + sign * pltpu.roll(out[PART:], V, 1)


def field_kernel(
    lev_ref, from_x_ref, from_y_ref, conv_ref, cb_ref, mix_ref, mb_ref, dec_ref,
    hi_ref, lo_ref, _, send_ref, nf_ref, edge_ref, feat_ref, ext_ref, hot_ref,
):
    first_x = lax.axis_index("px") == 0
    first_y = lax.axis_index("py") == 0
    own = jnp.concatenate([from_y_ref[:ROWS, :], lev_ref[...].astype(F32)], axis=1)
    ext = jnp.concatenate([from_x_ref[:, : 128 + COLS], own], axis=0)
    lane = iota((24, COLS), 1)
    for b in range(3):
        window = pltpu.roll(ext, 3 - b, 1)[:, 128:]
        if b != 1:
            cut = first_y & (lane == (2 if b == 0 else 1))
            window = jnp.where(cut, -1.0, window)
        ext_ref[b] = window
    level_ids = iota((LEVELS, COLS), 0).astype(F32)
    for o in range(4):
        for b in range(3):
            at = pl.ds(o * SLOT + b * LEVELS, LEVELS)
            for w in range(2):
                q = 2 * w + o
                hot_ref[w, at, :] = one_hot(ext_ref[b, q + 5 : q + 6, :], level_ids)
            for t in range(6):
                q = 2 * t + 4 + o
                hot_ref[2, at, t * 128 : (t + 1) * 128] = one_hot(
                    ext_ref[b, q + 5 : q + 6, :128], level_ids[:, :128]
                )
    conv_bias = jnp.broadcast_to(cb_ref[...], (2 * HID, COLS))
    mix_bias = jnp.broadcast_to(mb_ref[...], (2 * HID, COLS))
    slot = iota((1, WINDOW), 1) // SLOT
    for w in range(2):
        keep = jnp.where(first_x & (slot == (3 if w == 0 else 0)), 0.0, 1.0).astype(BF16)
        at = (BLOCK + 2 * w) * HID
        feat_ref[at : at + 2 * HID, :] = features(
            hot_ref[w], conv_ref[...] * keep, conv_bias, mix_ref[...], mix_bias
        )
    tiles = features(
        hot_ref[2, :, :768], conv_ref[...], conv_bias[:, :768], mix_ref[...], mix_bias[:, :768]
    )
    for t in range(6):
        at = (2 * BLOCK + 2 * t) * HID
        feat_ref[at : at + 2 * HID, :128] = tiles[:, t * 128 : (t + 1) * 128]

    lane = iota((1, COLS), 1)
    near = iota((1, 128), 1)
    pillar = iota((1, 2 * BLOCK * HID), 1) // HID
    for i in range(ROWS_EXT // BLOCK):
        dec = dec_ref[...]
        if i < 2:
            keep = jnp.where(first_x & ((pillar >= 6) if i == 0 else (pillar < 2)), 0.0, 1.0)
            dec = dec * keep.astype(BF16)
        at = i * BLOCK * HID
        taps = jnp.dot(
            dec, feat_ref[at : at + 2 * BLOCK * HID, :], preferred_element_type=F32
        )
        acc = jnp.zeros((2 * HALF, COLS), F32)
        edge = jnp.zeros((2 * HALF, 128), F32)
        for s in range(KS):
            part = taps[2 * HALF * s : 2 * HALF * (s + 1), :]
            k = KS - 1 - s
            ok = (lane < COLS - k) & ((lane + k >= 2) | jnp.logical_not(first_y))
            moved = part if k == 0 else pltpu.roll(part, COLS - k, 1)
            acc = acc + jnp.where(ok, moved, 0.0)
            ok = (near >= s) & (near < HALO) & ((near - s < 2) | jnp.logical_not(first_y))
            part = part[:, :128]
            moved = part if s == 0 else pltpu.roll(part, s, 1)
            edge = edge + jnp.where(ok, moved, 0.0)
        for part, values in enumerate(split2(acc)):
            for k in range(2):
                at = (2 * part + k) * PART + i * HALF
                nf_ref[at : at + HALF, :] = values[k * HALF : (k + 1) * HALF]
        for k in range(2):
            at = k * PART + i * HALF
            edge_ref[at : at + HALF, :] = edge[k * HALF : (k + 1) * HALF]

    column_sum(hi_ref, lo_ref, nf_ref, edge_ref, from_y_ref, send_ref, 4)


def field(levels, from_x, from_y, conv_w, conv_b, mix_w, mix_b, dec_w, hi, lo, feat):
    return pl.pallas_call(
        field_kernel,
        in_specs=[VMEM] * 11,
        out_specs=[VMEM] * 4,
        out_shape=[
            jax.ShapeDtypeStruct((4, PART, 128), F32),
            jax.ShapeDtypeStruct((4 * PART, COLS), BF16),
            jax.ShapeDtypeStruct((2 * PART, 128), F32),
            jax.ShapeDtypeStruct(feat.shape, BF16),
        ],
        input_output_aliases={10: 3},
        scratch_shapes=[
            pltpu.VMEM((3, 24, COLS), F32),
            pltpu.VMEM((3, WINDOW, COLS), BF16),
        ],
        compiler_params=params(16),
        name="field",
    )(levels, from_x, from_y, conv_w, conv_b, mix_w, mix_b, dec_w, hi, lo, feat)


def keep_kernel(hi_ref, lo_ref, nf_ref, edge_ref, from_y_ref, out_ref):
    column_sum(hi_ref, lo_ref, nf_ref, edge_ref, from_y_ref, out_ref, 0)


def keep_half(hi, lo, nf, edge, from_y):
    return pl.pallas_call(
        keep_kernel,
        in_specs=[VMEM] * 5,
        out_specs=VMEM,
        out_shape=jax.ShapeDtypeStruct((4, PART, 128), F32),
        compiler_params=params(8),
        name="keep_half",
    )(hi, lo, nf, edge, from_y)


def rows_kernel(from_x_ref, rows_ref, order_ref, out_ref):
    z = lax.axis_index("py")
    green = jnp.concatenate([rows_ref[z, 0], rows_ref[z, 1]], axis=1)
    green = jnp.concatenate([from_x_ref[:, 128 + COLS :], green], axis=0)
    n = ROWS + 8
    green = jnp.concatenate(split2(green), axis=0)
    pick = (order_ref[...] == iota((U, U * 4), 0)).astype(BF16)
    row = iota((3 * PART, 2 * n), 0)
    source = (row % PART) // 4 + (8 - HALO) + jnp.where(row // PART == 1, n, 0)
    spread = (iota((3 * PART, 2 * n), 1) == source).astype(BF16)
    mask = iota((3 * PART, U * 4), 0) % 4 == iota((3 * PART, U * 4), 1) % 4
    for j in range(2):
        ordered = jnp.dot(green[:, j * U : (j + 1) * U], pick, preferred_element_type=F32)
        wide = jnp.dot(spread, ordered.astype(BF16), preferred_element_type=F32)
        out_ref[j * U * 4 : (j + 1) * U * 4, :] = jnp.where(mask, wide, 0.0).T.astype(BF16)


def row_factors(from_x, rows_t, order):
    return pl.pallas_call(
        rows_kernel,
        in_specs=[VMEM] * 3,
        out_specs=VMEM,
        out_shape=jax.ShapeDtypeStruct((2 * U * 4, 3 * PART), BF16),
        compiler_params=params(4),
        name="row_factors",
    )(from_x, rows_t, order)


def focal_kernel(factor_ref, keep_ref, got_ref, b_ref, c_ref, d_ref, out_ref):
    t = ((keep_ref[0] + got_ref[0]) + b_ref[...]) + (c_ref[...] + d_ref[...])
    hi, lo = split2(t)
    out = jnp.dot(
        factor_ref[...], jnp.concatenate([hi, hi, lo], axis=0), preferred_element_type=F32
    )
    n = U * 4
    sign = jnp.where(iota((1, 128), 1) < V, -1.0, 1.0)
    out_ref[...] = (out[:n] + sign * pltpu.roll(out[n:], V, 1)).reshape(out_ref.shape)


def focal_share(factors, keep, got, b, c, d):
    return pl.pallas_call(
        focal_kernel,
        in_specs=[VMEM] * 6,
        out_specs=VMEM,
        out_shape=jax.ShapeDtypeStruct((U // 2, 8, 128), F32),
        compiler_params=params(4),
        name="focal_share",
    )(factors, keep, got, b, c, d)


def total_kernel(x_ref, out_ref):
    s = jnp.sum(x_ref[...], axis=0)
    for u in range(2):
        for k in range(2):
            for p in range(4):
                at = (k * 4 + p) * V
                row = u * 4 + p
                out_ref[0, u : u + 1, at : at + V] = s[row : row + 1, k * V : (k + 1) * V]


def total(parts):
    return pl.pallas_call(
        total_kernel,
        in_specs=[VMEM],
        out_specs=VMEM,
        out_shape=jax.ShapeDtypeStruct((1, 2, 8 * V), F32),
        compiler_params=params(4),
        name="total",
    )(parts)


def conv_weights(conv_table):
    return jnp.concatenate(
        [jnp.pad(conv_table, ((0, 0), (0, SLOT))), jnp.pad(conv_table, ((0, 0), (SLOT, 0)))], axis=0
    )


def mix_weights(mix_weight):
    w = mix_weight * jnp.asarray(0.5, BF16)
    return jnp.concatenate(
        [jnp.pad(w, ((0, 0), (0, HID))), jnp.pad(w, ((0, 0), (HID, 0)))], axis=0
    )


def decoder_weights(decoder):
    d = decoder * jnp.asarray(0.5, BF16)
    d = d[::-1].reshape(KS, KS, 2, 4, HID).transpose(1, 2, 3, 0, 4)
    rows = [
        jnp.pad(d, ((0, 0), (0, 0), (0, 0), (r, BLOCK - 1 - r), (0, 0))) for r in range(BLOCK)
    ]
    return jnp.stack(rows, axis=2).reshape(KS * CH * BLOCK, 2 * BLOCK * HID)


def bias_column(bias):
    return jnp.concatenate([bias, bias])[:, None]


def on_device(
    levels, conv_table, conv_bias, mix_weight, mix_bias, decoder, green_rows, green_cols, focal_order
):
    count_px = lax.axis_size("px")
    count_py = lax.axis_size("py")
    rows_t = jnp.swapaxes(green_rows, 2, 3)
    next_x = [(i, (i + 1) % count_px) for i in range(count_px)]
    next_y = [(i, (i + 1) % count_py) for i in range(count_py)]
    conv_w = conv_weights(conv_table)
    mix_w = mix_weights(mix_weight)
    dec_w = decoder_weights(decoder)
    conv_b = bias_column(conv_bias)
    mix_b = bias_column(mix_bias)
    order = jnp.broadcast_to(focal_order[:, None], (U, 4)).reshape(1, U * 4)
    conv_w, conv_b, mix_w, mix_b, dec_w, order = lax.optimization_barrier(
        (conv_w, conv_b, mix_w, mix_b, dec_w, order)
    )

    from_y = lax.ppermute(pack_y(levels, green_cols), "py", next_y)
    feat, cols = inner(levels, conv_w, conv_b, mix_w, mix_b, green_cols)
    from_y, feat, cols = lax.optimization_barrier((from_y, feat, cols))
    from_x = lax.ppermute(pack_x(levels, rows_t, from_y), "px", next_x)
    hi, lo = split_cols(cols)
    send, nf, edge, _ = field(
        levels, from_x, from_y, conv_w, conv_b, mix_w, mix_b, dec_w, hi, lo, feat
    )

    def swap(x, mask):
        return lax.ppermute(x, "py", [(i, i ^ mask) for i in range(count_py)])

    got = swap(send, 1)
    keep = keep_half(hi, lo, nf, edge, from_y)
    b, c, d = (swap(keep[i] + got[i], 2 * i) for i in (1, 2, 3))
    factors = row_factors(from_x, rows_t, order)
    share = focal_share(factors, keep, got, b, c, d)
    return total(lax.all_to_all(share, "px", 0, 0))


def solution(mesh):
    return jax.shard_map(
        on_device,
        mesh=mesh,
        in_specs=(
            P("px", "py"),
            P(),
            P(),
            P(),
            P(),
            P(),
            P(None, None, None, "px"),
            P(None, None, None, "py"),
            P(),
        ),
        out_specs=P("py", "px", None),
        check_vma=False,
    )
```

time: 58.3 us -> 54.7 us (0.938)
  Pallas kernels: 14.6 us -> 11.7 us
  starting transfers between devices: 12.2 us -> 11.3 us
  blocking collectives: 22.1 us -> 22.7 us
    pallas_call x3 -> x7, Pallas kernels: 13.6 us -> 10.7 us  [the longest x1 3.69 us: field(): pl.pallas_call(field_kernel, in_specs=[VMEM] * 11, out_specs=[VMEM] * 4,...]
    ppermute x3 -> x2, starting transfers between devices: 7.51 us -> 6.76 us  [the longest x1 6.68 us: on_device(): from_x = lax.ppermute(pack_x(levels, rows_t, from_y), 'px', next_x)]
    all_to_all x1, blocking collectives: 22.1 us -> 22.7 us  [on_device(): return total(lax.all_to_all(share, 'px', 0, 0))]
    ppermute x3 -> x2, waiting for transfers between devices: 3.12 us -> 3.02 us  [the longest x1 1.52 us: on_device(): from_x = lax.ppermute(pack_x(levels, rows_t, from_y), 'px', next_x)]
  transfers between devices with their start and end apart: 7 -> 6, of which waited for: 4 -> 4; matrix products, arithmetic and copies ran while one was open for 2% -> 2% of each run, Pallas kernels for 8% -> 10%
where the time goes in v2:
time: 54.7 us; the launch traced here: 54.6 us
  blocking collectives  22.7 us (41%)
  Pallas kernels  11.7 us (21%)
  starting transfers between devices  11.3 us (21%)
  waiting for transfers between devices  7.5 us (14%)
  local copies, waits for them, and re-layouts  0.78 us (1%)
    all_to_all x1, blocking collectives, on_device(): return total(lax.all_to_all(share, 'px', 0, 0))  22.7 us
    ppermute x1, starting transfers between devices, on_device(): from_x = lax.ppermute(pack_x(levels, rows_t, from_y), 'px', next_x)  6.68 us
    ppermute x4, starting transfers between devices, swap(): return lax.ppermute(x, 'py', [(i, i ^ mask) for i in range(count_py)])  4.57 us
    ppermute x4, waiting for transfers between devices, swap(): return lax.ppermute(x, 'py', [(i, i ^ mask) for i in range(count_py)])  4.48 us
    pallas_call x1, Pallas kernels, field(): pl.pallas_call(field_kernel, in_specs=[VMEM] * 11, out_specs=[VMEM] * 4,...  3.69 us
    pallas_call x1, Pallas kernels, inner(): pl.pallas_call(inner_kernel, in_specs=[VMEM] * 5 + [HBM], out_specs=[VMEM...  2.86 us
    ppermute x1, waiting for transfers between devices, on_device(): from_x = lax.ppermute(pack_x(levels, rows_t, from_y), 'px', next_x)  1.52 us
    ppermute x1, waiting for transfers between devices, on_device(): from_y = lax.ppermute(pack_y(levels, green_cols), 'py', next_y)  1.5 us
  transfers between devices with their start and end apart: 6, of which 4 were waited for; matrix products, arithmetic and copies ran while one was open for 2% of the time, Pallas kernels for 10%

profile of v2, /device:TPU:2, one launch (start us, length us, event | category | flops | bytes accessed | tf_op | source)
XLA Modules:
  0.0 54.6 jit_solution(16619448804642514070)
XLA Ops:
  0.0 0.0 copy-start
  0.0 0.0 copy-start.2
  0.0 0.0 copy-start.3
  0.0 0.0 copy-start.4
  0.0 0.0 copy-start.6
  0.0 0.0 copy-start.7
  0.0 0.0 copy-start.5
  0.0 1.3 %pack_y.1 = f32[48,128]{1,0:T(8,128)S(1)} custom-call(s32[16,1024]{1,0:T(8,128)} %lev_ref.5, f32[8,2,64,1024]{3,2,1,0:T(8,128)} %cols_hbm.3), custom_call_target="tpu_custom_call" | custom-call | tf_op jit(solution)/shard_map/pack_y/pallas_call | solution.py:76
  1.4 0.1 collective-permute-start
  1.5 0.0 copy-done.2
  1.6 0.0 copy-start.1
  1.6 0.1 pad_bitcast_fusion.3
  1.7 0.0 copy-done.3
  1.7 0.1 fusion.2.conv_ref
  1.8 0.0 copy-done.4
  1.8 0.1 fusion.8.mix_ref
  1.8 0.1 pad_maximum_fusion
  1.9 0.0 copy-done.6
  1.9 0.0 copy-done.7
  2.0 0.1 maximum_bitcast_fusion
  2.0 0.2 reshape.14.dec_ref
  2.3 0.0 copy-done.5
  2.3 0.1 broadcast_in_dim.14
  2.3 0.1 reshape.15.order_ref
  2.5 0.1 copy.23.cb_ref
  2.6 0.1 copy.24.mb_ref
  2.7 0.0 copy-done
  2.7 2.9 %inner.1 = (bf16[1536,1024]{1,0:T(8,128)(2,1)S(1)}, f32[8,2,64,1024]{3,2,1,0:T(8,128)S(1)}) custom-call(s32[16,1024]{1,0:T(8,128)S(1)} %copy-done, bf16[128,192]{1,0:T(8,128)(2,1)S(1)} %fusion.2.conv_ref, f32[128,1]{1,0:T(8,128)S(1)} %copy.23.cb_ref, bf16[128,128]{1,0:T(8,128)(2,1)S(1)} %fusion.8.mix_ref, f32[128,1]{1,0:T(8,128)S(1)} %copy.24.mb_ref, ...), custom_call_target="tpu_custom_call" | custom-call | tf_op jit(solution)/shard_map/inner/pallas_call | solution.py:163
  5.6 1.5 %collective-permute-done.from_y_ref = f32[48,128]{1,0:T(8,128)S(1)} collective-permute-done((f32[48,128]{1,0:T(8,128)S(1)}, f32[48,128]{1,0:T(8,128)S(1)}, u32[]{:S(2)}, u32[]{:S(2)}) %collective-permute-start) | collective-permute-done | bytes 24608 | tf_op jit(solution)/shard_map/ppermute | solution.py:447
  7.1 0.0 copy-done.1
  7.1 0.1 pack_x.1
  7.1 6.7 %collective-permute-start.1 = (f32[8,1280]{1,0:T(8,128)S(1)}, f32[8,1280]{1,0:T(8,128)S(1)}, u32[]{:S(2)}, u32[]{:S(2)}) collective-permute-start(f32[8,1280]{1,0:T(8,128)S(1)} %pack_x.1), channel_id=1, source_target_pairs={{0,8},{8,16},{16,24},{24,32},{32,40},{40,48},{48,56},{56,64},{64,7... | collective-permute-start | bytes 122888 | tf_op jit(solution)/shard_map/ppermute | solution.py:450
  13.8 0.7 %split_cols.1 = (bf16[8,128,1024]{2,1,0:T(8,128)(2,1)S(1)}, bf16[8,128,1024]{2,1,0:T(8,128)(2,1)S(1)}) custom-call(f32[8,2,64,1024]{3,2,1,0:T(8,128)S(1)} %get-tuple-element.29.cols_ref), custom_call_target="tpu_custom_call" | custom-call | tf_op jit(solution)/shard_map/split_cols/pallas_call | solution.py:190
  14.6 1.5 %collective-permute-done.1.from_x_ref = f32[8,1280]{1,0:T(8,128)S(1)} collective-permute-done((f32[8,1280]{1,0:T(8,128)S(1)}, f32[8,1280]{1,0:T(8,128)S(1)}, u32[]{:S(2)}, u32[]{:S(2)}) %collective-permute-start.1) | collective-permute-done | bytes 40992 | tf_op jit(solution)/shard_map/ppermute | solution.py:450
  16.1 3.7 %field.1 = (f32[4,80,128]{2,1,0:T(8,128)S(1)}, bf16[320,1024]{1,0:T(8,128)(2,1)S(1)}, f32[160,128]{1,0:T(8,128)S(1)}, bf16[1536,1024]{1,0:T(8,128)(2,1)S(1)}) custom-call(s32[16,1024]{1,0:T(8,128)S(1)} %copy-done, f32[8,1280]{1,0:T(8,128)S(1)} %collective-permute-done.1.from_x_ref, ...), custom_call_target="tpu_custom_call", output_to_operand_aliasing={{3}: (10, {})} | custom-call | tf_op jit(solution)/shard_map/field/pallas_call | solution.py:297
  19.8 0.1 collective-permute-start.2
  19.9 1.5 %keep_half.1.keep_ref = f32[4,80,128]{2,1,0:T(8,128)S(1)} custom-call(bf16[8,128,1024]{2,1,0:T(8,128)(2,1)S(1)} %get-tuple-element.30.hi_ref, bf16[8,128,1024]{2,1,0:T(8,128)(2,1)S(1)} %get-tuple-element.31.lo_ref, bf16[320,1024]{1,0:T(8,128)(2,1)S(1)} %get-tuple-element.34.nf_ref, f32[160,128]{1,0:T(8,128)S(1)} %get-tuple-element.35.edge_ref, ...), custom_call_target="tpu_custom_call" | custom-call | tf_op jit(solution)/shard_map/keep_half/pallas_call | solution.py:322
  21.4 0.0 collective-permute-done.2.got_ref
  21.4 1.4 %collective-permute-start.3 = (f32[80,128]{1,0:T(8,128)S(1)}, f32[80,128]{1,0:T(8,128)S(1)}, u32[]{:S(2)}, u32[]{:S(2)}) collective-permute-start(f32[80,128]{1,0:T(8,128)S(1)} %get-tuple-element.39), channel_id=1, source_target_pairs={{0,2},{1,3},{2,0},{3,1},{4,6},{5,7},{6,4},{7,5},{8,10},{9,11},{10,... | collective-permute-start | bytes 122888 | tf_op jit(solution)/shard_map/ppermute | solution.py:457
  22.8 2.3 %collective-permute-start.4 = (f32[80,128]{1,0:T(8,128)S(1)}, f32[80,128]{1,0:T(8,128)S(1)}, u32[]{:S(2)}, u32[]{:S(2)}) collective-permute-start(f32[80,128]{1,0:T(8,128)S(1)} %get-tuple-element.38), channel_id=1, source_target_pairs={{0,4},{1,5},{2,6},{3,7},{4,0},{5,1},{6,2},{7,3},{8,12},{9,13},{10,... | collective-permute-start | bytes 122888 | tf_op jit(solution)/shard_map/ppermute | solution.py:457
  25.1 0.8 %collective-permute-start.5 = (f32[80,128]{1,0:T(8,128)S(1)}, f32[80,128]{1,0:T(8,128)S(1)}, u32[]{:S(2)}, u32[]{:S(2)}) collective-permute-start(f32[80,128]{1,0:T(8,128)S(1)} %get-tuple-element.37), channel_id=1, source_target_pairs={{0,6},{1,7},{2,4},{3,5},{4,2},{5,3},{6,0},{7,1},{8,14},{9,15},{10,... | collective-permute-start | bytes 122888 | tf_op jit(solution)/shard_map/ppermute | solution.py:457
  25.9 0.5 row_factors.1.factor_ref
  26.4 0.0 collective-permute-done.3.b_ref
  26.4 1.6 %collective-permute-done.4.c_ref = f32[80,128]{1,0:T(8,128)S(1)} collective-permute-done((f32[80,128]{1,0:T(8,128)S(1)}, f32[80,128]{1,0:T(8,128)S(1)}, u32[]{:S(2)}, u32[]{:S(2)}) %collective-permute-start.4) | collective-permute-done | bytes 40992 | tf_op jit(solution)/shard_map/ppermute | solution.py:457
  28.0 2.9 %collective-permute-done.5.d_ref = f32[80,128]{1,0:T(8,128)S(1)} collective-permute-done((f32[80,128]{1,0:T(8,128)S(1)}, f32[80,128]{1,0:T(8,128)S(1)}, u32[]{:S(2)}, u32[]{:S(2)}) %collective-permute-start.5) | collective-permute-done | bytes 40992 | tf_op jit(solution)/shard_map/ppermute | solution.py:457
  30.9 0.3 focal_share.1
  31.2 22.7 %all_to_all.5.x_ref = f32[32,8,128]{2,1,0:T(8,128)S(1)} all-to-all(f32[32,8,128]{2,1,0:T(8,128)S(1)} %focal_share.1), channel_id=1, replica_groups=mesh['px'=32,'py'=8] {'px'}, dimensions={0} | all-to-all | bytes 262144 | tf_op jit(solution)/shard_map/all_to_all | solution.py:464
  53.9 0.7 %total.1 = f32[1,2,512]{2,1,0:T(2,128)} custom-call(f32[32,8,128]{2,1,0:T(8,128)S(1)} %all_to_all.5.x_ref), custom_call_target="tpu_custom_call" | custom-call | tf_op jit(solution)/shard_map/total/pallas_call | solution.py:393
  (4 shorter events, 0.1 us)
Async XLA Ops:
  0.0 2.7 %copy-start = (s32[16,1024]{1,0:T(8,128)S(1)}, s32[16,1024]{1,0:T(8,128)}, u32[]{:S(2)}) copy-start(s32[16,1024]{1,0:T(8,128)} %lev_ref.5) | copy-start | bytes 196612
  0.0 1.5 %copy-start.2 = (bf16[5,40,64]{2,1,0:T(8,128)(2,1)S(1)}, bf16[5,40,64]{2,1,0:T(8,128)(2,1)}, u32[]{:S(2)}) copy-start(bf16[5,40,64]{2,1,0:T(8,128)(2,1)} %param.14) | copy-start | bytes 76804
  0.0 1.7 %copy-start.3 = (bf16[64,144]{1,0:T(8,128)(2,1)S(1)}, bf16[64,144]{1,0:T(8,128)(2,1)}, u32[]{:S(2)}) copy-start(bf16[64,144]{1,0:T(8,128)(2,1)} %param.10) | copy-start | bytes 55300
  0.0 1.8 %copy-start.4 = (bf16[64,64]{1,0:T(8,128)(2,1)S(1)}, bf16[64,64]{1,0:T(8,128)(2,1)}, u32[]{:S(2)}) copy-start(bf16[64,64]{1,0:T(8,128)(2,1)} %param.12) | copy-start | bytes 24580
  0.0 1.9 %copy-start.6 = (f32[64]{0:T(128)S(1)}, f32[64]{0:T(128)}, u32[]{:S(2)}) copy-start(f32[64]{0:T(128)} %param.11) | copy-start | bytes 772
  0.0 1.9 %copy-start.7 = (f32[64]{0:T(128)S(1)}, f32[64]{0:T(128)}, u32[]{:S(2)}) copy-start(f32[64]{0:T(128)} %param.13) | copy-start | bytes 772
  0.0 2.2 %copy-start.5 = (s32[64]{0:T(128)S(1)}, s32[64]{0:T(128)}, u32[]{:S(2)}) copy-start(s32[64]{0:T(128)} %param.17) | copy-start | bytes 772
  1.4 5.7 %collective-permute-start = (f32[48,128]{1,0:T(8,128)S(1)}, f32[48,128]{1,0:T(8,128)S(1)}, u32[]{:S(2)}, u32[]{:S(2)}) collective-permute-start(f32[48,128]{1,0:T(8,128)S(1)} %pack_y.1), channel_id=1, source_target_pairs={{0,1},{1,2},{2,3},{3,4},{4,5},{5,6},{6,7},{7,0},{8,9},{9,10},{10,1... | collective-permute-start | bytes 73736 | tf_op jit(solution)/shard_map/ppermute | solution.py:447
  1.6 5.5 %copy-start.1 = (f32[8,2,64,16]{2,3,1,0:T(8,128)S(1)}, f32[8,2,64,16]{2,3,1,0:T(8,128)}, u32[]{:S(2)}) copy-start(f32[8,2,64,16]{2,3,1,0:T(8,128)} %param.15) | copy-start | bytes 196612
  7.1 8.9 %collective-permute-start.1 = (f32[8,1280]{1,0:T(8,128)S(1)}, f32[8,1280]{1,0:T(8,128)S(1)}, u32[]{:S(2)}, u32[]{:S(2)}) collective-permute-start(f32[8,1280]{1,0:T(8,128)S(1)} %pack_x.1), channel_id=1, source_target_pairs={{0,8},{8,16},{16,24},{24,32},{32,40},{40,48},{48,56},{56,64},{64,7... | collective-permute-start | bytes 122888 | tf_op jit(solution)/shard_map/ppermute | solution.py:450
  19.8 1.6 %collective-permute-start.2 = (f32[4,80,128]{2,1,0:T(8,128)S(1)}, f32[4,80,128]{2,1,0:T(8,128)S(1)}, u32[]{:S(2)}, u32[]{:S(2)}) collective-permute-start(f32[4,80,128]{2,1,0:T(8,128)S(1)} %get-tuple-element.36), channel_id=1, source_target_pairs={{0,1},{1,0},{2,3},{3,2},{4,5},{5,4},{6,7},{7,6},{8,9},{9,8},{10,11... | collective-permute-start | bytes 491528 | tf_op jit(solution)/shard_map/ppermute | solution.py:457
  21.4 5.0 %collective-permute-start.3 = (f32[80,128]{1,0:T(8,128)S(1)}, f32[80,128]{1,0:T(8,128)S(1)}, u32[]{:S(2)}, u32[]{:S(2)}) collective-permute-start(f32[80,128]{1,0:T(8,128)S(1)} %get-tuple-element.39), channel_id=1, source_target_pairs={{0,2},{1,3},{2,0},{3,1},{4,6},{5,7},{6,4},{7,5},{8,10},{9,11},{10,... | collective-permute-start | bytes 122888 | tf_op jit(solution)/shard_map/ppermute | solution.py:457
  22.8 5.2 %collective-permute-start.4 = (f32[80,128]{1,0:T(8,128)S(1)}, f32[80,128]{1,0:T(8,128)S(1)}, u32[]{:S(2)}, u32[]{:S(2)}) collective-permute-start(f32[80,128]{1,0:T(8,128)S(1)} %get-tuple-element.38), channel_id=1, source_target_pairs={{0,4},{1,5},{2,6},{3,7},{4,0},{5,1},{6,2},{7,3},{8,12},{9,13},{10,... | collective-permute-start | bytes 122888 | tf_op jit(solution)/shard_map/ppermute | solution.py:457
  25.1 5.8 %collective-permute-start.5 = (f32[80,128]{1,0:T(8,128)S(1)}, f32[80,128]{1,0:T(8,128)S(1)}, u32[]{:S(2)}, u32[]{:S(2)}) collective-permute-start(f32[80,128]{1,0:T(8,128)S(1)} %get-tuple-element.37), channel_id=1, source_target_pairs={{0,6},{1,7},{2,4},{3,5},{4,2},{5,3},{6,0},{7,1},{8,14},{9,15},{10,... | collective-permute-start | bytes 122888 | tf_op jit(solution)/shard_map/ppermute | solution.py:457

commit v3 on v2

--- a/solution.py
+++ b/solution.py
@@ -56,56 +56,47 @@
     return pltpu.with_memory_space_constraint(x, pltpu.HBM)
 
 
-def pack_y_kernel(lev_hbm, cols_hbm, out_ref, tile_ref, cols_ref, sems):
+def pack_kernel(lev_hbm, rows_hbm, cols_hbm, to_x_ref, to_y_ref, lev_ref, tile_ref, rows_ref, cols_ref, sems):
+    z = lax.axis_index("py")
     last = pl.ds(COLS - 128, 128)
     copies = [
         pltpu.make_async_copy(cols_hbm.at[:, :, :, last], cols_ref, sems.at[0]),
-        pltpu.make_async_copy(lev_hbm.at[:, last], tile_ref, sems.at[1]),
+        pltpu.make_async_copy(lev_hbm.at[pl.ds(8, 8), :], lev_ref, sems.at[1]),
+        pltpu.make_async_copy(lev_hbm.at[:, last], tile_ref, sems.at[2]),
+        pltpu.make_async_copy(rows_hbm.at[z], rows_ref, sems.at[3]),
     ]
     for copy in copies:
         copy.start()
-    copies[1].wait()
-    out_ref[:ROWS, :] = tile_ref[...].astype(F32)
+    for copy in copies[1:]:
+        copy.wait()
+    to_x_ref[:, :COLS] = lev_ref[...].astype(F32)
+    to_x_ref[:, COLS:] = jnp.concatenate([rows_ref[0, 8:, :], rows_ref[1, 8:, :]], axis=1)
+    to_y_ref[:ROWS, :] = tile_ref[...].astype(F32)
     copies[0].wait()
     for i in range(Z):
         edge = cols_ref[i].reshape(2 * V, 128).T
-        out_ref[ROWS + HALO * i : ROWS + HALO * (i + 1), :] = edge[128 - HALO :, :]
-
-
-def pack_y(levels, green_cols):
-    return pl.pallas_call(
-        pack_y_kernel,
-        in_specs=[HBM] * 2,
-        out_specs=VMEM,
-        out_shape=jax.ShapeDtypeStruct((ROWS + Z * HALO, 128), F32),
+        to_y_ref[ROWS + HALO * i : ROWS + HALO * (i + 1), :] = edge[128 - HALO :, :]
+
+
+def pack(levels, rows_t, green_cols):
+    return pl.pallas_call(
+        pack_kernel,
+        in_specs=[HBM] * 3,
+        out_specs=[VMEM] * 2,
+        out_shape=[
+            jax.ShapeDtypeStruct((8, COLS + 128), F32),
+            jax.ShapeDtypeStruct((ROWS + Z * HALO, 128), F32),
+        ],
         scratch_shapes=[
+            pltpu.VMEM((8, COLS), jnp.int32),
             pltpu.VMEM((ROWS, 128), jnp.int32),
+            pltpu.VMEM((2, ROWS, U), F32),
             pltpu.VMEM((Z, 2, V, 128), F32),
-            pltpu.SemaphoreType.DMA((2,)),
+            pltpu.SemaphoreType.DMA((4,)),
         ],
         compiler_params=params(4),
-        name="pack_y",
-    )(hbm(levels), hbm(green_cols))
-
-
-def pack_x_kernel(lev_ref, rows_ref, from_y_ref, out_ref):
-    z = lax.axis_index("py")
-    out_ref[:, :128] = from_y_ref[8:ROWS, :]
-    out_ref[:, 128 : 128 + COLS] = lev_ref[8:, :].astype(F32)
-    out_ref[:, 128 + COLS :] = jnp.concatenate(
-        [rows_ref[z, 0, 8:, :], rows_ref[z, 1, 8:, :]], axis=1
-    )
-
-
-def pack_x(levels, rows_t, from_y):
-    return pl.pallas_call(
-        pack_x_kernel,
-        in_specs=[VMEM] * 3,
-        out_specs=VMEM,
-        out_shape=jax.ShapeDtypeStruct((8, COLS + 256), F32),
-        compiler_params=params(4),
-        name="pack_x",
-    )(levels, rows_t, from_y)
+        name="pack",
+    )(hbm(levels), hbm(rows_t), hbm(green_cols))
 
 
 def one_hot(row, level_ids):
@@ -121,7 +112,8 @@
 
 
 def inner_kernel(
-    lev_ref, conv_ref, cb_ref, mix_ref, mb_ref, cols_hbm, feat_ref, cols_ref, ext_ref, hot_ref, sems
+    lev_ref, conv_ref, cb_ref, mix_ref, mb_ref, cols_hbm, feat_ref, hi_ref, lo_ref,
+    ext_ref, hot_ref, cols_ref, sems,
 ):
     z = lax.axis_index("py")
     copies = [
@@ -157,20 +149,28 @@
     for copy in copies:
         copy.wait()
 
+    def split(g, _):
+        hi_ref[g], lo_ref[g] = split2(cols_ref[g].reshape(2 * V, COLS))
+        return 0
+
+    lax.fori_loop(0, Z, split, 0)
+
 
 def inner(levels, conv_w, conv_b, mix_w, mix_b, green_cols):
     wide = COLS - 128
     return pl.pallas_call(
         inner_kernel,
         in_specs=[VMEM] * 5 + [HBM],
-        out_specs=[VMEM] * 2,
+        out_specs=[VMEM] * 3,
         out_shape=[
             jax.ShapeDtypeStruct(((ROWS + 2 * BLOCK) * HID, COLS), BF16),
-            jax.ShapeDtypeStruct((Z, 2, V, COLS), F32),
+            jax.ShapeDtypeStruct((Z, 2 * V, COLS), BF16),
+            jax.ShapeDtypeStruct((Z, 2 * V, COLS), BF16),
         ],
         scratch_shapes=[
             pltpu.VMEM((3, ROWS, wide), F32),
             pltpu.VMEM(((ROWS - 2) * SLOT, wide), BF16),
+            pltpu.VMEM((Z, 2, V, COLS), F32),
             pltpu.SemaphoreType.DMA((Z,)),
         ],
         compiler_params=params(16),
@@ -178,35 +178,80 @@
     )(levels, conv_w, conv_b, mix_w, mix_b, hbm(green_cols))
 
 
-def split_kernel(cols_ref, hi_ref, lo_ref):
-    def split(g, _):
-        hi_ref[g], lo_ref[g] = split2(cols_ref[g].reshape(2 * V, COLS))
-        return 0
-
-    lax.fori_loop(0, Z, split, 0)
-
-
-def split_cols(cols):
-    return pl.pallas_call(
-        split_kernel,
-        in_specs=[VMEM],
-        out_specs=[VMEM] * 2,
-        out_shape=[jax.ShapeDtypeStruct((Z, 2 * V, COLS), BF16)] * 2,
-        compiler_params=params(4),
-        name="split_cols",
-    )(cols)
-
-
-def column_sum(hi_ref, lo_ref, nf_ref, edge_ref, from_y_ref, out_ref, first):
+def outer_kernel(
+    lev_ref, from_x_ref, from_y_ref, conv_ref, cb_ref, mix_ref, mb_ref, _, feat_ref, ext_ref, hot_ref
+):
+    first_x = lax.axis_index("px") == 0
+    first_y = lax.axis_index("py") == 0
+    ext = jnp.concatenate([from_x_ref[:, :COLS], lev_ref[...].astype(F32)], axis=0)
+    left = jnp.concatenate([jnp.zeros((8, 128), F32), from_y_ref[:ROWS, :]], axis=0)
+    lane = iota((24, 128), 1)
+    for b in range(3):
+        window = pltpu.roll(ext, 3 - b, 1)
+        tile = pltpu.roll(jnp.concatenate([left, ext[:, :128]], axis=1), 3 - b, 1)[:, 128:]
+        if b != 1:
+            tile = jnp.where(first_y & (lane == (2 if b == 0 else 1)), -1.0, tile)
+        ext_ref[b] = jnp.concatenate([tile, window[:, 128:]], axis=1)
+    wide = COLS - 128
+    level_ids = iota((LEVELS, wide), 0).astype(F32)
+    for o in range(4):
+        for b in range(3):
+            at = pl.ds(o * SLOT + b * LEVELS, LEVELS)
+            for w in range(2):
+                q = 2 * w + o
+                hot_ref[w, at, :] = one_hot(ext_ref[b, q + 5 : q + 6, 128:], level_ids)
+            for t in range(6):
+                q = 2 * t + 4 + o
+                hot_ref[2, at, t * 128 : (t + 1) * 128] = one_hot(
+                    ext_ref[b, q + 5 : q + 6, :128], level_ids[:, :128]
+                )
+    conv_bias = jnp.broadcast_to(cb_ref[...], (2 * HID, wide))
+    mix_bias = jnp.broadcast_to(mb_ref[...], (2 * HID, wide))
+    for w in range(2):
+        at = (BLOCK + 2 * w) * HID
+        feat_ref[at : at + 2 * HID, 128:] = features(
+            hot_ref[w], cut_conv(conv_ref[...], w, first_x), conv_bias, mix_ref[...], mix_bias
+        )
+    tiles = features(
+        hot_ref[2, :, :768], conv_ref[...], conv_bias[:, :768], mix_ref[...], mix_bias[:, :768]
+    )
+    for t in range(6):
+        at = (2 * BLOCK + 2 * t) * HID
+        feat_ref[at : at + 2 * HID, :128] = tiles[:, t * 128 : (t + 1) * 128]
+
+
+def cut_conv(conv, w, first_x):
+    slot = iota((1, WINDOW), 1) // SLOT
+    keep = jnp.where(first_x & (slot == (3 if w == 0 else 0)), 0.0, 1.0)
+    return conv * keep.astype(BF16)
+
+
+def outer(levels, from_x, from_y, conv_w, conv_b, mix_w, mix_b, feat):
+    return pl.pallas_call(
+        outer_kernel,
+        in_specs=[VMEM] * 8,
+        out_specs=VMEM,
+        out_shape=jax.ShapeDtypeStruct(feat.shape, BF16),
+        input_output_aliases={7: 0},
+        scratch_shapes=[
+            pltpu.VMEM((3, 24, COLS), F32),
+            pltpu.VMEM((3, WINDOW, COLS - 128), BF16),
+        ],
+        compiler_params=params(12),
+        name="outer",
+    )(levels, from_x, from_y, conv_w, conv_b, mix_w, mix_b, feat)
+
+
+def column_sum(hi_ref, lo_ref, nf_ref, edge_ref, from_y_ref, out_ref, first, count):
     iy = lax.axis_index("py")
     n = 2 * PART
     sign = jnp.where(iota((1, 128), 1) < V, -1.0, 1.0)
-    hi = hi_ref[first : first + 4].reshape(8 * V, COLS)
-    lo = lo_ref[first : first + 4].reshape(8 * V, COLS)
+    hi = hi_ref[first : first + count].reshape(2 * V * count, COLS)
+    lo = lo_ref[first : first + count].reshape(2 * V * count, COLS)
     both = lax.dot_general(hi, nf_ref[:n, :], NT, preferred_element_type=F32)
     both = both + lax.dot_general(lo, nf_ref[:n, :], NT, preferred_element_type=F32)
     both = both + lax.dot_general(hi, nf_ref[n:, :], NT, preferred_element_type=F32)
-    for g in range(4):
+    for g in range(count):
         out = both[2 * V * g : 2 * V * (g + 1)].T
         z = iy ^ REL_ORDER[first + g]
         green = from_y_ref[pl.ds(ROWS + HALO * z, HALO), :]
@@ -216,52 +261,37 @@
 
 
 def field_kernel(
-    lev_ref, from_x_ref, from_y_ref, conv_ref, cb_ref, mix_ref, mb_ref, dec_ref,
+    lev_ref, from_x_ref, from_y_ref, from_d_ref, conv_ref, cb_ref, mix_ref, mb_ref, dec_ref,
     hi_ref, lo_ref, _, send_ref, nf_ref, edge_ref, feat_ref, ext_ref, hot_ref,
 ):
     first_x = lax.axis_index("px") == 0
     first_y = lax.axis_index("py") == 0
-    own = jnp.concatenate([from_y_ref[:ROWS, :], lev_ref[...].astype(F32)], axis=1)
-    ext = jnp.concatenate([from_x_ref[:, : 128 + COLS], own], axis=0)
-    lane = iota((24, COLS), 1)
+    tile = jnp.concatenate([from_x_ref[:, :128], lev_ref[:8, :128].astype(F32)], axis=0)
+    left = jnp.concatenate([from_d_ref[:, COLS - 128 : COLS], from_y_ref[:8, :]], axis=0)
+    ext = jnp.concatenate([left, tile], axis=1)
+    lane = iota((16, 128), 1)
     for b in range(3):
         window = pltpu.roll(ext, 3 - b, 1)[:, 128:]
         if b != 1:
-            cut = first_y & (lane == (2 if b == 0 else 1))
-            window = jnp.where(cut, -1.0, window)
+            window = jnp.where(first_y & (lane == (2 if b == 0 else 1)), -1.0, window)
         ext_ref[b] = window
-    level_ids = iota((LEVELS, COLS), 0).astype(F32)
-    for o in range(4):
-        for b in range(3):
-            at = pl.ds(o * SLOT + b * LEVELS, LEVELS)
-            for w in range(2):
+    level_ids = iota((LEVELS, 128), 0).astype(F32)
+    for w in range(2):
+        for o in range(4):
+            for b in range(3):
                 q = 2 * w + o
-                hot_ref[w, at, :] = one_hot(ext_ref[b, q + 5 : q + 6, :], level_ids)
-            for t in range(6):
-                q = 2 * t + 4 + o
-                hot_ref[2, at, t * 128 : (t + 1) * 128] = one_hot(
-                    ext_ref[b, q + 5 : q + 6, :128], level_ids[:, :128]
-                )
-    conv_bias = jnp.broadcast_to(cb_ref[...], (2 * HID, COLS))
-    mix_bias = jnp.broadcast_to(mb_ref[...], (2 * HID, COLS))
-    slot = iota((1, WINDOW), 1) // SLOT
+                at = o * SLOT + b * LEVELS
+                hot_ref[w, at : at + LEVELS, :] = one_hot(ext_ref[b, q + 5 : q + 6, :], level_ids)
     for w in range(2):
-        keep = jnp.where(first_x & (slot == (3 if w == 0 else 0)), 0.0, 1.0).astype(BF16)
         at = (BLOCK + 2 * w) * HID
-        feat_ref[at : at + 2 * HID, :] = features(
-            hot_ref[w], conv_ref[...] * keep, conv_bias, mix_ref[...], mix_bias
+        feat_ref[at : at + 2 * HID, :128] = features(
+            hot_ref[w], cut_conv(conv_ref[...], w, first_x), cb_ref[...], mix_ref[...], mb_ref[...]
         )
-    tiles = features(
-        hot_ref[2, :, :768], conv_ref[...], conv_bias[:, :768], mix_ref[...], mix_bias[:, :768]
-    )
-    for t in range(6):
-        at = (2 * BLOCK + 2 * t) * HID
-        feat_ref[at : at + 2 * HID, :128] = tiles[:, t * 128 : (t + 1) * 128]
 
     lane = iota((1, COLS), 1)
     near = iota((1, 128), 1)
     pillar = iota((1, 2 * BLOCK * HID), 1) // HID
-    for i in range(ROWS_EXT // BLOCK):
+    for i in reversed(range(ROWS_EXT // BLOCK)):
         dec = dec_ref[...]
         if i < 2:
             keep = jnp.where(first_x & ((pillar >= 6) if i == 0 else (pillar < 2)), 0.0, 1.0)
@@ -290,13 +320,13 @@
             at = k * PART + i * HALF
             edge_ref[at : at + HALF, :] = edge[k * HALF : (k + 1) * HALF]
 
-    column_sum(hi_ref, lo_ref, nf_ref, edge_ref, from_y_ref, send_ref, 4)
-
-
-def field(levels, from_x, from_y, conv_w, conv_b, mix_w, mix_b, dec_w, hi, lo, feat):
+    column_sum(hi_ref, lo_ref, nf_ref, edge_ref, from_y_ref, send_ref, 4, 4)
+
+
+def field(levels, from_x, from_y, from_d, conv_w, conv_b, mix_w, mix_b, dec_w, hi, lo, feat):
     return pl.pallas_call(
         field_kernel,
-        in_specs=[VMEM] * 11,
+        in_specs=[VMEM] * 12,
         out_specs=[VMEM] * 4,
         out_shape=[
             jax.ShapeDtypeStruct((4, PART, 128), F32),
@@ -304,35 +334,34 @@
             jax.ShapeDtypeStruct((2 * PART, 128), F32),
             jax.ShapeDtypeStruct(feat.shape, BF16),
         ],
-        input_output_aliases={10: 3},
+        input_output_aliases={11: 3},
         scratch_shapes=[
-            pltpu.VMEM((3, 24, COLS), F32),
-            pltpu.VMEM((3, WINDOW, COLS), BF16),
-        ],
-        compiler_params=params(16),
+            pltpu.VMEM((3, 16, 128), F32),
+            pltpu.VMEM((2, WINDOW, 128), BF16),
+        ],
+        compiler_params=params(12),
         name="field",
-    )(levels, from_x, from_y, conv_w, conv_b, mix_w, mix_b, dec_w, hi, lo, feat)
-
-
-def keep_kernel(hi_ref, lo_ref, nf_ref, edge_ref, from_y_ref, out_ref):
-    column_sum(hi_ref, lo_ref, nf_ref, edge_ref, from_y_ref, out_ref, 0)
-
-
-def keep_half(hi, lo, nf, edge, from_y):
+    )(levels, from_x, from_y, from_d, conv_w, conv_b, mix_w, mix_b, dec_w, hi, lo, feat)
+
+
+def keep_planes(hi, lo, nf, edge, from_y, first, count):
+    def keep_kernel(hi_ref, lo_ref, nf_ref, edge_ref, from_y_ref, out_ref):
+        column_sum(hi_ref, lo_ref, nf_ref, edge_ref, from_y_ref, out_ref, first, count)
+
     return pl.pallas_call(
         keep_kernel,
         in_specs=[VMEM] * 5,
         out_specs=VMEM,
-        out_shape=jax.ShapeDtypeStruct((4, PART, 128), F32),
+        out_shape=jax.ShapeDtypeStruct((count, PART, 128), F32),
         compiler_params=params(8),
-        name="keep_half",
+        name="keep_planes",
     )(hi, lo, nf, edge, from_y)
 
 
 def rows_kernel(from_x_ref, rows_ref, order_ref, out_ref):
     z = lax.axis_index("py")
     green = jnp.concatenate([rows_ref[z, 0], rows_ref[z, 1]], axis=1)
-    green = jnp.concatenate([from_x_ref[:, 128 + COLS :], green], axis=0)
+    green = jnp.concatenate([from_x_ref[:, COLS:], green], axis=0)
     n = ROWS + 8
     green = jnp.concatenate(split2(green), axis=0)
     pick = (order_ref[...] == iota((U, U * 4), 0)).astype(BF16)
@@ -444,21 +473,24 @@
         (conv_w, conv_b, mix_w, mix_b, dec_w, order)
     )
 
-    from_y = lax.ppermute(pack_y(levels, green_cols), "py", next_y)
-    feat, cols = inner(levels, conv_w, conv_b, mix_w, mix_b, green_cols)
-    from_y, feat, cols = lax.optimization_barrier((from_y, feat, cols))
-    from_x = lax.ppermute(pack_x(levels, rows_t, from_y), "px", next_x)
-    hi, lo = split_cols(cols)
+    to_x, to_y = pack(levels, rows_t, green_cols)
+    from_x = lax.ppermute(to_x, "px", next_x)
+    from_y = lax.ppermute(to_y, "py", next_y)
+    feat, hi, lo = inner(levels, conv_w, conv_b, mix_w, mix_b, green_cols)
+    from_x, from_y, feat = lax.optimization_barrier((from_x, from_y, feat))
+    from_d = lax.ppermute(from_x, "py", next_y)
+    feat = outer(levels, from_x, from_y, conv_w, conv_b, mix_w, mix_b, feat)
     send, nf, edge, _ = field(
-        levels, from_x, from_y, conv_w, conv_b, mix_w, mix_b, dec_w, hi, lo, feat
+        levels, from_x, from_y, from_d, conv_w, conv_b, mix_w, mix_b, dec_w, hi, lo, feat
     )
 
     def swap(x, mask):
         return lax.ppermute(x, "py", [(i, i ^ mask) for i in range(count_py)])
 
     got = swap(send, 1)
-    keep = keep_half(hi, lo, nf, edge, from_y)
-    b, c, d = (swap(keep[i] + got[i], 2 * i) for i in (1, 2, 3))
+    keep = keep_planes(hi, lo, nf, edge, from_y, 1, 3)
+    b, c, d = (swap(keep[i - 1] + got[i], 2 * i) for i in (1, 2, 3))
+    keep = keep_planes(hi, lo, nf, edge, from_y, 0, 1)
     factors = row_factors(from_x, rows_t, order)
     share = focal_share(factors, keep, got, b, c, d)
     return total(lax.all_to_all(share, "px", 0, 0))

time: 54.7 us -> 53.4 us (0.976)
  waiting for transfers between devices: 7.5 us -> 4.71 us
  starting transfers between devices: 11.3 us -> 12.8 us
  blocking collectives: 22.7 us -> 21.5 us
  Pallas kernels: 11.7 us -> 12.7 us
    ppermute x4, waiting for transfers between devices: 4.48 us -> 1.58 us  [swap(): return lax.ppermute(x, 'py', [(i, i ^ mask) for i in range(count_py)])]
    ppermute x2 -> x3, starting transfers between devices: 6.76 us -> 8.22 us  [the longest x1 7.27 us: on_device(): from_x = lax.ppermute(to_x, 'px', next_x)]
    all_to_all x1, blocking collectives: 22.7 us -> 21.5 us  [on_device(): return total(lax.all_to_all(share, 'px', 0, 0))]
    pallas_call x1, Pallas kernels: 2.86 us -> 3.59 us  [inner(): pl.pallas_call(inner_kernel, in_specs=[VMEM] * 5 + [HBM], out_specs=[VMEM...]
    ppermute x2 -> x3, waiting for transfers between devices: 3.02 us -> 3.13 us  [the longest x1 2.85 us: on_device(): from_d = lax.ppermute(from_x, 'py', next_y)]
  transfers between devices with their start and end apart: 6 -> 7, of which waited for: 4 -> 4; matrix products, arithmetic and copies ran while one was open for 2% -> 2% of each run, Pallas kernels for 10% -> 14%
where the time goes in v3:
time: 53.4 us; the launch traced here: 53 us
  blocking collectives  21.5 us (40%)
  starting transfers between devices  12.8 us (24%)
  Pallas kernels  12.7 us (24%)
  waiting for transfers between devices  4.71 us (9%)
  local copies, waits for them, and re-layouts  0.78 us (1%)
    all_to_all x1, blocking collectives, on_device(): return total(lax.all_to_all(share, 'px', 0, 0))  21.5 us
    ppermute x1, starting transfers between devices, on_device(): from_x = lax.ppermute(to_x, 'px', next_x)  7.27 us
    ppermute x4, starting transfers between devices, swap(): return lax.ppermute(x, 'py', [(i, i ^ mask) for i in range(count_py)])  4.56 us
    pallas_call x1, Pallas kernels, inner(): pl.pallas_call(inner_kernel, in_specs=[VMEM] * 5 + [HBM], out_specs=[VMEM...  3.59 us
    pallas_call x1, Pallas kernels, field(): pl.pallas_call(field_kernel, in_specs=[VMEM] * 12, out_specs=[VMEM] * 4,...  2.98 us
    ppermute x1, waiting for transfers between devices, on_device(): from_d = lax.ppermute(from_x, 'py', next_y)  2.85 us
    pallas_call x2, Pallas kernels, keep_planes(): pl.pallas_call(keep_kernel, in_specs=[VMEM] * 5, out_specs=VMEM, out_shap...  1.83 us
    ppermute x4, waiting for transfers between devices, swap(): return lax.ppermute(x, 'py', [(i, i ^ mask) for i in range(count_py)])  1.58 us
  transfers between devices with their start and end apart: 7, of which 4 were waited for; matrix products, arithmetic and copies ran while one was open for 2% of the time, Pallas kernels for 14%

profile of v3, /device:TPU:2, one launch (start us, length us, event | category | flops | bytes accessed | tf_op | source)
XLA Modules:
  0.0 53.0 jit_solution(3881054803144071833)
XLA Ops:
  0.0 0.0 copy-start.2
  0.0 0.0 copy-start.6
  0.0 0.0 copy-start.7
  0.0 0.0 copy-start.5
  0.0 0.0 copy-start
  0.0 1.4 %pack.1 = (f32[8,1152]{1,0:T(8,128)S(1)}, f32[48,128]{1,0:T(8,128)S(1)}) custom-call(s32[16,1024]{1,0:T(8,128)} %lev_ref.5, f32[8,2,16,64]{3,2,1,0:T(8,128)} %bitcast.31, f32[8,2,64,1024]{3,2,1,0:T(8,128)} %cols_hbm.3), custom_call_target="tpu_custom_call" | custom-call | tf_op jit(solution)/shard_map/pack/pallas_call | solution.py:82
  1.4 7.3 %collective-permute-start = (f32[8,1152]{1,0:T(8,128)S(1)}, f32[8,1152]{1,0:T(8,128)S(1)}, u32[]{:S(2)}, u32[]{:S(2)}) collective-permute-start(f32[8,1152]{1,0:T(8,128)S(1)} %get-tuple-element.22), channel_id=1, source_target_pairs={{0,8},{8,16},{16,24},{24,32},{32,40},{40,48},{48,56},{56,64},{64,7... | collective-permute-start | bytes 110600 | tf_op jit(solution)/shard_map/ppermute | solution.py:477
  8.7 0.0 collective-permute-start.1
  8.7 0.0 copy-done.2
  8.7 0.1 pad_bitcast_fusion.3
  8.8 0.0 copy-done.3
  8.8 0.1 fusion.2.conv_ref
  8.9 0.0 copy-done.4
  8.9 0.1 fusion.8.mix_ref
  9.0 0.1 pad_maximum_fusion
  9.1 0.0 copy-done.6
  9.1 0.0 copy-done.7
  9.1 0.1 maximum_bitcast_fusion
  9.2 0.2 reshape.14.dec_ref
  9.4 0.0 copy-done.5
  9.4 0.1 broadcast_in_dim.14
  9.5 0.1 reshape.15.order_ref
  9.6 0.1 copy.26.cb_ref
  9.7 0.1 copy.27.mb_ref
  9.9 0.0 copy-done
  9.9 3.6 %inner.1 = (bf16[1536,1024]{1,0:T(8,128)(2,1)S(1)}, bf16[8,128,1024]{2,1,0:T(8,128)(2,1)S(1)}, bf16[8,128,1024]{2,1,0:T(8,128)(2,1)S(1)}) custom-call(s32[16,1024]{1,0:T(8,128)S(1)} %copy-done, bf16[128,192]{1,0:T(8,128)(2,1)S(1)} %fusion.2.conv_ref, f32[128,1]{1,0:T(8,128)S(1)} %copy.26.cb_ref, bf16[128,128]{1,0:T(8,128)(2,1)S(1)} %fusion.8.mix_ref, ...), custom_call_target="tpu_custom_call" | custom-call | tf_op jit(solution)/shard_map/inner/pallas_call | solution.py:161
  13.5 0.3 collective-permute-done.1.from_y_ref
  13.7 0.0 collective-permute-done.from_x_ref
  13.7 0.9 %collective-permute-start.2 = (f32[8,1152]{1,0:T(8,128)S(1)}, f32[8,1152]{1,0:T(8,128)S(1)}, u32[]{:S(2)}, u32[]{:S(2)}) collective-permute-start(f32[8,1152]{1,0:T(8,128)S(1)} %collective-permute-done.from_x_ref), channel_id=1, source_target_pairs={{0,1},{1,2},{2,3},{3,4},{4,5},{5,6},{6,7},{7,0},{8,9},{9,10},{10,1... | collective-permute-start | bytes 110600 | tf_op jit(solution)/shard_map/ppermute | solution.py:481
  14.7 1.4 %outer.1._ = bf16[1536,1024]{1,0:T(8,128)(2,1)S(1)} custom-call(s32[16,1024]{1,0:T(8,128)S(1)} %copy-done, f32[8,1152]{1,0:T(8,128)S(1)} %collective-permute-done.from_x_ref, f32[48,128]{1,0:T(8,128)S(1)} %collective-permute-done.1.from_y_ref, bf16[128,192]{1,0:T(8,128)(2,1)S(1)} %fusion.2.conv_ref, ...), custom_call_target="tpu_custom_call", output_to_operand_aliasing={{}: (7, {})} | custom-call | tf_op jit(solution)/shard_map/outer/pallas_call | solution.py:230
  16.1 2.9 %collective-permute-done.2.from_d_ref = f32[8,1152]{1,0:T(8,128)S(1)} collective-permute-done((f32[8,1152]{1,0:T(8,128)S(1)}, f32[8,1152]{1,0:T(8,128)S(1)}, u32[]{:S(2)}, u32[]{:S(2)}) %collective-permute-start.2) | collective-permute-done | bytes 36896 | tf_op jit(solution)/shard_map/ppermute | solution.py:481
  18.9 3.0 %field.1 = (f32[4,80,128]{2,1,0:T(8,128)S(1)}, bf16[320,1024]{1,0:T(8,128)(2,1)S(1)}, f32[160,128]{1,0:T(8,128)S(1)}, bf16[1536,1024]{1,0:T(8,128)(2,1)S(1)}) custom-call(s32[16,1024]{1,0:T(8,128)S(1)} %copy-done, f32[8,1152]{1,0:T(8,128)S(1)} %collective-permute-done.from_x_ref, ...), custom_call_target="tpu_custom_call", output_to_operand_aliasing={{3}: (11, {})} | custom-call | tf_op jit(solution)/shard_map/field/pallas_call | solution.py:327
  21.9 0.0 copy-start.1
  21.9 0.1 collective-permute-start.3
  22.0 1.2 %keep_planes.3 = f32[3,80,128]{2,1,0:T(8,128)S(1)} custom-call(bf16[8,128,1024]{2,1,0:T(8,128)(2,1)S(1)} %get-tuple-element.31.hi_ref, bf16[8,128,1024]{2,1,0:T(8,128)(2,1)S(1)} %get-tuple-element.32.lo_ref, bf16[320,1024]{1,0:T(8,128)(2,1)S(1)} %get-tuple-element.36.nf_ref, f32[160,128]{1,0:T(8,128)S(1)} %get-tuple-element.37.edge_ref, ...), custom_call_target="tpu_custom_call" | custom-call | tf_op jit(solution)/shard_map/keep_planes/pallas_call | solution.py:351
  23.2 0.2 collective-permute-done.3.got_ref
  23.4 0.1 collective-permute-start.4
  23.5 0.5 collective-permute-start.5
  24.0 3.9 %collective-permute-start.6 = (f32[80,128]{1,0:T(8,128)S(1)}, f32[80,128]{1,0:T(8,128)S(1)}, u32[]{:S(2)}, u32[]{:S(2)}) collective-permute-start(f32[80,128]{1,0:T(8,128)S(1)} %get-tuple-element.39), channel_id=1, source_target_pairs={{0,6},{1,7},{2,4},{3,5},{4,2},{5,3},{6,0},{7,1},{8,14},{9,15},{10,... | collective-permute-start | bytes 122888 | tf_op jit(solution)/shard_map/ppermute | solution.py:488
  27.9 0.0 copy-done.1
  27.9 0.5 row_factors.1.factor_ref
  28.4 0.7 %keep_planes.2.keep_ref = f32[1,80,128]{2,1,0:T(8,128)S(1)} custom-call(bf16[8,128,1024]{2,1,0:T(8,128)(2,1)S(1)} %get-tuple-element.31.hi_ref, bf16[8,128,1024]{2,1,0:T(8,128)(2,1)S(1)} %get-tuple-element.32.lo_ref, bf16[320,1024]{1,0:T(8,128)(2,1)S(1)} %get-tuple-element.36.nf_ref, f32[160,128]{1,0:T(8,128)S(1)} %get-tuple-element.37.edge_ref, ...), custom_call_target="tpu_custom_call" | custom-call | tf_op jit(solution)/shard_map/keep_planes/pallas_call | solution.py:351
  29.1 0.0 collective-permute-done.4.b_ref
  29.1 1.4 %collective-permute-done.5.c_ref = f32[80,128]{1,0:T(8,128)S(1)} collective-permute-done((f32[80,128]{1,0:T(8,128)S(1)}, f32[80,128]{1,0:T(8,128)S(1)}, u32[]{:S(2)}, u32[]{:S(2)}) %collective-permute-start.5) | collective-permute-done | bytes 40992 | tf_op jit(solution)/shard_map/ppermute | solution.py:488
  30.5 0.0 collective-permute-done.6.d_ref
  30.5 0.3 focal_share.1
  30.8 21.5 %all_to_all.5.x_ref = f32[32,8,128]{2,1,0:T(8,128)S(1)} all-to-all(f32[32,8,128]{2,1,0:T(8,128)S(1)} %focal_share.1), channel_id=1, replica_groups=mesh['px'=32,'py'=8] {'px'}, dimensions={0} | all-to-all | bytes 262144 | tf_op jit(solution)/shard_map/all_to_all | solution.py:496
  52.3 0.7 %total.1 = f32[1,2,512]{2,1,0:T(2,128)} custom-call(f32[32,8,128]{2,1,0:T(8,128)S(1)} %all_to_all.5.x_ref), custom_call_target="tpu_custom_call" | custom-call | tf_op jit(solution)/shard_map/total/pallas_call | solution.py:422
  (6 shorter events, 0.1 us)
Async XLA Ops:
  0.0 8.7 %copy-start.2 = (bf16[5,40,64]{2,1,0:T(8,128)(2,1)S(1)}, bf16[5,40,64]{2,1,0:T(8,128)(2,1)}, u32[]{:S(2)}) copy-start(bf16[5,40,64]{2,1,0:T(8,128)(2,1)} %param.14) | copy-start | bytes 76804
  0.0 8.8 %copy-start.3 = (bf16[64,144]{1,0:T(8,128)(2,1)S(1)}, bf16[64,144]{1,0:T(8,128)(2,1)}, u32[]{:S(2)}) copy-start(bf16[64,144]{1,0:T(8,128)(2,1)} %param.10) | copy-start | bytes 55300
  0.0 8.9 %copy-start.4 = (bf16[64,64]{1,0:T(8,128)(2,1)S(1)}, bf16[64,64]{1,0:T(8,128)(2,1)}, u32[]{:S(2)}) copy-start(bf16[64,64]{1,0:T(8,128)(2,1)} %param.12) | copy-start | bytes 24580
  0.0 9.1 %copy-start.6 = (f32[64]{0:T(128)S(1)}, f32[64]{0:T(128)}, u32[]{:S(2)}) copy-start(f32[64]{0:T(128)} %param.11) | copy-start | bytes 772
  0.0 9.1 %copy-start.7 = (f32[64]{0:T(128)S(1)}, f32[64]{0:T(128)}, u32[]{:S(2)}) copy-start(f32[64]{0:T(128)} %param.13) | copy-start | bytes 772
  0.0 9.4 %copy-start.5 = (s32[64]{0:T(128)S(1)}, s32[64]{0:T(128)}, u32[]{:S(2)}) copy-start(s32[64]{0:T(128)} %param.17) | copy-start | bytes 772
  0.0 9.8 %copy-start = (s32[16,1024]{1,0:T(8,128)S(1)}, s32[16,1024]{1,0:T(8,128)}, u32[]{:S(2)}) copy-start(s32[16,1024]{1,0:T(8,128)} %lev_ref.5) | copy-start | bytes 196612
  1.4 12.3 %collective-permute-start = (f32[8,1152]{1,0:T(8,128)S(1)}, f32[8,1152]{1,0:T(8,128)S(1)}, u32[]{:S(2)}, u32[]{:S(2)}) collective-permute-start(f32[8,1152]{1,0:T(8,128)S(1)} %get-tuple-element.22), channel_id=1, source_target_pairs={{0,8},{8,16},{16,24},{24,32},{32,40},{40,48},{48,56},{56,64},{64,7... | collective-permute-start | bytes 110600 | tf_op jit(solution)/shard_map/ppermute | solution.py:477
  8.7 5.0 %collective-permute-start.1 = (f32[48,128]{1,0:T(8,128)S(1)}, f32[48,128]{1,0:T(8,128)S(1)}, u32[]{:S(2)}, u32[]{:S(2)}) collective-permute-start(f32[48,128]{1,0:T(8,128)S(1)} %get-tuple-element.23), channel_id=1, source_target_pairs={{0,1},{1,2},{2,3},{3,4},{4,5},{5,6},{6,7},{7,0},{8,9},{9,10},{10,1... | collective-permute-start | bytes 73736 | tf_op jit(solution)/shard_map/ppermute | solution.py:478
  13.7 5.2 %collective-permute-start.2 = (f32[8,1152]{1,0:T(8,128)S(1)}, f32[8,1152]{1,0:T(8,128)S(1)}, u32[]{:S(2)}, u32[]{:S(2)}) collective-permute-start(f32[8,1152]{1,0:T(8,128)S(1)} %collective-permute-done.from_x_ref), channel_id=1, source_target_pairs={{0,1},{1,2},{2,3},{3,4},{4,5},{5,6},{6,7},{7,0},{8,9},{9,10},{10,1... | collective-permute-start | bytes 110600 | tf_op jit(solution)/shard_map/ppermute | solution.py:481
  21.9 6.0 %copy-start.1 = (f32[8,2,64,16]{2,3,1,0:T(8,128)S(1)}, f32[8,2,64,16]{2,3,1,0:T(8,128)}, u32[]{:S(2)}) copy-start(f32[8,2,64,16]{2,3,1,0:T(8,128)} %param.15) | copy-start | bytes 196612
  21.9 1.5 %collective-permute-start.3 = (f32[4,80,128]{2,1,0:T(8,128)S(1)}, f32[4,80,128]{2,1,0:T(8,128)S(1)}, u32[]{:S(2)}, u32[]{:S(2)}) collective-permute-start(f32[4,80,128]{2,1,0:T(8,128)S(1)} %get-tuple-element.38), channel_id=1, source_target_pairs={{0,1},{1,0},{2,3},{3,2},{4,5},{5,4},{6,7},{7,6},{8,9},{9,8},{10,11... | collective-permute-start | bytes 491528 | tf_op jit(solution)/shard_map/ppermute | solution.py:488
  23.4 5.7 %collective-permute-start.4 = (f32[80,128]{1,0:T(8,128)S(1)}, f32[80,128]{1,0:T(8,128)S(1)}, u32[]{:S(2)}, u32[]{:S(2)}) collective-permute-start(f32[80,128]{1,0:T(8,128)S(1)} %get-tuple-element.41), channel_id=1, source_target_pairs={{0,2},{1,3},{2,0},{3,1},{4,6},{5,7},{6,4},{7,5},{8,10},{9,11},{10,... | collective-permute-start | bytes 122888 | tf_op jit(solution)/shard_map/ppermute | solution.py:488
  23.5 7.0 %collective-permute-start.5 = (f32[80,128]{1,0:T(8,128)S(1)}, f32[80,128]{1,0:T(8,128)S(1)}, u32[]{:S(2)}, u32[]{:S(2)}) collective-permute-start(f32[80,128]{1,0:T(8,128)S(1)} %get-tuple-element.40), channel_id=1, source_target_pairs={{0,4},{1,5},{2,6},{3,7},{4,0},{5,1},{6,2},{7,3},{8,12},{9,13},{10,... | collective-permute-start | bytes 122888 | tf_op jit(solution)/shard_map/ppermute | solution.py:488
  24.0 6.4 %collective-permute-start.6 = (f32[80,128]{1,0:T(8,128)S(1)}, f32[80,128]{1,0:T(8,128)S(1)}, u32[]{:S(2)}, u32[]{:S(2)}) collective-permute-start(f32[80,128]{1,0:T(8,128)S(1)} %get-tuple-element.39), channel_id=1, source_target_pairs={{0,6},{1,7},{2,4},{3,5},{4,2},{5,3},{6,0},{7,1},{8,14},{9,15},{10,... | collective-permute-start | bytes 122888 | tf_op jit(solution)/shard_map/ppermute | solution.py:488

commit v4 on v3

--- a/solution.py
+++ b/solution.py
@@ -21,12 +21,13 @@
 U = 64
 V = 64
 HALO = 4
-ROWS_EXT = ROWS + HALO
+SHIFT = 5
+PILLAR_ROWS = ROWS + KS - 1
 SLOT = 3 * LEVELS
 WINDOW = 4 * SLOT
 BLOCK = 4
 REL_ORDER = (0, 2, 4, 6, 1, 3, 5, 7)
-PART = ROWS_EXT * CH // 2
+PART = ROWS * CH // 2
 HALF = BLOCK * CH // 2
 VMEM = pl.BlockSpec(memory_space=pltpu.VMEM)
 HBM = pl.BlockSpec(memory_space=pltpu.HBM)
@@ -131,17 +132,15 @@
     def make_hot(q, _):
         for b in range(3):
             hot_ref[pl.ds(q * SLOT + b * LEVELS, LEVELS), :] = one_hot(
-                ext_ref[b, pl.ds(q + 1, 1), :], level_ids
+                ext_ref[b, pl.ds(q, 1), :], level_ids
             )
         return 0
 
     lax.fori_loop(0, ROWS - 2, make_hot, 0, unroll=2)
-    feat_ref[: BLOCK * HID, :] = jnp.zeros((BLOCK * HID, COLS), BF16)
-    feat_ref[(BLOCK + ROWS) * HID :, :] = jnp.zeros((BLOCK * HID, COLS), BF16)
     conv_bias = jnp.broadcast_to(cb_ref[...], (2 * HID, wide))
     mix_bias = jnp.broadcast_to(mb_ref[...], (2 * HID, wide))
     for i in range(ROWS // 2 - 2):
-        at = (2 * BLOCK + 2 * i) * HID
+        at = (8 + 2 * i) * HID
         feat_ref[at : at + 2 * HID, 128:] = features(
             hot_ref[i * 2 * SLOT : i * 2 * SLOT + WINDOW, :],
             conv_ref[...], conv_bias, mix_ref[...], mix_bias,
@@ -163,7 +162,7 @@
         in_specs=[VMEM] * 5 + [HBM],
         out_specs=[VMEM] * 3,
         out_shape=[
-            jax.ShapeDtypeStruct(((ROWS + 2 * BLOCK) * HID, COLS), BF16),
+            jax.ShapeDtypeStruct((PILLAR_ROWS * HID, COLS), BF16),
             jax.ShapeDtypeStruct((Z, 2 * V, COLS), BF16),
             jax.ShapeDtypeStruct((Z, 2 * V, COLS), BF16),
         ],
@@ -197,32 +196,34 @@
     for o in range(4):
         for b in range(3):
             at = pl.ds(o * SLOT + b * LEVELS, LEVELS)
-            for w in range(2):
-                q = 2 * w + o
-                hot_ref[w, at, :] = one_hot(ext_ref[b, q + 5 : q + 6, 128:], level_ids)
+            for w in range(4):
+                e = 2 * w + o
+                hot_ref[w, at, :] = one_hot(ext_ref[b, e : e + 1, 128:], level_ids)
             for t in range(6):
-                q = 2 * t + 4 + o
-                hot_ref[2, at, t * 128 : (t + 1) * 128] = one_hot(
-                    ext_ref[b, q + 5 : q + 6, :128], level_ids[:, :128]
+                e = 2 * t + 8 + o
+                hot_ref[4, at, t * 128 : (t + 1) * 128] = one_hot(
+                    ext_ref[b, e : e + 1, :128], level_ids[:, :128]
                 )
     conv_bias = jnp.broadcast_to(cb_ref[...], (2 * HID, wide))
     mix_bias = jnp.broadcast_to(mb_ref[...], (2 * HID, wide))
-    for w in range(2):
-        at = (BLOCK + 2 * w) * HID
+    for w in range(4):
+        at = 2 * w * HID
+        conv = cut_conv(conv_ref[...], first_x) if w == 3 else conv_ref[...]
         feat_ref[at : at + 2 * HID, 128:] = features(
-            hot_ref[w], cut_conv(conv_ref[...], w, first_x), conv_bias, mix_ref[...], mix_bias
+            hot_ref[w], conv, conv_bias, mix_ref[...], mix_bias
         )
     tiles = features(
-        hot_ref[2, :, :768], conv_ref[...], conv_bias[:, :768], mix_ref[...], mix_bias[:, :768]
+        hot_ref[4, :, :768], conv_ref[...], conv_bias[:, :768], mix_ref[...], mix_bias[:, :768]
     )
     for t in range(6):
-        at = (2 * BLOCK + 2 * t) * HID
+        at = (8 + 2 * t) * HID
         feat_ref[at : at + 2 * HID, :128] = tiles[:, t * 128 : (t + 1) * 128]
 
 
-def cut_conv(conv, w, first_x):
-    slot = iota((1, WINDOW), 1) // SLOT
-    keep = jnp.where(first_x & (slot == (3 if w == 0 else 0)), 0.0, 1.0)
+def cut_conv(conv, first_x):
+    slot = iota((2 * HID, WINDOW), 1) // SLOT
+    row = iota((2 * HID, WINDOW), 0) // HID
+    keep = jnp.where(first_x & (slot + row == 2) & (slot > 0), 0.0, 1.0)
     return conv * keep.astype(BF16)
 
 
@@ -235,7 +236,7 @@
         input_output_aliases={7: 0},
         scratch_shapes=[
             pltpu.VMEM((3, 24, COLS), F32),
-            pltpu.VMEM((3, WINDOW, COLS - 128), BF16),
+            pltpu.VMEM((5, WINDOW, COLS - 128), BF16),
         ],
         compiler_params=params(12),
         name="outer",
@@ -248,9 +249,9 @@
     sign = jnp.where(iota((1, 128), 1) < V, -1.0, 1.0)
     hi = hi_ref[first : first + count].reshape(2 * V * count, COLS)
     lo = lo_ref[first : first + count].reshape(2 * V * count, COLS)
-    both = lax.dot_general(hi, nf_ref[:n, :], NT, preferred_element_type=F32)
+    both = lax.dot_general(hi, nf_ref[...], NT, preferred_element_type=F32)
+    both = both[:, :n] + both[:, n:]
     both = both + lax.dot_general(lo, nf_ref[:n, :], NT, preferred_element_type=F32)
-    both = both + lax.dot_general(hi, nf_ref[n:, :], NT, preferred_element_type=F32)
     for g in range(count):
         out = both[2 * V * g : 2 * V * (g + 1)].T
         z = iy ^ REL_ORDER[first + g]
@@ -276,25 +277,34 @@
             window = jnp.where(first_y & (lane == (2 if b == 0 else 1)), -1.0, window)
         ext_ref[b] = window
     level_ids = iota((LEVELS, 128), 0).astype(F32)
-    for w in range(2):
+    for w in range(4):
         for o in range(4):
             for b in range(3):
-                q = 2 * w + o
+                e = 2 * w + o
                 at = o * SLOT + b * LEVELS
-                hot_ref[w, at : at + LEVELS, :] = one_hot(ext_ref[b, q + 5 : q + 6, :], level_ids)
-    for w in range(2):
-        at = (BLOCK + 2 * w) * HID
-        feat_ref[at : at + 2 * HID, :128] = features(
-            hot_ref[w], cut_conv(conv_ref[...], w, first_x), cb_ref[...], mix_ref[...], mb_ref[...]
-        )
+                hot_ref[at : at + LEVELS, w * 128 : (w + 1) * 128] = one_hot(
+                    ext_ref[b, e : e + 1, :], level_ids
+                )
+    tiles = features(
+        hot_ref[:, :384], conv_ref[...], cb_ref[...], mix_ref[...], mb_ref[...]
+    )
+    for w in range(3):
+        feat_ref[2 * w * HID : (2 * w + 2) * HID, :128] = tiles[:, w * 128 : (w + 1) * 128]
+    feat_ref[6 * HID : 8 * HID, :128] = features(
+        hot_ref[:, 384:], cut_conv(conv_ref[...], first_x), cb_ref[...], mix_ref[...], mb_ref[...]
+    )
 
     lane = iota((1, COLS), 1)
     near = iota((1, 128), 1)
-    pillar = iota((1, 2 * BLOCK * HID), 1) // HID
-    for i in reversed(range(ROWS_EXT // BLOCK)):
+    shape = (KS * CH * BLOCK, 2 * BLOCK * HID)
+    sample = iota(shape, 0) // 4 % BLOCK - SHIFT
+    pillar = iota(shape, 1) // HID - SHIFT - 2
+    for i in reversed(range(ROWS // BLOCK)):
         dec = dec_ref[...]
         if i < 2:
-            keep = jnp.where(first_x & ((pillar >= 6) if i == 0 else (pillar < 2)), 0.0, 1.0)
+            at = i * BLOCK
+            apart = (sample + at >= 0) != (pillar + at >= 0)
+            keep = jnp.where(first_x & apart, 0.0, 1.0)
             dec = dec * keep.astype(BF16)
         at = i * BLOCK * HID
         taps = jnp.dot(
@@ -337,7 +347,7 @@
         input_output_aliases={11: 3},
         scratch_shapes=[
             pltpu.VMEM((3, 16, 128), F32),
-            pltpu.VMEM((2, WINDOW, 128), BF16),
+            pltpu.VMEM((WINDOW, 512), BF16),
         ],
         compiler_params=params(12),
         name="field",
@@ -366,7 +376,7 @@
     green = jnp.concatenate(split2(green), axis=0)
     pick = (order_ref[...] == iota((U, U * 4), 0)).astype(BF16)
     row = iota((3 * PART, 2 * n), 0)
-    source = (row % PART) // 4 + (8 - HALO) + jnp.where(row // PART == 1, n, 0)
+    source = (row % PART) // 4 + (8 - SHIFT) + jnp.where(row // PART == 1, n, 0)
     spread = (iota((3 * PART, 2 * n), 1) == source).astype(BF16)
     mask = iota((3 * PART, U * 4), 0) % 4 == iota((3 * PART, U * 4), 1) % 4
     for j in range(2):

time: 53.4 us -> 52.4 us (0.981)
    pallas_call x1, Pallas kernels: 1.37 us -> 2.12 us  [outer(): pl.pallas_call(outer_kernel, in_specs=[VMEM] * 8, out_specs=VMEM, out_sha...]
    ppermute x1, waiting for transfers between devices: 2.85 us -> 2.11 us  [on_device(): from_d = lax.ppermute(from_x, 'py', next_y)]
    pallas_call x1, Pallas kernels: 2.98 us -> 2.41 us  [field(): pl.pallas_call(field_kernel, in_specs=[VMEM] * 12, out_specs=[VMEM] * 4,...]
  transfers between devices with their start and end apart: 7 -> 7, of which waited for: 4 -> 4; matrix products, arithmetic and copies ran while one was open for 2% -> 2% of each run, Pallas kernels for 14% -> 15%
where the time goes in v4:
time: 52.4 us; the launch traced here: 52.2 us
  blocking collectives  21.4 us (41%)
  starting transfers between devices  12.8 us (24%)
  Pallas kernels  12.4 us (24%)
  waiting for transfers between devices  4.38 us (8%)
  local copies, waits for them, and re-layouts  0.78 us (1%)
    all_to_all x1, blocking collectives, on_device(): return total(lax.all_to_all(share, 'px', 0, 0))  21.4 us
    ppermute x1, starting transfers between devices, on_device(): from_x = lax.ppermute(to_x, 'px', next_x)  7.27 us
    ppermute x4, starting transfers between devices, swap(): return lax.ppermute(x, 'py', [(i, i ^ mask) for i in range(count_py)])  4.56 us
    pallas_call x1, Pallas kernels, inner(): pl.pallas_call(inner_kernel, in_specs=[VMEM] * 5 + [HBM], out_specs=[VMEM...  3.58 us
    pallas_call x1, Pallas kernels, field(): pl.pallas_call(field_kernel, in_specs=[VMEM] * 12, out_specs=[VMEM] * 4,...  2.41 us
    pallas_call x1, Pallas kernels, outer(): pl.pallas_call(outer_kernel, in_specs=[VMEM] * 8, out_specs=VMEM, out_sha...  2.12 us
    ppermute x1, waiting for transfers between devices, on_device(): from_d = lax.ppermute(from_x, 'py', next_y)  2.11 us
    ppermute x4, waiting for transfers between devices, swap(): return lax.ppermute(x, 'py', [(i, i ^ mask) for i in range(count_py)])  1.98 us
  transfers between devices with their start and end apart: 7, of which 4 were waited for; matrix products, arithmetic and copies ran while one was open for 2% of the time, Pallas kernels for 15%

profile of v4, /device:TPU:2, one launch (start us, length us, event | category | flops | bytes accessed | tf_op | source)
XLA Modules:
  0.0 52.2 jit_solution(15504308639827015249)
XLA Ops:
  0.0 0.0 copy-start.2
  0.0 0.0 copy-start.6
  0.0 0.0 copy-start.7
  0.0 0.0 copy-start.5
  0.0 0.0 copy-start
  0.0 1.4 %pack.1 = (f32[8,1152]{1,0:T(8,128)S(1)}, f32[48,128]{1,0:T(8,128)S(1)}) custom-call(s32[16,1024]{1,0:T(8,128)} %lev_ref.5, f32[8,2,16,64]{3,2,1,0:T(8,128)} %bitcast.31, f32[8,2,64,1024]{3,2,1,0:T(8,128)} %cols_hbm.3), custom_call_target="tpu_custom_call" | custom-call | tf_op jit(solution)/shard_map/pack/pallas_call | solution.py:83
  1.4 7.3 %collective-permute-start = (f32[8,1152]{1,0:T(8,128)S(1)}, f32[8,1152]{1,0:T(8,128)S(1)}, u32[]{:S(2)}, u32[]{:S(2)}) collective-permute-start(f32[8,1152]{1,0:T(8,128)S(1)} %get-tuple-element.22), channel_id=1, source_target_pairs={{0,8},{8,16},{16,24},{24,32},{32,40},{40,48},{48,56},{56,64},{64,7... | collective-permute-start | bytes 110600 | tf_op jit(solution)/shard_map/ppermute | solution.py:487
  8.7 0.0 collective-permute-start.1
  8.7 0.0 copy-done.2
  8.7 0.1 pad_bitcast_fusion.3
  8.8 0.0 copy-done.3
  8.8 0.1 fusion.2.conv_ref
  8.9 0.0 copy-done.4
  8.9 0.1 fusion.5.mix_ref
  9.0 0.1 pad_maximum_fusion
  9.1 0.0 copy-done.6
  9.1 0.0 copy-done.7
  9.1 0.1 maximum_bitcast_fusion
  9.2 0.2 reshape.14.dec_ref
  9.4 0.0 copy-done.5
  9.4 0.1 broadcast_in_dim.14
  9.5 0.1 reshape.15.order_ref
  9.6 0.1 copy.26.cb_ref
  9.7 0.1 copy.27.mb_ref
  9.9 0.0 copy-done
  9.9 3.6 %inner.1 = (bf16[1280,1024]{1,0:T(8,128)(2,1)S(1)}, bf16[8,128,1024]{2,1,0:T(8,128)(2,1)S(1)}, bf16[8,128,1024]{2,1,0:T(8,128)(2,1)S(1)}) custom-call(s32[16,1024]{1,0:T(8,128)S(1)} %copy-done, bf16[128,192]{1,0:T(8,128)(2,1)S(1)} %fusion.2.conv_ref, f32[128,1]{1,0:T(8,128)S(1)} %copy.26.cb_ref, bf16[128,128]{1,0:T(8,128)(2,1)S(1)} %fusion.5.mix_ref, ...), custom_call_target="tpu_custom_call" | custom-call | tf_op jit(solution)/shard_map/inner/pallas_call | solution.py:160
  13.5 0.3 collective-permute-done.1.from_y_ref
  13.7 0.0 collective-permute-done.from_x_ref
  13.7 0.9 %collective-permute-start.2 = (f32[8,1152]{1,0:T(8,128)S(1)}, f32[8,1152]{1,0:T(8,128)S(1)}, u32[]{:S(2)}, u32[]{:S(2)}) collective-permute-start(f32[8,1152]{1,0:T(8,128)S(1)} %collective-permute-done.from_x_ref), channel_id=1, source_target_pairs={{0,1},{1,2},{2,3},{3,4},{4,5},{5,6},{6,7},{7,0},{8,9},{9,10},{10,1... | collective-permute-start | bytes 110600 | tf_op jit(solution)/shard_map/ppermute | solution.py:491
  14.7 2.1 %outer.1._ = bf16[1280,1024]{1,0:T(8,128)(2,1)S(1)} custom-call(s32[16,1024]{1,0:T(8,128)S(1)} %copy-done, f32[8,1152]{1,0:T(8,128)S(1)} %collective-permute-done.from_x_ref, f32[48,128]{1,0:T(8,128)S(1)} %collective-permute-done.1.from_y_ref, bf16[128,192]{1,0:T(8,128)(2,1)S(1)} %fusion.2.conv_ref, ...), custom_call_target="tpu_custom_call", output_to_operand_aliasing={{}: (7, {})} | custom-call | tf_op jit(solution)/shard_map/outer/pallas_call | solution.py:231
  16.8 2.1 %collective-permute-done.2.from_d_ref = f32[8,1152]{1,0:T(8,128)S(1)} collective-permute-done((f32[8,1152]{1,0:T(8,128)S(1)}, f32[8,1152]{1,0:T(8,128)S(1)}, u32[]{:S(2)}, u32[]{:S(2)}) %collective-permute-start.2) | collective-permute-done | bytes 36896 | tf_op jit(solution)/shard_map/ppermute | solution.py:491
  18.9 2.4 %field.1 = (f32[4,64,128]{2,1,0:T(8,128)S(1)}, bf16[256,1024]{1,0:T(8,128)(2,1)S(1)}, f32[128,128]{1,0:T(8,128)S(1)}, bf16[1280,1024]{1,0:T(8,128)(2,1)S(1)}) custom-call(s32[16,1024]{1,0:T(8,128)S(1)} %copy-done, f32[8,1152]{1,0:T(8,128)S(1)} %collective-permute-done.from_x_ref, ...), custom_call_target="tpu_custom_call", output_to_operand_aliasing={{3}: (11, {})} | custom-call | tf_op jit(solution)/shard_map/field/pallas_call | solution.py:337
  21.3 0.0 copy-start.1
  21.4 0.1 collective-permute-start.3
  21.5 0.8 %keep_planes.3 = f32[3,64,128]{2,1,0:T(8,128)S(1)} custom-call(bf16[8,128,1024]{2,1,0:T(8,128)(2,1)S(1)} %get-tuple-element.31.hi_ref, bf16[8,128,1024]{2,1,0:T(8,128)(2,1)S(1)} %get-tuple-element.32.lo_ref, bf16[256,1024]{1,0:T(8,128)(2,1)S(1)} %get-tuple-element.36.nf_ref, f32[128,128]{1,0:T(8,128)S(1)} %get-tuple-element.37.edge_ref, ...), custom_call_target="tpu_custom_call" | custom-call | tf_op jit(solution)/shard_map/keep_planes/pallas_call | solution.py:361
  22.3 0.5 collective-permute-done.3.got_ref
  22.8 0.1 collective-permute-start.4
  22.9 1.2 %collective-permute-start.5 = (f32[64,128]{1,0:T(8,128)S(1)}, f32[64,128]{1,0:T(8,128)S(1)}, u32[]{:S(2)}, u32[]{:S(2)}) collective-permute-start(f32[64,128]{1,0:T(8,128)S(1)} %get-tuple-element.40), channel_id=1, source_target_pairs={{0,4},{1,5},{2,6},{3,7},{4,0},{5,1},{6,2},{7,3},{8,12},{9,13},{10,... | collective-permute-start | bytes 98312 | tf_op jit(solution)/shard_map/ppermute | solution.py:498
  24.2 3.1 %collective-permute-start.6 = (f32[64,128]{1,0:T(8,128)S(1)}, f32[64,128]{1,0:T(8,128)S(1)}, u32[]{:S(2)}, u32[]{:S(2)}) collective-permute-start(f32[64,128]{1,0:T(8,128)S(1)} %get-tuple-element.39), channel_id=1, source_target_pairs={{0,6},{1,7},{2,4},{3,5},{4,2},{5,3},{6,0},{7,1},{8,14},{9,15},{10,... | collective-permute-start | bytes 98312 | tf_op jit(solution)/shard_map/ppermute | solution.py:498
  27.3 0.0 copy-done.1
  27.3 0.5 row_factors.1.factor_ref
  27.8 0.6 %keep_planes.2.keep_ref = f32[1,64,128]{2,1,0:T(8,128)S(1)} custom-call(bf16[8,128,1024]{2,1,0:T(8,128)(2,1)S(1)} %get-tuple-element.31.hi_ref, bf16[8,128,1024]{2,1,0:T(8,128)(2,1)S(1)} %get-tuple-element.32.lo_ref, bf16[256,1024]{1,0:T(8,128)(2,1)S(1)} %get-tuple-element.36.nf_ref, f32[128,128]{1,0:T(8,128)S(1)} %get-tuple-element.37.edge_ref, ...), custom_call_target="tpu_custom_call" | custom-call | tf_op jit(solution)/shard_map/keep_planes/pallas_call | solution.py:361
  28.4 0.0 collective-permute-done.4.b_ref
  28.4 0.0 collective-permute-done.5.c_ref
  28.4 1.5 %collective-permute-done.6.d_ref = f32[64,128]{1,0:T(8,128)S(1)} collective-permute-done((f32[64,128]{1,0:T(8,128)S(1)}, f32[64,128]{1,0:T(8,128)S(1)}, u32[]{:S(2)}, u32[]{:S(2)}) %collective-permute-start.6) | collective-permute-done | bytes 32800 | tf_op jit(solution)/shard_map/ppermute | solution.py:498
  29.9 0.3 focal_share.1
  30.2 21.4 %all_to_all.5.x_ref = f32[32,8,128]{2,1,0:T(8,128)S(1)} all-to-all(f32[32,8,128]{2,1,0:T(8,128)S(1)} %focal_share.1), channel_id=1, replica_groups=mesh['px'=32,'py'=8] {'px'}, dimensions={0} | all-to-all | bytes 262144 | tf_op jit(solution)/shard_map/all_to_all | solution.py:506
  51.5 0.7 %total.1 = f32[1,2,512]{2,1,0:T(2,128)} custom-call(f32[32,8,128]{2,1,0:T(8,128)S(1)} %all_to_all.5.x_ref), custom_call_target="tpu_custom_call" | custom-call | tf_op jit(solution)/shard_map/total/pallas_call | solution.py:432
  (6 shorter events, 0.1 us)
Async XLA Ops:
  0.0 8.7 %copy-start.2 = (bf16[5,40,64]{2,1,0:T(8,128)(2,1)S(1)}, bf16[5,40,64]{2,1,0:T(8,128)(2,1)}, u32[]{:S(2)}) copy-start(bf16[5,40,64]{2,1,0:T(8,128)(2,1)} %param.14) | copy-start | bytes 76804
  0.0 8.8 %copy-start.3 = (bf16[64,144]{1,0:T(8,128)(2,1)S(1)}, bf16[64,144]{1,0:T(8,128)(2,1)}, u32[]{:S(2)}) copy-start(bf16[64,144]{1,0:T(8,128)(2,1)} %param.10) | copy-start | bytes 55300
  0.0 8.9 %copy-start.4 = (bf16[64,64]{1,0:T(8,128)(2,1)S(1)}, bf16[64,64]{1,0:T(8,128)(2,1)}, u32[]{:S(2)}) copy-start(bf16[64,64]{1,0:T(8,128)(2,1)} %param.12) | copy-start | bytes 24580
  0.0 9.1 %copy-start.6 = (f32[64]{0:T(128)S(1)}, f32[64]{0:T(128)}, u32[]{:S(2)}) copy-start(f32[64]{0:T(128)} %param.11) | copy-start | bytes 772
  0.0 9.1 %copy-start.7 = (f32[64]{0:T(128)S(1)}, f32[64]{0:T(128)}, u32[]{:S(2)}) copy-start(f32[64]{0:T(128)} %param.13) | copy-start | bytes 772
  0.0 9.4 %copy-start.5 = (s32[64]{0:T(128)S(1)}, s32[64]{0:T(128)}, u32[]{:S(2)}) copy-start(s32[64]{0:T(128)} %param.17) | copy-start | bytes 772
  0.0 9.8 %copy-start = (s32[16,1024]{1,0:T(8,128)S(1)}, s32[16,1024]{1,0:T(8,128)}, u32[]{:S(2)}) copy-start(s32[16,1024]{1,0:T(8,128)} %lev_ref.5) | copy-start | bytes 196612
  1.4 12.3 %collective-permute-start = (f32[8,1152]{1,0:T(8,128)S(1)}, f32[8,1152]{1,0:T(8,128)S(1)}, u32[]{:S(2)}, u32[]{:S(2)}) collective-permute-start(f32[8,1152]{1,0:T(8,128)S(1)} %get-tuple-element.22), channel_id=1, source_target_pairs={{0,8},{8,16},{16,24},{24,32},{32,40},{40,48},{48,56},{56,64},{64,7... | collective-permute-start | bytes 110600 | tf_op jit(solution)/shard_map/ppermute | solution.py:487
  8.7 5.0 %collective-permute-start.1 = (f32[48,128]{1,0:T(8,128)S(1)}, f32[48,128]{1,0:T(8,128)S(1)}, u32[]{:S(2)}, u32[]{:S(2)}) collective-permute-start(f32[48,128]{1,0:T(8,128)S(1)} %get-tuple-element.23), channel_id=1, source_target_pairs={{0,1},{1,2},{2,3},{3,4},{4,5},{5,6},{6,7},{7,0},{8,9},{9,10},{10,1... | collective-permute-start | bytes 73736 | tf_op jit(solution)/shard_map/ppermute | solution.py:488
  13.7 5.2 %collective-permute-start.2 = (f32[8,1152]{1,0:T(8,128)S(1)}, f32[8,1152]{1,0:T(8,128)S(1)}, u32[]{:S(2)}, u32[]{:S(2)}) collective-permute-start(f32[8,1152]{1,0:T(8,128)S(1)} %collective-permute-done.from_x_ref), channel_id=1, source_target_pairs={{0,1},{1,2},{2,3},{3,4},{4,5},{5,6},{6,7},{7,0},{8,9},{9,10},{10,1... | collective-permute-start | bytes 110600 | tf_op jit(solution)/shard_map/ppermute | solution.py:491
  21.3 5.9 %copy-start.1 = (f32[8,2,64,16]{2,3,1,0:T(8,128)S(1)}, f32[8,2,64,16]{2,3,1,0:T(8,128)}, u32[]{:S(2)}) copy-start(f32[8,2,64,16]{2,3,1,0:T(8,128)} %param.15) | copy-start | bytes 196612
  21.4 1.4 %collective-permute-start.3 = (f32[4,64,128]{2,1,0:T(8,128)S(1)}, f32[4,64,128]{2,1,0:T(8,128)S(1)}, u32[]{:S(2)}, u32[]{:S(2)}) collective-permute-start(f32[4,64,128]{2,1,0:T(8,128)S(1)} %get-tuple-element.38), channel_id=1, source_target_pairs={{0,1},{1,0},{2,3},{3,2},{4,5},{5,4},{6,7},{7,6},{8,9},{9,8},{10,11... | collective-permute-start | bytes 393224 | tf_op jit(solution)/shard_map/ppermute | solution.py:498
  22.8 5.6 %collective-permute-start.4 = (f32[64,128]{1,0:T(8,128)S(1)}, f32[64,128]{1,0:T(8,128)S(1)}, u32[]{:S(2)}, u32[]{:S(2)}) collective-permute-start(f32[64,128]{1,0:T(8,128)S(1)} %get-tuple-element.41), channel_id=1, source_target_pairs={{0,2},{1,3},{2,0},{3,1},{4,6},{5,7},{6,4},{7,5},{8,10},{9,11},{10,... | collective-permute-start | bytes 98312 | tf_op jit(solution)/shard_map/ppermute | solution.py:498
  22.9 5.5 %collective-permute-start.5 = (f32[64,128]{1,0:T(8,128)S(1)}, f32[64,128]{1,0:T(8,128)S(1)}, u32[]{:S(2)}, u32[]{:S(2)}) collective-permute-start(f32[64,128]{1,0:T(8,128)S(1)} %get-tuple-element.40), channel_id=1, source_target_pairs={{0,4},{1,5},{2,6},{3,7},{4,0},{5,1},{6,2},{7,3},{8,12},{9,13},{10,... | collective-permute-start | bytes 98312 | tf_op jit(solution)/shard_map/ppermute | solution.py:498
  24.2 5.7 %collective-permute-start.6 = (f32[64,128]{1,0:T(8,128)S(1)}, f32[64,128]{1,0:T(8,128)S(1)}, u32[]{:S(2)}, u32[]{:S(2)}) collective-permute-start(f32[64,128]{1,0:T(8,128)S(1)} %get-tuple-element.39), channel_id=1, source_target_pairs={{0,6},{1,7},{2,4},{3,5},{4,2},{5,3},{6,0},{7,1},{8,14},{9,15},{10,... | collective-permute-start | bytes 98312 | tf_op jit(solution)/shard_map/ppermute | solution.py:498

commit v5 on v4

--- a/solution.py
+++ b/solution.py
@@ -57,47 +57,56 @@
     return pltpu.with_memory_space_constraint(x, pltpu.HBM)
 
 
-def pack_kernel(lev_hbm, rows_hbm, cols_hbm, to_x_ref, to_y_ref, lev_ref, tile_ref, rows_ref, cols_ref, sems):
+def pack_kernel(lev_hbm, rows_hbm, to_x_ref, to_y_ref, lev_ref, tile_ref, rows_ref, sems):
     z = lax.axis_index("py")
-    last = pl.ds(COLS - 128, 128)
     copies = [
-        pltpu.make_async_copy(cols_hbm.at[:, :, :, last], cols_ref, sems.at[0]),
-        pltpu.make_async_copy(lev_hbm.at[pl.ds(8, 8), :], lev_ref, sems.at[1]),
-        pltpu.make_async_copy(lev_hbm.at[:, last], tile_ref, sems.at[2]),
-        pltpu.make_async_copy(rows_hbm.at[z], rows_ref, sems.at[3]),
+        pltpu.make_async_copy(lev_hbm.at[pl.ds(8, 8), :], lev_ref, sems.at[0]),
+        pltpu.make_async_copy(lev_hbm.at[:, pl.ds(COLS - 128, 128)], tile_ref, sems.at[1]),
+        pltpu.make_async_copy(rows_hbm.at[z], rows_ref, sems.at[2]),
     ]
     for copy in copies:
         copy.start()
-    for copy in copies[1:]:
+    for copy in copies:
         copy.wait()
     to_x_ref[:, :COLS] = lev_ref[...].astype(F32)
     to_x_ref[:, COLS:] = jnp.concatenate([rows_ref[0, 8:, :], rows_ref[1, 8:, :]], axis=1)
-    to_y_ref[:ROWS, :] = tile_ref[...].astype(F32)
-    copies[0].wait()
-    for i in range(Z):
-        edge = cols_ref[i].reshape(2 * V, 128).T
-        to_y_ref[ROWS + HALO * i : ROWS + HALO * (i + 1), :] = edge[128 - HALO :, :]
-
-
-def pack(levels, rows_t, green_cols):
+    to_y_ref[...] = tile_ref[...].astype(F32)
+
+
+def pack(levels, rows_t):
     return pl.pallas_call(
         pack_kernel,
-        in_specs=[HBM] * 3,
+        in_specs=[HBM] * 2,
         out_specs=[VMEM] * 2,
         out_shape=[
             jax.ShapeDtypeStruct((8, COLS + 128), F32),
-            jax.ShapeDtypeStruct((ROWS + Z * HALO, 128), F32),
+            jax.ShapeDtypeStruct((ROWS, 128), F32),
         ],
         scratch_shapes=[
             pltpu.VMEM((8, COLS), jnp.int32),
             pltpu.VMEM((ROWS, 128), jnp.int32),
             pltpu.VMEM((2, ROWS, U), F32),
-            pltpu.VMEM((Z, 2, V, 128), F32),
-            pltpu.SemaphoreType.DMA((4,)),
+            pltpu.SemaphoreType.DMA((3,)),
         ],
         compiler_params=params(4),
         name="pack",
-    )(hbm(levels), hbm(rows_t), hbm(green_cols))
+    )(hbm(levels), hbm(rows_t))
+
+
+def relay_kernel(from_x_ref, green_ref, out_ref):
+    out_ref[:8, :] = from_x_ref[:, COLS - 128 : COLS]
+    out_ref[8:, :] = green_ref[...]
+
+
+def relay(from_x, green):
+    return pl.pallas_call(
+        relay_kernel,
+        in_specs=[VMEM] * 2,
+        out_specs=VMEM,
+        out_shape=jax.ShapeDtypeStruct((8 + Z * HALO, 128), F32),
+        compiler_params=params(4),
+        name="relay",
+    )(from_x, green)
 
 
 def one_hot(row, level_ids):
@@ -113,7 +122,7 @@
 
 
 def inner_kernel(
-    lev_ref, conv_ref, cb_ref, mix_ref, mb_ref, cols_hbm, feat_ref, hi_ref, lo_ref,
+    lev_ref, conv_ref, cb_ref, mix_ref, mb_ref, cols_hbm, feat_ref, hi_ref, lo_ref, green_ref,
     ext_ref, hot_ref, cols_ref, sems,
 ):
     z = lax.axis_index("py")
@@ -153,6 +162,9 @@
         return 0
 
     lax.fori_loop(0, Z, split, 0)
+    for g in range(Z):
+        edge = cols_ref[g, :, :, COLS - 128 :].reshape(2 * V, 128).T
+        green_ref[HALO * g : HALO * (g + 1), :] = edge[128 - HALO :, :]
 
 
 def inner(levels, conv_w, conv_b, mix_w, mix_b, green_cols):
@@ -160,11 +172,12 @@
     return pl.pallas_call(
         inner_kernel,
         in_specs=[VMEM] * 5 + [HBM],
-        out_specs=[VMEM] * 3,
+        out_specs=[VMEM] * 4,
         out_shape=[
             jax.ShapeDtypeStruct((PILLAR_ROWS * HID, COLS), BF16),
             jax.ShapeDtypeStruct((Z, 2 * V, COLS), BF16),
             jax.ShapeDtypeStruct((Z, 2 * V, COLS), BF16),
+            jax.ShapeDtypeStruct((Z * HALO, 128), F32),
         ],
         scratch_shapes=[
             pltpu.VMEM((3, ROWS, wide), F32),
@@ -177,47 +190,103 @@
     )(levels, conv_w, conv_b, mix_w, mix_b, hbm(green_cols))
 
 
+def tile_windows(left, tile, first_y, ext_ref):
+    ext = jnp.concatenate([left, tile], axis=1)
+    lane = iota(tile.shape, 1)
+    for b in range(3):
+        window = pltpu.roll(ext, 3 - b, 1)[:, 128:]
+        if b != 1:
+            window = jnp.where(first_y & (lane == (2 if b == 0 else 1)), -1.0, window)
+        ext_ref[b] = window
+
+
+def near_field(i, dec, feat_ref, nf_ref, edge_ref, first_y):
+    lane = iota((1, COLS), 1)
+    near = iota((1, 128), 1)
+    at = i * BLOCK * HID
+    taps = jnp.dot(dec, feat_ref[at : at + 2 * BLOCK * HID, :], preferred_element_type=F32)
+    acc = jnp.zeros((2 * HALF, COLS), F32)
+    edge = jnp.zeros((2 * HALF, 128), F32)
+    for s in range(KS):
+        part = taps[2 * HALF * s : 2 * HALF * (s + 1), :]
+        k = KS - 1 - s
+        ok = (lane < COLS - k) & ((lane + k >= 2) | jnp.logical_not(first_y))
+        moved = part if k == 0 else pltpu.roll(part, COLS - k, 1)
+        acc = acc + jnp.where(ok, moved, 0.0)
+        ok = (near >= s) & (near < HALO) & ((near - s < 2) | jnp.logical_not(first_y))
+        part = part[:, :128]
+        moved = part if s == 0 else pltpu.roll(part, s, 1)
+        edge = edge + jnp.where(ok, moved, 0.0)
+    for part, values in enumerate(split2(acc)):
+        for k in range(2):
+            at = (2 * part + k) * PART + i * HALF
+            nf_ref[at : at + HALF, :] = values[k * HALF : (k + 1) * HALF]
+    for k in range(2):
+        at = k * PART + i * HALF
+        edge_ref[at : at + HALF, :] = edge[k * HALF : (k + 1) * HALF]
+
+
+def middle_kernel(
+    lev_ref, from_y_ref, conv_ref, cb_ref, mix_ref, mb_ref, dec_ref, _,
+    nf_ref, edge_ref, feat_ref, ext_ref, hot_ref,
+):
+    first_y = lax.axis_index("py") == 0
+    tile_windows(from_y_ref[...], lev_ref[:, :128].astype(F32), first_y, ext_ref)
+    level_ids = iota((LEVELS, 128), 0).astype(F32)
+    for q in range(ROWS - 2):
+        for b in range(3):
+            row = one_hot(ext_ref[b, q : q + 1, :], level_ids)
+            for t in range(6):
+                if 0 <= q - 2 * t < 4:
+                    at = (q - 2 * t) * SLOT + b * LEVELS
+                    hot_ref[at : at + LEVELS, t * 128 : (t + 1) * 128] = row
+    tiles = features(hot_ref[...], conv_ref[...], cb_ref[...], mix_ref[...], mb_ref[...])
+    for t in range(6):
+        at = (8 + 2 * t) * HID
+        feat_ref[at : at + 2 * HID, :128] = tiles[:, t * 128 : (t + 1) * 128]
+    for i in (2, 3):
+        near_field(i, dec_ref[...], feat_ref, nf_ref, edge_ref, first_y)
+
+
+def middle(levels, from_y, conv_w, conv_b, mix_w, mix_b, dec_w, feat):
+    return pl.pallas_call(
+        middle_kernel,
+        in_specs=[VMEM] * 8,
+        out_specs=[VMEM] * 3,
+        out_shape=[
+            jax.ShapeDtypeStruct((4 * PART, COLS), BF16),
+            jax.ShapeDtypeStruct((2 * PART, 128), F32),
+            jax.ShapeDtypeStruct(feat.shape, BF16),
+        ],
+        input_output_aliases={7: 2},
+        scratch_shapes=[pltpu.VMEM((3, ROWS, 128), F32), pltpu.VMEM((WINDOW, 768), BF16)],
+        compiler_params=params(8),
+        name="middle",
+    )(levels, from_y, conv_w, conv_b, mix_w, mix_b, dec_w, feat)
+
+
 def outer_kernel(
-    lev_ref, from_x_ref, from_y_ref, conv_ref, cb_ref, mix_ref, mb_ref, _, feat_ref, ext_ref, hot_ref
+    lev_ref, from_x_ref, conv_ref, cb_ref, mix_ref, mb_ref, _, feat_ref, ext_ref, hot_ref
 ):
     first_x = lax.axis_index("px") == 0
-    first_y = lax.axis_index("py") == 0
-    ext = jnp.concatenate([from_x_ref[:, :COLS], lev_ref[...].astype(F32)], axis=0)
-    left = jnp.concatenate([jnp.zeros((8, 128), F32), from_y_ref[:ROWS, :]], axis=0)
-    lane = iota((24, 128), 1)
+    ext = jnp.concatenate([from_x_ref[:, :COLS], lev_ref[:8, :].astype(F32)], axis=0)
     for b in range(3):
-        window = pltpu.roll(ext, 3 - b, 1)
-        tile = pltpu.roll(jnp.concatenate([left, ext[:, :128]], axis=1), 3 - b, 1)[:, 128:]
-        if b != 1:
-            tile = jnp.where(first_y & (lane == (2 if b == 0 else 1)), -1.0, tile)
-        ext_ref[b] = jnp.concatenate([tile, window[:, 128:]], axis=1)
+        ext_ref[b] = pltpu.roll(ext, 3 - b, 1)[:, 128:]
     wide = COLS - 128
     level_ids = iota((LEVELS, wide), 0).astype(F32)
-    for o in range(4):
+    for e in range(10):
         for b in range(3):
-            at = pl.ds(o * SLOT + b * LEVELS, LEVELS)
-            for w in range(4):
-                e = 2 * w + o
-                hot_ref[w, at, :] = one_hot(ext_ref[b, e : e + 1, 128:], level_ids)
-            for t in range(6):
-                e = 2 * t + 8 + o
-                hot_ref[4, at, t * 128 : (t + 1) * 128] = one_hot(
-                    ext_ref[b, e : e + 1, :128], level_ids[:, :128]
-                )
+            at = e * SLOT + b * LEVELS
+            hot_ref[at : at + LEVELS, :] = one_hot(ext_ref[b, e : e + 1, :], level_ids)
     conv_bias = jnp.broadcast_to(cb_ref[...], (2 * HID, wide))
     mix_bias = jnp.broadcast_to(mb_ref[...], (2 * HID, wide))
     for w in range(4):
         at = 2 * w * HID
         conv = cut_conv(conv_ref[...], first_x) if w == 3 else conv_ref[...]
         feat_ref[at : at + 2 * HID, 128:] = features(
-            hot_ref[w], conv, conv_bias, mix_ref[...], mix_bias
+            hot_ref[2 * w * SLOT : 2 * w * SLOT + WINDOW, :],
+            conv, conv_bias, mix_ref[...], mix_bias,
         )
-    tiles = features(
-        hot_ref[4, :, :768], conv_ref[...], conv_bias[:, :768], mix_ref[...], mix_bias[:, :768]
-    )
-    for t in range(6):
-        at = (8 + 2 * t) * HID
-        feat_ref[at : at + 2 * HID, :128] = tiles[:, t * 128 : (t + 1) * 128]
 
 
 def cut_conv(conv, first_x):
@@ -227,24 +296,26 @@
     return conv * keep.astype(BF16)
 
 
-def outer(levels, from_x, from_y, conv_w, conv_b, mix_w, mix_b, feat):
+def outer(levels, from_x, conv_w, conv_b, mix_w, mix_b, feat):
+    wide = COLS - 128
     return pl.pallas_call(
         outer_kernel,
-        in_specs=[VMEM] * 8,
+        in_specs=[VMEM] * 7,
         out_specs=VMEM,
         out_shape=jax.ShapeDtypeStruct(feat.shape, BF16),
-        input_output_aliases={7: 0},
+        input_output_aliases={6: 0},
         scratch_shapes=[
-            pltpu.VMEM((3, 24, COLS), F32),
-            pltpu.VMEM((5, WINDOW, COLS - 128), BF16),
-        ],
-        compiler_params=params(12),
+            pltpu.VMEM((3, 16, wide), F32),
+            pltpu.VMEM((10 * SLOT, wide), BF16),
+        ],
+        compiler_params=params(8),
         name="outer",
-    )(levels, from_x, from_y, conv_w, conv_b, mix_w, mix_b, feat)
-
-
-def column_sum(hi_ref, lo_ref, nf_ref, edge_ref, from_y_ref, out_ref, first, count):
+    )(levels, from_x, conv_w, conv_b, mix_w, mix_b, feat)
+
+
+def column_sum(hi_ref, lo_ref, nf_ref, edge_ref, from_d_ref, out_ref, first, count):
     iy = lax.axis_index("py")
+    before = (iy + lax.axis_size("py") - 1) % lax.axis_size("py")
     n = 2 * PART
     sign = jnp.where(iota((1, 128), 1) < V, -1.0, 1.0)
     hi = hi_ref[first : first + count].reshape(2 * V * count, COLS)
@@ -254,8 +325,9 @@
     both = both + lax.dot_general(lo, nf_ref[:n, :], NT, preferred_element_type=F32)
     for g in range(count):
         out = both[2 * V * g : 2 * V * (g + 1)].T
-        z = iy ^ REL_ORDER[first + g]
-        green = from_y_ref[pl.ds(ROWS + HALO * z, HALO), :]
+        rel = (iy ^ REL_ORDER[first + g]) ^ before
+        at = 8 + HALO * (rel // 2 + 4 * (rel % 2))
+        green = from_d_ref[pl.ds(at, HALO), :]
         green = jnp.concatenate([green, jnp.zeros((4, 128), F32)], axis=0)
         out = out + jnp.dot(edge_ref[:, :8], green, precision=HIGH, preferred_element_type=F32)
         out_ref[g] = out[:PART] + sign * pltpu.roll(out[PART:], V, 1)
@@ -263,19 +335,13 @@
 
 def field_kernel(
     lev_ref, from_x_ref, from_y_ref, from_d_ref, conv_ref, cb_ref, mix_ref, mb_ref, dec_ref,
-    hi_ref, lo_ref, _, send_ref, nf_ref, edge_ref, feat_ref, ext_ref, hot_ref,
+    hi_ref, lo_ref, _nf, _edge, _feat, send_ref, nf_ref, edge_ref, feat_ref, ext_ref, hot_ref,
 ):
     first_x = lax.axis_index("px") == 0
     first_y = lax.axis_index("py") == 0
     tile = jnp.concatenate([from_x_ref[:, :128], lev_ref[:8, :128].astype(F32)], axis=0)
-    left = jnp.concatenate([from_d_ref[:, COLS - 128 : COLS], from_y_ref[:8, :]], axis=0)
-    ext = jnp.concatenate([left, tile], axis=1)
-    lane = iota((16, 128), 1)
-    for b in range(3):
-        window = pltpu.roll(ext, 3 - b, 1)[:, 128:]
-        if b != 1:
-            window = jnp.where(first_y & (lane == (2 if b == 0 else 1)), -1.0, window)
-        ext_ref[b] = window
+    left = jnp.concatenate([from_d_ref[:8, :], from_y_ref[:8, :]], axis=0)
+    tile_windows(left, tile, first_y, ext_ref)
     level_ids = iota((LEVELS, 128), 0).astype(F32)
     for w in range(4):
         for o in range(4):
@@ -294,49 +360,24 @@
         hot_ref[:, 384:], cut_conv(conv_ref[...], first_x), cb_ref[...], mix_ref[...], mb_ref[...]
     )
 
-    lane = iota((1, COLS), 1)
-    near = iota((1, 128), 1)
     shape = (KS * CH * BLOCK, 2 * BLOCK * HID)
     sample = iota(shape, 0) // 4 % BLOCK - SHIFT
     pillar = iota(shape, 1) // HID - SHIFT - 2
-    for i in reversed(range(ROWS // BLOCK)):
-        dec = dec_ref[...]
-        if i < 2:
-            at = i * BLOCK
-            apart = (sample + at >= 0) != (pillar + at >= 0)
-            keep = jnp.where(first_x & apart, 0.0, 1.0)
-            dec = dec * keep.astype(BF16)
-        at = i * BLOCK * HID
-        taps = jnp.dot(
-            dec, feat_ref[at : at + 2 * BLOCK * HID, :], preferred_element_type=F32
-        )
-        acc = jnp.zeros((2 * HALF, COLS), F32)
-        edge = jnp.zeros((2 * HALF, 128), F32)
-        for s in range(KS):
-            part = taps[2 * HALF * s : 2 * HALF * (s + 1), :]
-            k = KS - 1 - s
-            ok = (lane < COLS - k) & ((lane + k >= 2) | jnp.logical_not(first_y))
-            moved = part if k == 0 else pltpu.roll(part, COLS - k, 1)
-            acc = acc + jnp.where(ok, moved, 0.0)
-            ok = (near >= s) & (near < HALO) & ((near - s < 2) | jnp.logical_not(first_y))
-            part = part[:, :128]
-            moved = part if s == 0 else pltpu.roll(part, s, 1)
-            edge = edge + jnp.where(ok, moved, 0.0)
-        for part, values in enumerate(split2(acc)):
-            for k in range(2):
-                at = (2 * part + k) * PART + i * HALF
-                nf_ref[at : at + HALF, :] = values[k * HALF : (k + 1) * HALF]
-        for k in range(2):
-            at = k * PART + i * HALF
-            edge_ref[at : at + HALF, :] = edge[k * HALF : (k + 1) * HALF]
-
-    column_sum(hi_ref, lo_ref, nf_ref, edge_ref, from_y_ref, send_ref, 4, 4)
-
-
-def field(levels, from_x, from_y, from_d, conv_w, conv_b, mix_w, mix_b, dec_w, hi, lo, feat):
+    for i in range(2):
+        at = i * BLOCK
+        apart = (sample + at >= 0) != (pillar + at >= 0)
+        keep = jnp.where(first_x & apart, 0.0, 1.0)
+        near_field(i, dec_ref[...] * keep.astype(BF16), feat_ref, nf_ref, edge_ref, first_y)
+
+    column_sum(hi_ref, lo_ref, nf_ref, edge_ref, from_d_ref, send_ref, 4, 4)
+
+
+def field(
+    levels, from_x, from_y, from_d, conv_w, conv_b, mix_w, mix_b, dec_w, hi, lo, nf, edge, feat
+):
     return pl.pallas_call(
         field_kernel,
-        in_specs=[VMEM] * 12,
+        in_specs=[VMEM] * 14,
         out_specs=[VMEM] * 4,
         out_shape=[
             jax.ShapeDtypeStruct((4, PART, 128), F32),
@@ -344,19 +385,21 @@
             jax.ShapeDtypeStruct((2 * PART, 128), F32),
             jax.ShapeDtypeStruct(feat.shape, BF16),
         ],
-        input_output_aliases={11: 3},
+        input_output_aliases={11: 1, 12: 2, 13: 3},
         scratch_shapes=[
             pltpu.VMEM((3, 16, 128), F32),
             pltpu.VMEM((WINDOW, 512), BF16),
         ],
         compiler_params=params(12),
         name="field",
-    )(levels, from_x, from_y, from_d, conv_w, conv_b, mix_w, mix_b, dec_w, hi, lo, feat)
-
-
-def keep_planes(hi, lo, nf, edge, from_y, first, count):
-    def keep_kernel(hi_ref, lo_ref, nf_ref, edge_ref, from_y_ref, out_ref):
-        column_sum(hi_ref, lo_ref, nf_ref, edge_ref, from_y_ref, out_ref, first, count)
+    )(
+        levels, from_x, from_y, from_d, conv_w, conv_b, mix_w, mix_b, dec_w, hi, lo, nf, edge, feat
+    )
+
+
+def keep_planes(hi, lo, nf, edge, from_d, first, count):
+    def keep_kernel(hi_ref, lo_ref, nf_ref, edge_ref, from_d_ref, out_ref):
+        column_sum(hi_ref, lo_ref, nf_ref, edge_ref, from_d_ref, out_ref, first, count)
 
     return pl.pallas_call(
         keep_kernel,
@@ -365,7 +408,7 @@
         out_shape=jax.ShapeDtypeStruct((count, PART, 128), F32),
         compiler_params=params(8),
         name="keep_planes",
-    )(hi, lo, nf, edge, from_y)
+    )(hi, lo, nf, edge, from_d)
 
 
 def rows_kernel(from_x_ref, rows_ref, order_ref, out_ref):
@@ -483,24 +526,26 @@
         (conv_w, conv_b, mix_w, mix_b, dec_w, order)
     )
 
-    to_x, to_y = pack(levels, rows_t, green_cols)
+    to_x, to_y = pack(levels, rows_t)
     from_x = lax.ppermute(to_x, "px", next_x)
     from_y = lax.ppermute(to_y, "py", next_y)
-    feat, hi, lo = inner(levels, conv_w, conv_b, mix_w, mix_b, green_cols)
-    from_x, from_y, feat = lax.optimization_barrier((from_x, from_y, feat))
-    from_d = lax.ppermute(from_x, "py", next_y)
-    feat = outer(levels, from_x, from_y, conv_w, conv_b, mix_w, mix_b, feat)
+    feat, hi, lo, green = inner(levels, conv_w, conv_b, mix_w, mix_b, green_cols)
+    from_y, feat = lax.optimization_barrier((from_y, feat))
+    nf, edge, feat = middle(levels, from_y, conv_w, conv_b, mix_w, mix_b, dec_w, feat)
+    from_x, feat, nf, edge = lax.optimization_barrier((from_x, feat, nf, edge))
+    from_d = lax.ppermute(relay(from_x, green), "py", next_y)
+    feat = outer(levels, from_x, conv_w, conv_b, mix_w, mix_b, feat)
     send, nf, edge, _ = field(
-        levels, from_x, from_y, from_d, conv_w, conv_b, mix_w, mix_b, dec_w, hi, lo, feat
+        levels, from_x, from_y, from_d, conv_w, conv_b, mix_w, mix_b, dec_w, hi, lo, nf, edge, feat
     )
 
     def swap(x, mask):
         return lax.ppermute(x, "py", [(i, i ^ mask) for i in range(count_py)])
 
     got = swap(send, 1)
-    keep = keep_planes(hi, lo, nf, edge, from_y, 1, 3)
+    keep = keep_planes(hi, lo, nf, edge, from_d, 1, 3)
     b, c, d = (swap(keep[i - 1] + got[i], 2 * i) for i in (1, 2, 3))
-    keep = keep_planes(hi, lo, nf, edge, from_y, 0, 1)
+    keep = keep_planes(hi, lo, nf, edge, from_d, 0, 1)
     factors = row_factors(from_x, rows_t, order)
     share = focal_share(factors, keep, got, b, c, d)
     return total(lax.all_to_all(share, "px", 0, 0))

time: 52.4 us -> 55.9 us (1.067)
  other arithmetic: 0.35 us -> 3.44 us
  local copies, waits for them, and re-layouts: 0.78 us -> 2.24 us
  blocking collectives: 21.4 us -> 20.1 us
    all_to_all x1, blocking collectives: 21.4 us -> 20.1 us  [on_device(): return total(lax.all_to_all(share, 'px', 0, 0))]
    concatenate x1, other arithmetic: 0.08 us -> 0.92 us  [conv_weights(): jnp.concatenate([jnp.pad(conv_table, ((0, 0), (0, SLOT))), jnp.pad(conv_t...]
    unnamed x16 -> x4, local copies, waits for them, and re-layouts: 0.03 us -> 0.84 us
    rev x1, other arithmetic: 0.01 us -> 0.82 us  [decoder_weights(): d = d[::-1].reshape(KS, KS, 2, 4, HID).transpose(1, 2, 3, 0, 4)]
    broadcast_in_dim x1, other arithmetic: 0.08 us -> 0.81 us  [bias_column(): return jnp.concatenate([bias, bias])[:, None]]
    mul x1, other arithmetic: 0.01 us -> 0.72 us  [mix_weights(): w = mix_weight * jnp.asarray(0.5, BF16)]
    broadcast_in_dim x1, local copies, waits for them, and re-layouts: 0.07 us -> 0.73 us  [on_device(): order = jnp.broadcast_to(focal_order[:, None], (U, 4)).reshape(1, U * 4)]
    pallas_call x3 -> x5, Pallas kernels: 5.9 us -> 5.89 us  [the longest x1 2.13 us: field(): pl.pallas_call(field_kernel, in_specs=[VMEM] * 14, out_specs=[VMEM] * 4,...]
  transfers between devices with their start and end apart: 7 -> 7, of which waited for: 4 -> 3; matrix products, arithmetic and copies ran while one was open for 2% -> 9% of each run, Pallas kernels for 15% -> 15%
where the time goes in v5:
time: 55.9 us; the launch traced here: 55.4 us
  blocking collectives  20.1 us (36%)
  starting transfers between devices  12.7 us (23%)
  Pallas kernels  12.6 us (23%)
  waiting for transfers between devices  4.16 us (7%)
  other arithmetic  3.44 us (6%)
  local copies, waits for them, and re-layouts  2.24 us (4%)
    all_to_all x1, blocking collectives, on_device(): return total(lax.all_to_all(share, 'px', 0, 0))  20.1 us
    ppermute x1, starting transfers between devices, on_device(): from_x = lax.ppermute(to_x, 'px', next_x)  7.27 us
    ppermute x4, starting transfers between devices, swap(): return lax.ppermute(x, 'py', [(i, i ^ mask) for i in range(count_py)])  4.56 us
    pallas_call x1, Pallas kernels, inner(): pl.pallas_call(inner_kernel, in_specs=[VMEM] * 5 + [HBM], out_specs=[VMEM...  3.78 us
    ppermute x1, waiting for transfers between devices, on_device(): from_d = lax.ppermute(relay(from_x, green), 'py', next_y)  2.49 us
    pallas_call x1, Pallas kernels, field(): pl.pallas_call(field_kernel, in_specs=[VMEM] * 14, out_specs=[VMEM] * 4,...  2.13 us
    pallas_call x1, Pallas kernels, outer(): pl.pallas_call(outer_kernel, in_specs=[VMEM] * 7, out_specs=VMEM, out_sha...  1.74 us
    ppermute x4, waiting for transfers between devices, swap(): return lax.ppermute(x, 'py', [(i, i ^ mask) for i in range(count_py)])  1.67 us
  transfers between devices with their start and end apart: 7, of which 3 were waited for; matrix products, arithmetic and copies ran while one was open for 9% of the time, Pallas kernels for 15%

profile of v5, /device:TPU:2, one launch (start us, length us, event | category | flops | bytes accessed | tf_op | source)
XLA Modules:
  0.0 55.4 jit_solution(5702822370235667013)
XLA Ops:
  0.0 0.9 %pack.1 = (f32[8,1152]{1,0:T(8,128)S(1)}, f32[16,128]{1,0:T(8,128)S(1)}) custom-call(s32[16,1024]{1,0:T(8,128)} %lev_ref.7, f32[8,2,16,64]{3,2,1,0:T(8,128)} %bitcast.31), custom_call_target="tpu_custom_call" | custom-call | tf_op jit(solution)/shard_map/pack/pallas_call | solution.py:77
  0.9 0.1 collective-permute-start.1
  1.0 7.3 %collective-permute-start = (f32[8,1152]{1,0:T(8,128)S(1)}, f32[8,1152]{1,0:T(8,128)S(1)}, u32[]{:S(2)}, u32[]{:S(2)}) collective-permute-start(f32[8,1152]{1,0:T(8,128)S(1)} %get-tuple-element.29), channel_id=1, source_target_pairs={{0,8},{8,16},{16,24},{24,32},{32,40},{40,48},{48,56},{56,64},{64,7... | collective-permute-start | bytes 110600 | tf_op jit(solution)/shard_map/ppermute | solution.py:530
  8.2 0.8 %reverse_multiply_fusion = bf16[5,40,64]{2,1,0:T(8,128)(2,1)S(1)} fusion(bf16[5,40,64]{2,1,0:T(8,128)(2,1)} %param.14), kind=kLoop, calls=%fused_computation.15 | loop fusion | flops 51200 | bytes 51200 | tf_op jit(solution)/shard_map/rev | solution.py:500
  9.1 0.1 pad_bitcast_fusion.3
  9.2 0.9 %fusion.2.conv_ref = bf16[128,192]{1,0:T(8,128)(2,1)S(1)} fusion(bf16[64,144]{1,0:T(8,128)(2,1)} %param.10), kind=kLoop, calls=%fused_computation.10 | loop fusion | flops 196608 | bytes 67584 | tf_op jit(solution)/shard_map/concatenate | solution.py:486
  10.1 0.7 %broadcast_multiply_fusion = bf16[64,64]{1,0:T(8,128)(2,1)S(1)} fusion(bf16[64,64]{1,0:T(8,128)(2,1)} %param.12), kind=kLoop, calls=%fused_computation.23 | loop fusion | flops 4096 | bytes 16384 | tf_op jit(solution)/shard_map/mul | solution.py:492
  10.8 0.1 fusion.5.mix_ref
  10.9 0.1 pad_maximum_fusion
  11.0 0.8 %maximum_bitcast_fusion = (f32[128,1]{0,1:T(1,128)S(1)}, f32[128,1]{0,1:T(1,128)S(1)}) fusion(f32[64]{0:T(128)} %param.11, f32[64]{0:T(128)} %param.13), kind=kLoop, calls=%fused_computation.24 | loop fusion | flops 256 | bytes 1536 | tf_op jit(solution)/shard_map/broadcast_in_dim | solution.py:508
  11.8 0.2 reshape.14.dec_ref
  12.0 0.7 %broadcast_in_dim.14 = s32[64,4]{1,0:T(8,128)S(1)} broadcast(s32[64]{0:T(128)} %param.17), dimensions={0} | broadcast | bytes 1280 | tf_op jit(solution)/shard_map/broadcast_in_dim | solution.py:524
  12.8 0.1 reshape.15.order_ref
  12.9 0.1 copy.31.cb_ref
  13.0 0.1 copy.32.mb_ref
  13.1 0.0 copy-start
  13.1 0.8 %copy-done = s32[16,1024]{1,0:T(8,128)S(1)} copy-done((s32[16,1024]{1,0:T(8,128)S(1)}, s32[16,1024]{1,0:T(8,128)}, u32[]{:S(2)}) %copy-start) | copy-done | bytes 65560
  13.9 3.8 %inner.1 = (bf16[1280,1024]{1,0:T(8,128)(2,1)S(1)}, bf16[8,128,1024]{2,1,0:T(8,128)(2,1)S(1)}, bf16[8,128,1024]{2,1,0:T(8,128)(2,1)S(1)}, f32[32,128]{1,0:T(8,128)S(1)}) custom-call(s32[16,1024]{1,0:T(8,128)S(1)} %copy-done, bf16[128,192]{1,0:T(8,128)(2,1)S(1)} %fusion.2.conv_ref, f32[128,1]{1,0:T(8,128)S(1)} %copy.31.cb_ref, ...), custom_call_target="tpu_custom_call" | custom-call | tf_op jit(solution)/shard_map/inner/pallas_call | solution.py:172
  17.7 0.0 collective-permute-done.1.from_y_ref
  17.7 1.1 %middle.1 = (bf16[256,1024]{1,0:T(8,128)(2,1)S(1)}, f32[128,128]{1,0:T(8,128)S(1)}, bf16[1280,1024]{1,0:T(8,128)(2,1)S(1)}) custom-call(s32[16,1024]{1,0:T(8,128)S(1)} %copy-done, f32[16,128]{1,0:T(8,128)S(1)} %collective-permute-done.1.from_y_ref, bf16[128,192]{1,0:T(8,128)(2,1)S(1)} %fusion.2.conv_ref, ...), custom_call_target="tpu_custom_call", output_to_operand_aliasing={{2}: (7, {})} | custom-call | tf_op jit(solution)/shard_map/middle/pallas_call | solution.py:252
  18.9 0.0 collective-permute-done.from_x_ref
  18.9 0.8 %collective-permute-start.2 = (f32[40,128]{1,0:T(8,128)S(1)}, f32[40,128]{1,0:T(8,128)S(1)}, u32[]{:S(2)}, u32[]{:S(2)}) collective-permute-start(f32[40,128]{1,0:T(8,128)S(1)} %relay.1), channel_id=1, source_target_pairs={{0,1},{1,2},{2,3},{3,4},{4,5},{5,6},{6,7},{7,0},{8,9},{9,10},{10,1... | collective-permute-start | bytes 61448 | tf_op jit(solution)/shard_map/ppermute | solution.py:536
  19.8 1.7 %outer.1._feat = bf16[1280,1024]{1,0:T(8,128)(2,1)S(1)} custom-call(s32[16,1024]{1,0:T(8,128)S(1)} %copy-done, f32[8,1152]{1,0:T(8,128)S(1)} %collective-permute-done.from_x_ref, bf16[128,192]{1,0:T(8,128)(2,1)S(1)} %fusion.2.conv_ref, f32[128,1]{1,0:T(8,128)S(1)} %copy.31.cb_ref, ...), custom_call_target="tpu_custom_call", output_to_operand_aliasing={{}: (6, {})} | custom-call | tf_op jit(solution)/shard_map/outer/pallas_call | solution.py:301
  21.5 2.5 %collective-permute-done.2.from_d_ref = f32[40,128]{1,0:T(8,128)S(1)} collective-permute-done((f32[40,128]{1,0:T(8,128)S(1)}, f32[40,128]{1,0:T(8,128)S(1)}, u32[]{:S(2)}, u32[]{:S(2)}) %collective-permute-start.2) | collective-permute-done | bytes 20512 | tf_op jit(solution)/shard_map/ppermute | solution.py:536
  24.0 2.1 %field.1 = (f32[4,64,128]{2,1,0:T(8,128)S(1)}, bf16[256,1024]{1,0:T(8,128)(2,1)S(1)}, f32[128,128]{1,0:T(8,128)S(1)}, bf16[1280,1024]{1,0:T(8,128)(2,1)S(1)}) custom-call(s32[16,1024]{1,0:T(8,128)S(1)} %copy-done, f32[8,1152]{1,0:T(8,128)S(1)} %collective-permute-done.from_x_ref, ...), custom_call_target="tpu_custom_call", output_to_operand_aliasing={{1}: (11, {}), {2}: (12, {}), {3}: (13, {})} | custom-call | tf_op jit(solution)/shard_map/field/pallas_call | solution.py:378
  26.1 0.0 copy-start.1
  26.2 0.1 collective-permute-start.3
  26.3 0.8 %keep_planes.3 = f32[3,64,128]{2,1,0:T(8,128)S(1)} custom-call(bf16[8,128,1024]{2,1,0:T(8,128)(2,1)S(1)} %get-tuple-element.44.hi_ref, bf16[8,128,1024]{2,1,0:T(8,128)(2,1)S(1)} %get-tuple-element.45.lo_ref, bf16[256,1024]{1,0:T(8,128)(2,1)S(1)} %get-tuple-element.50.nf_ref, f32[128,128]{1,0:T(8,128)S(1)} %get-tuple-element.51.edge_ref, ...), custom_call_target="tpu_custom_call" | custom-call | tf_op jit(solution)/shard_map/keep_planes/pallas_call | solution.py:404
  27.1 0.5 collective-permute-done.3.got_ref
  27.6 0.1 collective-permute-start.4
  27.7 0.9 %collective-permute-start.5 = (f32[64,128]{1,0:T(8,128)S(1)}, f32[64,128]{1,0:T(8,128)S(1)}, u32[]{:S(2)}, u32[]{:S(2)}) collective-permute-start(f32[64,128]{1,0:T(8,128)S(1)} %get-tuple-element.54), channel_id=1, source_target_pairs={{0,4},{1,5},{2,6},{3,7},{4,0},{5,1},{6,2},{7,3},{8,12},{9,13},{10,... | collective-permute-start | bytes 98312 | tf_op jit(solution)/shard_map/ppermute | solution.py:543
  28.6 3.5 %collective-permute-start.6 = (f32[64,128]{1,0:T(8,128)S(1)}, f32[64,128]{1,0:T(8,128)S(1)}, u32[]{:S(2)}, u32[]{:S(2)}) collective-permute-start(f32[64,128]{1,0:T(8,128)S(1)} %get-tuple-element.53), channel_id=1, source_target_pairs={{0,6},{1,7},{2,4},{3,5},{4,2},{5,3},{6,0},{7,1},{8,14},{9,15},{10,... | collective-permute-start | bytes 98312 | tf_op jit(solution)/shard_map/ppermute | solution.py:543
  32.1 0.0 copy-done.1
  32.1 0.5 row_factors.1.factor_ref
  32.6 0.6 %keep_planes.2.keep_ref = f32[1,64,128]{2,1,0:T(8,128)S(1)} custom-call(bf16[8,128,1024]{2,1,0:T(8,128)(2,1)S(1)} %get-tuple-element.44.hi_ref, bf16[8,128,1024]{2,1,0:T(8,128)(2,1)S(1)} %get-tuple-element.45.lo_ref, bf16[256,1024]{1,0:T(8,128)(2,1)S(1)} %get-tuple-element.50.nf_ref, f32[128,128]{1,0:T(8,128)S(1)} %get-tuple-element.51.edge_ref, ...), custom_call_target="tpu_custom_call" | custom-call | tf_op jit(solution)/shard_map/keep_planes/pallas_call | solution.py:404
  33.2 0.0 collective-permute-done.4.b_ref
  33.2 0.0 collective-permute-done.5.c_ref
  33.2 1.2 %collective-permute-done.6.d_ref = f32[64,128]{1,0:T(8,128)S(1)} collective-permute-done((f32[64,128]{1,0:T(8,128)S(1)}, f32[64,128]{1,0:T(8,128)S(1)}, u32[]{:S(2)}, u32[]{:S(2)}) %collective-permute-start.6) | collective-permute-done | bytes 32800 | tf_op jit(solution)/shard_map/ppermute | solution.py:543
  34.4 0.3 focal_share.1
  34.7 20.1 %all_to_all.5.x_ref = f32[32,8,128]{2,1,0:T(8,128)S(1)} all-to-all(f32[32,8,128]{2,1,0:T(8,128)S(1)} %focal_share.1), channel_id=1, replica_groups=mesh['px'=32,'py'=8] {'px'}, dimensions={0} | all-to-all | bytes 262144 | tf_op jit(solution)/shard_map/all_to_all | solution.py:551
  54.7 0.7 %total.1 = f32[1,2,512]{2,1,0:T(2,128)} custom-call(f32[32,8,128]{2,1,0:T(8,128)S(1)} %all_to_all.5.x_ref), custom_call_target="tpu_custom_call" | custom-call | tf_op jit(solution)/shard_map/total/pallas_call | solution.py:475
  (3 shorter events, 0.0 us)
Async XLA Ops:
  0.9 16.9 %collective-permute-start.1 = (f32[16,128]{1,0:T(8,128)S(1)}, f32[16,128]{1,0:T(8,128)S(1)}, u32[]{:S(2)}, u32[]{:S(2)}) collective-permute-start(f32[16,128]{1,0:T(8,128)S(1)} %get-tuple-element.30), channel_id=1, source_target_pairs={{0,1},{1,2},{2,3},{3,4},{4,5},{5,6},{6,7},{7,0},{8,9},{9,10},{10,1... | collective-permute-start | bytes 24584 | tf_op jit(solution)/shard_map/ppermute | solution.py:531
  1.0 17.9 %collective-permute-start = (f32[8,1152]{1,0:T(8,128)S(1)}, f32[8,1152]{1,0:T(8,128)S(1)}, u32[]{:S(2)}, u32[]{:S(2)}) collective-permute-start(f32[8,1152]{1,0:T(8,128)S(1)} %get-tuple-element.29), channel_id=1, source_target_pairs={{0,8},{8,16},{16,24},{24,32},{32,40},{40,48},{48,56},{56,64},{64,7... | collective-permute-start | bytes 110600 | tf_op jit(solution)/shard_map/ppermute | solution.py:530
  13.1 0.8 %copy-start = (s32[16,1024]{1,0:T(8,128)S(1)}, s32[16,1024]{1,0:T(8,128)}, u32[]{:S(2)}) copy-start(s32[16,1024]{1,0:T(8,128)} %lev_ref.7) | copy-start | bytes 196612
  18.9 5.1 %collective-permute-start.2 = (f32[40,128]{1,0:T(8,128)S(1)}, f32[40,128]{1,0:T(8,128)S(1)}, u32[]{:S(2)}, u32[]{:S(2)}) collective-permute-start(f32[40,128]{1,0:T(8,128)S(1)} %relay.1), channel_id=1, source_target_pairs={{0,1},{1,2},{2,3},{3,4},{4,5},{5,6},{6,7},{7,0},{8,9},{9,10},{10,1... | collective-permute-start | bytes 61448 | tf_op jit(solution)/shard_map/ppermute | solution.py:536
  26.1 5.9 %copy-start.1 = (f32[8,2,64,16]{2,3,1,0:T(8,128)S(1)}, f32[8,2,64,16]{2,3,1,0:T(8,128)}, u32[]{:S(2)}) copy-start(f32[8,2,64,16]{2,3,1,0:T(8,128)} %param.15) | copy-start | bytes 196612
  26.2 1.4 %collective-permute-start.3 = (f32[4,64,128]{2,1,0:T(8,128)S(1)}, f32[4,64,128]{2,1,0:T(8,128)S(1)}, u32[]{:S(2)}, u32[]{:S(2)}) collective-permute-start(f32[4,64,128]{2,1,0:T(8,128)S(1)} %get-tuple-element.52), channel_id=1, source_target_pairs={{0,1},{1,0},{2,3},{3,2},{4,5},{5,4},{6,7},{7,6},{8,9},{9,8},{10,11... | collective-permute-start | bytes 393224 | tf_op jit(solution)/shard_map/ppermute | solution.py:543
  27.6 5.6 %collective-permute-start.4 = (f32[64,128]{1,0:T(8,128)S(1)}, f32[64,128]{1,0:T(8,128)S(1)}, u32[]{:S(2)}, u32[]{:S(2)}) collective-permute-start(f32[64,128]{1,0:T(8,128)S(1)} %get-tuple-element.55), channel_id=1, source_target_pairs={{0,2},{1,3},{2,0},{3,1},{4,6},{5,7},{6,4},{7,5},{8,10},{9,11},{10,... | collective-permute-start | bytes 98312 | tf_op jit(solution)/shard_map/ppermute | solution.py:543
  27.7 5.5 %collective-permute-start.5 = (f32[64,128]{1,0:T(8,128)S(1)}, f32[64,128]{1,0:T(8,128)S(1)}, u32[]{:S(2)}, u32[]{:S(2)}) collective-permute-start(f32[64,128]{1,0:T(8,128)S(1)} %get-tuple-element.54), channel_id=1, source_target_pairs={{0,4},{1,5},{2,6},{3,7},{4,0},{5,1},{6,2},{7,3},{8,12},{9,13},{10,... | collective-permute-start | bytes 98312 | tf_op jit(solution)/shard_map/ppermute | solution.py:543
  28.6 5.8 %collective-permute-start.6 = (f32[64,128]{1,0:T(8,128)S(1)}, f32[64,128]{1,0:T(8,128)S(1)}, u32[]{:S(2)}, u32[]{:S(2)}) collective-permute-start(f32[64,128]{1,0:T(8,128)S(1)} %get-tuple-element.53), channel_id=1, source_target_pairs={{0,6},{1,7},{2,4},{3,5},{4,2},{5,3},{6,0},{7,1},{8,14},{9,15},{10,... | collective-permute-start | bytes 98312 | tf_op jit(solution)/shard_map/ppermute | solution.py:543

commit v6 on v5

--- a/solution.py
+++ b/solution.py
@@ -121,17 +121,65 @@
     return twice_gelu(mixed).astype(BF16)
 
 
+def lanes_from(x, count, offset):
+    shape = (x.shape[1], count)
+    move = (iota(shape, 1) == iota(shape, 0) + offset).astype(BF16)
+    return jnp.dot(x, move, preferred_element_type=F32)
+
+
+def bias_column(row):
+    shape = (2 * HID, HID)
+    own = iota(shape, 1) == iota(shape, 0) % HID
+    return jnp.sum(jnp.where(own, row, 0.0), axis=1, keepdims=True)
+
+
+def lay_out_decoder(dec_ref, out_ref):
+    n = KS * CH * BLOCK
+    row = iota((n, n), 0)
+    source = row // 4 % BLOCK * (KS * CH) + row // (4 * BLOCK) * 4 + row % 4
+    move = (iota((n, n), 1) == source).astype(BF16)
+    dec = dec_ref[...].astype(F32)
+    none = jnp.zeros((KS * CH, HID), F32)
+
+    def column(pillar):
+        taps = [r - pillar + KS - 1 for r in range(BLOCK)]
+        return jnp.concatenate([dec[t] if 0 <= t < KS else none for t in taps], axis=0)
+
+    for i in range(BLOCK):
+        pair = jnp.concatenate([column(2 * i), column(2 * i + 1)], axis=1).astype(BF16)
+        wide = jnp.dot(move, pair, preferred_element_type=F32)
+        out_ref[:, 2 * i * HID : (2 * i + 2) * HID] = (0.5 * wide).astype(BF16)
+
+
 def inner_kernel(
-    lev_ref, conv_ref, cb_ref, mix_ref, mb_ref, cols_hbm, feat_ref, hi_ref, lo_ref, green_ref,
-    ext_ref, hot_ref, cols_ref, sems,
+    lev_hbm, table_hbm, cb_hbm, mix_hbm, mb_hbm, dec_hbm, cols_hbm,
+    feat_ref, hi_ref, lo_ref, green_ref, conv_ref, cb_ref, mixer_ref, mb_ref, dec_ref,
+    ext_ref, hot_ref, cols_ref, lev_ref, table_ref, cbr_ref, mix_ref, mbr_ref, raw_ref, sems,
 ):
     z = lax.axis_index("py")
+    small = [
+        pltpu.make_async_copy(lev_hbm, lev_ref, sems.at[Z]),
+        pltpu.make_async_copy(table_hbm, table_ref, sems.at[Z + 1]),
+        pltpu.make_async_copy(cb_hbm, cbr_ref, sems.at[Z + 2]),
+        pltpu.make_async_copy(mix_hbm, mix_ref, sems.at[Z + 3]),
+        pltpu.make_async_copy(mb_hbm, mbr_ref, sems.at[Z + 4]),
+        pltpu.make_async_copy(dec_hbm, raw_ref, sems.at[Z + 5]),
+    ]
     copies = [
         pltpu.make_async_copy(cols_hbm.at[z ^ REL_ORDER[g]], cols_ref.at[g], sems.at[g])
         for g in range(Z)
     ]
-    for copy in copies:
+    for copy in small + copies:
         copy.start()
+    for copy in small:
+        copy.wait()
+    conv_ref[:HID, :] = lanes_from(table_ref[...], WINDOW, 0).astype(BF16)
+    conv_ref[HID:, :] = lanes_from(table_ref[...], WINDOW, SLOT).astype(BF16)
+    mixer_ref[:HID, :] = (0.5 * lanes_from(mix_ref[...], 2 * HID, 0)).astype(BF16)
+    mixer_ref[HID:, :] = (0.5 * lanes_from(mix_ref[...], 2 * HID, HID)).astype(BF16)
+    cb_ref[...] = bias_column(cbr_ref[...])
+    mb_ref[...] = bias_column(mbr_ref[...])
+    lay_out_decoder(raw_ref, dec_ref)
     wide = COLS - 128
     lev = lev_ref[...].astype(F32)
     for b in range(3):
@@ -152,7 +200,7 @@
         at = (8 + 2 * i) * HID
         feat_ref[at : at + 2 * HID, 128:] = features(
             hot_ref[i * 2 * SLOT : i * 2 * SLOT + WINDOW, :],
-            conv_ref[...], conv_bias, mix_ref[...], mix_bias,
+            conv_ref[...], conv_bias, mixer_ref[...], mix_bias,
         )
     for copy in copies:
         copy.wait()
@@ -167,27 +215,40 @@
         green_ref[HALO * g : HALO * (g + 1), :] = edge[128 - HALO :, :]
 
 
-def inner(levels, conv_w, conv_b, mix_w, mix_b, green_cols):
+def inner(levels, table, conv_bias, mix, mix_bias, decoder, green_cols):
     wide = COLS - 128
     return pl.pallas_call(
         inner_kernel,
-        in_specs=[VMEM] * 5 + [HBM],
-        out_specs=[VMEM] * 4,
+        in_specs=[HBM] * 7,
+        out_specs=[VMEM] * 9,
         out_shape=[
             jax.ShapeDtypeStruct((PILLAR_ROWS * HID, COLS), BF16),
             jax.ShapeDtypeStruct((Z, 2 * V, COLS), BF16),
             jax.ShapeDtypeStruct((Z, 2 * V, COLS), BF16),
             jax.ShapeDtypeStruct((Z * HALO, 128), F32),
+            jax.ShapeDtypeStruct((2 * HID, WINDOW), BF16),
+            jax.ShapeDtypeStruct((2 * HID, 1), F32),
+            jax.ShapeDtypeStruct((2 * HID, 2 * HID), BF16),
+            jax.ShapeDtypeStruct((2 * HID, 1), F32),
+            jax.ShapeDtypeStruct((KS * CH * BLOCK, 2 * BLOCK * HID), BF16),
         ],
         scratch_shapes=[
             pltpu.VMEM((3, ROWS, wide), F32),
             pltpu.VMEM(((ROWS - 2) * SLOT, wide), BF16),
             pltpu.VMEM((Z, 2, V, COLS), F32),
-            pltpu.SemaphoreType.DMA((Z,)),
+            pltpu.VMEM((ROWS, COLS), jnp.int32),
+            pltpu.VMEM(table.shape, BF16),
+            pltpu.VMEM((1, HID), F32),
+            pltpu.VMEM((HID, HID), BF16),
+            pltpu.VMEM((1, HID), F32),
+            pltpu.VMEM(decoder.shape, BF16),
+            pltpu.SemaphoreType.DMA((Z + 6,)),
         ],
         compiler_params=params(16),
         name="inner",
-    )(levels, conv_w, conv_b, mix_w, mix_b, hbm(green_cols))
+    )(*map(hbm, (
+        levels, table, conv_bias.reshape(1, HID), mix, mix_bias.reshape(1, HID), decoder, green_cols,
+    )))
 
 
 def tile_windows(left, tile, first_y, ext_ref):
@@ -417,7 +478,9 @@
     green = jnp.concatenate([from_x_ref[:, COLS:], green], axis=0)
     n = ROWS + 8
     green = jnp.concatenate(split2(green), axis=0)
-    pick = (order_ref[...] == iota((U, U * 4), 0)).astype(BF16)
+    pick = (order_ref[...] == iota((U, U), 0)).astype(BF16)
+    copies = (iota((U, U * 4), 1) // 4 == iota((U, U * 4), 0)).astype(BF16)
+    pick = jnp.dot(pick, copies, preferred_element_type=F32).astype(BF16)
     row = iota((3 * PART, 2 * n), 0)
     source = (row % PART) // 4 + (8 - SHIFT) + jnp.where(row // PART == 1, n, 0)
     spread = (iota((3 * PART, 2 * n), 1) == source).astype(BF16)
@@ -482,32 +545,6 @@
     )(parts)
 
 
-def conv_weights(conv_table):
-    return jnp.concatenate(
-        [jnp.pad(conv_table, ((0, 0), (0, SLOT))), jnp.pad(conv_table, ((0, 0), (SLOT, 0)))], axis=0
-    )
-
-
-def mix_weights(mix_weight):
-    w = mix_weight * jnp.asarray(0.5, BF16)
-    return jnp.concatenate(
-        [jnp.pad(w, ((0, 0), (0, HID))), jnp.pad(w, ((0, 0), (HID, 0)))], axis=0
-    )
-
-
-def decoder_weights(decoder):
-    d = decoder * jnp.asarray(0.5, BF16)
-    d = d[::-1].reshape(KS, KS, 2, 4, HID).transpose(1, 2, 3, 0, 4)
-    rows = [
-        jnp.pad(d, ((0, 0), (0, 0), (0, 0), (r, BLOCK - 1 - r), (0, 0))) for r in range(BLOCK)
-    ]
-    return jnp.stack(rows, axis=2).reshape(KS * CH * BLOCK, 2 * BLOCK * HID)
-
-
-def bias_column(bias):
-    return jnp.concatenate([bias, bias])[:, None]
-
-
 def on_device(
     levels, conv_table, conv_bias, mix_weight, mix_bias, decoder, green_rows, green_cols, focal_order
 ):
@@ -516,20 +553,14 @@
     rows_t = jnp.swapaxes(green_rows, 2, 3)
     next_x = [(i, (i + 1) % count_px) for i in range(count_px)]
     next_y = [(i, (i + 1) % count_py) for i in range(count_py)]
-    conv_w = conv_weights(conv_table)
-    mix_w = mix_weights(mix_weight)
-    dec_w = decoder_weights(decoder)
-    conv_b = bias_column(conv_bias)
-    mix_b = bias_column(mix_bias)
-    order = jnp.broadcast_to(focal_order[:, None], (U, 4)).reshape(1, U * 4)
-    conv_w, conv_b, mix_w, mix_b, dec_w, order = lax.optimization_barrier(
-        (conv_w, conv_b, mix_w, mix_b, dec_w, order)
-    )
+    order = focal_order.reshape(1, U)
 
     to_x, to_y = pack(levels, rows_t)
     from_x = lax.ppermute(to_x, "px", next_x)
     from_y = lax.ppermute(to_y, "py", next_y)
-    feat, hi, lo, green = inner(levels, conv_w, conv_b, mix_w, mix_b, green_cols)
+    feat, hi, lo, green, conv_w, conv_b, mix_w, mix_b, dec_w = inner(
+        levels, conv_table, conv_bias, mix_weight, mix_bias, decoder, green_cols
+    )
     from_y, feat = lax.optimization_barrier((from_y, feat))
     nf, edge, feat = middle(levels, from_y, conv_w, conv_b, mix_w, mix_b, dec_w, feat)
     from_x, feat, nf, edge = lax.optimization_barrier((from_x, feat, nf, edge))

time: 55.9 us -> 51.2 us (0.916)
  other arithmetic: 3.44 us -> 0.01 us
  local copies, waits for them, and re-layouts: 2.24 us -> 0.02 us
  Pallas kernels: 12.6 us -> 13.9 us
    pallas_call x1, Pallas kernels: 3.78 us -> 4.97 us  [inner(): pl.pallas_call(inner_kernel, in_specs=[HBM] * 7, out_specs=[VMEM] * 9, ou...]
    concatenate x2 -> x0, other arithmetic: 1 us -> none  [the longest x1 0.92 us: conv_weights(): jnp.concatenate([jnp.pad(conv_table, ((0, 0), (0, SLOT))), jnp.pad(conv_t...]
    unnamed x4 -> x6, local copies, waits for them, and re-layouts: 0.84 us -> 0.02 us
    rev x1 -> x0, other arithmetic: 0.82 us -> none  [decoder_weights(): d = d[::-1].reshape(KS, KS, 2, 4, HID).transpose(1, 2, 3, 0, 4)]
    broadcast_in_dim x1 -> x0, other arithmetic: 0.81 us -> none  [bias_column(): return jnp.concatenate([bias, bias])[:, None]]
    broadcast_in_dim x1 -> x0, local copies, waits for them, and re-layouts: 0.73 us -> none  [on_device(): order = jnp.broadcast_to(focal_order[:, None], (U, 4)).reshape(1, U * 4)]
    mul x1 -> x0, other arithmetic: 0.72 us -> none  [mix_weights(): w = mix_weight * jnp.asarray(0.5, BF16)]
  transfers between devices with their start and end apart: 7 -> 7, of which waited for: 3 -> 3; matrix products, arithmetic and copies ran while one was open for 9% -> 0% of each run, Pallas kernels for 15% -> 19%
where the time goes in v6:
time: 51.2 us; the launch traced here: 51 us
  blocking collectives  19.9 us (39%)
  Pallas kernels  13.9 us (27%)
  starting transfers between devices  13 us (25%)
  waiting for transfers between devices  4.05 us (8%)
    all_to_all x1, blocking collectives, on_device(): return total(lax.all_to_all(share, 'px', 0, 0))  19.9 us
    ppermute x1, starting transfers between devices, on_device(): from_x = lax.ppermute(to_x, 'px', next_x)  7.27 us
    pallas_call x1, Pallas kernels, inner(): pl.pallas_call(inner_kernel, in_specs=[HBM] * 7, out_specs=[VMEM] * 9, ou...  4.97 us
    ppermute x4, starting transfers between devices, swap(): return lax.ppermute(x, 'py', [(i, i ^ mask) for i in range(count_py)])  4.56 us
    pallas_call x1, Pallas kernels, field(): pl.pallas_call(field_kernel, in_specs=[VMEM] * 14, out_specs=[VMEM] * 4,...  2.14 us
    ppermute x1, waiting for transfers between devices, on_device(): from_d = lax.ppermute(relay(from_x, green), 'py', next_y)  2.12 us
    ppermute x4, waiting for transfers between devices, swap(): return lax.ppermute(x, 'py', [(i, i ^ mask) for i in range(count_py)])  1.92 us
    pallas_call x1, Pallas kernels, outer(): pl.pallas_call(outer_kernel, in_specs=[VMEM] * 7, out_specs=VMEM, out_sha...  1.75 us
  transfers between devices with their start and end apart: 7, of which 3 were waited for; matrix products, arithmetic and copies ran while one was open for 0% of the time, Pallas kernels for 19%

profile of v6, /device:TPU:2, one launch (start us, length us, event | category | flops | bytes accessed | tf_op | source)
XLA Modules:
  0.0 51.0 jit_solution(16070651471545154265)
XLA Ops:
  0.0 0.0 copy-start
  0.0 0.9 %pack.1 = (f32[8,1152]{1,0:T(8,128)S(1)}, f32[16,128]{1,0:T(8,128)S(1)}) custom-call(s32[16,1024]{1,0:T(8,128)} %lev_ref.5, f32[8,2,16,64]{3,2,1,0:T(8,128)} %bitcast.10), custom_call_target="tpu_custom_call" | custom-call | tf_op jit(solution)/shard_map/pack/pallas_call | solution.py:77
  0.9 7.3 %collective-permute-start = (f32[8,1152]{1,0:T(8,128)S(1)}, f32[8,1152]{1,0:T(8,128)S(1)}, u32[]{:S(2)}, u32[]{:S(2)}) collective-permute-start(f32[8,1152]{1,0:T(8,128)S(1)} %get-tuple-element.28), channel_id=1, source_target_pairs={{0,8},{8,16},{16,24},{24,32},{32,40},{40,48},{48,56},{56,64},{64,7... | collective-permute-start | bytes 110600 | tf_op jit(solution)/shard_map/ppermute | solution.py:559
  8.2 0.0 collective-permute-start.1
  8.2 5.0 %inner.1 = (bf16[1280,1024]{1,0:T(8,128)(2,1)S(1)}, bf16[8,128,1024]{2,1,0:T(8,128)(2,1)S(1)}, bf16[8,128,1024]{2,1,0:T(8,128)(2,1)S(1)}, f32[32,128]{1,0:T(8,12...) custom-call(s32[16,1024]{1,0:T(8,128)} %lev_ref.5, ...), custom_call_target="tpu_custom_call" | custom-call | tf_op jit(solution)/shard_map/inner/pallas_call | solution.py:220
  13.2 0.0 collective-permute-done.1.from_y_ref
  13.2 0.0 copy-done
  13.2 1.1 %middle.1 = (bf16[256,1024]{1,0:T(8,128)(2,1)S(1)}, f32[128,128]{1,0:T(8,128)S(1)}, bf16[1280,1024]{1,0:T(8,128)(2,1)S(1)}) custom-call(s32[16,1024]{1,0:T(8,128)S(1)} %copy-done, f32[16,128]{1,0:T(8,128)S(1)} %collective-permute-done.1.from_y_ref, bf16[128,192]{1,0:T(8,128)(2,1)S(1)} %get-tuple-element.32.conv_ref, ...), custom_call_target="tpu_custom_call", output_to_operand_aliasing={{2}: (7, {})} | custom-call | tf_op jit(solution)/shard_map/middle/pallas_call | solution.py:313
  14.4 0.0 collective-permute-done.from_x_ref
  14.4 1.2 %collective-permute-start.2 = (f32[40,128]{1,0:T(8,128)S(1)}, f32[40,128]{1,0:T(8,128)S(1)}, u32[]{:S(2)}, u32[]{:S(2)}) collective-permute-start(f32[40,128]{1,0:T(8,128)S(1)} %relay.1), channel_id=1, source_target_pairs={{0,1},{1,2},{2,3},{3,4},{4,5},{5,6},{6,7},{7,0},{8,9},{9,10},{10,1... | collective-permute-start | bytes 61448 | tf_op jit(solution)/shard_map/ppermute | solution.py:567
  15.6 1.7 %outer.1._feat = bf16[1280,1024]{1,0:T(8,128)(2,1)S(1)} custom-call(s32[16,1024]{1,0:T(8,128)S(1)} %copy-done, f32[8,1152]{1,0:T(8,128)S(1)} %collective-permute-done.from_x_ref, bf16[128,192]{1,0:T(8,128)(2,1)S(1)} %get-tuple-element.32.conv_ref, f32[128,1]{1,0:T(8,128)S(1)} %get-tuple-element.33.cb_ref, ...), custom_call_target="tpu_custom_call", output_to_operand_aliasing={{}: (6, {})} | custom-call | tf_op jit(solution)/shard_map/outer/pallas_call | solution.py:362
  17.3 2.1 %collective-permute-done.2.from_d_ref = f32[40,128]{1,0:T(8,128)S(1)} collective-permute-done((f32[40,128]{1,0:T(8,128)S(1)}, f32[40,128]{1,0:T(8,128)S(1)}, u32[]{:S(2)}, u32[]{:S(2)}) %collective-permute-start.2) | collective-permute-done | bytes 20512 | tf_op jit(solution)/shard_map/ppermute | solution.py:567
  19.5 2.1 %field.1 = (f32[4,64,128]{2,1,0:T(8,128)S(1)}, bf16[256,1024]{1,0:T(8,128)(2,1)S(1)}, f32[128,128]{1,0:T(8,128)S(1)}, bf16[1280,1024]{1,0:T(8,128)(2,1)S(1)}) custom-call(s32[16,1024]{1,0:T(8,128)S(1)} %copy-done, f32[8,1152]{1,0:T(8,128)S(1)} %collective-permute-done.from_x_ref, ...), custom_call_target="tpu_custom_call", output_to_operand_aliasing={{1}: (11, {}), {2}: (12, {}), {3}: (13, {})} | custom-call | tf_op jit(solution)/shard_map/field/pallas_call | solution.py:439
  21.6 0.0 copy-start.1
  21.6 0.0 copy-start.2
  21.6 0.1 collective-permute-start.3
  21.7 0.8 %keep_planes.3 = f32[3,64,128]{2,1,0:T(8,128)S(1)} custom-call(bf16[8,128,1024]{2,1,0:T(8,128)(2,1)S(1)} %get-tuple-element.42.hi_ref, bf16[8,128,1024]{2,1,0:T(8,128)(2,1)S(1)} %get-tuple-element.43.lo_ref, bf16[256,1024]{1,0:T(8,128)(2,1)S(1)} %get-tuple-element.48.nf_ref, f32[128,128]{1,0:T(8,128)S(1)} %get-tuple-element.49.edge_ref, ...), custom_call_target="tpu_custom_call" | custom-call | tf_op jit(solution)/shard_map/keep_planes/pallas_call | solution.py:465
  22.6 0.5 collective-permute-done.3.got_ref
  23.1 0.1 collective-permute-start.4
  23.2 1.2 %collective-permute-start.5 = (f32[64,128]{1,0:T(8,128)S(1)}, f32[64,128]{1,0:T(8,128)S(1)}, u32[]{:S(2)}, u32[]{:S(2)}) collective-permute-start(f32[64,128]{1,0:T(8,128)S(1)} %get-tuple-element.52), channel_id=1, source_target_pairs={{0,4},{1,5},{2,6},{3,7},{4,0},{5,1},{6,2},{7,3},{8,12},{9,13},{10,... | collective-permute-start | bytes 98312 | tf_op jit(solution)/shard_map/ppermute | solution.py:574
  24.4 3.1 %collective-permute-start.6 = (f32[64,128]{1,0:T(8,128)S(1)}, f32[64,128]{1,0:T(8,128)S(1)}, u32[]{:S(2)}, u32[]{:S(2)}) collective-permute-start(f32[64,128]{1,0:T(8,128)S(1)} %get-tuple-element.51), channel_id=1, source_target_pairs={{0,6},{1,7},{2,4},{3,5},{4,2},{5,3},{6,0},{7,1},{8,14},{9,15},{10,... | collective-permute-start | bytes 98312 | tf_op jit(solution)/shard_map/ppermute | solution.py:574
  27.6 0.0 copy-done.1
  27.6 0.0 copy-done.2
  27.6 0.6 %row_factors.1.factor_ref = bf16[512,192]{1,0:T(8,128)(2,1)S(1)} custom-call(f32[8,1152]{1,0:T(8,128)S(1)} %collective-permute-done.from_x_ref, f32[8,2,16,64]{3,2,1,0:T(8,128)S(1)} %bitcast.11, s32[1,64]{1,0:T(1,128)S(1)} %bitcast.12), custom_call_target="tpu_custom_call" | custom-call | tf_op jit(solution)/shard_map/row_factors/pallas_call | solution.py:495
  28.1 0.6 %keep_planes.2.keep_ref = f32[1,64,128]{2,1,0:T(8,128)S(1)} custom-call(bf16[8,128,1024]{2,1,0:T(8,128)(2,1)S(1)} %get-tuple-element.42.hi_ref, bf16[8,128,1024]{2,1,0:T(8,128)(2,1)S(1)} %get-tuple-element.43.lo_ref, bf16[256,1024]{1,0:T(8,128)(2,1)S(1)} %get-tuple-element.48.nf_ref, f32[128,128]{1,0:T(8,128)S(1)} %get-tuple-element.49.edge_ref, ...), custom_call_target="tpu_custom_call" | custom-call | tf_op jit(solution)/shard_map/keep_planes/pallas_call | solution.py:465
  28.7 0.0 collective-permute-done.4.b_ref
  28.7 0.0 collective-permute-done.5.c_ref
  28.7 1.4 %collective-permute-done.6.d_ref = f32[64,128]{1,0:T(8,128)S(1)} collective-permute-done((f32[64,128]{1,0:T(8,128)S(1)}, f32[64,128]{1,0:T(8,128)S(1)}, u32[]{:S(2)}, u32[]{:S(2)}) %collective-permute-start.6) | collective-permute-done | bytes 32800 | tf_op jit(solution)/shard_map/ppermute | solution.py:574
  30.2 0.3 focal_share.1
  30.4 19.9 %all_to_all.5.x_ref = f32[32,8,128]{2,1,0:T(8,128)S(1)} all-to-all(f32[32,8,128]{2,1,0:T(8,128)S(1)} %focal_share.1), channel_id=1, replica_groups=mesh['px'=32,'py'=8] {'px'}, dimensions={0} | all-to-all | bytes 262144 | tf_op jit(solution)/shard_map/all_to_all | solution.py:582
  50.3 0.7 %total.1 = f32[1,2,512]{2,1,0:T(2,128)} custom-call(f32[32,8,128]{2,1,0:T(8,128)S(1)} %all_to_all.5.x_ref), custom_call_target="tpu_custom_call" | custom-call | tf_op jit(solution)/shard_map/total/pallas_call | solution.py:538
  (2 shorter events, 0.0 us)
Async XLA Ops:
  0.0 13.2 %copy-start = (s32[16,1024]{1,0:T(8,128)S(1)}, s32[16,1024]{1,0:T(8,128)}, u32[]{:S(2)}) copy-start(s32[16,1024]{1,0:T(8,128)} %lev_ref.5) | copy-start | bytes 196612
  0.9 13.4 %collective-permute-start = (f32[8,1152]{1,0:T(8,128)S(1)}, f32[8,1152]{1,0:T(8,128)S(1)}, u32[]{:S(2)}, u32[]{:S(2)}) collective-permute-start(f32[8,1152]{1,0:T(8,128)S(1)} %get-tuple-element.28), channel_id=1, source_target_pairs={{0,8},{8,16},{16,24},{24,32},{32,40},{40,48},{48,56},{56,64},{64,7... | collective-permute-start | bytes 110600 | tf_op jit(solution)/shard_map/ppermute | solution.py:559
  8.2 5.0 %collective-permute-start.1 = (f32[16,128]{1,0:T(8,128)S(1)}, f32[16,128]{1,0:T(8,128)S(1)}, u32[]{:S(2)}, u32[]{:S(2)}) collective-permute-start(f32[16,128]{1,0:T(8,128)S(1)} %get-tuple-element.29), channel_id=1, source_target_pairs={{0,1},{1,2},{2,3},{3,4},{4,5},{5,6},{6,7},{7,0},{8,9},{9,10},{10,1... | collective-permute-start | bytes 24584 | tf_op jit(solution)/shard_map/ppermute | solution.py:560
  14.4 5.1 %collective-permute-start.2 = (f32[40,128]{1,0:T(8,128)S(1)}, f32[40,128]{1,0:T(8,128)S(1)}, u32[]{:S(2)}, u32[]{:S(2)}) collective-permute-start(f32[40,128]{1,0:T(8,128)S(1)} %relay.1), channel_id=1, source_target_pairs={{0,1},{1,2},{2,3},{3,4},{4,5},{5,6},{6,7},{7,0},{8,9},{9,10},{10,1... | collective-permute-start | bytes 61448 | tf_op jit(solution)/shard_map/ppermute | solution.py:567
  21.6 6.0 %copy-start.1 = (f32[8,2,64,16]{2,3,1,0:T(8,128)S(1)}, f32[8,2,64,16]{2,3,1,0:T(8,128)}, u32[]{:S(2)}) copy-start(f32[8,2,64,16]{2,3,1,0:T(8,128)} %param.15) | copy-start | bytes 196612
  21.6 5.9 %copy-start.2 = (s32[64]{0:T(128)S(1)}, s32[64]{0:T(128)}, u32[]{:S(2)}) copy-start(s32[64]{0:T(128)} %param.17) | copy-start | bytes 772
  21.6 1.4 %collective-permute-start.3 = (f32[4,64,128]{2,1,0:T(8,128)S(1)}, f32[4,64,128]{2,1,0:T(8,128)S(1)}, u32[]{:S(2)}, u32[]{:S(2)}) collective-permute-start(f32[4,64,128]{2,1,0:T(8,128)S(1)} %get-tuple-element.50), channel_id=1, source_target_pairs={{0,1},{1,0},{2,3},{3,2},{4,5},{5,4},{6,7},{7,6},{8,9},{9,8},{10,11... | collective-permute-start | bytes 393224 | tf_op jit(solution)/shard_map/ppermute | solution.py:574
  23.1 5.6 %collective-permute-start.4 = (f32[64,128]{1,0:T(8,128)S(1)}, f32[64,128]{1,0:T(8,128)S(1)}, u32[]{:S(2)}, u32[]{:S(2)}) collective-permute-start(f32[64,128]{1,0:T(8,128)S(1)} %get-tuple-element.53), channel_id=1, source_target_pairs={{0,2},{1,3},{2,0},{3,1},{4,6},{5,7},{6,4},{7,5},{8,10},{9,11},{10,... | collective-permute-start | bytes 98312 | tf_op jit(solution)/shard_map/ppermute | solution.py:574
  23.2 5.5 %collective-permute-start.5 = (f32[64,128]{1,0:T(8,128)S(1)}, f32[64,128]{1,0:T(8,128)S(1)}, u32[]{:S(2)}, u32[]{:S(2)}) collective-permute-start(f32[64,128]{1,0:T(8,128)S(1)} %get-tuple-element.52), channel_id=1, source_target_pairs={{0,4},{1,5},{2,6},{3,7},{4,0},{5,1},{6,2},{7,3},{8,12},{9,13},{10,... | collective-permute-start | bytes 98312 | tf_op jit(solution)/shard_map/ppermute | solution.py:574
  24.4 5.7 %collective-permute-start.6 = (f32[64,128]{1,0:T(8,128)S(1)}, f32[64,128]{1,0:T(8,128)S(1)}, u32[]{:S(2)}, u32[]{:S(2)}) collective-permute-start(f32[64,128]{1,0:T(8,128)S(1)} %get-tuple-element.51), channel_id=1, source_target_pairs={{0,6},{1,7},{2,4},{3,5},{4,2},{5,3},{6,0},{7,1},{8,14},{9,15},{10,... | collective-permute-start | bytes 98312 | tf_op jit(solution)/shard_map/ppermute | solution.py:574

commit v7 on v6

--- a/solution.py
+++ b/solution.py
@@ -57,36 +57,37 @@
     return pltpu.with_memory_space_constraint(x, pltpu.HBM)
 
 
-def pack_kernel(lev_hbm, rows_hbm, to_x_ref, to_y_ref, lev_ref, tile_ref, rows_ref, sems):
+def pack_kernel(lev_hbm, rows_hbm, to_x_ref, to_y_ref, out_ref, lev_ref, rows_ref, sems):
     z = lax.axis_index("py")
     copies = [
-        pltpu.make_async_copy(lev_hbm.at[pl.ds(8, 8), :], lev_ref, sems.at[0]),
-        pltpu.make_async_copy(lev_hbm.at[:, pl.ds(COLS - 128, 128)], tile_ref, sems.at[1]),
-        pltpu.make_async_copy(rows_hbm.at[z], rows_ref, sems.at[2]),
+        pltpu.make_async_copy(lev_hbm, lev_ref, sems.at[0]),
+        pltpu.make_async_copy(rows_hbm.at[z], rows_ref, sems.at[1]),
     ]
     for copy in copies:
         copy.start()
     for copy in copies:
         copy.wait()
-    to_x_ref[:, :COLS] = lev_ref[...].astype(F32)
+    lev = lev_ref[...].astype(F32)
+    out_ref[...] = lev
+    to_x_ref[:, :COLS] = lev[8:, :]
     to_x_ref[:, COLS:] = jnp.concatenate([rows_ref[0, 8:, :], rows_ref[1, 8:, :]], axis=1)
-    to_y_ref[...] = tile_ref[...].astype(F32)
+    to_y_ref[...] = lev[:, COLS - 128 :]
 
 
 def pack(levels, rows_t):
     return pl.pallas_call(
         pack_kernel,
         in_specs=[HBM] * 2,
-        out_specs=[VMEM] * 2,
+        out_specs=[VMEM] * 3,
         out_shape=[
             jax.ShapeDtypeStruct((8, COLS + 128), F32),
             jax.ShapeDtypeStruct((ROWS, 128), F32),
+            jax.ShapeDtypeStruct((ROWS, COLS), F32),
         ],
         scratch_shapes=[
-            pltpu.VMEM((8, COLS), jnp.int32),
-            pltpu.VMEM((ROWS, 128), jnp.int32),
+            pltpu.VMEM((ROWS, COLS), jnp.int32),
             pltpu.VMEM((2, ROWS, U), F32),
-            pltpu.SemaphoreType.DMA((3,)),
+            pltpu.SemaphoreType.DMA((2,)),
         ],
         compiler_params=params(4),
         name="pack",
@@ -152,18 +153,17 @@
 
 
 def inner_kernel(
-    lev_hbm, table_hbm, cb_hbm, mix_hbm, mb_hbm, dec_hbm, cols_hbm,
+    lev_ref, table_hbm, cb_hbm, mix_hbm, mb_hbm, dec_hbm, cols_hbm,
     feat_ref, hi_ref, lo_ref, green_ref, conv_ref, cb_ref, mixer_ref, mb_ref, dec_ref,
-    ext_ref, hot_ref, cols_ref, lev_ref, table_ref, cbr_ref, mix_ref, mbr_ref, raw_ref, sems,
+    ext_ref, hot_ref, cols_ref, table_ref, cbr_ref, mix_ref, mbr_ref, raw_ref, sems,
 ):
     z = lax.axis_index("py")
     small = [
-        pltpu.make_async_copy(lev_hbm, lev_ref, sems.at[Z]),
-        pltpu.make_async_copy(table_hbm, table_ref, sems.at[Z + 1]),
-        pltpu.make_async_copy(cb_hbm, cbr_ref, sems.at[Z + 2]),
-        pltpu.make_async_copy(mix_hbm, mix_ref, sems.at[Z + 3]),
-        pltpu.make_async_copy(mb_hbm, mbr_ref, sems.at[Z + 4]),
-        pltpu.make_async_copy(dec_hbm, raw_ref, sems.at[Z + 5]),
+        pltpu.make_async_copy(table_hbm, table_ref, sems.at[Z]),
+        pltpu.make_async_copy(cb_hbm, cbr_ref, sems.at[Z + 1]),
+        pltpu.make_async_copy(mix_hbm, mix_ref, sems.at[Z + 2]),
+        pltpu.make_async_copy(mb_hbm, mbr_ref, sems.at[Z + 3]),
+        pltpu.make_async_copy(dec_hbm, raw_ref, sems.at[Z + 4]),
     ]
     copies = [
         pltpu.make_async_copy(cols_hbm.at[z ^ REL_ORDER[g]], cols_ref.at[g], sems.at[g])
@@ -171,6 +171,20 @@
     ]
     for copy in small + copies:
         copy.start()
+    wide = COLS - 128
+    lev = lev_ref[...]
+    for b in range(3):
+        ext_ref[b] = pltpu.roll(lev, 3 - b, 1)[:, 128:]
+    level_ids = iota((LEVELS, wide), 0).astype(F32)
+
+    def make_hot(q, _):
+        for b in range(3):
+            hot_ref[pl.ds(q * SLOT + b * LEVELS, LEVELS), :] = one_hot(
+                ext_ref[b, pl.ds(q, 1), :], level_ids
+            )
+        return 0
+
+    lax.fori_loop(0, ROWS - 2, make_hot, 0, unroll=2)
     for copy in small:
         copy.wait()
     conv_ref[:HID, :] = lanes_from(table_ref[...], WINDOW, 0).astype(BF16)
@@ -180,20 +194,6 @@
     cb_ref[...] = bias_column(cbr_ref[...])
     mb_ref[...] = bias_column(mbr_ref[...])
     lay_out_decoder(raw_ref, dec_ref)
-    wide = COLS - 128
-    lev = lev_ref[...].astype(F32)
-    for b in range(3):
-        ext_ref[b] = pltpu.roll(lev, 3 - b, 1)[:, 128:]
-    level_ids = iota((LEVELS, wide), 0).astype(F32)
-
-    def make_hot(q, _):
-        for b in range(3):
-            hot_ref[pl.ds(q * SLOT + b * LEVELS, LEVELS), :] = one_hot(
-                ext_ref[b, pl.ds(q, 1), :], level_ids
-            )
-        return 0
-
-    lax.fori_loop(0, ROWS - 2, make_hot, 0, unroll=2)
     conv_bias = jnp.broadcast_to(cb_ref[...], (2 * HID, wide))
     mix_bias = jnp.broadcast_to(mb_ref[...], (2 * HID, wide))
     for i in range(ROWS // 2 - 2):
@@ -219,7 +219,7 @@
     wide = COLS - 128
     return pl.pallas_call(
         inner_kernel,
-        in_specs=[HBM] * 7,
+        in_specs=[VMEM] + [HBM] * 6,
         out_specs=[VMEM] * 9,
         out_shape=[
             jax.ShapeDtypeStruct((PILLAR_ROWS * HID, COLS), BF16),
@@ -236,18 +236,17 @@
             pltpu.VMEM((3, ROWS, wide), F32),
             pltpu.VMEM(((ROWS - 2) * SLOT, wide), BF16),
             pltpu.VMEM((Z, 2, V, COLS), F32),
-            pltpu.VMEM((ROWS, COLS), jnp.int32),
             pltpu.VMEM(table.shape, BF16),
             pltpu.VMEM((1, HID), F32),
             pltpu.VMEM((HID, HID), BF16),
             pltpu.VMEM((1, HID), F32),
             pltpu.VMEM(decoder.shape, BF16),
-            pltpu.SemaphoreType.DMA((Z + 6,)),
+            pltpu.SemaphoreType.DMA((Z + 5,)),
         ],
         compiler_params=params(16),
         name="inner",
-    )(*map(hbm, (
-        levels, table, conv_bias.reshape(1, HID), mix, mix_bias.reshape(1, HID), decoder, green_cols,
+    )(levels, *map(hbm, (
+        table, conv_bias.reshape(1, HID), mix, mix_bias.reshape(1, HID), decoder, green_cols,
     )))
 
 
@@ -292,7 +291,7 @@
     nf_ref, edge_ref, feat_ref, ext_ref, hot_ref,
 ):
     first_y = lax.axis_index("py") == 0
-    tile_windows(from_y_ref[...], lev_ref[:, :128].astype(F32), first_y, ext_ref)
+    tile_windows(from_y_ref[...], lev_ref[:, :128], first_y, ext_ref)
     level_ids = iota((LEVELS, 128), 0).astype(F32)
     for q in range(ROWS - 2):
         for b in range(3):
@@ -330,7 +329,7 @@
     lev_ref, from_x_ref, conv_ref, cb_ref, mix_ref, mb_ref, _, feat_ref, ext_ref, hot_ref
 ):
     first_x = lax.axis_index("px") == 0
-    ext = jnp.concatenate([from_x_ref[:, :COLS], lev_ref[:8, :].astype(F32)], axis=0)
+    ext = jnp.concatenate([from_x_ref[:, :COLS], lev_ref[:8, :]], axis=0)
     for b in range(3):
         ext_ref[b] = pltpu.roll(ext, 3 - b, 1)[:, 128:]
     wide = COLS - 128
@@ -384,13 +383,17 @@
     both = lax.dot_general(hi, nf_ref[...], NT, preferred_element_type=F32)
     both = both[:, :n] + both[:, n:]
     both = both + lax.dot_general(lo, nf_ref[:n, :], NT, preferred_element_type=F32)
+    greens = []
     for g in range(count):
-        out = both[2 * V * g : 2 * V * (g + 1)].T
         rel = (iy ^ REL_ORDER[first + g]) ^ before
         at = 8 + HALO * (rel // 2 + 4 * (rel % 2))
-        green = from_d_ref[pl.ds(at, HALO), :]
-        green = jnp.concatenate([green, jnp.zeros((4, 128), F32)], axis=0)
-        out = out + jnp.dot(edge_ref[:, :8], green, precision=HIGH, preferred_element_type=F32)
+        greens.append(from_d_ref[pl.ds(at, HALO), :])
+    green = jnp.concatenate(greens, axis=1)
+    green = jnp.concatenate([green, jnp.zeros((4, 2 * V * count), F32)], axis=0)
+    edge = jnp.dot(edge_ref[:, :8], green, precision=HIGH, preferred_element_type=F32)
+    for g in range(count):
+        at = 2 * V * g
+        out = both[at : at + 2 * V].T + edge[:, at : at + 2 * V]
         out_ref[g] = out[:PART] + sign * pltpu.roll(out[PART:], V, 1)
 
 
@@ -400,7 +403,7 @@
 ):
     first_x = lax.axis_index("px") == 0
     first_y = lax.axis_index("py") == 0
-    tile = jnp.concatenate([from_x_ref[:, :128], lev_ref[:8, :128].astype(F32)], axis=0)
+    tile = jnp.concatenate([from_x_ref[:, :128], lev_ref[:8, :128]], axis=0)
     left = jnp.concatenate([from_d_ref[:8, :], from_y_ref[:8, :]], axis=0)
     tile_windows(left, tile, first_y, ext_ref)
     level_ids = iota((LEVELS, 128), 0).astype(F32)
@@ -555,7 +558,7 @@
     next_y = [(i, (i + 1) % count_py) for i in range(count_py)]
     order = focal_order.reshape(1, U)
 
-    to_x, to_y = pack(levels, rows_t)
+    to_x, to_y, levels = pack(levels, rows_t)
     from_x = lax.ppermute(to_x, "px", next_x)
     from_y = lax.ppermute(to_y, "py", next_y)
     feat, hi, lo, green, conv_w, conv_b, mix_w, mix_b, dec_w = inner(

time: 51.2 us -> 51.2 us (level)
  waiting for transfers between devices: 4.05 us -> 4.67 us
  Pallas kernels: 13.9 us -> 13.3 us
    pallas_call x2, Pallas kernels: 5.9 us -> 5.32 us  [the longest x1 4.39 us: inner(): pl.pallas_call(inner_kernel, in_specs=[VMEM] + [HBM] * 6, out_specs=[VMEM...]
  transfers between devices with their start and end apart: 7 -> 7, of which waited for: 3 -> 4; matrix products, arithmetic and copies ran while one was open for 0% -> 0% of each run, Pallas kernels for 19% -> 18%
where the time goes in v7:
time: 51.2 us; the launch traced here: 51 us
  blocking collectives  20.3 us (40%)
  Pallas kernels  13.3 us (26%)
  starting transfers between devices  12.6 us (25%)
  waiting for transfers between devices  4.67 us (9%)
    all_to_all x1, blocking collectives, on_device(): return total(lax.all_to_all(share, 'px', 0, 0))  20.3 us
    ppermute x1, starting transfers between devices, on_device(): from_x = lax.ppermute(to_x, 'px', next_x)  7.27 us
    ppermute x4, starting transfers between devices, swap(): return lax.ppermute(x, 'py', [(i, i ^ mask) for i in range(count_py)])  4.56 us
    pallas_call x1, Pallas kernels, inner(): pl.pallas_call(inner_kernel, in_specs=[VMEM] + [HBM] * 6, out_specs=[VMEM...  4.39 us
    ppermute x1, waiting for transfers between devices, on_device(): from_d = lax.ppermute(relay(from_x, green), 'py', next_y)  2.58 us
    pallas_call x1, Pallas kernels, field(): pl.pallas_call(field_kernel, in_specs=[VMEM] * 14, out_specs=[VMEM] * 4,...  2.14 us
    pallas_call x1, Pallas kernels, outer(): pl.pallas_call(outer_kernel, in_specs=[VMEM] * 7, out_specs=VMEM, out_sha...  1.75 us
    ppermute x4, waiting for transfers between devices, swap(): return lax.ppermute(x, 'py', [(i, i ^ mask) for i in range(count_py)])  1.62 us
  transfers between devices with their start and end apart: 7, of which 4 were waited for; matrix products, arithmetic and copies ran while one was open for 0% of the time, Pallas kernels for 18%

profile of v7, /device:TPU:2, one launch (start us, length us, event | category | flops | bytes accessed | tf_op | source)
XLA Modules:
  0.0 51.0 jit_solution(14151764704492548439)
XLA Ops:
  0.0 0.9 %pack.1 = (f32[8,1152]{1,0:T(8,128)S(1)}, f32[16,128]{1,0:T(8,128)S(1)}, f32[16,1024]{1,0:T(8,128)S(1)}) custom-call(s32[16,1024]{1,0:T(8,128)} %lev_hbm.1, f32[8,2,16,64]{3,2,1,0:T(8,128)} %bitcast.10), custom_call_target="tpu_custom_call" | custom-call | tf_op jit(solution)/shard_map/pack/pallas_call | solution.py:78
  0.9 7.3 %collective-permute-start = (f32[8,1152]{1,0:T(8,128)S(1)}, f32[8,1152]{1,0:T(8,128)S(1)}, u32[]{:S(2)}, u32[]{:S(2)}) collective-permute-start(f32[8,1152]{1,0:T(8,128)S(1)} %get-tuple-element.29), channel_id=1, source_target_pairs={{0,8},{8,16},{16,24},{24,32},{32,40},{40,48},{48,56},{56,64},{64,7... | collective-permute-start | bytes 110600 | tf_op jit(solution)/shard_map/ppermute | solution.py:562
  8.2 0.0 collective-permute-start.1
  8.2 4.4 %inner.1 = (bf16[1280,1024]{1,0:T(8,128)(2,1)S(1)}, bf16[8,128,1024]{2,1,0:T(8,128)(2,1)S(1)}, bf16[8,128,1024]{2,1,0:T(8,128)(2,1)S(1)}, f32[32,128]{1,0:T(8,12...) custom-call(f32[16,1024]{1,0:T(8,128)S(1)} %get-tuple-element.30.lev, ...), custom_call_target="tpu_custom_call" | custom-call | tf_op jit(solution)/shard_map/inner/pallas_call | solution.py:220
  12.6 0.5 collective-permute-done.1.from_y_ref
  13.1 1.1 %middle.1 = (bf16[256,1024]{1,0:T(8,128)(2,1)S(1)}, f32[128,128]{1,0:T(8,128)S(1)}, bf16[1280,1024]{1,0:T(8,128)(2,1)S(1)}) custom-call(f32[16,1024]{1,0:T(8,128)S(1)} %get-tuple-element.30.lev_ref, f32[16,128]{1,0:T(8,128)S(1)} %collective-permute-done.1.from_y_ref, ...), custom_call_target="tpu_custom_call", output_to_operand_aliasing={{2}: (7, {})} | custom-call | tf_op jit(solution)/shard_map/middle/pallas_call | solution.py:312
  14.2 0.0 collective-permute-done.from_x_ref
  14.2 0.7 %collective-permute-start.2 = (f32[40,128]{1,0:T(8,128)S(1)}, f32[40,128]{1,0:T(8,128)S(1)}, u32[]{:S(2)}, u32[]{:S(2)}) collective-permute-start(f32[40,128]{1,0:T(8,128)S(1)} %relay.1), channel_id=1, source_target_pairs={{0,1},{1,2},{2,3},{3,4},{4,5},{5,6},{6,7},{7,0},{8,9},{9,10},{10,1... | collective-permute-start | bytes 61448 | tf_op jit(solution)/shard_map/ppermute | solution.py:570
  15.0 1.7 %outer.1._feat = bf16[1280,1024]{1,0:T(8,128)(2,1)S(1)} custom-call(f32[16,1024]{1,0:T(8,128)S(1)} %get-tuple-element.30.lev_ref, f32[8,1152]{1,0:T(8,128)S(1)} %collective-permute-done.from_x_ref, bf16[128,192]{1,0:T(8,128)(2,1)S(1)} %get-tuple-element.34.conv_ref, f32[128,1]{1,0:T(8,128)S(1)} %get-tuple-element.35.cb_ref, ...), custom_call_target="tpu_custom_call", output_to_operand_aliasing={{}: (6, {})} | custom-call | tf_op jit(solution)/shard_map/outer/pallas_call | solution.py:361
  16.8 2.6 %collective-permute-done.2.from_d_ref = f32[40,128]{1,0:T(8,128)S(1)} collective-permute-done((f32[40,128]{1,0:T(8,128)S(1)}, f32[40,128]{1,0:T(8,128)S(1)}, u32[]{:S(2)}, u32[]{:S(2)}) %collective-permute-start.2) | collective-permute-done | bytes 20512 | tf_op jit(solution)/shard_map/ppermute | solution.py:570
  19.3 2.1 %field.1 = (f32[4,64,128]{2,1,0:T(8,128)S(1)}, bf16[256,1024]{1,0:T(8,128)(2,1)S(1)}, f32[128,128]{1,0:T(8,128)S(1)}, bf16[1280,1024]{1,0:T(8,128)(2,1)S(1)}) custom-call(f32[16,1024]{1,0:T(8,128)S(1)} %get-tuple-element.30.lev_ref, f32[8,1152]{1,0:T(8,128)S(1)} %collective-permute-done.from_x_ref, ...), custom_call_target="tpu_custom_call", output_to_operand_aliasing={{1}: (11, {}), {2}: (12, {}), {3}: (13, {})} | custom-call | tf_op jit(solution)/shard_map/field/pallas_call | solution.py:442
  21.5 0.0 copy-start
  21.5 0.0 copy-start.1
  21.5 0.1 collective-permute-start.3
  21.6 0.8 %keep_planes.3 = f32[3,64,128]{2,1,0:T(8,128)S(1)} custom-call(bf16[8,128,1024]{2,1,0:T(8,128)(2,1)S(1)} %get-tuple-element.44.hi_ref, bf16[8,128,1024]{2,1,0:T(8,128)(2,1)S(1)} %get-tuple-element.45.lo_ref, bf16[256,1024]{1,0:T(8,128)(2,1)S(1)} %get-tuple-element.50.nf_ref, f32[128,128]{1,0:T(8,128)S(1)} %get-tuple-element.51.edge_ref, ...), custom_call_target="tpu_custom_call" | custom-call | tf_op jit(solution)/shard_map/keep_planes/pallas_call | solution.py:468
  22.4 0.5 collective-permute-done.3.got_ref
  23.0 0.1 collective-permute-start.4
  23.1 0.9 %collective-permute-start.5 = (f32[64,128]{1,0:T(8,128)S(1)}, f32[64,128]{1,0:T(8,128)S(1)}, u32[]{:S(2)}, u32[]{:S(2)}) collective-permute-start(f32[64,128]{1,0:T(8,128)S(1)} %get-tuple-element.54), channel_id=1, source_target_pairs={{0,4},{1,5},{2,6},{3,7},{4,0},{5,1},{6,2},{7,3},{8,12},{9,13},{10,... | collective-permute-start | bytes 98312 | tf_op jit(solution)/shard_map/ppermute | solution.py:577
  24.0 3.5 %collective-permute-start.6 = (f32[64,128]{1,0:T(8,128)S(1)}, f32[64,128]{1,0:T(8,128)S(1)}, u32[]{:S(2)}, u32[]{:S(2)}) collective-permute-start(f32[64,128]{1,0:T(8,128)S(1)} %get-tuple-element.53), channel_id=1, source_target_pairs={{0,6},{1,7},{2,4},{3,5},{4,2},{5,3},{6,0},{7,1},{8,14},{9,15},{10,... | collective-permute-start | bytes 98312 | tf_op jit(solution)/shard_map/ppermute | solution.py:577
  27.4 0.0 copy-done
  27.4 0.0 copy-done.1
  27.4 0.6 %row_factors.1.factor_ref = bf16[512,192]{1,0:T(8,128)(2,1)S(1)} custom-call(f32[8,1152]{1,0:T(8,128)S(1)} %collective-permute-done.from_x_ref, f32[8,2,16,64]{3,2,1,0:T(8,128)S(1)} %bitcast.11, s32[1,64]{1,0:T(1,128)S(1)} %bitcast.12), custom_call_target="tpu_custom_call" | custom-call | tf_op jit(solution)/shard_map/row_factors/pallas_call | solution.py:498
  28.0 0.6 %keep_planes.2.keep_ref = f32[1,64,128]{2,1,0:T(8,128)S(1)} custom-call(bf16[8,128,1024]{2,1,0:T(8,128)(2,1)S(1)} %get-tuple-element.44.hi_ref, bf16[8,128,1024]{2,1,0:T(8,128)(2,1)S(1)} %get-tuple-element.45.lo_ref, bf16[256,1024]{1,0:T(8,128)(2,1)S(1)} %get-tuple-element.50.nf_ref, f32[128,128]{1,0:T(8,128)S(1)} %get-tuple-element.51.edge_ref, ...), custom_call_target="tpu_custom_call" | custom-call | tf_op jit(solution)/shard_map/keep_planes/pallas_call | solution.py:468
  28.6 0.0 collective-permute-done.4.b_ref
  28.6 0.0 collective-permute-done.5.c_ref
  28.6 1.1 %collective-permute-done.6.d_ref = f32[64,128]{1,0:T(8,128)S(1)} collective-permute-done((f32[64,128]{1,0:T(8,128)S(1)}, f32[64,128]{1,0:T(8,128)S(1)}, u32[]{:S(2)}, u32[]{:S(2)}) %collective-permute-start.6) | collective-permute-done | bytes 32800 | tf_op jit(solution)/shard_map/ppermute | solution.py:577
  29.7 0.3 focal_share.1
  30.0 20.3 %all_to_all.5.x_ref = f32[32,8,128]{2,1,0:T(8,128)S(1)} all-to-all(f32[32,8,128]{2,1,0:T(8,128)S(1)} %focal_share.1), channel_id=1, replica_groups=mesh['px'=32,'py'=8] {'px'}, dimensions={0} | all-to-all | bytes 262144 | tf_op jit(solution)/shard_map/all_to_all | solution.py:585
  50.3 0.7 %total.1 = f32[1,2,512]{2,1,0:T(2,128)} custom-call(f32[32,8,128]{2,1,0:T(8,128)S(1)} %all_to_all.5.x_ref), custom_call_target="tpu_custom_call" | custom-call | tf_op jit(solution)/shard_map/total/pallas_call | solution.py:541
  (2 shorter events, 0.0 us)
Async XLA Ops:
  0.9 13.3 %collective-permute-start = (f32[8,1152]{1,0:T(8,128)S(1)}, f32[8,1152]{1,0:T(8,128)S(1)}, u32[]{:S(2)}, u32[]{:S(2)}) collective-permute-start(f32[8,1152]{1,0:T(8,128)S(1)} %get-tuple-element.29), channel_id=1, source_target_pairs={{0,8},{8,16},{16,24},{24,32},{32,40},{40,48},{48,56},{56,64},{64,7... | collective-permute-start | bytes 110600 | tf_op jit(solution)/shard_map/ppermute | solution.py:562
  8.2 4.9 %collective-permute-start.1 = (f32[16,128]{1,0:T(8,128)S(1)}, f32[16,128]{1,0:T(8,128)S(1)}, u32[]{:S(2)}, u32[]{:S(2)}) collective-permute-start(f32[16,128]{1,0:T(8,128)S(1)} %get-tuple-element.31), channel_id=1, source_target_pairs={{0,1},{1,2},{2,3},{3,4},{4,5},{5,6},{6,7},{7,0},{8,9},{9,10},{10,1... | collective-permute-start | bytes 24584 | tf_op jit(solution)/shard_map/ppermute | solution.py:563
  14.2 5.1 %collective-permute-start.2 = (f32[40,128]{1,0:T(8,128)S(1)}, f32[40,128]{1,0:T(8,128)S(1)}, u32[]{:S(2)}, u32[]{:S(2)}) collective-permute-start(f32[40,128]{1,0:T(8,128)S(1)} %relay.1), channel_id=1, source_target_pairs={{0,1},{1,2},{2,3},{3,4},{4,5},{5,6},{6,7},{7,0},{8,9},{9,10},{10,1... | collective-permute-start | bytes 61448 | tf_op jit(solution)/shard_map/ppermute | solution.py:570
  21.5 6.0 %copy-start = (f32[8,2,64,16]{2,3,1,0:T(8,128)S(1)}, f32[8,2,64,16]{2,3,1,0:T(8,128)}, u32[]{:S(2)}) copy-start(f32[8,2,64,16]{2,3,1,0:T(8,128)} %param.15) | copy-start | bytes 196612
  21.5 5.9 %copy-start.1 = (s32[64]{0:T(128)S(1)}, s32[64]{0:T(128)}, u32[]{:S(2)}) copy-start(s32[64]{0:T(128)} %param.17) | copy-start | bytes 772
  21.5 1.4 %collective-permute-start.3 = (f32[4,64,128]{2,1,0:T(8,128)S(1)}, f32[4,64,128]{2,1,0:T(8,128)S(1)}, u32[]{:S(2)}, u32[]{:S(2)}) collective-permute-start(f32[4,64,128]{2,1,0:T(8,128)S(1)} %get-tuple-element.52), channel_id=1, source_target_pairs={{0,1},{1,0},{2,3},{3,2},{4,5},{5,4},{6,7},{7,6},{8,9},{9,8},{10,11... | collective-permute-start | bytes 393224 | tf_op jit(solution)/shard_map/ppermute | solution.py:577
  23.0 5.6 %collective-permute-start.4 = (f32[64,128]{1,0:T(8,128)S(1)}, f32[64,128]{1,0:T(8,128)S(1)}, u32[]{:S(2)}, u32[]{:S(2)}) collective-permute-start(f32[64,128]{1,0:T(8,128)S(1)} %get-tuple-element.55), channel_id=1, source_target_pairs={{0,2},{1,3},{2,0},{3,1},{4,6},{5,7},{6,4},{7,5},{8,10},{9,11},{10,... | collective-permute-start | bytes 98312 | tf_op jit(solution)/shard_map/ppermute | solution.py:577
  23.1 5.5 %collective-permute-start.5 = (f32[64,128]{1,0:T(8,128)S(1)}, f32[64,128]{1,0:T(8,128)S(1)}, u32[]{:S(2)}, u32[]{:S(2)}) collective-permute-start(f32[64,128]{1,0:T(8,128)S(1)} %get-tuple-element.54), channel_id=1, source_target_pairs={{0,4},{1,5},{2,6},{3,7},{4,0},{5,1},{6,2},{7,3},{8,12},{9,13},{10,... | collective-permute-start | bytes 98312 | tf_op jit(solution)/shard_map/ppermute | solution.py:577
  24.0 5.8 %collective-permute-start.6 = (f32[64,128]{1,0:T(8,128)S(1)}, f32[64,128]{1,0:T(8,128)S(1)}, u32[]{:S(2)}, u32[]{:S(2)}) collective-permute-start(f32[64,128]{1,0:T(8,128)S(1)} %get-tuple-element.53), channel_id=1, source_target_pairs={{0,6},{1,7},{2,4},{3,5},{4,2},{5,3},{6,0},{7,1},{8,14},{9,15},{10,... | collective-permute-start | bytes 98312 | tf_op jit(solution)/shard_map/ppermute | solution.py:577

commit v8 on v7

--- a/solution.py
+++ b/solution.py
@@ -578,7 +578,7 @@
 
     got = swap(send, 1)
     keep = keep_planes(hi, lo, nf, edge, from_d, 1, 3)
-    b, c, d = (swap(keep[i - 1] + got[i], 2 * i) for i in (1, 2, 3))
+    b, c, d = (swap(keep[i - 1] + got[i], 2 * i) for i in (3, 2, 1))
     keep = keep_planes(hi, lo, nf, edge, from_d, 0, 1)
     factors = row_factors(from_x, rows_t, order)
     share = focal_share(factors, keep, got, b, c, d)

time: 51.2 us -> 52.5 us (1.025)
  the two profiles are of different devices: /device:TPU:2 before, /device:TPU:32 now
where the time goes in v8:
time: 52.5 us; the launch traced here: 52.4 us
  blocking collectives  21.4 us (41%)
  Pallas kernels  13.3 us (25%)
  starting transfers between devices  12.2 us (23%)
  waiting for transfers between devices  5.33 us (10%)
    all_to_all x1, blocking collectives, on_device(): return total(lax.all_to_all(share, 'px', 0, 0))  21.4 us
    ppermute x1, starting transfers between devices, on_device(): from_x = lax.ppermute(to_x, 'px', next_x)  6.37 us
    ppermute x4, starting transfers between devices, swap(): return lax.ppermute(x, 'py', [(i, i ^ mask) for i in range(count_py)])  5.63 us
    pallas_call x1, Pallas kernels, inner(): pl.pallas_call(inner_kernel, in_specs=[VMEM] + [HBM] * 6, out_specs=[VMEM...  4.39 us
    ppermute x4, waiting for transfers between devices, swap(): return lax.ppermute(x, 'py', [(i, i ^ mask) for i in range(count_py)])  3.06 us
    pallas_call x1, Pallas kernels, field(): pl.pallas_call(field_kernel, in_specs=[VMEM] * 14, out_specs=[VMEM] * 4,...  2.15 us
    pallas_call x1, Pallas kernels, outer(): pl.pallas_call(outer_kernel, in_specs=[VMEM] * 7, out_specs=VMEM, out_sha...  1.75 us
    pallas_call x2, Pallas kernels, keep_planes(): pl.pallas_call(keep_kernel, in_specs=[VMEM] * 5, out_specs=VMEM, out_shap...  1.39 us
  transfers between devices with their start and end apart: 7, of which 5 were waited for; matrix products, arithmetic and copies ran while one was open for 0% of the time, Pallas kernels for 18%

profile of v8, /device:TPU:32, one launch (start us, length us, event | category | flops | bytes accessed | tf_op | source)
XLA Modules:
  0.0 52.4 jit_solution(8277284747530417744)
XLA Ops:
  0.0 0.9 %pack.1 = (f32[8,1152]{1,0:T(8,128)S(1)}, f32[16,128]{1,0:T(8,128)S(1)}, f32[16,1024]{1,0:T(8,128)S(1)}) custom-call(s32[16,1024]{1,0:T(8,128)} %lev_hbm.1, f32[8,2,16,64]{3,2,1,0:T(8,128)} %bitcast.10), custom_call_target="tpu_custom_call" | custom-call | tf_op jit(solution)/shard_map/pack/pallas_call | solution.py:78
  0.9 6.4 %collective-permute-start = (f32[8,1152]{1,0:T(8,128)S(1)}, f32[8,1152]{1,0:T(8,128)S(1)}, u32[]{:S(2)}, u32[]{:S(2)}) collective-permute-start(f32[8,1152]{1,0:T(8,128)S(1)} %get-tuple-element.29), channel_id=1, source_target_pairs={{0,8},{8,16},{16,24},{24,32},{32,40},{40,48},{48,56},{56,64},{64,7... | collective-permute-start | bytes 110600 | tf_op jit(solution)/shard_map/ppermute | solution.py:562
  7.3 0.0 collective-permute-start.1
  7.3 4.4 %inner.1 = (bf16[1280,1024]{1,0:T(8,128)(2,1)S(1)}, bf16[8,128,1024]{2,1,0:T(8,128)(2,1)S(1)}, bf16[8,128,1024]{2,1,0:T(8,128)(2,1)S(1)}, f32[32,128]{1,0:T(8,12...) custom-call(f32[16,1024]{1,0:T(8,128)S(1)} %get-tuple-element.30.lev, ...), custom_call_target="tpu_custom_call" | custom-call | tf_op jit(solution)/shard_map/inner/pallas_call | solution.py:220
  11.7 0.0 collective-permute-done.1.from_y_ref
  11.7 1.1 %middle.1 = (bf16[256,1024]{1,0:T(8,128)(2,1)S(1)}, f32[128,128]{1,0:T(8,128)S(1)}, bf16[1280,1024]{1,0:T(8,128)(2,1)S(1)}) custom-call(f32[16,1024]{1,0:T(8,128)S(1)} %get-tuple-element.30.lev_ref, f32[16,128]{1,0:T(8,128)S(1)} %collective-permute-done.1.from_y_ref, ...), custom_call_target="tpu_custom_call", output_to_operand_aliasing={{2}: (7, {})} | custom-call | tf_op jit(solution)/shard_map/middle/pallas_call | solution.py:312
  12.9 1.0 %collective-permute-done.from_x_ref = f32[8,1152]{1,0:T(8,128)S(1)} collective-permute-done((f32[8,1152]{1,0:T(8,128)S(1)}, f32[8,1152]{1,0:T(8,128)S(1)}, u32[]{:S(2)}, u32[]{:S(2)}) %collective-permute-start) | collective-permute-done | bytes 36896 | tf_op jit(solution)/shard_map/ppermute | solution.py:562
  13.9 0.2 collective-permute-start.2
  14.1 1.7 %outer.1._feat = bf16[1280,1024]{1,0:T(8,128)(2,1)S(1)} custom-call(f32[16,1024]{1,0:T(8,128)S(1)} %get-tuple-element.30.lev_ref, f32[8,1152]{1,0:T(8,128)S(1)} %collective-permute-done.from_x_ref, bf16[128,192]{1,0:T(8,128)(2,1)S(1)} %get-tuple-element.34.conv_ref, f32[128,1]{1,0:T(8,128)S(1)} %get-tuple-element.35.cb_ref, ...), custom_call_target="tpu_custom_call", output_to_operand_aliasing={{}: (6, {})} | custom-call | tf_op jit(solution)/shard_map/outer/pallas_call | solution.py:361
  15.9 1.2 %collective-permute-done.2.from_d_ref = f32[40,128]{1,0:T(8,128)S(1)} collective-permute-done((f32[40,128]{1,0:T(8,128)S(1)}, f32[40,128]{1,0:T(8,128)S(1)}, u32[]{:S(2)}, u32[]{:S(2)}) %collective-permute-start.2) | collective-permute-done | bytes 20512 | tf_op jit(solution)/shard_map/ppermute | solution.py:570
  17.1 2.1 %field.1 = (f32[4,64,128]{2,1,0:T(8,128)S(1)}, bf16[256,1024]{1,0:T(8,128)(2,1)S(1)}, f32[128,128]{1,0:T(8,128)S(1)}, bf16[1280,1024]{1,0:T(8,128)(2,1)S(1)}) custom-call(f32[16,1024]{1,0:T(8,128)S(1)} %get-tuple-element.30.lev_ref, f32[8,1152]{1,0:T(8,128)S(1)} %collective-permute-done.from_x_ref, ...), custom_call_target="tpu_custom_call", output_to_operand_aliasing={{1}: (11, {}), {2}: (12, {}), {3}: (13, {})} | custom-call | tf_op jit(solution)/shard_map/field/pallas_call | solution.py:442
  19.3 0.0 copy-start
  19.3 0.0 copy-start.1
  19.3 0.3 collective-permute-start.3
  19.6 0.8 %keep_planes.3 = f32[3,64,128]{2,1,0:T(8,128)S(1)} custom-call(bf16[8,128,1024]{2,1,0:T(8,128)(2,1)S(1)} %get-tuple-element.44.hi_ref, bf16[8,128,1024]{2,1,0:T(8,128)(2,1)S(1)} %get-tuple-element.45.lo_ref, bf16[256,1024]{1,0:T(8,128)(2,1)S(1)} %get-tuple-element.50.nf_ref, f32[128,128]{1,0:T(8,128)S(1)} %get-tuple-element.51.edge_ref, ...), custom_call_target="tpu_custom_call" | custom-call | tf_op jit(solution)/shard_map/keep_planes/pallas_call | solution.py:468
  20.4 0.3 collective-permute-done.3.got_ref
  20.7 1.6 %collective-permute-start.4 = (f32[64,128]{1,0:T(8,128)S(1)}, f32[64,128]{1,0:T(8,128)S(1)}, u32[]{:S(2)}, u32[]{:S(2)}) collective-permute-start(f32[64,128]{1,0:T(8,128)S(1)} %get-tuple-element.55), channel_id=1, source_target_pairs={{0,6},{1,7},{2,4},{3,5},{4,2},{5,3},{6,0},{7,1},{8,14},{9,15},{10,... | collective-permute-start | bytes 98312 | tf_op jit(solution)/shard_map/ppermute | solution.py:577
  22.4 3.7 %collective-permute-start.5 = (f32[64,128]{1,0:T(8,128)S(1)}, f32[64,128]{1,0:T(8,128)S(1)}, u32[]{:S(2)}, u32[]{:S(2)}) collective-permute-start(f32[64,128]{1,0:T(8,128)S(1)} %get-tuple-element.54), channel_id=1, source_target_pairs={{0,4},{1,5},{2,6},{3,7},{4,0},{5,1},{6,2},{7,3},{8,12},{9,13},{10,... | collective-permute-start | bytes 98312 | tf_op jit(solution)/shard_map/ppermute | solution.py:577
  26.1 0.0 collective-permute-start.6
  26.1 0.0 copy-done
  26.1 0.0 copy-done.1
  26.1 0.6 %row_factors.1.factor_ref = bf16[512,192]{1,0:T(8,128)(2,1)S(1)} custom-call(f32[8,1152]{1,0:T(8,128)S(1)} %collective-permute-done.from_x_ref, f32[8,2,16,64]{3,2,1,0:T(8,128)S(1)} %bitcast.11, s32[1,64]{1,0:T(1,128)S(1)} %bitcast.12), custom_call_target="tpu_custom_call" | custom-call | tf_op jit(solution)/shard_map/row_factors/pallas_call | solution.py:498
  26.6 0.6 %keep_planes.2.keep_ref = f32[1,64,128]{2,1,0:T(8,128)S(1)} custom-call(bf16[8,128,1024]{2,1,0:T(8,128)(2,1)S(1)} %get-tuple-element.44.hi_ref, bf16[8,128,1024]{2,1,0:T(8,128)(2,1)S(1)} %get-tuple-element.45.lo_ref, bf16[256,1024]{1,0:T(8,128)(2,1)S(1)} %get-tuple-element.50.nf_ref, f32[128,128]{1,0:T(8,128)S(1)} %get-tuple-element.51.edge_ref, ...), custom_call_target="tpu_custom_call" | custom-call | tf_op jit(solution)/shard_map/keep_planes/pallas_call | solution.py:468
  27.2 0.0 collective-permute-done.4.b_ref
  27.2 1.4 %collective-permute-done.5.c_ref = f32[64,128]{1,0:T(8,128)S(1)} collective-permute-done((f32[64,128]{1,0:T(8,128)S(1)}, f32[64,128]{1,0:T(8,128)S(1)}, u32[]{:S(2)}, u32[]{:S(2)}) %collective-permute-start.5) | collective-permute-done | bytes 32800 | tf_op jit(solution)/shard_map/ppermute | solution.py:577
  28.7 1.3 %collective-permute-done.6.d_ref = f32[64,128]{1,0:T(8,128)S(1)} collective-permute-done((f32[64,128]{1,0:T(8,128)S(1)}, f32[64,128]{1,0:T(8,128)S(1)}, u32[]{:S(2)}, u32[]{:S(2)}) %collective-permute-start.6) | collective-permute-done | bytes 32800 | tf_op jit(solution)/shard_map/ppermute | solution.py:577
  30.0 0.3 focal_share.1
  30.3 21.4 %all_to_all.5.x_ref = f32[32,8,128]{2,1,0:T(8,128)S(1)} all-to-all(f32[32,8,128]{2,1,0:T(8,128)S(1)} %focal_share.1), channel_id=1, replica_groups=mesh['px'=32,'py'=8] {'px'}, dimensions={0} | all-to-all | bytes 262144 | tf_op jit(solution)/shard_map/all_to_all | solution.py:585
  51.7 0.7 %total.1 = f32[1,2,512]{2,1,0:T(2,128)} custom-call(f32[32,8,128]{2,1,0:T(8,128)S(1)} %all_to_all.5.x_ref), custom_call_target="tpu_custom_call" | custom-call | tf_op jit(solution)/shard_map/total/pallas_call | solution.py:541
  (2 shorter events, 0.0 us)
Async XLA Ops:
  0.9 13.0 %collective-permute-start = (f32[8,1152]{1,0:T(8,128)S(1)}, f32[8,1152]{1,0:T(8,128)S(1)}, u32[]{:S(2)}, u32[]{:S(2)}) collective-permute-start(f32[8,1152]{1,0:T(8,128)S(1)} %get-tuple-element.29), channel_id=1, source_target_pairs={{0,8},{8,16},{16,24},{24,32},{32,40},{40,48},{48,56},{56,64},{64,7... | collective-permute-start | bytes 110600 | tf_op jit(solution)/shard_map/ppermute | solution.py:562
  7.3 4.4 %collective-permute-start.1 = (f32[16,128]{1,0:T(8,128)S(1)}, f32[16,128]{1,0:T(8,128)S(1)}, u32[]{:S(2)}, u32[]{:S(2)}) collective-permute-start(f32[16,128]{1,0:T(8,128)S(1)} %get-tuple-element.31), channel_id=1, source_target_pairs={{0,1},{1,2},{2,3},{3,4},{4,5},{5,6},{6,7},{7,0},{8,9},{9,10},{10,1... | collective-permute-start | bytes 24584 | tf_op jit(solution)/shard_map/ppermute | solution.py:563
  13.9 3.2 %collective-permute-start.2 = (f32[40,128]{1,0:T(8,128)S(1)}, f32[40,128]{1,0:T(8,128)S(1)}, u32[]{:S(2)}, u32[]{:S(2)}) collective-permute-start(f32[40,128]{1,0:T(8,128)S(1)} %relay.1), channel_id=1, source_target_pairs={{0,1},{1,2},{2,3},{3,4},{4,5},{5,6},{6,7},{7,0},{8,9},{9,10},{10,1... | collective-permute-start | bytes 61448 | tf_op jit(solution)/shard_map/ppermute | solution.py:570
  19.3 6.8 %copy-start = (f32[8,2,64,16]{2,3,1,0:T(8,128)S(1)}, f32[8,2,64,16]{2,3,1,0:T(8,128)}, u32[]{:S(2)}) copy-start(f32[8,2,64,16]{2,3,1,0:T(8,128)} %param.15) | copy-start | bytes 196612
  19.3 6.8 %copy-start.1 = (s32[64]{0:T(128)S(1)}, s32[64]{0:T(128)}, u32[]{:S(2)}) copy-start(s32[64]{0:T(128)} %param.17) | copy-start | bytes 772
  19.3 1.4 %collective-permute-start.3 = (f32[4,64,128]{2,1,0:T(8,128)S(1)}, f32[4,64,128]{2,1,0:T(8,128)S(1)}, u32[]{:S(2)}, u32[]{:S(2)}) collective-permute-start(f32[4,64,128]{2,1,0:T(8,128)S(1)} %get-tuple-element.52), channel_id=1, source_target_pairs={{0,1},{1,0},{2,3},{3,2},{4,5},{5,4},{6,7},{7,6},{8,9},{9,8},{10,11... | collective-permute-start | bytes 393224 | tf_op jit(solution)/shard_map/ppermute | solution.py:577
  20.7 6.5 %collective-permute-start.4 = (f32[64,128]{1,0:T(8,128)S(1)}, f32[64,128]{1,0:T(8,128)S(1)}, u32[]{:S(2)}, u32[]{:S(2)}) collective-permute-start(f32[64,128]{1,0:T(8,128)S(1)} %get-tuple-element.55), channel_id=1, source_target_pairs={{0,6},{1,7},{2,4},{3,5},{4,2},{5,3},{6,0},{7,1},{8,14},{9,15},{10,... | collective-permute-start | bytes 98312 | tf_op jit(solution)/shard_map/ppermute | solution.py:577
  22.4 6.3 %collective-permute-start.5 = (f32[64,128]{1,0:T(8,128)S(1)}, f32[64,128]{1,0:T(8,128)S(1)}, u32[]{:S(2)}, u32[]{:S(2)}) collective-permute-start(f32[64,128]{1,0:T(8,128)S(1)} %get-tuple-element.54), channel_id=1, source_target_pairs={{0,4},{1,5},{2,6},{3,7},{4,0},{5,1},{6,2},{7,3},{8,12},{9,13},{10,... | collective-permute-start | bytes 98312 | tf_op jit(solution)/shard_map/ppermute | solution.py:577
  26.1 3.9 %collective-permute-start.6 = (f32[64,128]{1,0:T(8,128)S(1)}, f32[64,128]{1,0:T(8,128)S(1)}, u32[]{:S(2)}, u32[]{:S(2)}) collective-permute-start(f32[64,128]{1,0:T(8,128)S(1)} %get-tuple-element.53), channel_id=1, source_target_pairs={{0,2},{1,3},{2,0},{3,1},{4,6},{5,7},{6,4},{7,5},{8,10},{9,11},{10,... | collective-permute-start | bytes 98312 | tf_op jit(solution)/shard_map/ppermute | solution.py:577

commit v9 on v7

--- a/solution.py
+++ b/solution.py
@@ -287,8 +287,7 @@
 
 
 def middle_kernel(
-    lev_ref, from_y_ref, conv_ref, cb_ref, mix_ref, mb_ref, dec_ref, _,
-    nf_ref, edge_ref, feat_ref, ext_ref, hot_ref,
+    lev_ref, from_y_ref, conv_ref, cb_ref, mix_ref, mb_ref, _, feat_ref, ext_ref, hot_ref
 ):
     first_y = lax.axis_index("py") == 0
     tile_windows(from_y_ref[...], lev_ref[:, :128], first_y, ext_ref)
@@ -304,29 +303,24 @@
     for t in range(6):
         at = (8 + 2 * t) * HID
         feat_ref[at : at + 2 * HID, :128] = tiles[:, t * 128 : (t + 1) * 128]
-    for i in (2, 3):
-        near_field(i, dec_ref[...], feat_ref, nf_ref, edge_ref, first_y)
-
-
-def middle(levels, from_y, conv_w, conv_b, mix_w, mix_b, dec_w, feat):
+
+
+def middle(levels, from_y, conv_w, conv_b, mix_w, mix_b, feat):
     return pl.pallas_call(
         middle_kernel,
-        in_specs=[VMEM] * 8,
-        out_specs=[VMEM] * 3,
-        out_shape=[
-            jax.ShapeDtypeStruct((4 * PART, COLS), BF16),
-            jax.ShapeDtypeStruct((2 * PART, 128), F32),
-            jax.ShapeDtypeStruct(feat.shape, BF16),
-        ],
-        input_output_aliases={7: 2},
+        in_specs=[VMEM] * 7,
+        out_specs=VMEM,
+        out_shape=jax.ShapeDtypeStruct(feat.shape, BF16),
+        input_output_aliases={6: 0},
         scratch_shapes=[pltpu.VMEM((3, ROWS, 128), F32), pltpu.VMEM((WINDOW, 768), BF16)],
         compiler_params=params(8),
         name="middle",
-    )(levels, from_y, conv_w, conv_b, mix_w, mix_b, dec_w, feat)
+    )(levels, from_y, conv_w, conv_b, mix_w, mix_b, feat)
 
 
 def outer_kernel(
-    lev_ref, from_x_ref, conv_ref, cb_ref, mix_ref, mb_ref, _, feat_ref, ext_ref, hot_ref
+    lev_ref, from_x_ref, conv_ref, cb_ref, mix_ref, mb_ref, dec_ref, _,
+    nf_ref, edge_ref, feat_ref, ext_ref, hot_ref,
 ):
     first_x = lax.axis_index("px") == 0
     ext = jnp.concatenate([from_x_ref[:, :COLS], lev_ref[:8, :]], axis=0)
@@ -347,6 +341,8 @@
             hot_ref[2 * w * SLOT : 2 * w * SLOT + WINDOW, :],
             conv, conv_bias, mix_ref[...], mix_bias,
         )
+    for i in (2, 3):
+        near_field(i, dec_ref[...], feat_ref, nf_ref, edge_ref, lax.axis_index("py") == 0)
 
 
 def cut_conv(conv, first_x):
@@ -356,21 +352,25 @@
     return conv * keep.astype(BF16)
 
 
-def outer(levels, from_x, conv_w, conv_b, mix_w, mix_b, feat):
+def outer(levels, from_x, conv_w, conv_b, mix_w, mix_b, dec_w, feat):
     wide = COLS - 128
     return pl.pallas_call(
         outer_kernel,
-        in_specs=[VMEM] * 7,
-        out_specs=VMEM,
-        out_shape=jax.ShapeDtypeStruct(feat.shape, BF16),
-        input_output_aliases={6: 0},
+        in_specs=[VMEM] * 8,
+        out_specs=[VMEM] * 3,
+        out_shape=[
+            jax.ShapeDtypeStruct((4 * PART, COLS), BF16),
+            jax.ShapeDtypeStruct((2 * PART, 128), F32),
+            jax.ShapeDtypeStruct(feat.shape, BF16),
+        ],
+        input_output_aliases={7: 2},
         scratch_shapes=[
             pltpu.VMEM((3, 16, wide), F32),
             pltpu.VMEM((10 * SLOT, wide), BF16),
         ],
         compiler_params=params(8),
         name="outer",
-    )(levels, from_x, conv_w, conv_b, mix_w, mix_b, feat)
+    )(levels, from_x, conv_w, conv_b, mix_w, mix_b, dec_w, feat)
 
 
 def column_sum(hi_ref, lo_ref, nf_ref, edge_ref, from_d_ref, out_ref, first, count):
@@ -565,10 +565,10 @@
         levels, conv_table, conv_bias, mix_weight, mix_bias, decoder, green_cols
     )
     from_y, feat = lax.optimization_barrier((from_y, feat))
-    nf, edge, feat = middle(levels, from_y, conv_w, conv_b, mix_w, mix_b, dec_w, feat)
-    from_x, feat, nf, edge = lax.optimization_barrier((from_x, feat, nf, edge))
+    feat = middle(levels, from_y, conv_w, conv_b, mix_w, mix_b, feat)
+    from_x, feat = lax.optimization_barrier((from_x, feat))
     from_d = lax.ppermute(relay(from_x, green), "py", next_y)
-    feat = outer(levels, from_x, conv_w, conv_b, mix_w, mix_b, feat)
+    nf, edge, feat = outer(levels, from_x, conv_w, conv_b, mix_w, mix_b, dec_w, feat)
     send, nf, edge, _ = field(
         levels, from_x, from_y, from_d, conv_w, conv_b, mix_w, mix_b, dec_w, hi, lo, nf, edge, feat
     )

time: 51.2 us -> 51.6 us (level)
  blocking collectives: 20.3 us -> 20.9 us
    all_to_all x1, blocking collectives: 20.3 us -> 20.9 us  [on_device(): return total(lax.all_to_all(share, 'px', 0, 0))]
where the time goes in v9:
time: 51.6 us; the launch traced here: 51.5 us
  blocking collectives  20.9 us (41%)
  Pallas kernels  13.2 us (26%)
  starting transfers between devices  12.6 us (24%)
  waiting for transfers between devices  4.64 us (9%)
    all_to_all x1, blocking collectives, on_device(): return total(lax.all_to_all(share, 'px', 0, 0))  20.9 us
    ppermute x1, starting transfers between devices, on_device(): from_x = lax.ppermute(to_x, 'px', next_x)  7.27 us
    ppermute x4, starting transfers between devices, swap(): return lax.ppermute(x, 'py', [(i, i ^ mask) for i in range(count_py)])  4.56 us
    pallas_call x1, Pallas kernels, inner(): pl.pallas_call(inner_kernel, in_specs=[VMEM] + [HBM] * 6, out_specs=[VMEM...  4.39 us
    pallas_call x1, Pallas kernels, outer(): pl.pallas_call(outer_kernel, in_specs=[VMEM] * 8, out_specs=[VMEM] * 3, o...  2.22 us
    pallas_call x1, Pallas kernels, field(): pl.pallas_call(field_kernel, in_specs=[VMEM] * 14, out_specs=[VMEM] * 4,...  2.14 us
    ppermute x1, waiting for transfers between devices, on_device(): from_d = lax.ppermute(relay(from_x, green), 'py', next_y)  2.11 us
    ppermute x4, waiting for transfers between devices, swap(): return lax.ppermute(x, 'py', [(i, i ^ mask) for i in range(count_py)])  2.06 us
  transfers between devices with their start and end apart: 7, of which 4 were waited for; matrix products, arithmetic and copies ran while one was open for 0% of the time, Pallas kernels for 18%

profile of v9, /device:TPU:2, one launch (start us, length us, event | category | flops | bytes accessed | tf_op | source)
XLA Modules:
  0.0 51.5 jit_solution(16517973040666510356)
XLA Ops:
  0.0 0.9 %pack.1 = (f32[8,1152]{1,0:T(8,128)S(1)}, f32[16,128]{1,0:T(8,128)S(1)}, f32[16,1024]{1,0:T(8,128)S(1)}) custom-call(s32[16,1024]{1,0:T(8,128)} %lev_hbm.1, f32[8,2,16,64]{3,2,1,0:T(8,128)} %bitcast.10), custom_call_target="tpu_custom_call" | custom-call | tf_op jit(solution)/shard_map/pack/pallas_call | solution.py:78
  0.9 7.3 %collective-permute-start = (f32[8,1152]{1,0:T(8,128)S(1)}, f32[8,1152]{1,0:T(8,128)S(1)}, u32[]{:S(2)}, u32[]{:S(2)}) collective-permute-start(f32[8,1152]{1,0:T(8,128)S(1)} %get-tuple-element.27), channel_id=1, source_target_pairs={{0,8},{8,16},{16,24},{24,32},{32,40},{40,48},{48,56},{56,64},{64,7... | collective-permute-start | bytes 110600 | tf_op jit(solution)/shard_map/ppermute | solution.py:562
  8.2 0.0 collective-permute-start.1
  8.2 4.4 %inner.1 = (bf16[1280,1024]{1,0:T(8,128)(2,1)S(1)}, bf16[8,128,1024]{2,1,0:T(8,128)(2,1)S(1)}, bf16[8,128,1024]{2,1,0:T(8,128)(2,1)S(1)}, f32[32,128]{1,0:T(8,12...) custom-call(f32[16,1024]{1,0:T(8,128)S(1)} %get-tuple-element.28.lev, ...), custom_call_target="tpu_custom_call" | custom-call | tf_op jit(solution)/shard_map/inner/pallas_call | solution.py:220
  12.6 0.5 collective-permute-done.1.from_y_ref
  13.1 0.6 %middle.1._ = bf16[1280,1024]{1,0:T(8,128)(2,1)S(1)} custom-call(f32[16,1024]{1,0:T(8,128)S(1)} %get-tuple-element.28.lev_ref, f32[16,128]{1,0:T(8,128)S(1)} %collective-permute-done.1.from_y_ref, bf16[128,192]{1,0:T(8,128)(2,1)S(1)} %get-tuple-element.32.conv_ref, f32[128,1]{1,0:T(8,128)S(1)} %get-tuple-element.33.cb_ref, ...), custom_call_target="tpu_custom_call", output_to_operand_aliasing={{}: (6, {})} | custom-call | tf_op jit(solution)/shard_map/middle/pallas_call | solution.py:309
  13.7 0.0 collective-permute-done.from_x_ref
  13.7 0.7 %collective-permute-start.2 = (f32[40,128]{1,0:T(8,128)S(1)}, f32[40,128]{1,0:T(8,128)S(1)}, u32[]{:S(2)}, u32[]{:S(2)}) collective-permute-start(f32[40,128]{1,0:T(8,128)S(1)} %relay.1), channel_id=1, source_target_pairs={{0,1},{1,2},{2,3},{3,4},{4,5},{5,6},{6,7},{7,0},{8,9},{9,10},{10,1... | collective-permute-start | bytes 61448 | tf_op jit(solution)/shard_map/ppermute | solution.py:570
  14.5 2.2 %outer.1 = (bf16[256,1024]{1,0:T(8,128)(2,1)S(1)}, f32[128,128]{1,0:T(8,128)S(1)}, bf16[1280,1024]{1,0:T(8,128)(2,1)S(1)}) custom-call(f32[16,1024]{1,0:T(8,128)S(1)} %get-tuple-element.28.lev_ref, f32[8,1152]{1,0:T(8,128)S(1)} %collective-permute-done.from_x_ref, bf16[128,192]{1,0:T(8,128)(2,1)S(1)} %get-tuple-element.32.conv_ref, ...), custom_call_target="tpu_custom_call", output_to_operand_aliasing={{2}: (7, {})} | custom-call | tf_op jit(solution)/shard_map/outer/pallas_call | solution.py:357
  16.7 2.1 %collective-permute-done.2.from_d_ref = f32[40,128]{1,0:T(8,128)S(1)} collective-permute-done((f32[40,128]{1,0:T(8,128)S(1)}, f32[40,128]{1,0:T(8,128)S(1)}, u32[]{:S(2)}, u32[]{:S(2)}) %collective-permute-start.2) | collective-permute-done | bytes 20512 | tf_op jit(solution)/shard_map/ppermute | solution.py:570
  18.8 2.1 %field.1 = (f32[4,64,128]{2,1,0:T(8,128)S(1)}, bf16[256,1024]{1,0:T(8,128)(2,1)S(1)}, f32[128,128]{1,0:T(8,128)S(1)}, bf16[1280,1024]{1,0:T(8,128)(2,1)S(1)}) custom-call(f32[16,1024]{1,0:T(8,128)S(1)} %get-tuple-element.28.lev_ref, f32[8,1152]{1,0:T(8,128)S(1)} %collective-permute-done.from_x_ref, ...), custom_call_target="tpu_custom_call", output_to_operand_aliasing={{1}: (11, {}), {2}: (12, {}), {3}: (13, {})} | custom-call | tf_op jit(solution)/shard_map/field/pallas_call | solution.py:442
  20.9 0.0 copy-start
  21.0 0.0 copy-start.1
  21.0 0.1 collective-permute-start.3
  21.1 0.8 %keep_planes.3 = f32[3,64,128]{2,1,0:T(8,128)S(1)} custom-call(bf16[8,128,1024]{2,1,0:T(8,128)(2,1)S(1)} %get-tuple-element.38.hi_ref, bf16[8,128,1024]{2,1,0:T(8,128)(2,1)S(1)} %get-tuple-element.39.lo_ref, bf16[256,1024]{1,0:T(8,128)(2,1)S(1)} %get-tuple-element.46.nf_ref, f32[128,128]{1,0:T(8,128)S(1)} %get-tuple-element.47.edge_ref, ...), custom_call_target="tpu_custom_call" | custom-call | tf_op jit(solution)/shard_map/keep_planes/pallas_call | solution.py:468
  21.9 0.5 collective-permute-done.3.got_ref
  22.4 0.1 collective-permute-start.4
  22.5 1.4 %collective-permute-start.5 = (f32[64,128]{1,0:T(8,128)S(1)}, f32[64,128]{1,0:T(8,128)S(1)}, u32[]{:S(2)}, u32[]{:S(2)}) collective-permute-start(f32[64,128]{1,0:T(8,128)S(1)} %get-tuple-element.50), channel_id=1, source_target_pairs={{0,4},{1,5},{2,6},{3,7},{4,0},{5,1},{6,2},{7,3},{8,12},{9,13},{10,... | collective-permute-start | bytes 98312 | tf_op jit(solution)/shard_map/ppermute | solution.py:577
  23.9 3.0 %collective-permute-start.6 = (f32[64,128]{1,0:T(8,128)S(1)}, f32[64,128]{1,0:T(8,128)S(1)}, u32[]{:S(2)}, u32[]{:S(2)}) collective-permute-start(f32[64,128]{1,0:T(8,128)S(1)} %get-tuple-element.49), channel_id=1, source_target_pairs={{0,6},{1,7},{2,4},{3,5},{4,2},{5,3},{6,0},{7,1},{8,14},{9,15},{10,... | collective-permute-start | bytes 98312 | tf_op jit(solution)/shard_map/ppermute | solution.py:577
  26.9 0.0 copy-done
  26.9 0.0 copy-done.1
  26.9 0.6 %row_factors.1.factor_ref = bf16[512,192]{1,0:T(8,128)(2,1)S(1)} custom-call(f32[8,1152]{1,0:T(8,128)S(1)} %collective-permute-done.from_x_ref, f32[8,2,16,64]{3,2,1,0:T(8,128)S(1)} %bitcast.11, s32[1,64]{1,0:T(1,128)S(1)} %bitcast.12), custom_call_target="tpu_custom_call" | custom-call | tf_op jit(solution)/shard_map/row_factors/pallas_call | solution.py:498
  27.5 0.6 %keep_planes.2.keep_ref = f32[1,64,128]{2,1,0:T(8,128)S(1)} custom-call(bf16[8,128,1024]{2,1,0:T(8,128)(2,1)S(1)} %get-tuple-element.38.hi_ref, bf16[8,128,1024]{2,1,0:T(8,128)(2,1)S(1)} %get-tuple-element.39.lo_ref, bf16[256,1024]{1,0:T(8,128)(2,1)S(1)} %get-tuple-element.46.nf_ref, f32[128,128]{1,0:T(8,128)S(1)} %get-tuple-element.47.edge_ref, ...), custom_call_target="tpu_custom_call" | custom-call | tf_op jit(solution)/shard_map/keep_planes/pallas_call | solution.py:468
  28.0 0.0 collective-permute-done.4.b_ref
  28.1 0.0 collective-permute-done.5.c_ref
  28.1 1.5 %collective-permute-done.6.d_ref = f32[64,128]{1,0:T(8,128)S(1)} collective-permute-done((f32[64,128]{1,0:T(8,128)S(1)}, f32[64,128]{1,0:T(8,128)S(1)}, u32[]{:S(2)}, u32[]{:S(2)}) %collective-permute-start.6) | collective-permute-done | bytes 32800 | tf_op jit(solution)/shard_map/ppermute | solution.py:577
  29.6 0.3 focal_share.1
  29.9 20.9 %all_to_all.5.x_ref = f32[32,8,128]{2,1,0:T(8,128)S(1)} all-to-all(f32[32,8,128]{2,1,0:T(8,128)S(1)} %focal_share.1), channel_id=1, replica_groups=mesh['px'=32,'py'=8] {'px'}, dimensions={0} | all-to-all | bytes 262144 | tf_op jit(solution)/shard_map/all_to_all | solution.py:585
  50.8 0.7 %total.1 = f32[1,2,512]{2,1,0:T(2,128)} custom-call(f32[32,8,128]{2,1,0:T(8,128)S(1)} %all_to_all.5.x_ref), custom_call_target="tpu_custom_call" | custom-call | tf_op jit(solution)/shard_map/total/pallas_call | solution.py:541
  (2 shorter events, 0.0 us)
Async XLA Ops:
  0.9 12.8 %collective-permute-start = (f32[8,1152]{1,0:T(8,128)S(1)}, f32[8,1152]{1,0:T(8,128)S(1)}, u32[]{:S(2)}, u32[]{:S(2)}) collective-permute-start(f32[8,1152]{1,0:T(8,128)S(1)} %get-tuple-element.27), channel_id=1, source_target_pairs={{0,8},{8,16},{16,24},{24,32},{32,40},{40,48},{48,56},{56,64},{64,7... | collective-permute-start | bytes 110600 | tf_op jit(solution)/shard_map/ppermute | solution.py:562
  8.2 4.9 %collective-permute-start.1 = (f32[16,128]{1,0:T(8,128)S(1)}, f32[16,128]{1,0:T(8,128)S(1)}, u32[]{:S(2)}, u32[]{:S(2)}) collective-permute-start(f32[16,128]{1,0:T(8,128)S(1)} %get-tuple-element.29), channel_id=1, source_target_pairs={{0,1},{1,2},{2,3},{3,4},{4,5},{5,6},{6,7},{7,0},{8,9},{9,10},{10,1... | collective-permute-start | bytes 24584 | tf_op jit(solution)/shard_map/ppermute | solution.py:563
  13.7 5.1 %collective-permute-start.2 = (f32[40,128]{1,0:T(8,128)S(1)}, f32[40,128]{1,0:T(8,128)S(1)}, u32[]{:S(2)}, u32[]{:S(2)}) collective-permute-start(f32[40,128]{1,0:T(8,128)S(1)} %relay.1), channel_id=1, source_target_pairs={{0,1},{1,2},{2,3},{3,4},{4,5},{5,6},{6,7},{7,0},{8,9},{9,10},{10,1... | collective-permute-start | bytes 61448 | tf_op jit(solution)/shard_map/ppermute | solution.py:570
  20.9 6.0 %copy-start = (f32[8,2,64,16]{2,3,1,0:T(8,128)S(1)}, f32[8,2,64,16]{2,3,1,0:T(8,128)}, u32[]{:S(2)}) copy-start(f32[8,2,64,16]{2,3,1,0:T(8,128)} %param.15) | copy-start | bytes 196612
  21.0 5.9 %copy-start.1 = (s32[64]{0:T(128)S(1)}, s32[64]{0:T(128)}, u32[]{:S(2)}) copy-start(s32[64]{0:T(128)} %param.17) | copy-start | bytes 772
  21.0 1.4 %collective-permute-start.3 = (f32[4,64,128]{2,1,0:T(8,128)S(1)}, f32[4,64,128]{2,1,0:T(8,128)S(1)}, u32[]{:S(2)}, u32[]{:S(2)}) collective-permute-start(f32[4,64,128]{2,1,0:T(8,128)S(1)} %get-tuple-element.48), channel_id=1, source_target_pairs={{0,1},{1,0},{2,3},{3,2},{4,5},{5,4},{6,7},{7,6},{8,9},{9,8},{10,11... | collective-permute-start | bytes 393224 | tf_op jit(solution)/shard_map/ppermute | solution.py:577
  22.4 5.6 %collective-permute-start.4 = (f32[64,128]{1,0:T(8,128)S(1)}, f32[64,128]{1,0:T(8,128)S(1)}, u32[]{:S(2)}, u32[]{:S(2)}) collective-permute-start(f32[64,128]{1,0:T(8,128)S(1)} %get-tuple-element.51), channel_id=1, source_target_pairs={{0,2},{1,3},{2,0},{3,1},{4,6},{5,7},{6,4},{7,5},{8,10},{9,11},{10,... | collective-permute-start | bytes 98312 | tf_op jit(solution)/shard_map/ppermute | solution.py:577
  22.5 5.5 %collective-permute-start.5 = (f32[64,128]{1,0:T(8,128)S(1)}, f32[64,128]{1,0:T(8,128)S(1)}, u32[]{:S(2)}, u32[]{:S(2)}) collective-permute-start(f32[64,128]{1,0:T(8,128)S(1)} %get-tuple-element.50), channel_id=1, source_target_pairs={{0,4},{1,5},{2,6},{3,7},{4,0},{5,1},{6,2},{7,3},{8,12},{9,13},{10,... | collective-permute-start | bytes 98312 | tf_op jit(solution)/shard_map/ppermute | solution.py:577
  23.9 5.7 %collective-permute-start.6 = (f32[64,128]{1,0:T(8,128)S(1)}, f32[64,128]{1,0:T(8,128)S(1)}, u32[]{:S(2)}, u32[]{:S(2)}) collective-permute-start(f32[64,128]{1,0:T(8,128)S(1)} %get-tuple-element.49), channel_id=1, source_target_pairs={{0,6},{1,7},{2,4},{3,5},{4,2},{5,3},{6,0},{7,1},{8,14},{9,15},{10,... | collective-permute-start | bytes 98312 | tf_op jit(solution)/shard_map/ppermute | solution.py:577

commit v10 on v7

--- a/solution.py
+++ b/solution.py
@@ -117,6 +117,10 @@
 
 def features(window, conv, conv_bias, mix, mix_bias):
     pre = jnp.dot(conv, window, preferred_element_type=F32) + conv_bias
+    return activate(pre, mix, mix_bias)
+
+
+def activate(pre, mix, mix_bias):
     hidden = twice_gelu(pre).astype(BF16)
     mixed = jnp.dot(mix, hidden, preferred_element_type=F32) + mix_bias
     return twice_gelu(mixed).astype(BF16)
@@ -149,7 +153,7 @@
     for i in range(BLOCK):
         pair = jnp.concatenate([column(2 * i), column(2 * i + 1)], axis=1).astype(BF16)
         wide = jnp.dot(move, pair, preferred_element_type=F32)
-        out_ref[:, 2 * i * HID : (2 * i + 2) * HID] = (0.5 * wide).astype(BF16)
+        out_ref[2, :, 2 * i * HID : (2 * i + 2) * HID] = (0.5 * wide).astype(BF16)
 
 
 def inner_kernel(
@@ -187,20 +191,29 @@
     lax.fori_loop(0, ROWS - 2, make_hot, 0, unroll=2)
     for copy in small:
         copy.wait()
-    conv_ref[:HID, :] = lanes_from(table_ref[...], WINDOW, 0).astype(BF16)
-    conv_ref[HID:, :] = lanes_from(table_ref[...], WINDOW, SLOT).astype(BF16)
+    first_x = lax.axis_index("px") == 0
+    conv_ref[0, :HID, :] = lanes_from(table_ref[...], WINDOW, 0).astype(BF16)
+    conv_ref[0, HID:, :] = lanes_from(table_ref[...], WINDOW, SLOT).astype(BF16)
+    conv_ref[1] = cut_conv(conv_ref[0], first_x)
     mixer_ref[:HID, :] = (0.5 * lanes_from(mix_ref[...], 2 * HID, 0)).astype(BF16)
     mixer_ref[HID:, :] = (0.5 * lanes_from(mix_ref[...], 2 * HID, HID)).astype(BF16)
     cb_ref[...] = bias_column(cbr_ref[...])
     mb_ref[...] = bias_column(mbr_ref[...])
     lay_out_decoder(raw_ref, dec_ref)
+    shape = dec_ref.shape[1:]
+    sample = iota(shape, 0) // 4 % BLOCK - SHIFT
+    pillar = iota(shape, 1) // HID - SHIFT - 2
+    for i in range(2):
+        at = i * BLOCK
+        apart = (sample + at >= 0) != (pillar + at >= 0)
+        dec_ref[i] = dec_ref[2] * jnp.where(first_x & apart, 0.0, 1.0).astype(BF16)
     conv_bias = jnp.broadcast_to(cb_ref[...], (2 * HID, wide))
     mix_bias = jnp.broadcast_to(mb_ref[...], (2 * HID, wide))
     for i in range(ROWS // 2 - 2):
         at = (8 + 2 * i) * HID
         feat_ref[at : at + 2 * HID, 128:] = features(
             hot_ref[i * 2 * SLOT : i * 2 * SLOT + WINDOW, :],
-            conv_ref[...], conv_bias, mixer_ref[...], mix_bias,
+            conv_ref[0], conv_bias, mixer_ref[...], mix_bias,
         )
     for copy in copies:
         copy.wait()
@@ -226,11 +239,11 @@
             jax.ShapeDtypeStruct((Z, 2 * V, COLS), BF16),
             jax.ShapeDtypeStruct((Z, 2 * V, COLS), BF16),
             jax.ShapeDtypeStruct((Z * HALO, 128), F32),
-            jax.ShapeDtypeStruct((2 * HID, WINDOW), BF16),
+            jax.ShapeDtypeStruct((2, 2 * HID, WINDOW), BF16),
             jax.ShapeDtypeStruct((2 * HID, 1), F32),
             jax.ShapeDtypeStruct((2 * HID, 2 * HID), BF16),
             jax.ShapeDtypeStruct((2 * HID, 1), F32),
-            jax.ShapeDtypeStruct((KS * CH * BLOCK, 2 * BLOCK * HID), BF16),
+            jax.ShapeDtypeStruct((3, KS * CH * BLOCK, 2 * BLOCK * HID), BF16),
         ],
         scratch_shapes=[
             pltpu.VMEM((3, ROWS, wide), F32),
@@ -300,12 +313,12 @@
                 if 0 <= q - 2 * t < 4:
                     at = (q - 2 * t) * SLOT + b * LEVELS
                     hot_ref[at : at + LEVELS, t * 128 : (t + 1) * 128] = row
-    tiles = features(hot_ref[...], conv_ref[...], cb_ref[...], mix_ref[...], mb_ref[...])
+    tiles = features(hot_ref[...], conv_ref[0], cb_ref[...], mix_ref[...], mb_ref[...])
     for t in range(6):
         at = (8 + 2 * t) * HID
         feat_ref[at : at + 2 * HID, :128] = tiles[:, t * 128 : (t + 1) * 128]
     for i in (2, 3):
-        near_field(i, dec_ref[...], feat_ref, nf_ref, edge_ref, first_y)
+        near_field(i, dec_ref[2], feat_ref, nf_ref, edge_ref, first_y)
 
 
 def middle(levels, from_y, conv_w, conv_b, mix_w, mix_b, dec_w, feat):
@@ -328,7 +341,6 @@
 def outer_kernel(
     lev_ref, from_x_ref, conv_ref, cb_ref, mix_ref, mb_ref, _, feat_ref, ext_ref, hot_ref
 ):
-    first_x = lax.axis_index("px") == 0
     ext = jnp.concatenate([from_x_ref[:, :COLS], lev_ref[:8, :]], axis=0)
     for b in range(3):
         ext_ref[b] = pltpu.roll(ext, 3 - b, 1)[:, 128:]
@@ -342,10 +354,9 @@
     mix_bias = jnp.broadcast_to(mb_ref[...], (2 * HID, wide))
     for w in range(4):
         at = 2 * w * HID
-        conv = cut_conv(conv_ref[...], first_x) if w == 3 else conv_ref[...]
         feat_ref[at : at + 2 * HID, 128:] = features(
             hot_ref[2 * w * SLOT : 2 * w * SLOT + WINDOW, :],
-            conv, conv_bias, mix_ref[...], mix_bias,
+            conv_ref[w // 3], conv_bias, mix_ref[...], mix_bias,
         )
 
 
@@ -401,37 +412,28 @@
     lev_ref, from_x_ref, from_y_ref, from_d_ref, conv_ref, cb_ref, mix_ref, mb_ref, dec_ref,
     hi_ref, lo_ref, _nf, _edge, _feat, send_ref, nf_ref, edge_ref, feat_ref, ext_ref, hot_ref,
 ):
-    first_x = lax.axis_index("px") == 0
     first_y = lax.axis_index("py") == 0
     tile = jnp.concatenate([from_x_ref[:, :128], lev_ref[:8, :128]], axis=0)
     left = jnp.concatenate([from_d_ref[:8, :], from_y_ref[:8, :]], axis=0)
     tile_windows(left, tile, first_y, ext_ref)
     level_ids = iota((LEVELS, 128), 0).astype(F32)
+    for e in range(10):
+        for b in range(3):
+            row = one_hot(ext_ref[b, e : e + 1, :], level_ids)
+            for w in range(4):
+                if 0 <= e - 2 * w < 4:
+                    at = (e - 2 * w) * SLOT + b * LEVELS
+                    hot_ref[at : at + LEVELS, w * 128 : (w + 1) * 128] = row
+    pre = [
+        jnp.dot(conv_ref[0], hot_ref[:, :384], preferred_element_type=F32),
+        jnp.dot(conv_ref[1], hot_ref[:, 384:], preferred_element_type=F32),
+    ]
+    tiles = activate(jnp.concatenate(pre, axis=1) + cb_ref[...], mix_ref[...], mb_ref[...])
     for w in range(4):
-        for o in range(4):
-            for b in range(3):
-                e = 2 * w + o
-                at = o * SLOT + b * LEVELS
-                hot_ref[at : at + LEVELS, w * 128 : (w + 1) * 128] = one_hot(
-                    ext_ref[b, e : e + 1, :], level_ids
-                )
-    tiles = features(
-        hot_ref[:, :384], conv_ref[...], cb_ref[...], mix_ref[...], mb_ref[...]
-    )
-    for w in range(3):
         feat_ref[2 * w * HID : (2 * w + 2) * HID, :128] = tiles[:, w * 128 : (w + 1) * 128]
-    feat_ref[6 * HID : 8 * HID, :128] = features(
-        hot_ref[:, 384:], cut_conv(conv_ref[...], first_x), cb_ref[...], mix_ref[...], mb_ref[...]
-    )
-
-    shape = (KS * CH * BLOCK, 2 * BLOCK * HID)
-    sample = iota(shape, 0) // 4 % BLOCK - SHIFT
-    pillar = iota(shape, 1) // HID - SHIFT - 2
+
     for i in range(2):
-        at = i * BLOCK
-        apart = (sample + at >= 0) != (pillar + at >= 0)
-        keep = jnp.where(first_x & apart, 0.0, 1.0)
-        near_field(i, dec_ref[...] * keep.astype(BF16), feat_ref, nf_ref, edge_ref, first_y)
+        near_field(i, dec_ref[i], feat_ref, nf_ref, edge_ref, first_y)
 
     column_sum(hi_ref, lo_ref, nf_ref, edge_ref, from_d_ref, send_ref, 4, 4)
 

time: 51.2 us -> 51.1 us (level)
  no operation moved by 1% of the time
where the time goes in v10:
time: 51.1 us; the launch traced here: 50.9 us
  blocking collectives  20.3 us (40%)
  Pallas kernels  13.2 us (26%)
  starting transfers between devices  12.6 us (25%)
  waiting for transfers between devices  4.59 us (9%)
    all_to_all x1, blocking collectives, on_device(): return total(lax.all_to_all(share, 'px', 0, 0))  20.3 us
    ppermute x1, starting transfers between devices, on_device(): from_x = lax.ppermute(to_x, 'px', next_x)  7.27 us
    ppermute x4, starting transfers between devices, swap(): return lax.ppermute(x, 'py', [(i, i ^ mask) for i in range(count_py)])  4.56 us
    pallas_call x1, Pallas kernels, inner(): pl.pallas_call(inner_kernel, in_specs=[VMEM] + [HBM] * 6, out_specs=[VMEM...  4.42 us
    ppermute x1, waiting for transfers between devices, on_device(): from_d = lax.ppermute(relay(from_x, green), 'py', next_y)  2.54 us
    pallas_call x1, Pallas kernels, field(): pl.pallas_call(field_kernel, in_specs=[VMEM] * 14, out_specs=[VMEM] * 4,...  2.02 us
    pallas_call x1, Pallas kernels, outer(): pl.pallas_call(outer_kernel, in_specs=[VMEM] * 7, out_specs=VMEM, out_sha...  1.74 us
    ppermute x4, waiting for transfers between devices, swap(): return lax.ppermute(x, 'py', [(i, i ^ mask) for i in range(count_py)])  1.61 us
  transfers between devices with their start and end apart: 7, of which 4 were waited for; matrix products, arithmetic and copies ran while one was open for 0% of the time, Pallas kernels for 18%

profile of v10, /device:TPU:2, one launch (start us, length us, event | category | flops | bytes accessed | tf_op | source)
XLA Modules:
  0.0 50.9 jit_solution(18223924816623959829)
XLA Ops:
  0.0 0.9 %pack.1 = (f32[8,1152]{1,0:T(8,128)S(1)}, f32[16,128]{1,0:T(8,128)S(1)}, f32[16,1024]{1,0:T(8,128)S(1)}) custom-call(s32[16,1024]{1,0:T(8,128)} %lev_hbm.1, f32[8,2,16,64]{3,2,1,0:T(8,128)} %bitcast.10), custom_call_target="tpu_custom_call" | custom-call | tf_op jit(solution)/shard_map/pack/pallas_call | solution.py:78
  0.9 7.3 %collective-permute-start = (f32[8,1152]{1,0:T(8,128)S(1)}, f32[8,1152]{1,0:T(8,128)S(1)}, u32[]{:S(2)}, u32[]{:S(2)}) collective-permute-start(f32[8,1152]{1,0:T(8,128)S(1)} %get-tuple-element.29), channel_id=1, source_target_pairs={{0,8},{8,16},{16,24},{24,32},{32,40},{40,48},{48,56},{56,64},{64,7... | collective-permute-start | bytes 110600 | tf_op jit(solution)/shard_map/ppermute | solution.py:564
  8.2 0.0 collective-permute-start.1
  8.2 4.4 %inner.1 = (bf16[1280,1024]{1,0:T(8,128)(2,1)S(1)}, bf16[8,128,1024]{2,1,0:T(8,128)(2,1)S(1)}, bf16[8,128,1024]{2,1,0:T(8,128)(2,1)S(1)}, f32[32,128]{1,0:T(8,12...) custom-call(f32[16,1024]{1,0:T(8,128)S(1)} %get-tuple-element.30.lev, ...), custom_call_target="tpu_custom_call" | custom-call | tf_op jit(solution)/shard_map/inner/pallas_call | solution.py:233
  12.6 0.4 collective-permute-done.1.from_y_ref
  13.1 1.1 %middle.1 = (bf16[256,1024]{1,0:T(8,128)(2,1)S(1)}, f32[128,128]{1,0:T(8,128)S(1)}, bf16[1280,1024]{1,0:T(8,128)(2,1)S(1)}) custom-call(f32[16,1024]{1,0:T(8,128)S(1)} %get-tuple-element.30.lev_ref, f32[16,128]{1,0:T(8,128)S(1)} %collective-permute-done.1.from_y_ref, ...), custom_call_target="tpu_custom_call", output_to_operand_aliasing={{2}: (7, {})} | custom-call | tf_op jit(solution)/shard_map/middle/pallas_call | solution.py:325
  14.2 0.0 collective-permute-done.from_x_ref
  14.2 0.8 %collective-permute-start.2 = (f32[40,128]{1,0:T(8,128)S(1)}, f32[40,128]{1,0:T(8,128)S(1)}, u32[]{:S(2)}, u32[]{:S(2)}) collective-permute-start(f32[40,128]{1,0:T(8,128)S(1)} %relay.1), channel_id=1, source_target_pairs={{0,1},{1,2},{2,3},{3,4},{4,5},{5,6},{6,7},{7,0},{8,9},{9,10},{10,1... | collective-permute-start | bytes 61448 | tf_op jit(solution)/shard_map/ppermute | solution.py:572
  15.0 1.7 %outer.1._feat = bf16[1280,1024]{1,0:T(8,128)(2,1)S(1)} custom-call(f32[16,1024]{1,0:T(8,128)S(1)} %get-tuple-element.30.lev_ref, f32[8,1152]{1,0:T(8,128)S(1)} %collective-permute-done.from_x_ref, bf16[2,128,192]{2,1,0:T(8,128)(2,1)S(1)} %get-tuple-element.34.conv_ref, f32[128,1]{1,0:T(8,128)S(1)} %get-tuple-element.35.cb_ref, ...), custom_call_target="tpu_custom_call", output_to_operand_aliasing={{}: (6, {})} | custom-call | tf_op jit(solution)/shard_map/outer/pallas_call | solution.py:372
  16.8 2.5 %collective-permute-done.2.from_d_ref = f32[40,128]{1,0:T(8,128)S(1)} collective-permute-done((f32[40,128]{1,0:T(8,128)S(1)}, f32[40,128]{1,0:T(8,128)S(1)}, u32[]{:S(2)}, u32[]{:S(2)}) %collective-permute-start.2) | collective-permute-done | bytes 20512 | tf_op jit(solution)/shard_map/ppermute | solution.py:572
  19.3 2.0 %field.1 = (f32[4,64,128]{2,1,0:T(8,128)S(1)}, bf16[256,1024]{1,0:T(8,128)(2,1)S(1)}, f32[128,128]{1,0:T(8,128)S(1)}, bf16[1280,1024]{1,0:T(8,128)(2,1)S(1)}) custom-call(f32[16,1024]{1,0:T(8,128)S(1)} %get-tuple-element.30.lev_ref, f32[8,1152]{1,0:T(8,128)S(1)} %collective-permute-done.from_x_ref, ...), custom_call_target="tpu_custom_call", output_to_operand_aliasing={{1}: (11, {}), {2}: (12, {}), {3}: (13, {})} | custom-call | tf_op jit(solution)/shard_map/field/pallas_call | solution.py:444
  21.4 0.0 copy-start
  21.4 0.0 copy-start.1
  21.4 0.1 collective-permute-start.3
  21.5 0.8 %keep_planes.3 = f32[3,64,128]{2,1,0:T(8,128)S(1)} custom-call(bf16[8,128,1024]{2,1,0:T(8,128)(2,1)S(1)} %get-tuple-element.44.hi_ref, bf16[8,128,1024]{2,1,0:T(8,128)(2,1)S(1)} %get-tuple-element.45.lo_ref, bf16[256,1024]{1,0:T(8,128)(2,1)S(1)} %get-tuple-element.50.nf_ref, f32[128,128]{1,0:T(8,128)S(1)} %get-tuple-element.51.edge_ref, ...), custom_call_target="tpu_custom_call" | custom-call | tf_op jit(solution)/shard_map/keep_planes/pallas_call | solution.py:470
  22.3 0.5 collective-permute-done.3.got_ref
  22.8 0.1 collective-permute-start.4
  22.9 0.9 %collective-permute-start.5 = (f32[64,128]{1,0:T(8,128)S(1)}, f32[64,128]{1,0:T(8,128)S(1)}, u32[]{:S(2)}, u32[]{:S(2)}) collective-permute-start(f32[64,128]{1,0:T(8,128)S(1)} %get-tuple-element.54), channel_id=1, source_target_pairs={{0,4},{1,5},{2,6},{3,7},{4,0},{5,1},{6,2},{7,3},{8,12},{9,13},{10,... | collective-permute-start | bytes 98312 | tf_op jit(solution)/shard_map/ppermute | solution.py:579
  23.8 3.5 %collective-permute-start.6 = (f32[64,128]{1,0:T(8,128)S(1)}, f32[64,128]{1,0:T(8,128)S(1)}, u32[]{:S(2)}, u32[]{:S(2)}) collective-permute-start(f32[64,128]{1,0:T(8,128)S(1)} %get-tuple-element.53), channel_id=1, source_target_pairs={{0,6},{1,7},{2,4},{3,5},{4,2},{5,3},{6,0},{7,1},{8,14},{9,15},{10,... | collective-permute-start | bytes 98312 | tf_op jit(solution)/shard_map/ppermute | solution.py:579
  27.3 0.0 copy-done
  27.3 0.0 copy-done.1
  27.3 0.6 %row_factors.1.factor_ref = bf16[512,192]{1,0:T(8,128)(2,1)S(1)} custom-call(f32[8,1152]{1,0:T(8,128)S(1)} %collective-permute-done.from_x_ref, f32[8,2,16,64]{3,2,1,0:T(8,128)S(1)} %bitcast.11, s32[1,64]{1,0:T(1,128)S(1)} %bitcast.12), custom_call_target="tpu_custom_call" | custom-call | tf_op jit(solution)/shard_map/row_factors/pallas_call | solution.py:500
  27.9 0.6 %keep_planes.2.keep_ref = f32[1,64,128]{2,1,0:T(8,128)S(1)} custom-call(bf16[8,128,1024]{2,1,0:T(8,128)(2,1)S(1)} %get-tuple-element.44.hi_ref, bf16[8,128,1024]{2,1,0:T(8,128)(2,1)S(1)} %get-tuple-element.45.lo_ref, bf16[256,1024]{1,0:T(8,128)(2,1)S(1)} %get-tuple-element.50.nf_ref, f32[128,128]{1,0:T(8,128)S(1)} %get-tuple-element.51.edge_ref, ...), custom_call_target="tpu_custom_call" | custom-call | tf_op jit(solution)/shard_map/keep_planes/pallas_call | solution.py:470
  28.5 0.0 collective-permute-done.4.b_ref
  28.5 0.0 collective-permute-done.5.c_ref
  28.5 1.1 %collective-permute-done.6.d_ref = f32[64,128]{1,0:T(8,128)S(1)} collective-permute-done((f32[64,128]{1,0:T(8,128)S(1)}, f32[64,128]{1,0:T(8,128)S(1)}, u32[]{:S(2)}, u32[]{:S(2)}) %collective-permute-start.6) | collective-permute-done | bytes 32800 | tf_op jit(solution)/shard_map/ppermute | solution.py:579
  29.6 0.3 focal_share.1
  29.9 20.3 %all_to_all.5.x_ref = f32[32,8,128]{2,1,0:T(8,128)S(1)} all-to-all(f32[32,8,128]{2,1,0:T(8,128)S(1)} %focal_share.1), channel_id=1, replica_groups=mesh['px'=32,'py'=8] {'px'}, dimensions={0} | all-to-all | bytes 262144 | tf_op jit(solution)/shard_map/all_to_all | solution.py:587
  50.2 0.7 %total.1 = f32[1,2,512]{2,1,0:T(2,128)} custom-call(f32[32,8,128]{2,1,0:T(8,128)S(1)} %all_to_all.5.x_ref), custom_call_target="tpu_custom_call" | custom-call | tf_op jit(solution)/shard_map/total/pallas_call | solution.py:543
  (2 shorter events, 0.0 us)
Async XLA Ops:
  0.9 13.3 %collective-permute-start = (f32[8,1152]{1,0:T(8,128)S(1)}, f32[8,1152]{1,0:T(8,128)S(1)}, u32[]{:S(2)}, u32[]{:S(2)}) collective-permute-start(f32[8,1152]{1,0:T(8,128)S(1)} %get-tuple-element.29), channel_id=1, source_target_pairs={{0,8},{8,16},{16,24},{24,32},{32,40},{40,48},{48,56},{56,64},{64,7... | collective-permute-start | bytes 110600 | tf_op jit(solution)/shard_map/ppermute | solution.py:564
  8.2 4.9 %collective-permute-start.1 = (f32[16,128]{1,0:T(8,128)S(1)}, f32[16,128]{1,0:T(8,128)S(1)}, u32[]{:S(2)}, u32[]{:S(2)}) collective-permute-start(f32[16,128]{1,0:T(8,128)S(1)} %get-tuple-element.31), channel_id=1, source_target_pairs={{0,1},{1,2},{2,3},{3,4},{4,5},{5,6},{6,7},{7,0},{8,9},{9,10},{10,1... | collective-permute-start | bytes 24584 | tf_op jit(solution)/shard_map/ppermute | solution.py:565
  14.2 5.1 %collective-permute-start.2 = (f32[40,128]{1,0:T(8,128)S(1)}, f32[40,128]{1,0:T(8,128)S(1)}, u32[]{:S(2)}, u32[]{:S(2)}) collective-permute-start(f32[40,128]{1,0:T(8,128)S(1)} %relay.1), channel_id=1, source_target_pairs={{0,1},{1,2},{2,3},{3,4},{4,5},{5,6},{6,7},{7,0},{8,9},{9,10},{10,1... | collective-permute-start | bytes 61448 | tf_op jit(solution)/shard_map/ppermute | solution.py:572
  21.4 6.0 %copy-start = (f32[8,2,64,16]{2,3,1,0:T(8,128)S(1)}, f32[8,2,64,16]{2,3,1,0:T(8,128)}, u32[]{:S(2)}) copy-start(f32[8,2,64,16]{2,3,1,0:T(8,128)} %param.15) | copy-start | bytes 196612
  21.4 5.9 %copy-start.1 = (s32[64]{0:T(128)S(1)}, s32[64]{0:T(128)}, u32[]{:S(2)}) copy-start(s32[64]{0:T(128)} %param.17) | copy-start | bytes 772
  21.4 1.4 %collective-permute-start.3 = (f32[4,64,128]{2,1,0:T(8,128)S(1)}, f32[4,64,128]{2,1,0:T(8,128)S(1)}, u32[]{:S(2)}, u32[]{:S(2)}) collective-permute-start(f32[4,64,128]{2,1,0:T(8,128)S(1)} %get-tuple-element.52), channel_id=1, source_target_pairs={{0,1},{1,0},{2,3},{3,2},{4,5},{5,4},{6,7},{7,6},{8,9},{9,8},{10,11... | collective-permute-start | bytes 393224 | tf_op jit(solution)/shard_map/ppermute | solution.py:579
  22.8 5.6 %collective-permute-start.4 = (f32[64,128]{1,0:T(8,128)S(1)}, f32[64,128]{1,0:T(8,128)S(1)}, u32[]{:S(2)}, u32[]{:S(2)}) collective-permute-start(f32[64,128]{1,0:T(8,128)S(1)} %get-tuple-element.55), channel_id=1, source_target_pairs={{0,2},{1,3},{2,0},{3,1},{4,6},{5,7},{6,4},{7,5},{8,10},{9,11},{10,... | collective-permute-start | bytes 98312 | tf_op jit(solution)/shard_map/ppermute | solution.py:579
  22.9 5.5 %collective-permute-start.5 = (f32[64,128]{1,0:T(8,128)S(1)}, f32[64,128]{1,0:T(8,128)S(1)}, u32[]{:S(2)}, u32[]{:S(2)}) collective-permute-start(f32[64,128]{1,0:T(8,128)S(1)} %get-tuple-element.54), channel_id=1, source_target_pairs={{0,4},{1,5},{2,6},{3,7},{4,0},{5,1},{6,2},{7,3},{8,12},{9,13},{10,... | collective-permute-start | bytes 98312 | tf_op jit(solution)/shard_map/ppermute | solution.py:579
  23.8 5.8 %collective-permute-start.6 = (f32[64,128]{1,0:T(8,128)S(1)}, f32[64,128]{1,0:T(8,128)S(1)}, u32[]{:S(2)}, u32[]{:S(2)}) collective-permute-start(f32[64,128]{1,0:T(8,128)S(1)} %get-tuple-element.53), channel_id=1, source_target_pairs={{0,6},{1,7},{2,4},{3,5},{4,2},{5,3},{6,0},{7,1},{8,14},{9,15},{10,... | collective-permute-start | bytes 98312 | tf_op jit(solution)/shard_map/ppermute | solution.py:579

commit v11 on v10

--- a/solution.py
+++ b/solution.py
@@ -21,7 +21,7 @@
 U = 64
 V = 64
 HALO = 4
-SHIFT = 5
+SHIFT = 3
 PILLAR_ROWS = ROWS + KS - 1
 SLOT = 3 * LEVELS
 WINDOW = 4 * SLOT
@@ -188,7 +188,7 @@
             )
         return 0
 
-    lax.fori_loop(0, ROWS - 2, make_hot, 0, unroll=2)
+    lax.fori_loop(0, ROWS, make_hot, 0, unroll=2)
     for copy in small:
         copy.wait()
     first_x = lax.axis_index("px") == 0
@@ -209,8 +209,8 @@
         dec_ref[i] = dec_ref[2] * jnp.where(first_x & apart, 0.0, 1.0).astype(BF16)
     conv_bias = jnp.broadcast_to(cb_ref[...], (2 * HID, wide))
     mix_bias = jnp.broadcast_to(mb_ref[...], (2 * HID, wide))
-    for i in range(ROWS // 2 - 2):
-        at = (8 + 2 * i) * HID
+    for i in range(ROWS // 2 - 1):
+        at = (6 + 2 * i) * HID
         feat_ref[at : at + 2 * HID, 128:] = features(
             hot_ref[i * 2 * SLOT : i * 2 * SLOT + WINDOW, :],
             conv_ref[0], conv_bias, mixer_ref[...], mix_bias,
@@ -247,7 +247,7 @@
         ],
         scratch_shapes=[
             pltpu.VMEM((3, ROWS, wide), F32),
-            pltpu.VMEM(((ROWS - 2) * SLOT, wide), BF16),
+            pltpu.VMEM((ROWS * SLOT, wide), BF16),
             pltpu.VMEM((Z, 2, V, COLS), F32),
             pltpu.VMEM(table.shape, BF16),
             pltpu.VMEM((1, HID), F32),
@@ -306,16 +306,16 @@
     first_y = lax.axis_index("py") == 0
     tile_windows(from_y_ref[...], lev_ref[:, :128], first_y, ext_ref)
     level_ids = iota((LEVELS, 128), 0).astype(F32)
-    for q in range(ROWS - 2):
+    for q in range(ROWS):
         for b in range(3):
             row = one_hot(ext_ref[b, q : q + 1, :], level_ids)
-            for t in range(6):
+            for t in range(7):
                 if 0 <= q - 2 * t < 4:
                     at = (q - 2 * t) * SLOT + b * LEVELS
                     hot_ref[at : at + LEVELS, t * 128 : (t + 1) * 128] = row
     tiles = features(hot_ref[...], conv_ref[0], cb_ref[...], mix_ref[...], mb_ref[...])
-    for t in range(6):
-        at = (8 + 2 * t) * HID
+    for t in range(7):
+        at = (6 + 2 * t) * HID
         feat_ref[at : at + 2 * HID, :128] = tiles[:, t * 128 : (t + 1) * 128]
     for i in (2, 3):
         near_field(i, dec_ref[2], feat_ref, nf_ref, edge_ref, first_y)
@@ -332,7 +332,7 @@
             jax.ShapeDtypeStruct(feat.shape, BF16),
         ],
         input_output_aliases={7: 2},
-        scratch_shapes=[pltpu.VMEM((3, ROWS, 128), F32), pltpu.VMEM((WINDOW, 768), BF16)],
+        scratch_shapes=[pltpu.VMEM((3, ROWS, 128), F32), pltpu.VMEM((WINDOW, 896), BF16)],
         compiler_params=params(8),
         name="middle",
     )(levels, from_y, conv_w, conv_b, mix_w, mix_b, dec_w, feat)
@@ -346,17 +346,17 @@
         ext_ref[b] = pltpu.roll(ext, 3 - b, 1)[:, 128:]
     wide = COLS - 128
     level_ids = iota((LEVELS, wide), 0).astype(F32)
-    for e in range(10):
+    for e in range(2, 10):
         for b in range(3):
-            at = e * SLOT + b * LEVELS
+            at = (e - 2) * SLOT + b * LEVELS
             hot_ref[at : at + LEVELS, :] = one_hot(ext_ref[b, e : e + 1, :], level_ids)
     conv_bias = jnp.broadcast_to(cb_ref[...], (2 * HID, wide))
     mix_bias = jnp.broadcast_to(mb_ref[...], (2 * HID, wide))
-    for w in range(4):
+    for w in range(3):
         at = 2 * w * HID
         feat_ref[at : at + 2 * HID, 128:] = features(
             hot_ref[2 * w * SLOT : 2 * w * SLOT + WINDOW, :],
-            conv_ref[w // 3], conv_bias, mix_ref[...], mix_bias,
+            conv_ref[w // 2], conv_bias, mix_ref[...], mix_bias,
         )
 
 
@@ -377,7 +377,7 @@
         input_output_aliases={6: 0},
         scratch_shapes=[
             pltpu.VMEM((3, 16, wide), F32),
-            pltpu.VMEM((10 * SLOT, wide), BF16),
+            pltpu.VMEM((8 * SLOT, wide), BF16),
         ],
         compiler_params=params(8),
         name="outer",
@@ -417,19 +417,19 @@
     left = jnp.concatenate([from_d_ref[:8, :], from_y_ref[:8, :]], axis=0)
     tile_windows(left, tile, first_y, ext_ref)
     level_ids = iota((LEVELS, 128), 0).astype(F32)
-    for e in range(10):
+    for e in range(2, 10):
         for b in range(3):
             row = one_hot(ext_ref[b, e : e + 1, :], level_ids)
-            for w in range(4):
-                if 0 <= e - 2 * w < 4:
-                    at = (e - 2 * w) * SLOT + b * LEVELS
+            for w in range(3):
+                if 0 <= e - 2 - 2 * w < 4:
+                    at = (e - 2 - 2 * w) * SLOT + b * LEVELS
                     hot_ref[at : at + LEVELS, w * 128 : (w + 1) * 128] = row
     pre = [
-        jnp.dot(conv_ref[0], hot_ref[:, :384], preferred_element_type=F32),
-        jnp.dot(conv_ref[1], hot_ref[:, 384:], preferred_element_type=F32),
+        jnp.dot(conv_ref[0], hot_ref[:, :256], preferred_element_type=F32),
+        jnp.dot(conv_ref[1], hot_ref[:, 256:], preferred_element_type=F32),
     ]
     tiles = activate(jnp.concatenate(pre, axis=1) + cb_ref[...], mix_ref[...], mb_ref[...])
-    for w in range(4):
+    for w in range(3):
         feat_ref[2 * w * HID : (2 * w + 2) * HID, :128] = tiles[:, w * 128 : (w + 1) * 128]
 
     for i in range(2):
@@ -454,7 +454,7 @@
         input_output_aliases={11: 1, 12: 2, 13: 3},
         scratch_shapes=[
             pltpu.VMEM((3, 16, 128), F32),
-            pltpu.VMEM((WINDOW, 512), BF16),
+            pltpu.VMEM((WINDOW, 384), BF16),
         ],
         compiler_params=params(12),
         name="field",

time: 51.1 us -> 51.1 us (level)
  transfers between devices with their start and end apart: 7 -> 7, of which waited for: 4 -> 3; matrix products, arithmetic and copies ran while one was open for 0% -> 0% of each run, Pallas kernels for 18% -> 18%
where the time goes in v11:
time: 51.1 us; the launch traced here: 50.9 us
  blocking collectives  20.3 us (40%)
  Pallas kernels  13.3 us (26%)
  starting transfers between devices  13 us (25%)
  waiting for transfers between devices  4.15 us (8%)
    all_to_all x1, blocking collectives, on_device(): return total(lax.all_to_all(share, 'px', 0, 0))  20.3 us
    ppermute x1, starting transfers between devices, on_device(): from_x = lax.ppermute(to_x, 'px', next_x)  7.27 us
    pallas_call x1, Pallas kernels, inner(): pl.pallas_call(inner_kernel, in_specs=[VMEM] + [HBM] * 6, out_specs=[VMEM...  4.84 us
    ppermute x4, starting transfers between devices, swap(): return lax.ppermute(x, 'py', [(i, i ^ mask) for i in range(count_py)])  4.56 us
    ppermute x1, waiting for transfers between devices, on_device(): from_d = lax.ppermute(relay(from_x, green), 'py', next_y)  2.52 us
    pallas_call x1, Pallas kernels, field(): pl.pallas_call(field_kernel, in_specs=[VMEM] * 14, out_specs=[VMEM] * 4,...  2 us
    ppermute x4, waiting for transfers between devices, swap(): return lax.ppermute(x, 'py', [(i, i ^ mask) for i in range(count_py)])  1.62 us
    pallas_call x2, Pallas kernels, keep_planes(): pl.pallas_call(keep_kernel, in_specs=[VMEM] * 5, out_specs=VMEM, out_shap...  1.4 us
  transfers between devices with their start and end apart: 7, of which 3 were waited for; matrix products, arithmetic and copies ran while one was open for 0% of the time, Pallas kernels for 18%

profile of v11, /device:TPU:2, one launch (start us, length us, event | category | flops | bytes accessed | tf_op | source)
XLA Modules:
  0.0 50.9 jit_solution(9715034770934872380)
XLA Ops:
  0.0 0.9 %pack.1 = (f32[8,1152]{1,0:T(8,128)S(1)}, f32[16,128]{1,0:T(8,128)S(1)}, f32[16,1024]{1,0:T(8,128)S(1)}) custom-call(s32[16,1024]{1,0:T(8,128)} %lev_hbm.1, f32[8,2,16,64]{3,2,1,0:T(8,128)} %bitcast.10), custom_call_target="tpu_custom_call" | custom-call | tf_op jit(solution)/shard_map/pack/pallas_call | solution.py:78
  0.9 7.3 %collective-permute-start = (f32[8,1152]{1,0:T(8,128)S(1)}, f32[8,1152]{1,0:T(8,128)S(1)}, u32[]{:S(2)}, u32[]{:S(2)}) collective-permute-start(f32[8,1152]{1,0:T(8,128)S(1)} %get-tuple-element.29), channel_id=1, source_target_pairs={{0,8},{8,16},{16,24},{24,32},{32,40},{40,48},{48,56},{56,64},{64,7... | collective-permute-start | bytes 110600 | tf_op jit(solution)/shard_map/ppermute | solution.py:564
  8.2 0.0 collective-permute-start.1
  8.2 4.8 %inner.1 = (bf16[1280,1024]{1,0:T(8,128)(2,1)S(1)}, bf16[8,128,1024]{2,1,0:T(8,128)(2,1)S(1)}, bf16[8,128,1024]{2,1,0:T(8,128)(2,1)S(1)}, f32[32,128]{1,0:T(8,12...) custom-call(f32[16,1024]{1,0:T(8,128)S(1)} %get-tuple-element.30.lev, ...), custom_call_target="tpu_custom_call" | custom-call | tf_op jit(solution)/shard_map/inner/pallas_call | solution.py:233
  13.1 0.0 collective-permute-done.1.from_y_ref
  13.1 1.2 %middle.1 = (bf16[256,1024]{1,0:T(8,128)(2,1)S(1)}, f32[128,128]{1,0:T(8,128)S(1)}, bf16[1280,1024]{1,0:T(8,128)(2,1)S(1)}) custom-call(f32[16,1024]{1,0:T(8,128)S(1)} %get-tuple-element.30.lev_ref, f32[16,128]{1,0:T(8,128)S(1)} %collective-permute-done.1.from_y_ref, ...), custom_call_target="tpu_custom_call", output_to_operand_aliasing={{2}: (7, {})} | custom-call | tf_op jit(solution)/shard_map/middle/pallas_call | solution.py:325
  14.3 0.0 collective-permute-done.from_x_ref
  14.3 1.2 %collective-permute-start.2 = (f32[40,128]{1,0:T(8,128)S(1)}, f32[40,128]{1,0:T(8,128)S(1)}, u32[]{:S(2)}, u32[]{:S(2)}) collective-permute-start(f32[40,128]{1,0:T(8,128)S(1)} %relay.1), channel_id=1, source_target_pairs={{0,1},{1,2},{2,3},{3,4},{4,5},{5,6},{6,7},{7,0},{8,9},{9,10},{10,1... | collective-permute-start | bytes 61448 | tf_op jit(solution)/shard_map/ppermute | solution.py:572
  15.5 1.4 %outer.1._feat = bf16[1280,1024]{1,0:T(8,128)(2,1)S(1)} custom-call(f32[16,1024]{1,0:T(8,128)S(1)} %get-tuple-element.30.lev_ref, f32[8,1152]{1,0:T(8,128)S(1)} %collective-permute-done.from_x_ref, bf16[2,128,192]{2,1,0:T(8,128)(2,1)S(1)} %get-tuple-element.34.conv_ref, f32[128,1]{1,0:T(8,128)S(1)} %get-tuple-element.35.cb_ref, ...), custom_call_target="tpu_custom_call", output_to_operand_aliasing={{}: (6, {})} | custom-call | tf_op jit(solution)/shard_map/outer/pallas_call | solution.py:372
  16.9 2.5 %collective-permute-done.2.from_d_ref = f32[40,128]{1,0:T(8,128)S(1)} collective-permute-done((f32[40,128]{1,0:T(8,128)S(1)}, f32[40,128]{1,0:T(8,128)S(1)}, u32[]{:S(2)}, u32[]{:S(2)}) %collective-permute-start.2) | collective-permute-done | bytes 20512 | tf_op jit(solution)/shard_map/ppermute | solution.py:572
  19.4 2.0 %field.1 = (f32[4,64,128]{2,1,0:T(8,128)S(1)}, bf16[256,1024]{1,0:T(8,128)(2,1)S(1)}, f32[128,128]{1,0:T(8,128)S(1)}, bf16[1280,1024]{1,0:T(8,128)(2,1)S(1)}) custom-call(f32[16,1024]{1,0:T(8,128)S(1)} %get-tuple-element.30.lev_ref, f32[8,1152]{1,0:T(8,128)S(1)} %collective-permute-done.from_x_ref, ...), custom_call_target="tpu_custom_call", output_to_operand_aliasing={{1}: (11, {}), {2}: (12, {}), {3}: (13, {})} | custom-call | tf_op jit(solution)/shard_map/field/pallas_call | solution.py:444
  21.4 0.0 copy-start
  21.4 0.0 copy-start.1
  21.4 0.1 collective-permute-start.3
  21.5 0.8 %keep_planes.3 = f32[3,64,128]{2,1,0:T(8,128)S(1)} custom-call(bf16[8,128,1024]{2,1,0:T(8,128)(2,1)S(1)} %get-tuple-element.44.hi_ref, bf16[8,128,1024]{2,1,0:T(8,128)(2,1)S(1)} %get-tuple-element.45.lo_ref, bf16[256,1024]{1,0:T(8,128)(2,1)S(1)} %get-tuple-element.50.nf_ref, f32[128,128]{1,0:T(8,128)S(1)} %get-tuple-element.51.edge_ref, ...), custom_call_target="tpu_custom_call" | custom-call | tf_op jit(solution)/shard_map/keep_planes/pallas_call | solution.py:470
  22.4 0.5 collective-permute-done.3.got_ref
  22.9 0.1 collective-permute-start.4
  23.0 0.9 %collective-permute-start.5 = (f32[64,128]{1,0:T(8,128)S(1)}, f32[64,128]{1,0:T(8,128)S(1)}, u32[]{:S(2)}, u32[]{:S(2)}) collective-permute-start(f32[64,128]{1,0:T(8,128)S(1)} %get-tuple-element.54), channel_id=1, source_target_pairs={{0,4},{1,5},{2,6},{3,7},{4,0},{5,1},{6,2},{7,3},{8,12},{9,13},{10,... | collective-permute-start | bytes 98312 | tf_op jit(solution)/shard_map/ppermute | solution.py:579
  23.8 3.5 %collective-permute-start.6 = (f32[64,128]{1,0:T(8,128)S(1)}, f32[64,128]{1,0:T(8,128)S(1)}, u32[]{:S(2)}, u32[]{:S(2)}) collective-permute-start(f32[64,128]{1,0:T(8,128)S(1)} %get-tuple-element.53), channel_id=1, source_target_pairs={{0,6},{1,7},{2,4},{3,5},{4,2},{5,3},{6,0},{7,1},{8,14},{9,15},{10,... | collective-permute-start | bytes 98312 | tf_op jit(solution)/shard_map/ppermute | solution.py:579
  27.4 0.0 copy-done
  27.4 0.0 copy-done.1
  27.4 0.6 %row_factors.1.factor_ref = bf16[512,192]{1,0:T(8,128)(2,1)S(1)} custom-call(f32[8,1152]{1,0:T(8,128)S(1)} %collective-permute-done.from_x_ref, f32[8,2,16,64]{3,2,1,0:T(8,128)S(1)} %bitcast.11, s32[1,64]{1,0:T(1,128)S(1)} %bitcast.12), custom_call_target="tpu_custom_call" | custom-call | tf_op jit(solution)/shard_map/row_factors/pallas_call | solution.py:500
  27.9 0.6 %keep_planes.2.keep_ref = f32[1,64,128]{2,1,0:T(8,128)S(1)} custom-call(bf16[8,128,1024]{2,1,0:T(8,128)(2,1)S(1)} %get-tuple-element.44.hi_ref, bf16[8,128,1024]{2,1,0:T(8,128)(2,1)S(1)} %get-tuple-element.45.lo_ref, bf16[256,1024]{1,0:T(8,128)(2,1)S(1)} %get-tuple-element.50.nf_ref, f32[128,128]{1,0:T(8,128)S(1)} %get-tuple-element.51.edge_ref, ...), custom_call_target="tpu_custom_call" | custom-call | tf_op jit(solution)/shard_map/keep_planes/pallas_call | solution.py:470
  28.5 0.0 collective-permute-done.4.b_ref
  28.5 0.0 collective-permute-done.5.c_ref
  28.5 1.1 %collective-permute-done.6.d_ref = f32[64,128]{1,0:T(8,128)S(1)} collective-permute-done((f32[64,128]{1,0:T(8,128)S(1)}, f32[64,128]{1,0:T(8,128)S(1)}, u32[]{:S(2)}, u32[]{:S(2)}) %collective-permute-start.6) | collective-permute-done | bytes 32800 | tf_op jit(solution)/shard_map/ppermute | solution.py:579
  29.6 0.3 focal_share.1
  29.9 20.3 %all_to_all.5.x_ref = f32[32,8,128]{2,1,0:T(8,128)S(1)} all-to-all(f32[32,8,128]{2,1,0:T(8,128)S(1)} %focal_share.1), channel_id=1, replica_groups=mesh['px'=32,'py'=8] {'px'}, dimensions={0} | all-to-all | bytes 262144 | tf_op jit(solution)/shard_map/all_to_all | solution.py:587
  50.2 0.7 %total.1 = f32[1,2,512]{2,1,0:T(2,128)} custom-call(f32[32,8,128]{2,1,0:T(8,128)S(1)} %all_to_all.5.x_ref), custom_call_target="tpu_custom_call" | custom-call | tf_op jit(solution)/shard_map/total/pallas_call | solution.py:543
  (2 shorter events, 0.0 us)
Async XLA Ops:
  0.9 13.4 %collective-permute-start = (f32[8,1152]{1,0:T(8,128)S(1)}, f32[8,1152]{1,0:T(8,128)S(1)}, u32[]{:S(2)}, u32[]{:S(2)}) collective-permute-start(f32[8,1152]{1,0:T(8,128)S(1)} %get-tuple-element.29), channel_id=1, source_target_pairs={{0,8},{8,16},{16,24},{24,32},{32,40},{40,48},{48,56},{56,64},{64,7... | collective-permute-start | bytes 110600 | tf_op jit(solution)/shard_map/ppermute | solution.py:564
  8.2 4.9 %collective-permute-start.1 = (f32[16,128]{1,0:T(8,128)S(1)}, f32[16,128]{1,0:T(8,128)S(1)}, u32[]{:S(2)}, u32[]{:S(2)}) collective-permute-start(f32[16,128]{1,0:T(8,128)S(1)} %get-tuple-element.31), channel_id=1, source_target_pairs={{0,1},{1,2},{2,3},{3,4},{4,5},{5,6},{6,7},{7,0},{8,9},{9,10},{10,1... | collective-permute-start | bytes 24584 | tf_op jit(solution)/shard_map/ppermute | solution.py:565
  14.3 5.1 %collective-permute-start.2 = (f32[40,128]{1,0:T(8,128)S(1)}, f32[40,128]{1,0:T(8,128)S(1)}, u32[]{:S(2)}, u32[]{:S(2)}) collective-permute-start(f32[40,128]{1,0:T(8,128)S(1)} %relay.1), channel_id=1, source_target_pairs={{0,1},{1,2},{2,3},{3,4},{4,5},{5,6},{6,7},{7,0},{8,9},{9,10},{10,1... | collective-permute-start | bytes 61448 | tf_op jit(solution)/shard_map/ppermute | solution.py:572
  21.4 6.0 %copy-start = (f32[8,2,64,16]{2,3,1,0:T(8,128)S(1)}, f32[8,2,64,16]{2,3,1,0:T(8,128)}, u32[]{:S(2)}) copy-start(f32[8,2,64,16]{2,3,1,0:T(8,128)} %param.15) | copy-start | bytes 196612
  21.4 5.9 %copy-start.1 = (s32[64]{0:T(128)S(1)}, s32[64]{0:T(128)}, u32[]{:S(2)}) copy-start(s32[64]{0:T(128)} %param.17) | copy-start | bytes 772
  21.4 1.4 %collective-permute-start.3 = (f32[4,64,128]{2,1,0:T(8,128)S(1)}, f32[4,64,128]{2,1,0:T(8,128)S(1)}, u32[]{:S(2)}, u32[]{:S(2)}) collective-permute-start(f32[4,64,128]{2,1,0:T(8,128)S(1)} %get-tuple-element.52), channel_id=1, source_target_pairs={{0,1},{1,0},{2,3},{3,2},{4,5},{5,4},{6,7},{7,6},{8,9},{9,8},{10,11... | collective-permute-start | bytes 393224 | tf_op jit(solution)/shard_map/ppermute | solution.py:579
  22.9 5.6 %collective-permute-start.4 = (f32[64,128]{1,0:T(8,128)S(1)}, f32[64,128]{1,0:T(8,128)S(1)}, u32[]{:S(2)}, u32[]{:S(2)}) collective-permute-start(f32[64,128]{1,0:T(8,128)S(1)} %get-tuple-element.55), channel_id=1, source_target_pairs={{0,2},{1,3},{2,0},{3,1},{4,6},{5,7},{6,4},{7,5},{8,10},{9,11},{10,... | collective-permute-start | bytes 98312 | tf_op jit(solution)/shard_map/ppermute | solution.py:579
  23.0 5.5 %collective-permute-start.5 = (f32[64,128]{1,0:T(8,128)S(1)}, f32[64,128]{1,0:T(8,128)S(1)}, u32[]{:S(2)}, u32[]{:S(2)}) collective-permute-start(f32[64,128]{1,0:T(8,128)S(1)} %get-tuple-element.54), channel_id=1, source_target_pairs={{0,4},{1,5},{2,6},{3,7},{4,0},{5,1},{6,2},{7,3},{8,12},{9,13},{10,... | collective-permute-start | bytes 98312 | tf_op jit(solution)/shard_map/ppermute | solution.py:579
  23.8 5.8 %collective-permute-start.6 = (f32[64,128]{1,0:T(8,128)S(1)}, f32[64,128]{1,0:T(8,128)S(1)}, u32[]{:S(2)}, u32[]{:S(2)}) collective-permute-start(f32[64,128]{1,0:T(8,128)S(1)} %get-tuple-element.53), channel_id=1, source_target_pairs={{0,6},{1,7},{2,4},{3,5},{4,2},{5,3},{6,0},{7,1},{8,14},{9,15},{10,... | collective-permute-start | bytes 98312 | tf_op jit(solution)/shard_map/ppermute | solution.py:579

commit v12 on v10

--- a/solution.py
+++ b/solution.py
@@ -580,7 +580,7 @@
 
     got = swap(send, 1)
     keep = keep_planes(hi, lo, nf, edge, from_d, 1, 3)
-    b, c, d = (swap(keep[i - 1] + got[i], 2 * i) for i in (1, 2, 3))
+    b, c, d = (swap(keep[i - 1] + got[i], 2 * i) for i in (1, 3, 2))
     keep = keep_planes(hi, lo, nf, edge, from_d, 0, 1)
     factors = row_factors(from_x, rows_t, order)
     share = focal_share(factors, keep, got, b, c, d)

time: 51.1 us -> 51.2 us (level)
  waiting for transfers between devices: 4.59 us -> 5.58 us
  starting transfers between devices: 12.6 us -> 11.7 us
    ppermute x4, waiting for transfers between devices: 1.61 us -> 2.6 us  [swap(): return lax.ppermute(x, 'py', [(i, i ^ mask) for i in range(count_py)])]
    ppermute x4, starting transfers between devices: 4.56 us -> 3.66 us  [swap(): return lax.ppermute(x, 'py', [(i, i ^ mask) for i in range(count_py)])]
  transfers between devices with their start and end apart: 7 -> 7, of which waited for: 4 -> 5; matrix products, arithmetic and copies ran while one was open for 0% -> 0% of each run, Pallas kernels for 18% -> 18%
where the time goes in v12:
time: 51.2 us; the launch traced here: 51 us
  blocking collectives  20.3 us (40%)
  Pallas kernels  13.2 us (26%)
  starting transfers between devices  11.7 us (23%)
  waiting for transfers between devices  5.58 us (11%)
    all_to_all x1, blocking collectives, on_device(): return total(lax.all_to_all(share, 'px', 0, 0))  20.3 us
    ppermute x1, starting transfers between devices, on_device(): from_x = lax.ppermute(to_x, 'px', next_x)  7.27 us
    pallas_call x1, Pallas kernels, inner(): pl.pallas_call(inner_kernel, in_specs=[VMEM] + [HBM] * 6, out_specs=[VMEM...  4.42 us
    ppermute x4, starting transfers between devices, swap(): return lax.ppermute(x, 'py', [(i, i ^ mask) for i in range(count_py)])  3.66 us
    ppermute x4, waiting for transfers between devices, swap(): return lax.ppermute(x, 'py', [(i, i ^ mask) for i in range(count_py)])  2.6 us
    ppermute x1, waiting for transfers between devices, on_device(): from_d = lax.ppermute(relay(from_x, green), 'py', next_y)  2.54 us
    pallas_call x1, Pallas kernels, field(): pl.pallas_call(field_kernel, in_specs=[VMEM] * 14, out_specs=[VMEM] * 4,...  2.02 us
    pallas_call x1, Pallas kernels, outer(): pl.pallas_call(outer_kernel, in_specs=[VMEM] * 7, out_specs=VMEM, out_sha...  1.74 us
  transfers between devices with their start and end apart: 7, of which 5 were waited for; matrix products, arithmetic and copies ran while one was open for 0% of the time, Pallas kernels for 18%

profile of v12, /device:TPU:2, one launch (start us, length us, event | category | flops | bytes accessed | tf_op | source)
XLA Modules:
  0.0 51.0 jit_solution(13492483801890309561)
XLA Ops:
  0.0 0.9 %pack.1 = (f32[8,1152]{1,0:T(8,128)S(1)}, f32[16,128]{1,0:T(8,128)S(1)}, f32[16,1024]{1,0:T(8,128)S(1)}) custom-call(s32[16,1024]{1,0:T(8,128)} %lev_hbm.1, f32[8,2,16,64]{3,2,1,0:T(8,128)} %bitcast.10), custom_call_target="tpu_custom_call" | custom-call | tf_op jit(solution)/shard_map/pack/pallas_call | solution.py:78
  0.9 7.3 %collective-permute-start = (f32[8,1152]{1,0:T(8,128)S(1)}, f32[8,1152]{1,0:T(8,128)S(1)}, u32[]{:S(2)}, u32[]{:S(2)}) collective-permute-start(f32[8,1152]{1,0:T(8,128)S(1)} %get-tuple-element.29), channel_id=1, source_target_pairs={{0,8},{8,16},{16,24},{24,32},{32,40},{40,48},{48,56},{56,64},{64,7... | collective-permute-start | bytes 110600 | tf_op jit(solution)/shard_map/ppermute | solution.py:564
  8.2 0.0 collective-permute-start.1
  8.2 4.4 %inner.1 = (bf16[1280,1024]{1,0:T(8,128)(2,1)S(1)}, bf16[8,128,1024]{2,1,0:T(8,128)(2,1)S(1)}, bf16[8,128,1024]{2,1,0:T(8,128)(2,1)S(1)}, f32[32,128]{1,0:T(8,12...) custom-call(f32[16,1024]{1,0:T(8,128)S(1)} %get-tuple-element.30.lev, ...), custom_call_target="tpu_custom_call" | custom-call | tf_op jit(solution)/shard_map/inner/pallas_call | solution.py:233
  12.6 0.4 collective-permute-done.1.from_y_ref
  13.1 1.1 %middle.1 = (bf16[256,1024]{1,0:T(8,128)(2,1)S(1)}, f32[128,128]{1,0:T(8,128)S(1)}, bf16[1280,1024]{1,0:T(8,128)(2,1)S(1)}) custom-call(f32[16,1024]{1,0:T(8,128)S(1)} %get-tuple-element.30.lev_ref, f32[16,128]{1,0:T(8,128)S(1)} %collective-permute-done.1.from_y_ref, ...), custom_call_target="tpu_custom_call", output_to_operand_aliasing={{2}: (7, {})} | custom-call | tf_op jit(solution)/shard_map/middle/pallas_call | solution.py:325
  14.2 0.0 collective-permute-done.from_x_ref
  14.2 0.8 %collective-permute-start.2 = (f32[40,128]{1,0:T(8,128)S(1)}, f32[40,128]{1,0:T(8,128)S(1)}, u32[]{:S(2)}, u32[]{:S(2)}) collective-permute-start(f32[40,128]{1,0:T(8,128)S(1)} %relay.1), channel_id=1, source_target_pairs={{0,1},{1,2},{2,3},{3,4},{4,5},{5,6},{6,7},{7,0},{8,9},{9,10},{10,1... | collective-permute-start | bytes 61448 | tf_op jit(solution)/shard_map/ppermute | solution.py:572
  15.0 1.7 %outer.1._feat = bf16[1280,1024]{1,0:T(8,128)(2,1)S(1)} custom-call(f32[16,1024]{1,0:T(8,128)S(1)} %get-tuple-element.30.lev_ref, f32[8,1152]{1,0:T(8,128)S(1)} %collective-permute-done.from_x_ref, bf16[2,128,192]{2,1,0:T(8,128)(2,1)S(1)} %get-tuple-element.34.conv_ref, f32[128,1]{1,0:T(8,128)S(1)} %get-tuple-element.35.cb_ref, ...), custom_call_target="tpu_custom_call", output_to_operand_aliasing={{}: (6, {})} | custom-call | tf_op jit(solution)/shard_map/outer/pallas_call | solution.py:372
  16.8 2.5 %collective-permute-done.2.from_d_ref = f32[40,128]{1,0:T(8,128)S(1)} collective-permute-done((f32[40,128]{1,0:T(8,128)S(1)}, f32[40,128]{1,0:T(8,128)S(1)}, u32[]{:S(2)}, u32[]{:S(2)}) %collective-permute-start.2) | collective-permute-done | bytes 20512 | tf_op jit(solution)/shard_map/ppermute | solution.py:572
  19.3 2.0 %field.1 = (f32[4,64,128]{2,1,0:T(8,128)S(1)}, bf16[256,1024]{1,0:T(8,128)(2,1)S(1)}, f32[128,128]{1,0:T(8,128)S(1)}, bf16[1280,1024]{1,0:T(8,128)(2,1)S(1)}) custom-call(f32[16,1024]{1,0:T(8,128)S(1)} %get-tuple-element.30.lev_ref, f32[8,1152]{1,0:T(8,128)S(1)} %collective-permute-done.from_x_ref, ...), custom_call_target="tpu_custom_call", output_to_operand_aliasing={{1}: (11, {}), {2}: (12, {}), {3}: (13, {})} | custom-call | tf_op jit(solution)/shard_map/field/pallas_call | solution.py:444
  21.4 0.0 copy-start
  21.4 0.0 copy-start.1
  21.4 0.1 collective-permute-start.3
  21.5 0.8 %keep_planes.3 = f32[3,64,128]{2,1,0:T(8,128)S(1)} custom-call(bf16[8,128,1024]{2,1,0:T(8,128)(2,1)S(1)} %get-tuple-element.44.hi_ref, bf16[8,128,1024]{2,1,0:T(8,128)(2,1)S(1)} %get-tuple-element.45.lo_ref, bf16[256,1024]{1,0:T(8,128)(2,1)S(1)} %get-tuple-element.50.nf_ref, f32[128,128]{1,0:T(8,128)S(1)} %get-tuple-element.51.edge_ref, ...), custom_call_target="tpu_custom_call" | custom-call | tf_op jit(solution)/shard_map/keep_planes/pallas_call | solution.py:470
  22.3 0.5 collective-permute-done.3.got_ref
  22.8 0.1 collective-permute-start.4
  22.9 0.7 %collective-permute-start.5 = (f32[64,128]{1,0:T(8,128)S(1)}, f32[64,128]{1,0:T(8,128)S(1)}, u32[]{:S(2)}, u32[]{:S(2)}) collective-permute-start(f32[64,128]{1,0:T(8,128)S(1)} %get-tuple-element.54), channel_id=1, source_target_pairs={{0,6},{1,7},{2,4},{3,5},{4,2},{5,3},{6,0},{7,1},{8,14},{9,15},{10,... | collective-permute-start | bytes 98312 | tf_op jit(solution)/shard_map/ppermute | solution.py:579
  23.6 2.8 %collective-permute-start.6 = (f32[64,128]{1,0:T(8,128)S(1)}, f32[64,128]{1,0:T(8,128)S(1)}, u32[]{:S(2)}, u32[]{:S(2)}) collective-permute-start(f32[64,128]{1,0:T(8,128)S(1)} %get-tuple-element.53), channel_id=1, source_target_pairs={{0,4},{1,5},{2,6},{3,7},{4,0},{5,1},{6,2},{7,3},{8,12},{9,13},{10,... | collective-permute-start | bytes 98312 | tf_op jit(solution)/shard_map/ppermute | solution.py:579
  26.4 0.0 copy-done
  26.4 0.0 copy-done.1
  26.4 0.6 %row_factors.1.factor_ref = bf16[512,192]{1,0:T(8,128)(2,1)S(1)} custom-call(f32[8,1152]{1,0:T(8,128)S(1)} %collective-permute-done.from_x_ref, f32[8,2,16,64]{3,2,1,0:T(8,128)S(1)} %bitcast.11, s32[1,64]{1,0:T(1,128)S(1)} %bitcast.12), custom_call_target="tpu_custom_call" | custom-call | tf_op jit(solution)/shard_map/row_factors/pallas_call | solution.py:500
  27.0 0.6 %keep_planes.2.keep_ref = f32[1,64,128]{2,1,0:T(8,128)S(1)} custom-call(bf16[8,128,1024]{2,1,0:T(8,128)(2,1)S(1)} %get-tuple-element.44.hi_ref, bf16[8,128,1024]{2,1,0:T(8,128)(2,1)S(1)} %get-tuple-element.45.lo_ref, bf16[256,1024]{1,0:T(8,128)(2,1)S(1)} %get-tuple-element.50.nf_ref, f32[128,128]{1,0:T(8,128)S(1)} %get-tuple-element.51.edge_ref, ...), custom_call_target="tpu_custom_call" | custom-call | tf_op jit(solution)/shard_map/keep_planes/pallas_call | solution.py:470
  27.6 0.0 collective-permute-done.4.b_ref
  27.6 1.2 %collective-permute-done.5.c_ref = f32[64,128]{1,0:T(8,128)S(1)} collective-permute-done((f32[64,128]{1,0:T(8,128)S(1)}, f32[64,128]{1,0:T(8,128)S(1)}, u32[]{:S(2)}, u32[]{:S(2)}) %collective-permute-start.5) | collective-permute-done | bytes 32800 | tf_op jit(solution)/shard_map/ppermute | solution.py:579
  28.8 0.9 %collective-permute-done.6.d_ref = f32[64,128]{1,0:T(8,128)S(1)} collective-permute-done((f32[64,128]{1,0:T(8,128)S(1)}, f32[64,128]{1,0:T(8,128)S(1)}, u32[]{:S(2)}, u32[]{:S(2)}) %collective-permute-start.6) | collective-permute-done | bytes 32800 | tf_op jit(solution)/shard_map/ppermute | solution.py:579
  29.7 0.3 focal_share.1
  30.0 20.3 %all_to_all.5.x_ref = f32[32,8,128]{2,1,0:T(8,128)S(1)} all-to-all(f32[32,8,128]{2,1,0:T(8,128)S(1)} %focal_share.1), channel_id=1, replica_groups=mesh['px'=32,'py'=8] {'px'}, dimensions={0} | all-to-all | bytes 262144 | tf_op jit(solution)/shard_map/all_to_all | solution.py:587
  50.3 0.7 %total.1 = f32[1,2,512]{2,1,0:T(2,128)} custom-call(f32[32,8,128]{2,1,0:T(8,128)S(1)} %all_to_all.5.x_ref), custom_call_target="tpu_custom_call" | custom-call | tf_op jit(solution)/shard_map/total/pallas_call | solution.py:543
  (2 shorter events, 0.0 us)
Async XLA Ops:
  0.9 13.3 %collective-permute-start = (f32[8,1152]{1,0:T(8,128)S(1)}, f32[8,1152]{1,0:T(8,128)S(1)}, u32[]{:S(2)}, u32[]{:S(2)}) collective-permute-start(f32[8,1152]{1,0:T(8,128)S(1)} %get-tuple-element.29), channel_id=1, source_target_pairs={{0,8},{8,16},{16,24},{24,32},{32,40},{40,48},{48,56},{56,64},{64,7... | collective-permute-start | bytes 110600 | tf_op jit(solution)/shard_map/ppermute | solution.py:564
  8.2 4.9 %collective-permute-start.1 = (f32[16,128]{1,0:T(8,128)S(1)}, f32[16,128]{1,0:T(8,128)S(1)}, u32[]{:S(2)}, u32[]{:S(2)}) collective-permute-start(f32[16,128]{1,0:T(8,128)S(1)} %get-tuple-element.31), channel_id=1, source_target_pairs={{0,1},{1,2},{2,3},{3,4},{4,5},{5,6},{6,7},{7,0},{8,9},{9,10},{10,1... | collective-permute-start | bytes 24584 | tf_op jit(solution)/shard_map/ppermute | solution.py:565
  14.2 5.1 %collective-permute-start.2 = (f32[40,128]{1,0:T(8,128)S(1)}, f32[40,128]{1,0:T(8,128)S(1)}, u32[]{:S(2)}, u32[]{:S(2)}) collective-permute-start(f32[40,128]{1,0:T(8,128)S(1)} %relay.1), channel_id=1, source_target_pairs={{0,1},{1,2},{2,3},{3,4},{4,5},{5,6},{6,7},{7,0},{8,9},{9,10},{10,1... | collective-permute-start | bytes 61448 | tf_op jit(solution)/shard_map/ppermute | solution.py:572
  21.4 5.1 %copy-start = (f32[8,2,64,16]{2,3,1,0:T(8,128)S(1)}, f32[8,2,64,16]{2,3,1,0:T(8,128)}, u32[]{:S(2)}) copy-start(f32[8,2,64,16]{2,3,1,0:T(8,128)} %param.15) | copy-start | bytes 196612
  21.4 5.0 %copy-start.1 = (s32[64]{0:T(128)S(1)}, s32[64]{0:T(128)}, u32[]{:S(2)}) copy-start(s32[64]{0:T(128)} %param.17) | copy-start | bytes 772
  21.4 1.4 %collective-permute-start.3 = (f32[4,64,128]{2,1,0:T(8,128)S(1)}, f32[4,64,128]{2,1,0:T(8,128)S(1)}, u32[]{:S(2)}, u32[]{:S(2)}) collective-permute-start(f32[4,64,128]{2,1,0:T(8,128)S(1)} %get-tuple-element.52), channel_id=1, source_target_pairs={{0,1},{1,0},{2,3},{3,2},{4,5},{5,4},{6,7},{7,6},{8,9},{9,8},{10,11... | collective-permute-start | bytes 393224 | tf_op jit(solution)/shard_map/ppermute | solution.py:579
  22.8 4.7 %collective-permute-start.4 = (f32[64,128]{1,0:T(8,128)S(1)}, f32[64,128]{1,0:T(8,128)S(1)}, u32[]{:S(2)}, u32[]{:S(2)}) collective-permute-start(f32[64,128]{1,0:T(8,128)S(1)} %get-tuple-element.55), channel_id=1, source_target_pairs={{0,2},{1,3},{2,0},{3,1},{4,6},{5,7},{6,4},{7,5},{8,10},{9,11},{10,... | collective-permute-start | bytes 98312 | tf_op jit(solution)/shard_map/ppermute | solution.py:579
  22.9 5.8 %collective-permute-start.5 = (f32[64,128]{1,0:T(8,128)S(1)}, f32[64,128]{1,0:T(8,128)S(1)}, u32[]{:S(2)}, u32[]{:S(2)}) collective-permute-start(f32[64,128]{1,0:T(8,128)S(1)} %get-tuple-element.54), channel_id=1, source_target_pairs={{0,6},{1,7},{2,4},{3,5},{4,2},{5,3},{6,0},{7,1},{8,14},{9,15},{10,... | collective-permute-start | bytes 98312 | tf_op jit(solution)/shard_map/ppermute | solution.py:579
  23.6 6.0 %collective-permute-start.6 = (f32[64,128]{1,0:T(8,128)S(1)}, f32[64,128]{1,0:T(8,128)S(1)}, u32[]{:S(2)}, u32[]{:S(2)}) collective-permute-start(f32[64,128]{1,0:T(8,128)S(1)} %get-tuple-element.53), channel_id=1, source_target_pairs={{0,4},{1,5},{2,6},{3,7},{4,0},{5,1},{6,2},{7,3},{8,12},{9,13},{10,... | collective-permute-start | bytes 98312 | tf_op jit(solution)/shard_map/ppermute | solution.py:579

commit v13 on v11

--- a/solution.py
+++ b/solution.py
@@ -22,6 +22,7 @@
 V = 64
 HALO = 4
 SHIFT = 3
+UP = 6
 PILLAR_ROWS = ROWS + KS - 1
 SLOT = 3 * LEVELS
 WINDOW = 4 * SLOT
@@ -69,8 +70,9 @@
         copy.wait()
     lev = lev_ref[...].astype(F32)
     out_ref[...] = lev
-    to_x_ref[:, :COLS] = lev[8:, :]
-    to_x_ref[:, COLS:] = jnp.concatenate([rows_ref[0, 8:, :], rows_ref[1, 8:, :]], axis=1)
+    for t in range(COLS // 128):
+        to_x_ref[UP * t : UP * (t + 1), :] = lev[ROWS - UP :, 128 * t : 128 * (t + 1)]
+    to_x_ref[UP * COLS // 128 :, :] = jnp.concatenate([rows_ref[0, 8:, :], rows_ref[1, 8:, :]], axis=1)
     to_y_ref[...] = lev[:, COLS - 128 :]
 
 
@@ -80,7 +82,7 @@
         in_specs=[HBM] * 2,
         out_specs=[VMEM] * 3,
         out_shape=[
-            jax.ShapeDtypeStruct((8, COLS + 128), F32),
+            jax.ShapeDtypeStruct((UP * COLS // 128 + 8, 128), F32),
             jax.ShapeDtypeStruct((ROWS, 128), F32),
             jax.ShapeDtypeStruct((ROWS, COLS), F32),
         ],
@@ -95,7 +97,8 @@
 
 
 def relay_kernel(from_x_ref, green_ref, out_ref):
-    out_ref[:8, :] = from_x_ref[:, COLS - 128 : COLS]
+    at = UP * (COLS // 128 - 1)
+    out_ref[:8, :] = from_x_ref[at : at + 8, :]
     out_ref[8:, :] = green_ref[...]
 
 
@@ -341,14 +344,15 @@
 def outer_kernel(
     lev_ref, from_x_ref, conv_ref, cb_ref, mix_ref, mb_ref, _, feat_ref, ext_ref, hot_ref
 ):
-    ext = jnp.concatenate([from_x_ref[:, :COLS], lev_ref[:8, :]], axis=0)
+    tiles = [from_x_ref[UP * t : UP * (t + 1), :] for t in range(COLS // 128)]
+    ext = jnp.concatenate([jnp.concatenate(tiles, axis=1), lev_ref[:2, :]], axis=0)
     for b in range(3):
         ext_ref[b] = pltpu.roll(ext, 3 - b, 1)[:, 128:]
     wide = COLS - 128
     level_ids = iota((LEVELS, wide), 0).astype(F32)
-    for e in range(2, 10):
+    for e in range(8):
         for b in range(3):
-            at = (e - 2) * SLOT + b * LEVELS
+            at = e * SLOT + b * LEVELS
             hot_ref[at : at + LEVELS, :] = one_hot(ext_ref[b, e : e + 1, :], level_ids)
     conv_bias = jnp.broadcast_to(cb_ref[...], (2 * HID, wide))
     mix_bias = jnp.broadcast_to(mb_ref[...], (2 * HID, wide))
@@ -376,7 +380,7 @@
         out_shape=jax.ShapeDtypeStruct(feat.shape, BF16),
         input_output_aliases={6: 0},
         scratch_shapes=[
-            pltpu.VMEM((3, 16, wide), F32),
+            pltpu.VMEM((3, 8, wide), F32),
             pltpu.VMEM((8 * SLOT, wide), BF16),
         ],
         compiler_params=params(8),
@@ -413,16 +417,16 @@
     hi_ref, lo_ref, _nf, _edge, _feat, send_ref, nf_ref, edge_ref, feat_ref, ext_ref, hot_ref,
 ):
     first_y = lax.axis_index("py") == 0
-    tile = jnp.concatenate([from_x_ref[:, :128], lev_ref[:8, :128]], axis=0)
-    left = jnp.concatenate([from_d_ref[:8, :], from_y_ref[:8, :]], axis=0)
+    tile = jnp.concatenate([from_x_ref[:UP, :], lev_ref[:2, :128]], axis=0)
+    left = jnp.concatenate([from_d_ref[:UP, :], from_y_ref[:2, :]], axis=0)
     tile_windows(left, tile, first_y, ext_ref)
     level_ids = iota((LEVELS, 128), 0).astype(F32)
-    for e in range(2, 10):
+    for e in range(8):
         for b in range(3):
             row = one_hot(ext_ref[b, e : e + 1, :], level_ids)
             for w in range(3):
-                if 0 <= e - 2 - 2 * w < 4:
-                    at = (e - 2 - 2 * w) * SLOT + b * LEVELS
+                if 0 <= e - 2 * w < 4:
+                    at = (e - 2 * w) * SLOT + b * LEVELS
                     hot_ref[at : at + LEVELS, w * 128 : (w + 1) * 128] = row
     pre = [
         jnp.dot(conv_ref[0], hot_ref[:, :256], preferred_element_type=F32),
@@ -453,7 +457,7 @@
         ],
         input_output_aliases={11: 1, 12: 2, 13: 3},
         scratch_shapes=[
-            pltpu.VMEM((3, 16, 128), F32),
+            pltpu.VMEM((3, 8, 128), F32),
             pltpu.VMEM((WINDOW, 384), BF16),
         ],
         compiler_params=params(12),
@@ -480,7 +484,7 @@
 def rows_kernel(from_x_ref, rows_ref, order_ref, out_ref):
     z = lax.axis_index("py")
     green = jnp.concatenate([rows_ref[z, 0], rows_ref[z, 1]], axis=1)
-    green = jnp.concatenate([from_x_ref[:, COLS:], green], axis=0)
+    green = jnp.concatenate([from_x_ref[UP * COLS // 128 :, :], green], axis=0)
     n = ROWS + 8
     green = jnp.concatenate(split2(green), axis=0)
     pick = (order_ref[...] == iota((U, U), 0)).astype(BF16)

time: 51.1 us -> 50.9 us (level)
  no operation moved by 1% of the time
where the time goes in v13:
time: 50.9 us; the launch traced here: 50.7 us
  blocking collectives  20.1 us (39%)
  Pallas kernels  13.3 us (26%)
  starting transfers between devices  13 us (26%)
  waiting for transfers between devices  4.15 us (8%)
    all_to_all x1, blocking collectives, on_device(): return total(lax.all_to_all(share, 'px', 0, 0))  20.1 us
    ppermute x1, starting transfers between devices, on_device(): from_x = lax.ppermute(to_x, 'px', next_x)  7.27 us
    pallas_call x1, Pallas kernels, inner(): pl.pallas_call(inner_kernel, in_specs=[VMEM] + [HBM] * 6, out_specs=[VMEM...  4.85 us
    ppermute x4, starting transfers between devices, swap(): return lax.ppermute(x, 'py', [(i, i ^ mask) for i in range(count_py)])  4.56 us
    ppermute x1, waiting for transfers between devices, on_device(): from_d = lax.ppermute(relay(from_x, green), 'py', next_y)  2.52 us
    pallas_call x1, Pallas kernels, field(): pl.pallas_call(field_kernel, in_specs=[VMEM] * 14, out_specs=[VMEM] * 4,...  2 us
    ppermute x4, waiting for transfers between devices, swap(): return lax.ppermute(x, 'py', [(i, i ^ mask) for i in range(count_py)])  1.61 us
    pallas_call x2, Pallas kernels, keep_planes(): pl.pallas_call(keep_kernel, in_specs=[VMEM] * 5, out_specs=VMEM, out_shap...  1.4 us
  transfers between devices with their start and end apart: 7, of which 3 were waited for; matrix products, arithmetic and copies ran while one was open for 0% of the time, Pallas kernels for 18%

profile of v13, /device:TPU:2, one launch (start us, length us, event | category | flops | bytes accessed | tf_op | source)
XLA Modules:
  0.0 50.7 jit_solution(9522833259164710275)
XLA Ops:
  0.0 0.9 %pack.1 = (f32[56,128]{1,0:T(8,128)S(1)}, f32[16,128]{1,0:T(8,128)S(1)}, f32[16,1024]{1,0:T(8,128)S(1)}) custom-call(s32[16,1024]{1,0:T(8,128)} %lev_hbm.1, f32[8,2,16,64]{3,2,1,0:T(8,128)} %bitcast.10), custom_call_target="tpu_custom_call" | custom-call | tf_op jit(solution)/shard_map/pack/pallas_call | solution.py:80
  0.9 7.3 %collective-permute-start = (f32[56,128]{1,0:T(8,128)S(1)}, f32[56,128]{1,0:T(8,128)S(1)}, u32[]{:S(2)}, u32[]{:S(2)}) collective-permute-start(f32[56,128]{1,0:T(8,128)S(1)} %get-tuple-element.29), channel_id=1, source_target_pairs={{0,8},{8,16},{16,24},{24,32},{32,40},{40,48},{48,56},{56,64},{64,7... | collective-permute-start | bytes 86024 | tf_op jit(solution)/shard_map/ppermute | solution.py:568
  8.2 0.0 collective-permute-start.1
  8.2 4.9 %inner.1 = (bf16[1280,1024]{1,0:T(8,128)(2,1)S(1)}, bf16[8,128,1024]{2,1,0:T(8,128)(2,1)S(1)}, bf16[8,128,1024]{2,1,0:T(8,128)(2,1)S(1)}, f32[32,128]{1,0:T(8,12...) custom-call(f32[16,1024]{1,0:T(8,128)S(1)} %get-tuple-element.30.lev, ...), custom_call_target="tpu_custom_call" | custom-call | tf_op jit(solution)/shard_map/inner/pallas_call | solution.py:236
  13.1 0.0 collective-permute-done.1.from_y_ref
  13.1 1.2 %middle.1 = (bf16[256,1024]{1,0:T(8,128)(2,1)S(1)}, f32[128,128]{1,0:T(8,128)S(1)}, bf16[1280,1024]{1,0:T(8,128)(2,1)S(1)}) custom-call(f32[16,1024]{1,0:T(8,128)S(1)} %get-tuple-element.30.lev_ref, f32[16,128]{1,0:T(8,128)S(1)} %collective-permute-done.1.from_y_ref, ...), custom_call_target="tpu_custom_call", output_to_operand_aliasing={{2}: (7, {})} | custom-call | tf_op jit(solution)/shard_map/middle/pallas_call | solution.py:328
  14.3 0.0 collective-permute-done.from_x_ref
  14.3 1.2 %collective-permute-start.2 = (f32[40,128]{1,0:T(8,128)S(1)}, f32[40,128]{1,0:T(8,128)S(1)}, u32[]{:S(2)}, u32[]{:S(2)}) collective-permute-start(f32[40,128]{1,0:T(8,128)S(1)} %relay.1), channel_id=1, source_target_pairs={{0,1},{1,2},{2,3},{3,4},{4,5},{5,6},{6,7},{7,0},{8,9},{9,10},{10,1... | collective-permute-start | bytes 61448 | tf_op jit(solution)/shard_map/ppermute | solution.py:576
  15.5 1.3 %outer.1._feat = bf16[1280,1024]{1,0:T(8,128)(2,1)S(1)} custom-call(f32[16,1024]{1,0:T(8,128)S(1)} %get-tuple-element.30.lev_ref, f32[56,128]{1,0:T(8,128)S(1)} %collective-permute-done.from_x_ref, bf16[2,128,192]{2,1,0:T(8,128)(2,1)S(1)} %get-tuple-element.34.conv_ref, f32[128,1]{1,0:T(8,128)S(1)} %get-tuple-element.35.cb_ref, ...), custom_call_target="tpu_custom_call", output_to_operand_aliasing={{}: (6, {})} | custom-call | tf_op jit(solution)/shard_map/outer/pallas_call | solution.py:376
  16.9 2.5 %collective-permute-done.2.from_d_ref = f32[40,128]{1,0:T(8,128)S(1)} collective-permute-done((f32[40,128]{1,0:T(8,128)S(1)}, f32[40,128]{1,0:T(8,128)S(1)}, u32[]{:S(2)}, u32[]{:S(2)}) %collective-permute-start.2) | collective-permute-done | bytes 20512 | tf_op jit(solution)/shard_map/ppermute | solution.py:576
  19.4 2.0 %field.1 = (f32[4,64,128]{2,1,0:T(8,128)S(1)}, bf16[256,1024]{1,0:T(8,128)(2,1)S(1)}, f32[128,128]{1,0:T(8,128)S(1)}, bf16[1280,1024]{1,0:T(8,128)(2,1)S(1)}) custom-call(f32[16,1024]{1,0:T(8,128)S(1)} %get-tuple-element.30.lev_ref, f32[56,128]{1,0:T(8,128)S(1)} %collective-permute-done.from_x_ref, ...), custom_call_target="tpu_custom_call", output_to_operand_aliasing={{1}: (11, {}), {2}: (12, {}), {3}: (13, {})} | custom-call | tf_op jit(solution)/shard_map/field/pallas_call | solution.py:448
  21.4 0.0 copy-start
  21.4 0.0 copy-start.1
  21.4 0.1 collective-permute-start.3
  21.5 0.8 %keep_planes.3 = f32[3,64,128]{2,1,0:T(8,128)S(1)} custom-call(bf16[8,128,1024]{2,1,0:T(8,128)(2,1)S(1)} %get-tuple-element.44.hi_ref, bf16[8,128,1024]{2,1,0:T(8,128)(2,1)S(1)} %get-tuple-element.45.lo_ref, bf16[256,1024]{1,0:T(8,128)(2,1)S(1)} %get-tuple-element.50.nf_ref, f32[128,128]{1,0:T(8,128)S(1)} %get-tuple-element.51.edge_ref, ...), custom_call_target="tpu_custom_call" | custom-call | tf_op jit(solution)/shard_map/keep_planes/pallas_call | solution.py:474
  22.4 0.5 collective-permute-done.3.got_ref
  22.9 0.1 collective-permute-start.4
  23.0 0.8 %collective-permute-start.5 = (f32[64,128]{1,0:T(8,128)S(1)}, f32[64,128]{1,0:T(8,128)S(1)}, u32[]{:S(2)}, u32[]{:S(2)}) collective-permute-start(f32[64,128]{1,0:T(8,128)S(1)} %get-tuple-element.54), channel_id=1, source_target_pairs={{0,4},{1,5},{2,6},{3,7},{4,0},{5,1},{6,2},{7,3},{8,12},{9,13},{10,... | collective-permute-start | bytes 98312 | tf_op jit(solution)/shard_map/ppermute | solution.py:583
  23.8 3.5 %collective-permute-start.6 = (f32[64,128]{1,0:T(8,128)S(1)}, f32[64,128]{1,0:T(8,128)S(1)}, u32[]{:S(2)}, u32[]{:S(2)}) collective-permute-start(f32[64,128]{1,0:T(8,128)S(1)} %get-tuple-element.53), channel_id=1, source_target_pairs={{0,6},{1,7},{2,4},{3,5},{4,2},{5,3},{6,0},{7,1},{8,14},{9,15},{10,... | collective-permute-start | bytes 98312 | tf_op jit(solution)/shard_map/ppermute | solution.py:583
  27.4 0.0 copy-done
  27.4 0.0 copy-done.1
  27.4 0.6 %row_factors.1.factor_ref = bf16[512,192]{1,0:T(8,128)(2,1)S(1)} custom-call(f32[56,128]{1,0:T(8,128)S(1)} %collective-permute-done.from_x_ref, f32[8,2,16,64]{3,2,1,0:T(8,128)S(1)} %bitcast.11, s32[1,64]{1,0:T(1,128)S(1)} %bitcast.12), custom_call_target="tpu_custom_call" | custom-call | tf_op jit(solution)/shard_map/row_factors/pallas_call | solution.py:504
  27.9 0.6 %keep_planes.2.keep_ref = f32[1,64,128]{2,1,0:T(8,128)S(1)} custom-call(bf16[8,128,1024]{2,1,0:T(8,128)(2,1)S(1)} %get-tuple-element.44.hi_ref, bf16[8,128,1024]{2,1,0:T(8,128)(2,1)S(1)} %get-tuple-element.45.lo_ref, bf16[256,1024]{1,0:T(8,128)(2,1)S(1)} %get-tuple-element.50.nf_ref, f32[128,128]{1,0:T(8,128)S(1)} %get-tuple-element.51.edge_ref, ...), custom_call_target="tpu_custom_call" | custom-call | tf_op jit(solution)/shard_map/keep_planes/pallas_call | solution.py:474
  28.5 0.0 collective-permute-done.4.b_ref
  28.5 0.0 collective-permute-done.5.c_ref
  28.5 1.1 %collective-permute-done.6.d_ref = f32[64,128]{1,0:T(8,128)S(1)} collective-permute-done((f32[64,128]{1,0:T(8,128)S(1)}, f32[64,128]{1,0:T(8,128)S(1)}, u32[]{:S(2)}, u32[]{:S(2)}) %collective-permute-start.6) | collective-permute-done | bytes 32800 | tf_op jit(solution)/shard_map/ppermute | solution.py:583
  29.7 0.3 focal_share.1
  29.9 20.1 %all_to_all.5.x_ref = f32[32,8,128]{2,1,0:T(8,128)S(1)} all-to-all(f32[32,8,128]{2,1,0:T(8,128)S(1)} %focal_share.1), channel_id=1, replica_groups=mesh['px'=32,'py'=8] {'px'}, dimensions={0} | all-to-all | bytes 262144 | tf_op jit(solution)/shard_map/all_to_all | solution.py:591
  50.0 0.7 %total.1 = f32[1,2,512]{2,1,0:T(2,128)} custom-call(f32[32,8,128]{2,1,0:T(8,128)S(1)} %all_to_all.5.x_ref), custom_call_target="tpu_custom_call" | custom-call | tf_op jit(solution)/shard_map/total/pallas_call | solution.py:547
  (2 shorter events, 0.0 us)
Async XLA Ops:
  0.9 13.4 %collective-permute-start = (f32[56,128]{1,0:T(8,128)S(1)}, f32[56,128]{1,0:T(8,128)S(1)}, u32[]{:S(2)}, u32[]{:S(2)}) collective-permute-start(f32[56,128]{1,0:T(8,128)S(1)} %get-tuple-element.29), channel_id=1, source_target_pairs={{0,8},{8,16},{16,24},{24,32},{32,40},{40,48},{48,56},{56,64},{64,7... | collective-permute-start | bytes 86024 | tf_op jit(solution)/shard_map/ppermute | solution.py:568
  8.2 4.9 %collective-permute-start.1 = (f32[16,128]{1,0:T(8,128)S(1)}, f32[16,128]{1,0:T(8,128)S(1)}, u32[]{:S(2)}, u32[]{:S(2)}) collective-permute-start(f32[16,128]{1,0:T(8,128)S(1)} %get-tuple-element.31), channel_id=1, source_target_pairs={{0,1},{1,2},{2,3},{3,4},{4,5},{5,6},{6,7},{7,0},{8,9},{9,10},{10,1... | collective-permute-start | bytes 24584 | tf_op jit(solution)/shard_map/ppermute | solution.py:569
  14.3 5.1 %collective-permute-start.2 = (f32[40,128]{1,0:T(8,128)S(1)}, f32[40,128]{1,0:T(8,128)S(1)}, u32[]{:S(2)}, u32[]{:S(2)}) collective-permute-start(f32[40,128]{1,0:T(8,128)S(1)} %relay.1), channel_id=1, source_target_pairs={{0,1},{1,2},{2,3},{3,4},{4,5},{5,6},{6,7},{7,0},{8,9},{9,10},{10,1... | collective-permute-start | bytes 61448 | tf_op jit(solution)/shard_map/ppermute | solution.py:576
  21.4 6.0 %copy-start = (f32[8,2,64,16]{2,3,1,0:T(8,128)S(1)}, f32[8,2,64,16]{2,3,1,0:T(8,128)}, u32[]{:S(2)}) copy-start(f32[8,2,64,16]{2,3,1,0:T(8,128)} %param.15) | copy-start | bytes 196612
  21.4 5.9 %copy-start.1 = (s32[64]{0:T(128)S(1)}, s32[64]{0:T(128)}, u32[]{:S(2)}) copy-start(s32[64]{0:T(128)} %param.17) | copy-start | bytes 772
  21.4 1.4 %collective-permute-start.3 = (f32[4,64,128]{2,1,0:T(8,128)S(1)}, f32[4,64,128]{2,1,0:T(8,128)S(1)}, u32[]{:S(2)}, u32[]{:S(2)}) collective-permute-start(f32[4,64,128]{2,1,0:T(8,128)S(1)} %get-tuple-element.52), channel_id=1, source_target_pairs={{0,1},{1,0},{2,3},{3,2},{4,5},{5,4},{6,7},{7,6},{8,9},{9,8},{10,11... | collective-permute-start | bytes 393224 | tf_op jit(solution)/shard_map/ppermute | solution.py:583
  22.9 5.6 %collective-permute-start.4 = (f32[64,128]{1,0:T(8,128)S(1)}, f32[64,128]{1,0:T(8,128)S(1)}, u32[]{:S(2)}, u32[]{:S(2)}) collective-permute-start(f32[64,128]{1,0:T(8,128)S(1)} %get-tuple-element.55), channel_id=1, source_target_pairs={{0,2},{1,3},{2,0},{3,1},{4,6},{5,7},{6,4},{7,5},{8,10},{9,11},{10,... | collective-permute-start | bytes 98312 | tf_op jit(solution)/shard_map/ppermute | solution.py:583
  23.0 5.5 %collective-permute-start.5 = (f32[64,128]{1,0:T(8,128)S(1)}, f32[64,128]{1,0:T(8,128)S(1)}, u32[]{:S(2)}, u32[]{:S(2)}) collective-permute-start(f32[64,128]{1,0:T(8,128)S(1)} %get-tuple-element.54), channel_id=1, source_target_pairs={{0,4},{1,5},{2,6},{3,7},{4,0},{5,1},{6,2},{7,3},{8,12},{9,13},{10,... | collective-permute-start | bytes 98312 | tf_op jit(solution)/shard_map/ppermute | solution.py:583
  23.8 5.8 %collective-permute-start.6 = (f32[64,128]{1,0:T(8,128)S(1)}, f32[64,128]{1,0:T(8,128)S(1)}, u32[]{:S(2)}, u32[]{:S(2)}) collective-permute-start(f32[64,128]{1,0:T(8,128)S(1)} %get-tuple-element.53), channel_id=1, source_target_pairs={{0,6},{1,7},{2,4},{3,5},{4,2},{5,3},{6,0},{7,1},{8,14},{9,15},{10,... | collective-permute-start | bytes 98312 | tf_op jit(solution)/shard_map/ppermute | solution.py:583
